TPU v7x, 128 devices: a whole 4x4x4 slice. The times are simulated.
128 devices in a mesh: space: 32 (over z, y, core), mode: 4 (over x).
Axes of the slice: x: 4, y: 4, z: 4, core: 2. Of those that a mesh axis runs over, the one named last changes fastest.
Arguments:
- velocity: float32 [3, 512, 512, 256], P(None, 'space', 'mode'), may hold values from -6 to 6
- basis: float32 [32, 3145728], P('mode', 'space'), may hold values from -42 to 42
- levels: float32 [8], replicated, may hold values from 0.02 to 0.15
- profile_index: int32 [256], replicated, may hold values from 0 to 7
- advect: float32 [256], replicated, may hold values from 0 to 0.4
Outputs:
- modes: float32 [32, 3145728], P('mode', 'space')
- sigma: float32 [32], replicated
Inputs may be any that keep to these rules, and one draw needn't show every extreme that they name: `profile_index`: each entry picks one of the 8 viscosity levels.
All inputs are finite; a program needn't handle non-finite values.
Results may differ from a plain program's by a relative error of at most 0.0055.
Values sent between devices are 32-bit elements; how exact they have to be, the bound alone decides.
No kernel may reach another device: no remote copies, remote signals or barrier semaphores. Data moves between devices by JAX's collectives and lax.ppermute only.
A program may use at most 128 MiB of HBM per device.

v0:
```python
import functools

import jax
import jax.numpy as jnp
import numpy as np
from jax import lax
from jax.experimental import pallas as pl
from jax.experimental.pallas import tpu as pltpu
from jax.sharding import PartitionSpec as P

STRIDE = 4
MODES = 32
SWEEPS = 2
COUNT = 34
ROWS = 40
LANES = 128
PAD = 8
VMEM_SPEC = pl.BlockSpec(memory_space=pltpu.VMEM)
HBM_SPEC = pl.BlockSpec(memory_space=pltpu.HBM)


PLACE = np.array([0, 1] + list(range(PAD, PAD + MODES)))


def near(x):
    return pltpu.with_memory_space_constraint(x, pltpu.VMEM)


def far(x):
    return pltpu.with_memory_space_constraint(x, pltpu.HBM)


def pair_tables():
    rounds = COUNT - 1
    partner = np.tile(np.arange(LANES, dtype=np.int32), (ROWS, 1))
    orient = np.ones((ROWS, LANES), np.float32)
    for turn in range(rounds):
        players = [0] + [1 + (i - 1 + turn) % rounds for i in range(1, COUNT)]
        for k in range(COUNT // 2):
            lead, trail = PLACE[players[k]], PLACE[players[COUNT - 1 - k]]
            partner[turn, lead] = trail
            partner[turn, trail] = lead
            orient[turn, lead] = -1.0
    keep = np.zeros((1, LANES), np.int32)
    keep[0, :MODES] = PLACE[:MODES]
    return partner, orient, keep


def pack_kernel(vel_hbm, zfirst_ref, zlast_ref, buf, sems):
    comps, cx, cz, _ = vel_hbm.shape
    copies = []
    for c in range(comps):
        for side, at in enumerate((0, cz - PAD)):
            copies.append(
                pltpu.make_async_copy(
                    vel_hbm.at[c, :, pl.ds(at, PAD), :], buf.at[c, side], sems.at[c, side]
                )
            )
    for copy in copies:
        copy.start()
    for copy in copies:
        copy.wait()
    for c in range(comps):
        for i in range(cx):
            for k in range(2):
                row, last = (2 * c + k) * cx + i, PAD - 2 + k
                zfirst_ref[row : row + 1, :] = buf[c, 0, i, k : k + 1, :]
                zlast_ref[row : row + 1, :] = buf[c, 1, i, last : last + 1, :]


def pack(velocity):
    comps, cx, _, ny = velocity.shape
    edge = pltpu.VMEM((comps * 2 * cx, ny), jnp.float32)
    return pl.pallas_call(
        pack_kernel,
        in_specs=[HBM_SPEC],
        out_specs=[VMEM_SPEC] * 2,
        out_shape=[edge, edge],
        scratch_shapes=[
            pltpu.VMEM((comps, 2, cx, PAD, ny), jnp.float32),
            pltpu.SemaphoreType.DMA((comps, 2)),
        ],
        compiler_params=pltpu.CompilerParams(vmem_limit_bytes=4 << 20),
        name="pack",
    )(far(velocity))


def coefficients(levels_ref, index_ref, advect_ref):
    index = index_ref[...]
    visc = jnp.zeros(index.shape, jnp.float32)
    for level in range(levels_ref.shape[0]):
        visc = jnp.where(index == level, levels_ref[level], visc)
    cells = index.shape[1]
    lane = lax.broadcasted_iota(jnp.int32, index.shape, 1)
    first, last = lane == 0, lane == cells - 1
    up = jnp.where(last, visc, 0.5 * (visc + pltpu.roll(visc, cells - 1, 1)))
    down = jnp.where(first, visc, 0.5 * (visc + pltpu.roll(visc, 1, 1)))
    half = 0.5 * advect_ref[...]
    return (
        1.0 - 4.0 * visc - up - down,
        visc,
        visc - half,
        visc + half,
        jnp.where(last, 0.0, up),
        jnp.where(first, 0.0, down),
    )


def step(coefs, center, east, west, north, south):
    mid, visc, c_east, c_west, c_up, c_down = coefs
    cells = center.shape[-1]
    upward = pltpu.roll(center, cells - 1, 1)
    downward = pltpu.roll(center, 1, 1)
    return (
        mid * center
        + visc * (north + south)
        + c_east * east
        + c_west * west
        + c_up * upward
        + c_down * downward
    )


def split3(x):
    high = x.astype(jnp.bfloat16)
    rest = x - high.astype(jnp.float32)
    middle = rest.astype(jnp.bfloat16)
    low = (rest - middle.astype(jnp.float32)).astype(jnp.bfloat16)
    return high, middle, low


def stencil_kernel(
    levels_ref,
    index_ref,
    advect_ref,
    sum_ref,
    zlo_ref,
    zhi_ref,
    face_lo_ref,
    face_hi_ref,
    corner_lo_ref,
    corner_hi_ref,
    vel_hbm,
    xlo_hbm,
    xhi_hbm,
    out_ref,
    field,
    first,
    boxed,
    sems,
):
    comp = pl.program_id(0)
    cx, cz, ny = vel_hbm.shape[1:]
    inner = pl.ds(PAD, cz)

    def copies(c):
        return (
            pltpu.make_async_copy(
                vel_hbm.at[c], field.at[c, pl.ds(2, cx), inner, :], sems.at[c, 0]
            ),
            pltpu.make_async_copy(
                xlo_hbm.at[c], field.at[c, pl.ds(0, 2), inner, :], sems.at[c, 1]
            ),
            pltpu.make_async_copy(
                xhi_hbm.at[c], field.at[c, pl.ds(cx + 2, 2), inner, :], sems.at[c, 2]
            ),
        )

    @pl.when(comp == 0)
    def _():
        for c in range(3):
            for copy in copies(c):
                copy.start()

    coefs = coefficients(levels_ref, index_ref, advect_ref)

    def edge_row(ref, k):
        return ref[pl.ds(pl.multiple_of((2 * comp + k) * cx, 8), cx), :]

    zlo2, zlo1 = edge_row(zlo_ref, 0), edge_row(zlo_ref, 1)
    zhi1, zhi2 = edge_row(zhi_ref, 0), edge_row(zhi_ref, 1)
    lo_before, lo_after = corner_lo_ref[comp, 0:1], corner_hi_ref[comp, 0:1]
    hi_before, hi_after = corner_lo_ref[comp, 1:2], corner_hi_ref[comp, 1:2]
    plane = lax.broadcasted_iota(jnp.int32, (cx, ny), 0)

    def edge(row, before, after, north, south):
        east = jnp.where(plane == cx - 1, after, pltpu.roll(row, cx - 1, 0))
        west = jnp.where(plane == 0, before, pltpu.roll(row, 1, 0))
        return step(coefs, row, east, west, north, south)

    edge_lo = edge(zlo1, lo_before, lo_after, zlo2, edge_row(face_lo_ref, 0))
    edge_hi = edge(zhi1, hi_before, hi_after, edge_row(face_hi_ref, 1), zhi2)
    for i in range(cx):
        field[comp, 2 + i, PAD - 1 : PAD, :] = zlo1[i : i + 1]
        field[comp, 2 + i, PAD + cz : PAD + cz + 1, :] = zhi1[i : i + 1]
        first[1 + i, PAD - 1 : PAD, :] = edge_lo[i : i + 1]
        first[1 + i, PAD + cz : PAD + cz + 1, :] = edge_hi[i : i + 1]
    field[comp, 1, PAD - 1 : PAD, :] = lo_before
    field[comp, 1, PAD + cz : PAD + cz + 1, :] = hi_before
    field[comp, cx + 2, PAD - 1 : PAD, :] = lo_after
    field[comp, cx + 2, PAD + cz : PAD + cz + 1, :] = hi_after

    for copy in copies(comp):
        copy.wait()

    chunk = 16

    def first_plane(p, carry):
        for k in range(cz // chunk):
            at = PAD + k * chunk
            rows = pl.ds(at, chunk)
            first[p, rows, :] = step(
                coefs,
                field[comp, p + 1, rows, :],
                field[comp, p + 2, rows, :],
                field[comp, p, rows, :],
                field[comp, p + 1, pl.ds(at - 1, chunk), :],
                field[comp, p + 1, pl.ds(at + 1, chunk), :],
            )
        return carry

    lax.fori_loop(0, cx + 2, first_plane, 0)

    sums = sum_ref[...]
    lane = lax.broadcasted_iota(jnp.int32, (cz, LANES), 1)
    row = lax.broadcasted_iota(jnp.int32, (cz, LANES), 0)
    wanted = (lane // (LANES // 2)) == ((row // STRIDE) % 2)
    out_ref[...] = jnp.zeros(out_ref.shape, jnp.float32)

    def coarse(which, box):
        total = sum(
            jnp.dot(part, sums, preferred_element_type=jnp.float32)
            for part in split3(boxed[...])
        )
        total = jnp.where(wanted, total, 0.0)
        base = box * (cz // 8 * LANES)
        for r in range(cz // 8):
            line = jnp.sum(total[8 * r : 8 * r + 8], axis=0, keepdims=True) * 0.125
            at = pl.multiple_of(base + r * LANES, LANES)
            out_ref[which : which + 1, pl.ds(at, LANES)] = line

    def box_step(box, carry):
        start = 1 + STRIDE * box
        for k in range(cz // chunk):
            rows = pl.ds(PAD + k * chunk, chunk)
            boxed[pl.ds(k * chunk, chunk), :] = (
                first[start, rows, :] + first[start + 1, rows, :]
            ) + (first[start + 2, rows, :] + first[start + 3, rows, :])
        coarse(0, box)
        for k in range(cz // chunk):
            at = PAD + k * chunk
            rows = pl.ds(at, chunk)
            total = None
            for i in range(STRIDE):
                p = start + i
                value = step(
                    coefs,
                    first[p, rows, :],
                    first[p + 1, rows, :],
                    first[p - 1, rows, :],
                    first[p, pl.ds(at - 1, chunk), :],
                    first[p, pl.ds(at + 1, chunk), :],
                )
                total = value if total is None else total + value
            boxed[pl.ds(k * chunk, chunk), :] = total
        coarse(1, box)
        return carry

    lax.fori_loop(0, cx // STRIDE, box_step, 0)


def snapshots(velocity, levels, profile_index, advect, halos):
    comps, cx, cz, ny = velocity.shape
    cols = (cx // STRIDE) * (cz // STRIDE) * (ny // STRIDE)
    half = LANES // 2
    sums = np.zeros((ny, LANES), np.float32)
    for y in range(ny):
        sums[y, y // STRIDE] = 1.0
        sums[y, half + y // STRIDE] = 1.0
    return pl.pallas_call(
        stencil_kernel,
        grid=(comps,),
        in_specs=[
            pl.BlockSpec(memory_space=pltpu.SMEM),
            pl.BlockSpec((1, ny), lambda c: (0, 0)),
            pl.BlockSpec((1, ny), lambda c: (0, 0)),
            pl.BlockSpec((ny, LANES), lambda c: (0, 0)),
            *[VMEM_SPEC] * 6,
            HBM_SPEC,
            VMEM_SPEC,
            VMEM_SPEC,
        ],
        out_specs=pl.BlockSpec((PAD, cols), lambda c: (0, c)),
        out_shape=pltpu.HBM((PAD, comps * cols), jnp.float32),
        scratch_shapes=[
            pltpu.VMEM((comps, cx + 4, cz + 2 * PAD, ny), jnp.float32),
            pltpu.VMEM((cx + 2, cz + 2 * PAD, ny), jnp.float32),
            pltpu.VMEM((cz, ny), jnp.float32),
            pltpu.SemaphoreType.DMA((comps, 3)),
        ],
        compiler_params=pltpu.CompilerParams(vmem_limit_bytes=20 << 20),
        name="stencil",
    )(
        levels,
        profile_index.reshape(1, ny),
        advect.reshape(1, ny),
        jnp.asarray(sums, jnp.bfloat16),
        *[near(x) for x in halos[:6]],
        far(halos[6]),
        *[near(x) for x in halos[7:]],
    )


def stack_rows(snap, basis_ref, at):
    groups = basis_ref.shape[0]
    return jnp.concatenate(
        [snap] + [basis_ref[g, :, at] for g in range(groups)], axis=0
    )


def gram_kernel(snap_ref, basis_ref, out_ref, acc, *, chunk):
    step_at = pl.program_id(0)
    width = snap_ref.shape[1]

    @pl.when(step_at == 0)
    def _():
        acc[...] = jnp.zeros(acc.shape, jnp.float32)

    for i in range(width // chunk):
        at = pl.ds(pl.multiple_of(step_at * width + i * chunk, chunk), chunk)
        snap = snap_ref[:, i * chunk : (i + 1) * chunk]
        parts = split3(stack_rows(snap, basis_ref, at))
        joined = jnp.concatenate([part.astype(jnp.float32) for part in parts], axis=0)
        joined = joined.astype(jnp.bfloat16)
        acc[...] += lax.dot_general(
            joined, joined, (((1,), (1,)), ((), ())), preferred_element_type=jnp.float32
        )

    @pl.when(step_at == pl.num_programs(0) - 1)
    def _():
        n = ROWS
        total = acc[0:n, 0:n]
        cross = acc[0:n, n : 2 * n] + acc[n : 2 * n, 0:n]
        fine = acc[n : 2 * n, n : 2 * n] + (
            acc[0:n, 2 * n : 3 * n] + acc[2 * n : 3 * n, 0:n]
        )
        out_ref[...] = jnp.zeros(out_ref.shape, jnp.float32)
        out_ref[:, 0:n] = total + (cross + fine)


def gram(snap, basis, width=4096, chunk=2048):
    return pl.pallas_call(
        functools.partial(gram_kernel, chunk=chunk),
        grid=(snap.shape[1] // width,),
        in_specs=[pl.BlockSpec((PAD, width), lambda i: (0, i)), VMEM_SPEC],
        out_specs=VMEM_SPEC,
        out_shape=pltpu.VMEM((ROWS, LANES), jnp.float32),
        scratch_shapes=[pltpu.VMEM((3 * ROWS, 3 * ROWS), jnp.float32)],
        compiler_params=pltpu.CompilerParams(vmem_limit_bytes=12 << 20),
        name="gram",
    )(far(snap), near(basis))


def ring_moves(size, stride, width):
    moves = []
    for shift in range(1, width):
        pairs = []
        for i in range(size):
            k = (i // stride) % width
            pairs.append((i, i + ((k + shift) % width - k) * stride))
        moves.append(pairs)
    return moves


def ring_parts(x, axis, size, stride, width):
    return [lax.ppermute(x, axis, pairs) for pairs in ring_moves(size, stride, width)]


def ring_sum(x, parts):
    if len(parts) == 1:
        return x + parts[0]
    one, two, three = parts
    return (x + two) + (one + three)


def lane_sum(x):
    total = x[0:8]
    for k in range(1, ROWS // 8):
        total = total + x[8 * k : 8 * k + 8]
    total = total + pltpu.roll(total, 4, 0)
    total = total + pltpu.roll(total, 2, 0)
    return total + pltpu.roll(total, 1, 0)


def spread(x):
    return jnp.concatenate([x] * (ROWS // 8), axis=0)


def factor_kernel(
    g0_ref, g1_ref, g2_ref, g3_ref, partner_ref, orient_ref, keep_ref, mix_ref, sigma_ref
):
    a = (g0_ref[...] + g2_ref[...]) + (g1_ref[...] + g3_ref[...])
    lane = lax.broadcasted_iota(jnp.int32, (ROWS, LANES), 1)
    row = lax.broadcasted_iota(jnp.int32, (ROWS, LANES), 0)
    upper = jnp.zeros((ROWS, LANES), jnp.float32)
    for j in (int(k) for k in PLACE):
        line = jnp.broadcast_to(a[j : j + 1, :], (ROWS, LANES))
        column = jnp.broadcast_to(a[:, j : j + 1], (ROWS, LANES))
        pivot = jnp.broadcast_to(line[:, j : j + 1], (ROWS, LANES))
        scale = lax.rsqrt(pivot)
        line = line * scale
        a = a - (column * scale) * line
        upper = jnp.where((row == j) & (lane >= j), line, upper)

    def turn_step(i, state):
        x, v = state
        turn = lax.rem(i, COUNT - 1)
        other = jnp.broadcast_to(partner_ref[pl.ds(turn, 1), :], (ROWS, LANES))
        sign = jnp.broadcast_to(orient_ref[pl.ds(turn, 1), :], (8, LANES))
        y = jnp.take_along_axis(x, other, axis=1)
        vy = jnp.take_along_axis(v, other, axis=1)
        contrast = lane_sum(y * y) - lane_sum(x * x)
        inner = lane_sum(x * y)
        toward = jnp.where(contrast > 0.0, -1.0, jnp.where(contrast < 0.0, 1.0, sign))
        d = jnp.abs(contrast) + jnp.sqrt(contrast * contrast + 4.0 * inner * inner)
        positive = d > 0.0
        tangent = jnp.where(
            positive, 2.0 * inner * toward / jnp.where(positive, d, 1.0), 0.0
        )
        cosine = 1.0 / jnp.sqrt(1.0 + tangent * tangent)
        sine = spread(cosine * tangent)
        cosine = spread(cosine)
        return cosine * x + sine * y, cosine * v + sine * vy

    eye = jnp.where(row == lane, 1.0, 0.0)
    x, v = lax.fori_loop(0, SWEEPS * (COUNT - 1), turn_step, (upper, eye))
    keep = jnp.broadcast_to(keep_ref[...], (ROWS, LANES))
    sigma_ref[...] = jnp.take_along_axis(jnp.sqrt(lane_sum(x * x)), keep[0:8], axis=1)
    v = jnp.take_along_axis(v, keep, axis=1)
    high = v.astype(jnp.bfloat16).astype(jnp.float32)
    low = v - high
    mix = jnp.concatenate([high, high, low, jnp.zeros((8, LANES), jnp.float32)], axis=0)
    mix_ref[...] = jnp.transpose(mix)[0:MODES].astype(jnp.bfloat16)


def factor(parts):
    tables = [near(jnp.asarray(table)) for table in pair_tables()]
    return pl.pallas_call(
        factor_kernel,
        in_specs=[VMEM_SPEC] * 7,
        out_specs=(VMEM_SPEC, VMEM_SPEC),
        out_shape=(
            pltpu.VMEM((MODES, LANES), jnp.bfloat16),
            pltpu.VMEM((8, LANES), jnp.float32),
        ),
        compiler_params=pltpu.CompilerParams(vmem_limit_bytes=4 << 20),
        name="factor",
    )(*[near(x) for x in parts], *tables)


def update_kernel(mix_ref, snap_ref, basis_ref, out_ref, *, chunk):
    groups, _, width = out_ref.shape
    mix = mix_ref[...]
    base = pl.program_id(0) * width
    for i in range(width // chunk):
        at = pl.ds(pl.multiple_of(base + i * chunk, chunk), chunk)
        snap = snap_ref[:, i * chunk : (i + 1) * chunk]
        stack = stack_rows(snap, basis_ref, at)
        high = stack.astype(jnp.bfloat16).astype(jnp.float32)
        zero = jnp.zeros((8, chunk), jnp.float32)
        joined = jnp.concatenate([high, stack - high, high, zero], axis=0)
        out = jnp.dot(mix, joined.astype(jnp.bfloat16), preferred_element_type=jnp.float32)
        for g in range(groups):
            out_ref[g, :, i * chunk : (i + 1) * chunk] = out[8 * g : 8 * g + 8]


def update(mix, snap, basis, width=4096, chunk=1024):
    cols = snap.shape[1]
    return pl.pallas_call(
        functools.partial(update_kernel, chunk=chunk),
        grid=(cols // width,),
        in_specs=[VMEM_SPEC, pl.BlockSpec((PAD, width), lambda i: (0, i)), VMEM_SPEC],
        out_specs=pl.BlockSpec((4, PAD, width), lambda i: (0, 0, i)),
        out_shape=pltpu.HBM((4, PAD, cols), jnp.float32),
        compiler_params=pltpu.CompilerParams(vmem_limit_bytes=8 << 20),
        name="update",
    )(near(mix), far(snap), near(basis))


def program(velocity, basis, levels, profile_index, advect):
    n_space, n_mode = lax.axis_size("space"), lax.axis_size("mode")
    comps, cx, _, ny = velocity.shape
    modes_here, cols_here = basis.shape
    cols = cols_here // n_mode

    def shifted(x, axis, by):
        size = lax.axis_size(axis)
        return lax.ppermute(x, axis, [(i, (i + by) % size) for i in range(size)])

    face_lo, face_hi = pack(velocity)
    zlo = shifted(face_hi, "mode", 1)
    zhi = shifted(face_lo, "mode", -1)
    xlo = shifted(velocity[:, cx - 2 :], "space", 1)
    xhi = shifted(velocity[:, :2], "space", -1)
    near_lo = zlo.reshape(comps, 2, cx, ny)[:, 1]
    near_hi = zhi.reshape(comps, 2, cx, ny)[:, 0]
    corner_lo = jnp.stack([near_lo[:, -1], near_hi[:, -1]], axis=1)
    corner_hi = jnp.stack([near_lo[:, 0], near_hi[:, 0]], axis=1)
    corner_lo = shifted(corner_lo, "space", 1)
    corner_hi = shifted(corner_hi, "space", -1)
    shared = basis.reshape(modes_here, n_mode, cols).transpose(1, 0, 2)
    shared = lax.all_to_all(shared, "mode", split_axis=0, concat_axis=0, tiled=True)

    snap = snapshots(
        velocity,
        levels,
        profile_index,
        advect,
        (zlo, zhi, face_lo, face_hi, corner_lo, corner_hi, velocity, xlo, xhi),
    )
    total = gram(snap, shared)
    total = ring_sum(total, ring_parts(total, "space", n_space, 1, 2))
    total = ring_sum(total, ring_parts(total, "space", n_space, 2, 4))
    total = ring_sum(total, ring_parts(total, "space", n_space, 8, 4))
    mix, sigma = factor([total] + ring_parts(total, "mode", n_mode, 1, n_mode))
    updated = update(mix, snap, shared)
    modes = lax.all_to_all(updated, "mode", split_axis=0, concat_axis=0, tiled=True)
    modes = modes.transpose(1, 0, 2).reshape(modes_here, cols_here)
    return (modes, sigma[0, :MODES])


def solution(mesh):
    return jax.shard_map(
        program,
        mesh=mesh,
        in_specs=(P(None, "space", "mode", None), P("mode", "space"), P(), P(), P()),
        out_specs=(P("mode", "space"), P()),
        check_vma=False,
    )
```

profile of v0, /device:TPU:0, one launch (start us, length us, event | category | flops | bytes accessed | tf_op | source)
XLA Modules:
  0.0 157.4 jit_solution(6060035409036097380)
XLA Ops:
  0.6 4.4 %all-to-all-start = ((f32[4,8,24576]{2,1,0:T(8,128)}), f32[4,8,24576]{2,1,0:T(8,128)S(1)}, u32[]{:S(2)}, u32[]{:S(2)}) async-start(f32[4,8,24576]{2,1,0:T(8,128)} %bitcast.25), calls=%async_computation | async-start | bytes 6291456 | tf_op jit(solution)/shard_map/all_to_all | solution.py:512
  5.0 1.4 pack.1
  6.4 0.0 copy-start
  6.4 0.0 copy-start.3
  6.4 0.0 copy-start.4
  6.4 0.0 copy-start.5
  6.5 2.1 %collective-permute-start = (f32[96,256]{1,0:T(8,128)S(1)}, f32[96,256]{1,0:T(8,128)S(1)}, u32[]{:S(2)}, u32[]{:S(2)}) collective-permute-start(f32[96,256]{1,0:T(8,128)S(1)} %get-tuple-element.6.face_hi_ref), channel_id=1, source_target_pairs={{0,1},{1,2},{2,3},{3,0},{4,5},{5,6},{6,7},{7,4},{8,9},{9,10},{10,1... | collective-permute-start | bytes 294920 | tf_op jit(solution)/shard_map/ppermute | solution.py:498
  8.6 1.3 collective-permute-start.1
  9.8 1.5 fusion
  11.4 5.2 %collective-permute-start.5 = (f32[3,2,128,256]{3,2,1,0:T(8,128)S(1)}, f32[3,2,128,256]{3,2,1,0:T(8,128)S(1)}, u32[]{:S(2)}, u32[]{:S(2)}) collective-permute-start(f32[3,2,128,256]{3,2,1,0:T(8,128)S(1)} %get-tuple-element.10), channel_id=1, source_target_pairs={{0,124},{4,0},{8,4},{12,8},{16,12},{20,16},{24,20},{28,24},{32,28}... | collective-permute-start | bytes 2359304 | tf_op jit(solution)/shard_map/ppermute | solution.py:498
  16.6 0.0 collective-permute-start.4
  16.6 27.9 %collective-permute-done.zlo_ref = f32[96,256]{1,0:T(8,128)S(1)} collective-permute-done((f32[96,256]{1,0:T(8,128)S(1)}, f32[96,256]{1,0:T(8,128)S(1)}, u32[]{:S(2)}, u32[]{:S(2)}) %collective-permute-start) | collective-permute-done | bytes 98336 | tf_op jit(solution)/shard_map/ppermute | solution.py:498
  44.4 0.0 collective-permute-done.1.zhi_ref
  44.5 0.1 collective-permute-start.2
  44.6 5.1 %collective-permute-start.3 = (f32[3,2,256]{2,1,0:T(2,128)S(1)}, f32[3,2,256]{2,1,0:T(2,128)S(1)}, u32[]{:S(2)}, u32[]{:S(2)}) collective-permute-start(f32[3,2,256]{2,1,0:T(2,128)S(1)} %pad_maximum_fusion.1), channel_id=1, source_target_pairs={{0,124},{4,0},{8,4},{12,8},{16,12},{20,16},{24,20},{28,24},{32,28}... | collective-permute-start | bytes 18440 | tf_op jit(solution)/shard_map/ppermute | solution.py:498
  49.7 1.2 collective-permute-done.2.corner_lo_ref
  50.9 0.1 collective-permute-done.3.corner_hi_ref
  51.1 0.0 collective-permute-done.5.xhi_hbm
  51.1 0.0 collective-permute-done.4.xlo_hbm
  51.1 0.0 copy-done
  51.1 0.0 copy-done.3
  51.1 0.0 copy-done.4
  51.1 0.0 copy-done.5
  51.1 18.8 %stencil.1.snap_ref = f32[8,24576]{1,0:T(8,128)} custom-call(f32[8]{0:T(128)S(1)} %copy-done.5, s32[1,256]{1,0:T(1,128)S(1)} %bitcast.22, f32[1,256]{1,0:T(1,128)S(1)} %bitcast.23, bf16[256,128]{1,0:T(8,128)(2,1)S(1)} %copy-done, f32[96,256]{1,0:T(8,128)S(1)} %collective-permute-done.zlo_ref, f32[96,256]{1,0:T(8,128)S(1)} %collective-permute-done.1.zhi_ref, ...), custom_call_target="tpu_custom_call" | custom-call | tf_op jit(solution)/shard_map/stencil/pallas_call | solution.py:280
  69.9 0.0 copy-start.1
  69.9 0.0 copy-start.2
  69.9 0.0 copy-start.6
  69.9 0.0 all-to-all-done.basis_ref
  69.9 4.8 %gram.1 = f32[40,128]{1,0:T(8,128)S(1)} custom-call(f32[8,24576]{1,0:T(8,128)} %stencil.1.snap_ref, f32[4,8,24576]{2,1,0:T(8,128)S(1)} %all-to-all-done.basis_ref), custom_call_target="tpu_custom_call" | custom-call | tf_op jit(solution)/shard_map/gram/pallas_call | solution.py:352
  74.7 0.1 collective-permute-start.6
  74.8 1.2 collective-permute-done.6
  76.0 3.1 %collective-permute-start.9 = (f32[40,128]{1,0:T(8,128)S(1)}, f32[40,128]{1,0:T(8,128)S(1)}, u32[]{:S(2)}, u32[]{:S(2)}) collective-permute-start(f32[40,128]{1,0:T(8,128)S(1)} %add.21), channel_id=1, source_target_pairs={{0,24},{4,28},{8,0},{12,4},{16,8},{20,12},{24,16},{28,20},{32,56},... | collective-permute-start | bytes 61448 | tf_op jit(solution)/shard_map/ppermute | solution.py:376
  79.1 0.0 collective-permute-start.8
  79.1 1.5 collective-permute-start.7
  80.6 0.0 collective-permute-done.9
  80.6 3.5 %collective-permute-done.8 = f32[40,128]{1,0:T(8,128)S(1)} collective-permute-done((f32[40,128]{1,0:T(8,128)S(1)}, f32[40,128]{1,0:T(8,128)S(1)}, u32[]{:S(2)}, u32[]{:S(2)}) %collective-permute-start.8) | collective-permute-done | bytes 20512 | tf_op jit(solution)/shard_map/ppermute | solution.py:376
  84.1 0.3 collective-permute-done.7
  84.4 2.6 %collective-permute-start.12 = (f32[40,128]{1,0:T(8,128)S(1)}, f32[40,128]{1,0:T(8,128)S(1)}, u32[]{:S(2)}, u32[]{:S(2)}) collective-permute-start(f32[40,128]{1,0:T(8,128)S(1)} %add_add_fusion.1), channel_id=1, source_target_pairs={{0,96},{4,100},{8,104},{12,108},{16,112},{20,116},{24,120},{28,124... | collective-permute-start | bytes 61448 | tf_op jit(solution)/shard_map/ppermute | solution.py:376
  87.0 0.0 collective-permute-start.11
  87.0 3.1 %collective-permute-start.10 = (f32[40,128]{1,0:T(8,128)S(1)}, f32[40,128]{1,0:T(8,128)S(1)}, u32[]{:S(2)}, u32[]{:S(2)}) collective-permute-start(f32[40,128]{1,0:T(8,128)S(1)} %add_add_fusion.1), channel_id=1, source_target_pairs={{0,64},{4,68},{8,72},{12,76},{16,80},{20,84},{24,88},{28,92},{32,9... | collective-permute-start | bytes 61448 | tf_op jit(solution)/shard_map/ppermute | solution.py:376
  90.1 0.0 collective-permute-done.12
  90.1 1.9 %collective-permute-done.11 = f32[40,128]{1,0:T(8,128)S(1)} collective-permute-done((f32[40,128]{1,0:T(8,128)S(1)}, f32[40,128]{1,0:T(8,128)S(1)}, u32[]{:S(2)}, u32[]{:S(2)}) %collective-permute-start.11) | collective-permute-done | bytes 20512 | tf_op jit(solution)/shard_map/ppermute | solution.py:376
  92.0 0.3 collective-permute-done.10
  92.3 1.0 collective-permute-start.15
  93.3 1.4 collective-permute-start.14
  94.6 0.6 collective-permute-start.13
  95.3 0.9 collective-permute-done.15.g3_ref
  96.1 2.4 %collective-permute-done.14.g2_ref = f32[40,128]{1,0:T(8,128)S(1)} collective-permute-done((f32[40,128]{1,0:T(8,128)S(1)}, f32[40,128]{1,0:T(8,128)S(1)}, u32[]{:S(2)}, u32[]{:S(2)}) %collective-permute-start.14) | collective-permute-done | bytes 20512 | tf_op jit(solution)/shard_map/ppermute | solution.py:376
  98.5 1.1 collective-permute-done.13.g1_ref
  99.6 0.0 copy-done.1
  99.6 0.0 copy-done.2
  99.6 0.0 copy-done.6
  99.6 13.2 %factor.1 = (bf16[32,128]{1,0:T(8,128)(2,1)S(1)}, f32[8,128]{1,0:T(8,128)S(1)}) custom-call(f32[40,128]{1,0:T(8,128)S(1)} %add_add_fusion.g0_ref, f32[40,128]{1,0:T(8,128)S(1)} %collective-permute-done.13.g1_ref, f32[40,128]{1,0:T(8,128)S(1)} %collective-permute-done.14.g2_ref, f32[40,128]{1,0:T(8,128)S(1)} %collective-permute-done.15.g3_ref, ...), custom_call_target="tpu_custom_call" | custom-call | tf_op jit(solution)/shard_map/factor/pallas_call | solution.py:448
  112.9 5.4 %update.1 = f32[4,8,24576]{2,1,0:T(8,128)} custom-call(bf16[32,128]{1,0:T(8,128)(2,1)S(1)} %get-tuple-element.8.mix_ref, f32[8,24576]{1,0:T(8,128)} %stencil.1.snap_ref, f32[4,8,24576]{2,1,0:T(8,128)S(1)} %all-to-all-done.basis_ref), custom_call_target="tpu_custom_call" | custom-call | tf_op jit(solution)/shard_map/update/pallas_call | solution.py:479
  118.2 3.7 %all-to-all-start.1 = ((f32[4,8,24576]{2,1,0:T(8,128)}), f32[4,8,24576]{2,1,0:T(8,128)S(1)}, u32[]{:S(2)}, u32[]{:S(2)}) async-start(f32[4,8,24576]{2,1,0:T(8,128)} %update.1), calls=%async_computation.1 | async-start | bytes 6291456 | tf_op jit(solution)/shard_map/all_to_all | solution.py:527
  122.0 0.5 slice_bitcast_fusion.2
  122.5 33.2 %all-to-all-done.1 = f32[4,8,24576]{2,1,0:T(8,128)S(1)} async-done(((f32[4,8,24576]{2,1,0:T(8,128)}), f32[4,8,24576]{2,1,0:T(8,128)S(1)}, u32[]{:S(2)}, u32[]{:S(2)}) %all-to-all-start.1) | async-done | bytes 3145760 | tf_op jit(solution)/shard_map/all_to_all | solution.py:527
  155.7 1.7 %copy.16 = f32[8,98304]{1,0:T(8,128)} copy(f32[8,98304]{1,0:T(8,128)S(1)} %bitcast.24) | data formatting | bytes 6291456
  (8 shorter events, 0.1 us)
Async XLA Ops:
  0.6 69.3 %all-to-all-start = ((f32[4,8,24576]{2,1,0:T(8,128)}), f32[4,8,24576]{2,1,0:T(8,128)S(1)}, u32[]{:S(2)}, u32[]{:S(2)}) async-start(f32[4,8,24576]{2,1,0:T(8,128)} %bitcast.25), calls=%async_computation | async-start | bytes 6291456 | tf_op jit(solution)/shard_map/all_to_all | solution.py:512
  6.4 44.6 %copy-start = (bf16[256,128]{1,0:T(8,128)(2,1)S(1)}, bf16[256,128]{1,0:T(8,128)(2,1)}, u32[]{:S(2)}) copy-start(bf16[256,128]{1,0:T(8,128)(2,1)} %constant.8.clone.sum_ref) | copy-start | bytes 196612
  6.4 44.6 %copy-start.3 = (s32[256]{0:T(256)S(1)}, s32[256]{0:T(256)}, u32[]{:S(2)}) copy-start(s32[256]{0:T(256)} %param.12) | copy-start | bytes 3076
  6.4 44.6 %copy-start.4 = (f32[256]{0:T(256)S(1)}, f32[256]{0:T(256)}, u32[]{:S(2)}) copy-start(f32[256]{0:T(256)} %param.13) | copy-start | bytes 3076
  6.4 44.6 %copy-start.5 = (f32[8]{0:T(128)S(1)}, f32[8]{0:T(128)}, u32[]{:S(2)}) copy-start(f32[8]{0:T(128)} %levels_ref.1) | copy-start | bytes 100
  6.5 38.0 %collective-permute-start = (f32[96,256]{1,0:T(8,128)S(1)}, f32[96,256]{1,0:T(8,128)S(1)}, u32[]{:S(2)}, u32[]{:S(2)}) collective-permute-start(f32[96,256]{1,0:T(8,128)S(1)} %get-tuple-element.6.face_hi_ref), channel_id=1, source_target_pairs={{0,1},{1,2},{2,3},{3,0},{4,5},{5,6},{6,7},{7,4},{8,9},{9,10},{10,1... | collective-permute-start | bytes 294920 | tf_op jit(solution)/shard_map/ppermute | solution.py:498
  8.6 35.9 %collective-permute-start.1 = (f32[96,256]{1,0:T(8,128)S(1)}, f32[96,256]{1,0:T(8,128)S(1)}, u32[]{:S(2)}, u32[]{:S(2)}) collective-permute-start(f32[96,256]{1,0:T(8,128)S(1)} %get-tuple-element.7.face_lo_ref), channel_id=1, source_target_pairs={{0,3},{1,0},{2,1},{3,2},{4,7},{5,4},{6,5},{7,6},{8,11},{9,8},{10,9... | collective-permute-start | bytes 294920 | tf_op jit(solution)/shard_map/ppermute | solution.py:498
  11.4 39.7 %collective-permute-start.5 = (f32[3,2,128,256]{3,2,1,0:T(8,128)S(1)}, f32[3,2,128,256]{3,2,1,0:T(8,128)S(1)}, u32[]{:S(2)}, u32[]{:S(2)}) collective-permute-start(f32[3,2,128,256]{3,2,1,0:T(8,128)S(1)} %get-tuple-element.10), channel_id=1, source_target_pairs={{0,124},{4,0},{8,4},{12,8},{16,12},{20,16},{24,20},{28,24},{32,28}... | collective-permute-start | bytes 2359304 | tf_op jit(solution)/shard_map/ppermute | solution.py:498
  16.6 34.5 %collective-permute-start.4 = (f32[3,2,128,256]{3,2,1,0:T(8,128)S(1)}, f32[3,2,128,256]{3,2,1,0:T(8,128)S(1)}, u32[]{:S(2)}, u32[]{:S(2)}) collective-permute-start(f32[3,2,128,256]{3,2,1,0:T(8,128)S(1)} %get-tuple-element.11), channel_id=1, source_target_pairs={{0,4},{4,8},{8,12},{12,16},{16,20},{20,24},{24,28},{28,32},{32,36}... | collective-permute-start | bytes 2359304 | tf_op jit(solution)/shard_map/ppermute | solution.py:498
  44.5 6.4 %collective-permute-start.2 = (f32[3,2,256]{2,1,0:T(2,128)S(1)}, f32[3,2,256]{2,1,0:T(2,128)S(1)}, u32[]{:S(2)}, u32[]{:S(2)}) collective-permute-start(f32[3,2,256]{2,1,0:T(2,128)S(1)} %pad_maximum_fusion), channel_id=1, source_target_pairs={{0,4},{4,8},{8,12},{12,16},{16,20},{20,24},{24,28},{28,32},{32,36}... | collective-permute-start | bytes 18440 | tf_op jit(solution)/shard_map/ppermute | solution.py:498
  44.6 6.5 %collective-permute-start.3 = (f32[3,2,256]{2,1,0:T(2,128)S(1)}, f32[3,2,256]{2,1,0:T(2,128)S(1)}, u32[]{:S(2)}, u32[]{:S(2)}) collective-permute-start(f32[3,2,256]{2,1,0:T(2,128)S(1)} %pad_maximum_fusion.1), channel_id=1, source_target_pairs={{0,124},{4,0},{8,4},{12,8},{16,12},{20,16},{24,20},{28,24},{32,28}... | collective-permute-start | bytes 18440 | tf_op jit(solution)/shard_map/ppermute | solution.py:498
  69.9 29.8 %copy-start.1 = (f32[40,128]{1,0:T(8,128)S(1)}, f32[40,128]{1,0:T(8,128)}, u32[]{:S(2)}) copy-start(f32[40,128]{1,0:T(8,128)} %constant.10.clone.orient_ref) | copy-start | bytes 61444
  69.9 29.8 %copy-start.2 = (s32[40,128]{1,0:T(8,128)S(1)}, s32[40,128]{1,0:T(8,128)}, u32[]{:S(2)}) copy-start(s32[40,128]{1,0:T(8,128)} %constant.9.clone.partner_ref) | copy-start | bytes 61444
  69.9 29.8 %copy-start.6 = (s32[1,128]{1,0:T(1,128)S(1)}, s32[1,128]{1,0:T(1,128)}, u32[]{:S(2)}) copy-start(s32[1,128]{1,0:T(1,128)} %constant.11.clone.keep_ref) | copy-start | bytes 1540
  74.7 1.3 collective-permute-start.6
  76.0 4.6 %collective-permute-start.9 = (f32[40,128]{1,0:T(8,128)S(1)}, f32[40,128]{1,0:T(8,128)S(1)}, u32[]{:S(2)}, u32[]{:S(2)}) collective-permute-start(f32[40,128]{1,0:T(8,128)S(1)} %add.21), channel_id=1, source_target_pairs={{0,24},{4,28},{8,0},{12,4},{16,8},{20,12},{24,16},{28,20},{32,56},... | collective-permute-start | bytes 61448 | tf_op jit(solution)/shard_map/ppermute | solution.py:376
  79.1 5.0 %collective-permute-start.8 = (f32[40,128]{1,0:T(8,128)S(1)}, f32[40,128]{1,0:T(8,128)S(1)}, u32[]{:S(2)}, u32[]{:S(2)}) collective-permute-start(f32[40,128]{1,0:T(8,128)S(1)} %add.21), channel_id=1, source_target_pairs={{0,8},{4,12},{8,16},{12,20},{16,24},{20,28},{24,0},{28,4},{32,40},... | collective-permute-start | bytes 61448 | tf_op jit(solution)/shard_map/ppermute | solution.py:376
  79.1 5.3 %collective-permute-start.7 = (f32[40,128]{1,0:T(8,128)S(1)}, f32[40,128]{1,0:T(8,128)S(1)}, u32[]{:S(2)}, u32[]{:S(2)}) collective-permute-start(f32[40,128]{1,0:T(8,128)S(1)} %add.21), channel_id=1, source_target_pairs={{0,16},{4,20},{8,24},{12,28},{16,0},{20,4},{24,8},{28,12},{32,48},... | collective-permute-start | bytes 61448 | tf_op jit(solution)/shard_map/ppermute | solution.py:376
  84.4 5.7 %collective-permute-start.12 = (f32[40,128]{1,0:T(8,128)S(1)}, f32[40,128]{1,0:T(8,128)S(1)}, u32[]{:S(2)}, u32[]{:S(2)}) collective-permute-start(f32[40,128]{1,0:T(8,128)S(1)} %add_add_fusion.1), channel_id=1, source_target_pairs={{0,96},{4,100},{8,104},{12,108},{16,112},{20,116},{24,120},{28,124... | collective-permute-start | bytes 61448 | tf_op jit(solution)/shard_map/ppermute | solution.py:376
  87.0 5.0 %collective-permute-start.11 = (f32[40,128]{1,0:T(8,128)S(1)}, f32[40,128]{1,0:T(8,128)S(1)}, u32[]{:S(2)}, u32[]{:S(2)}) collective-permute-start(f32[40,128]{1,0:T(8,128)S(1)} %add_add_fusion.1), channel_id=1, source_target_pairs={{0,32},{4,36},{8,40},{12,44},{16,48},{20,52},{24,56},{28,60},{32,6... | collective-permute-start | bytes 61448 | tf_op jit(solution)/shard_map/ppermute | solution.py:376
  87.0 5.3 %collective-permute-start.10 = (f32[40,128]{1,0:T(8,128)S(1)}, f32[40,128]{1,0:T(8,128)S(1)}, u32[]{:S(2)}, u32[]{:S(2)}) collective-permute-start(f32[40,128]{1,0:T(8,128)S(1)} %add_add_fusion.1), channel_id=1, source_target_pairs={{0,64},{4,68},{8,72},{12,76},{16,80},{20,84},{24,88},{28,92},{32,9... | collective-permute-start | bytes 61448 | tf_op jit(solution)/shard_map/ppermute | solution.py:376
  92.3 3.8 %collective-permute-start.15 = (f32[40,128]{1,0:T(8,128)S(1)}, f32[40,128]{1,0:T(8,128)S(1)}, u32[]{:S(2)}, u32[]{:S(2)}) collective-permute-start(f32[40,128]{1,0:T(8,128)S(1)} %add_add_fusion.g0_ref), channel_id=1, source_target_pairs={{0,3},{1,0},{2,1},{3,2},{4,7},{5,4},{6,5},{7,6},{8,11},{9,8},{10,9... | collective-permute-start | bytes 61448 | tf_op jit(solution)/shard_map/ppermute | solution.py:376
  93.3 5.3 %collective-permute-start.14 = (f32[40,128]{1,0:T(8,128)S(1)}, f32[40,128]{1,0:T(8,128)S(1)}, u32[]{:S(2)}, u32[]{:S(2)}) collective-permute-start(f32[40,128]{1,0:T(8,128)S(1)} %add_add_fusion.g0_ref), channel_id=1, source_target_pairs={{0,2},{1,3},{2,0},{3,1},{4,6},{5,7},{6,4},{7,5},{8,10},{9,11},{10,... | collective-permute-start | bytes 61448 | tf_op jit(solution)/shard_map/ppermute | solution.py:376
  94.6 5.0 %collective-permute-start.13 = (f32[40,128]{1,0:T(8,128)S(1)}, f32[40,128]{1,0:T(8,128)S(1)}, u32[]{:S(2)}, u32[]{:S(2)}) collective-permute-start(f32[40,128]{1,0:T(8,128)S(1)} %add_add_fusion.g0_ref), channel_id=1, source_target_pairs={{0,1},{1,2},{2,3},{3,0},{4,5},{5,6},{6,7},{7,4},{8,9},{9,10},{10,1... | collective-permute-start | bytes 61448 | tf_op jit(solution)/shard_map/ppermute | solution.py:376
  118.2 37.5 %all-to-all-start.1 = ((f32[4,8,24576]{2,1,0:T(8,128)}), f32[4,8,24576]{2,1,0:T(8,128)S(1)}, u32[]{:S(2)}, u32[]{:S(2)}) async-start(f32[4,8,24576]{2,1,0:T(8,128)} %update.1), calls=%async_computation.1 | async-start | bytes 6291456 | tf_op jit(solution)/shard_map/all_to_all | solution.py:527
where the time goes:
time: 158 us; the launch traced here: 157 us
  waiting for transfers between devices  74 us (47%)
  Pallas kernels  43.5 us (28%)
  starting transfers between devices  35.2 us (22%)
  local copies, waits for them, and re-layouts  3.79 us (2%)
    all_to_all x1, waiting for transfers between devices, program(): lax.all_to_all(updated, 'mode', split_axis=0, concat_axis=0, tiled=True)  33.2 us
    ppermute x6, waiting for transfers between devices, shifted(): return lax.ppermute(x, axis, [(i, (i + by) % size) for i in range(size)])  29.2 us
    pallas_call x1, Pallas kernels, snapshots(): pl.pallas_call(stencil_kernel, grid=(comps,), in_specs=[pl.BlockSpec(memo...  18.8 us
    ppermute x6, starting transfers between devices, shifted(): return lax.ppermute(x, axis, [(i, (i + by) % size) for i in range(size)])  13.7 us
    ppermute x10, starting transfers between devices, ring_parts(): lax.ppermute(x, axis, pairs)  13.3 us
    pallas_call x1, Pallas kernels, factor(): pl.pallas_call(factor_kernel, in_specs=[VMEM_SPEC] * 7, out_specs=(VMEM_S...  13.2 us
    ppermute x10, waiting for transfers between devices, ring_parts(): lax.ppermute(x, axis, pairs)  11.6 us
    pallas_call x1, Pallas kernels, update(): pl.pallas_call(functools.partial(update_kernel, chunk=chunk), grid=(cols...  5.38 us
  transfers between devices with their start and end apart: 18, of which 12 were waited for; matrix products, arithmetic and copies ran while one was open for 1% of the time, Pallas kernels for 13%

commit v1 on v0

--- a/solution.py
+++ b/solution.py
@@ -17,7 +17,11 @@
 PAD = 8
 VMEM_SPEC = pl.BlockSpec(memory_space=pltpu.VMEM)
 HBM_SPEC = pl.BlockSpec(memory_space=pltpu.HBM)
-
+SMEM_SPEC = pl.BlockSpec(memory_space=pltpu.SMEM)
+
+
+SHARED = 8192
+FOLD = SHARED // 4
 
 PLACE = np.array([0, 1] + list(range(PAD, PAD + MODES)))
 
@@ -46,19 +50,40 @@
     return partner, orient, keep
 
 
-def pack_kernel(vel_hbm, zfirst_ref, zlast_ref, buf, sems):
+def pack_kernel(
+    here_ref,
+    vel_hbm,
+    basis_hbm,
+    zfirst_ref,
+    zlast_ref,
+    xfirst_ref,
+    xlast_ref,
+    mine_ref,
+    next_ref,
+    far_ref,
+    prev_ref,
+    buf,
+    edge_sems,
+    face_sems,
+    block_sems,
+):
     comps, cx, cz, _ = vel_hbm.shape
-    copies = []
+    cols = mine_ref.shape[1]
+    edges, rest = [], []
     for c in range(comps):
         for side, at in enumerate((0, cz - PAD)):
-            copies.append(
-                pltpu.make_async_copy(
-                    vel_hbm.at[c, :, pl.ds(at, PAD), :], buf.at[c, side], sems.at[c, side]
-                )
-            )
-    for copy in copies:
+            source = vel_hbm.at[c, :, pl.ds(at, PAD), :]
+            edges.append(pltpu.make_async_copy(source, buf.at[c, side], edge_sems.at[c, side]))
+        for side, (at, ref) in enumerate(((0, xfirst_ref), (cx - 2, xlast_ref))):
+            source = vel_hbm.at[c, pl.ds(at, 2)]
+            rest.append(pltpu.make_async_copy(source, ref.at[c], face_sems.at[c, side]))
+    for k, ref in enumerate((mine_ref, next_ref, far_ref, prev_ref)):
+        at = pl.multiple_of(lax.rem(here_ref[0] + k, 4) * cols, LANES)
+        source = basis_hbm.at[:, pl.ds(at, cols)]
+        rest.append(pltpu.make_async_copy(source, ref, block_sems.at[k]))
+    for copy in edges + rest:
         copy.start()
-    for copy in copies:
+    for copy in edges:
         copy.wait()
     for c in range(comps):
         for i in range(cx):
@@ -66,23 +91,29 @@
                 row, last = (2 * c + k) * cx + i, PAD - 2 + k
                 zfirst_ref[row : row + 1, :] = buf[c, 0, i, k : k + 1, :]
                 zlast_ref[row : row + 1, :] = buf[c, 1, i, last : last + 1, :]
-
-
-def pack(velocity):
-    comps, cx, _, ny = velocity.shape
+    for copy in rest:
+        copy.wait()
+
+
+def pack(here, velocity, basis):
+    comps, cx, cz, ny = velocity.shape
     edge = pltpu.VMEM((comps * 2 * cx, ny), jnp.float32)
+    face = pltpu.VMEM((comps, 2, cz, ny), jnp.float32)
+    block = pltpu.VMEM((PAD, basis.shape[1] // 4), jnp.float32)
     return pl.pallas_call(
         pack_kernel,
-        in_specs=[HBM_SPEC],
-        out_specs=[VMEM_SPEC] * 2,
-        out_shape=[edge, edge],
+        in_specs=[SMEM_SPEC, HBM_SPEC, HBM_SPEC],
+        out_specs=[VMEM_SPEC] * 8,
+        out_shape=[edge, edge, face, face] + [block] * 4,
         scratch_shapes=[
             pltpu.VMEM((comps, 2, cx, PAD, ny), jnp.float32),
             pltpu.SemaphoreType.DMA((comps, 2)),
+            pltpu.SemaphoreType.DMA((comps, 2)),
+            pltpu.SemaphoreType.DMA((4,)),
         ],
         compiler_params=pltpu.CompilerParams(vmem_limit_bytes=4 << 20),
         name="pack",
-    )(far(velocity))
+    )(here, far(velocity), far(basis))
 
 
 def coefficients(levels_ref, index_ref, advect_ref):
@@ -129,6 +160,18 @@
     return high, middle, low
 
 
+def offer_copies(here, basis_hbm, refs, sems):
+    cols = basis_hbm.shape[1] // 4
+    copies = []
+    for side, (ref, skip) in enumerate(zip(refs, (2, 0, 3))):
+        for k in range(3):
+            at = pl.multiple_of(lax.rem(here + skip + k, 4) * cols, LANES)
+            source = basis_hbm.at[:, pl.ds(at, SHARED)]
+            target = ref.at[:, pl.ds(k * SHARED, SHARED)]
+            copies.append(pltpu.make_async_copy(source, target, sems.at[side, k]))
+    return copies
+
+
 def stencil_kernel(
     levels_ref,
     index_ref,
@@ -140,16 +183,24 @@
     face_hi_ref,
     corner_lo_ref,
     corner_hi_ref,
+    here_ref,
+    basis_hbm,
     vel_hbm,
     xlo_hbm,
     xhi_hbm,
     out_ref,
+    plus_ref,
+    minus_ref,
+    over_ref,
     field,
     first,
     boxed,
     sems,
+    offer_sems,
 ):
     comp = pl.program_id(0)
+    offer_refs = (plus_ref, minus_ref, over_ref)
+    offers = offer_copies(here_ref[0], basis_hbm, offer_refs, offer_sems)
     cx, cz, ny = vel_hbm.shape[1:]
     inner = pl.ds(PAD, cz)
 
@@ -171,6 +222,13 @@
         for c in range(3):
             for copy in copies(c):
                 copy.start()
+        for copy in offers:
+            copy.start()
+
+    @pl.when(comp == pl.num_programs(0) - 1)
+    def _():
+        for copy in offers:
+            copy.wait()
 
     coefs = coefficients(levels_ref, index_ref, advect_ref)
 
@@ -225,7 +283,9 @@
     lane = lax.broadcasted_iota(jnp.int32, (cz, LANES), 1)
     row = lax.broadcasted_iota(jnp.int32, (cz, LANES), 0)
     wanted = (lane // (LANES // 2)) == ((row // STRIDE) % 2)
-    out_ref[...] = jnp.zeros(out_ref.shape, jnp.float32)
+    part = out_ref.shape[1] // vel_hbm.shape[0]
+    offset = pl.multiple_of(comp * part, LANES)
+    out_ref[:, pl.ds(offset, part)] = jnp.zeros((PAD, part), jnp.float32)
 
     def coarse(which, box):
         total = sum(
@@ -233,11 +293,18 @@
             for part in split3(boxed[...])
         )
         total = jnp.where(wanted, total, 0.0)
-        base = box * (cz // 8 * LANES)
+        base = offset + box * (cz // 8 * LANES)
         for r in range(cz // 8):
             line = jnp.sum(total[8 * r : 8 * r + 8], axis=0, keepdims=True) * 0.125
             at = pl.multiple_of(base + r * LANES, LANES)
             out_ref[which : which + 1, pl.ds(at, LANES)] = line
+
+            @pl.when(comp == 0)
+            def _(line=line, r=r):
+                group = which * (SHARED // LANES // 8) + box * (cz // 64) + r // 8
+                spot = pl.ds(pl.multiple_of(3 * SHARED + group * LANES, LANES), LANES)
+                for ref in offer_refs:
+                    ref[r % 8 : r % 8 + 1, spot] = line
 
     def box_step(box, carry):
         start = 1 + STRIDE * box
@@ -269,7 +336,7 @@
     lax.fori_loop(0, cx // STRIDE, box_step, 0)
 
 
-def snapshots(velocity, levels, profile_index, advect, halos):
+def snapshots(velocity, levels, profile_index, advect, here, basis, halos):
     comps, cx, cz, ny = velocity.shape
     cols = (cx // STRIDE) * (cz // STRIDE) * (ny // STRIDE)
     half = LANES // 2
@@ -281,22 +348,26 @@
         stencil_kernel,
         grid=(comps,),
         in_specs=[
-            pl.BlockSpec(memory_space=pltpu.SMEM),
+            SMEM_SPEC,
             pl.BlockSpec((1, ny), lambda c: (0, 0)),
             pl.BlockSpec((1, ny), lambda c: (0, 0)),
             pl.BlockSpec((ny, LANES), lambda c: (0, 0)),
             *[VMEM_SPEC] * 6,
+            SMEM_SPEC,
+            HBM_SPEC,
             HBM_SPEC,
             VMEM_SPEC,
             VMEM_SPEC,
         ],
-        out_specs=pl.BlockSpec((PAD, cols), lambda c: (0, c)),
-        out_shape=pltpu.HBM((PAD, comps * cols), jnp.float32),
+        out_specs=[VMEM_SPEC] * 4,
+        out_shape=[pltpu.VMEM((PAD, comps * cols), jnp.float32)]
+        + [pltpu.VMEM((PAD, 3 * SHARED + FOLD), jnp.float32)] * 3,
         scratch_shapes=[
             pltpu.VMEM((comps, cx + 4, cz + 2 * PAD, ny), jnp.float32),
             pltpu.VMEM((cx + 2, cz + 2 * PAD, ny), jnp.float32),
             pltpu.VMEM((cz, ny), jnp.float32),
             pltpu.SemaphoreType.DMA((comps, 3)),
+            pltpu.SemaphoreType.DMA((3, 3)),
         ],
         compiler_params=pltpu.CompilerParams(vmem_limit_bytes=20 << 20),
         name="stencil",
@@ -306,59 +377,51 @@
         advect.reshape(1, ny),
         jnp.asarray(sums, jnp.bfloat16),
         *[near(x) for x in halos[:6]],
+        here,
+        far(basis),
         far(halos[6]),
         *[near(x) for x in halos[7:]],
     )
 
 
-def stack_rows(snap, basis_ref, at):
-    groups = basis_ref.shape[0]
-    return jnp.concatenate(
-        [snap] + [basis_ref[g, :, at] for g in range(groups)], axis=0
-    )
-
-
-def gram_kernel(snap_ref, basis_ref, out_ref, acc, *, chunk):
-    step_at = pl.program_id(0)
-    width = snap_ref.shape[1]
-
-    @pl.when(step_at == 0)
-    def _():
-        acc[...] = jnp.zeros(acc.shape, jnp.float32)
-
-    for i in range(width // chunk):
-        at = pl.ds(pl.multiple_of(step_at * width + i * chunk, chunk), chunk)
-        snap = snap_ref[:, i * chunk : (i + 1) * chunk]
-        parts = split3(stack_rows(snap, basis_ref, at))
-        joined = jnp.concatenate([part.astype(jnp.float32) for part in parts], axis=0)
-        joined = joined.astype(jnp.bfloat16)
-        acc[...] += lax.dot_general(
+def stacked(refs, at):
+    return jnp.concatenate([ref[:, at] for ref in refs], axis=0)
+
+
+def gram_kernel(here_ref, *refs, chunk):
+    stack_refs, out_ref = refs[:-1], refs[-1]
+    here = here_ref[0]
+    n, acc = ROWS, None
+    for start in range(0, stack_refs[0].shape[1], chunk):
+        stack = stacked(stack_refs, slice(start, start + chunk))
+        high = stack.astype(jnp.bfloat16).astype(jnp.float32)
+        joined = jnp.concatenate([high, stack - high], axis=0).astype(jnp.bfloat16)
+        part = lax.dot_general(
             joined, joined, (((1,), (1,)), ((), ())), preferred_element_type=jnp.float32
         )
-
-    @pl.when(step_at == pl.num_programs(0) - 1)
-    def _():
-        n = ROWS
-        total = acc[0:n, 0:n]
-        cross = acc[0:n, n : 2 * n] + acc[n : 2 * n, 0:n]
-        fine = acc[n : 2 * n, n : 2 * n] + (
-            acc[0:n, 2 * n : 3 * n] + acc[2 * n : 3 * n, 0:n]
-        )
-        out_ref[...] = jnp.zeros(out_ref.shape, jnp.float32)
-        out_ref[:, 0:n] = total + (cross + fine)
-
-
-def gram(snap, basis, width=4096, chunk=2048):
+        acc = part if acc is None else acc + part
+    cross = acc[0:n, n : 2 * n] + acc[n : 2 * n, 0:n]
+    total = acc[0:n, 0:n] + (cross + acc[n : 2 * n, n : 2 * n])
+    total = jnp.concatenate([total, jnp.zeros((n, LANES - n), jnp.float32)], axis=1)
+    lane = lax.broadcasted_iota(jnp.int32, (n, LANES), 1)
+    turned = PAD + lax.rem(lane - PAD + MODES - PAD * here + MODES, MODES)
+    inside = (lane >= PAD) & (lane < n)
+    total = jnp.take_along_axis(total, jnp.where(inside, turned, lane), axis=1)
+    out_ref[0:PAD, :] = total[0:PAD]
+    for g in range(4):
+        at = pl.multiple_of(PAD + PAD * lax.rem(here + g, 4), PAD)
+        out_ref[pl.ds(at, PAD), :] = total[PAD + PAD * g : 2 * PAD + PAD * g]
+
+
+def gram(here, stack, chunk=2048):
     return pl.pallas_call(
         functools.partial(gram_kernel, chunk=chunk),
-        grid=(snap.shape[1] // width,),
-        in_specs=[pl.BlockSpec((PAD, width), lambda i: (0, i)), VMEM_SPEC],
+        in_specs=[SMEM_SPEC] + [VMEM_SPEC] * 5,
         out_specs=VMEM_SPEC,
         out_shape=pltpu.VMEM((ROWS, LANES), jnp.float32),
-        scratch_shapes=[pltpu.VMEM((3 * ROWS, 3 * ROWS), jnp.float32)],
-        compiler_params=pltpu.CompilerParams(vmem_limit_bytes=12 << 20),
+        compiler_params=pltpu.CompilerParams(vmem_limit_bytes=8 << 20),
         name="gram",
-    )(far(snap), near(basis))
+    )(here, *[near(x) for x in stack])
 
 
 def ring_moves(size, stride, width):
@@ -440,7 +503,7 @@
     high = v.astype(jnp.bfloat16).astype(jnp.float32)
     low = v - high
     mix = jnp.concatenate([high, high, low, jnp.zeros((8, LANES), jnp.float32)], axis=0)
-    mix_ref[...] = jnp.transpose(mix)[0:MODES].astype(jnp.bfloat16)
+    mix_ref[...] = jnp.transpose(mix)[0:MODES]
 
 
 def factor(parts):
@@ -450,7 +513,7 @@
         in_specs=[VMEM_SPEC] * 7,
         out_specs=(VMEM_SPEC, VMEM_SPEC),
         out_shape=(
-            pltpu.VMEM((MODES, LANES), jnp.bfloat16),
+            pltpu.VMEM((MODES, LANES), jnp.float32),
             pltpu.VMEM((8, LANES), jnp.float32),
         ),
         compiler_params=pltpu.CompilerParams(vmem_limit_bytes=4 << 20),
@@ -458,74 +521,185 @@
     )(*[near(x) for x in parts], *tables)
 
 
-def update_kernel(mix_ref, snap_ref, basis_ref, out_ref, *, chunk):
-    groups, _, width = out_ref.shape
-    mix = mix_ref[...]
-    base = pl.program_id(0) * width
-    for i in range(width // chunk):
-        at = pl.ds(pl.multiple_of(base + i * chunk, chunk), chunk)
-        snap = snap_ref[:, i * chunk : (i + 1) * chunk]
-        stack = stack_rows(snap, basis_ref, at)
-        high = stack.astype(jnp.bfloat16).astype(jnp.float32)
-        zero = jnp.zeros((8, chunk), jnp.float32)
-        joined = jnp.concatenate([high, stack - high, high, zero], axis=0)
-        out = jnp.dot(mix, joined.astype(jnp.bfloat16), preferred_element_type=jnp.float32)
-        for g in range(groups):
-            out_ref[g, :, i * chunk : (i + 1) * chunk] = out[8 * g : 8 * g + 8]
-
-
-def update(mix, snap, basis, width=4096, chunk=1024):
-    cols = snap.shape[1]
+def turned_mix(mix, here):
+    lane = lax.broadcasted_iota(jnp.int32, mix.shape, 1)
+    inside = lax.rem(lane, ROWS)
+    turned = lane - inside + PAD + lax.rem(inside + (MODES - PAD) + PAD * here, MODES)
+    source = jnp.where((inside < PAD) | (lane >= 3 * ROWS), lane, turned)
+    return jnp.take_along_axis(mix, source, axis=1).astype(jnp.bfloat16)
+
+
+def mix_rows(mix_ref, here, g):
+    at = pl.multiple_of(PAD * lax.rem(here + g, 4), PAD)
+    return mix_ref[pl.ds(at, PAD), :]
+
+
+def mixed(mix, stack):
+    high = stack.astype(jnp.bfloat16).astype(jnp.float32)
+    zero = jnp.zeros((8, stack.shape[1]), jnp.float32)
+    joined = jnp.concatenate([high, stack - high, high, zero], axis=0)
+    return jnp.dot(mix, joined.astype(jnp.bfloat16), preferred_element_type=jnp.float32)
+
+
+def update_kernel(here_ref, mix_ref, *refs, chunk):
+    stack_refs, out_refs = refs[:5], refs[5:]
+    here = here_ref[0]
+    mix = jnp.concatenate([mix_rows(mix_ref, here, g) for g in range(4)], axis=0)
+    mix = turned_mix(mix, here)
+    for start in range(0, out_refs[0].shape[1], chunk):
+        first = SHARED + start
+        out = mixed(mix, stacked(stack_refs, slice(first, first + chunk)))
+        for g, ref in enumerate(out_refs):
+            ref[:, start : start + chunk] = out[PAD * g : PAD * g + PAD]
+
+
+def update(here, mix, stack, chunk=1024):
+    cols = stack[0].shape[1] - SHARED
     return pl.pallas_call(
         functools.partial(update_kernel, chunk=chunk),
-        grid=(cols // width,),
-        in_specs=[VMEM_SPEC, pl.BlockSpec((PAD, width), lambda i: (0, i)), VMEM_SPEC],
-        out_specs=pl.BlockSpec((4, PAD, width), lambda i: (0, 0, i)),
-        out_shape=pltpu.HBM((4, PAD, cols), jnp.float32),
+        in_specs=[SMEM_SPEC] + [VMEM_SPEC] * 6,
+        out_specs=[VMEM_SPEC] * 4,
+        out_shape=[pltpu.VMEM((PAD, cols), jnp.float32)] * 4,
         compiler_params=pltpu.CompilerParams(vmem_limit_bytes=8 << 20),
         name="update",
-    )(near(mix), far(snap), near(basis))
+    )(here, near(mix), *[near(x) for x in stack])
+
+
+def own_kernel(here_ref, mix_ref, *refs, cols, chunk):
+    stack_refs, (hi_ref, over_ref, lo_ref) = refs[:5], refs[5:8]
+    basis_hbm, out_hbm, mine, snap, buf, in_sems, out_sems = refs[8:]
+    here = here_ref[0]
+    tiles = SHARED // LANES
+    blocks = [lax.rem(here + 1 + b, 4) for b in range(4)]
+    reads = []
+    for b in range(3):
+        at = pl.multiple_of(blocks[b] * cols, LANES)
+        source = basis_hbm.at[:, pl.ds(at, SHARED)]
+        reads.append(pltpu.make_async_copy(source, mine.at[b], in_sems.at[b]))
+    for copy in reads:
+        copy.start()
+    mix = turned_mix(mix_rows(mix_ref, here, 0), here)
+    for b, ref in enumerate((hi_ref, over_ref, lo_ref)):
+        snap[b] = jnp.zeros((PAD, SHARED), jnp.float32)
+        for k in range(2 * tiles):
+            which, tile = divmod(k, tiles)
+            at = 3 * SHARED + k // 8 * LANES
+            line = ref[k % 8 : k % 8 + 1, at : at + LANES]
+            snap[b, which : which + 1, tile * LANES : (tile + 1) * LANES] = line
+    for copy in reads:
+        copy.wait()
+    writes = []
+    for b in range(4):
+        for start in range(0, SHARED, chunk):
+            at = slice(start, start + chunk)
+            if b == 3:
+                stack = stacked(stack_refs, at)
+            else:
+                wide = slice(b * SHARED + start, b * SHARED + start + chunk)
+                rows = [snap[b, :, at], mine[b, :, at]]
+                rows += [ref[:, wide] for ref in (hi_ref, over_ref, lo_ref)]
+                stack = jnp.concatenate(rows, axis=0)
+            buf[b, :, at] = mixed(mix, stack)
+        target = pl.ds(pl.multiple_of(blocks[b] * cols, LANES), SHARED)
+        writes.append(pltpu.make_async_copy(buf.at[b], out_hbm.at[:, target], out_sems.at[b]))
+        writes[-1].start()
+    for copy in writes:
+        copy.wait()
+
+
+def own(here, mix, stack, received, basis, chunk=1024):
+    cols = basis.shape[1] // 4
+    return pl.pallas_call(
+        functools.partial(own_kernel, cols=cols, chunk=chunk),
+        in_specs=[SMEM_SPEC] + [VMEM_SPEC] * 9 + [HBM_SPEC],
+        out_specs=HBM_SPEC,
+        out_shape=pltpu.HBM(basis.shape, jnp.float32),
+        scratch_shapes=[
+            pltpu.VMEM((3, PAD, SHARED), jnp.float32),
+            pltpu.VMEM((3, PAD, SHARED), jnp.float32),
+            pltpu.VMEM((4, PAD, SHARED), jnp.float32),
+            pltpu.SemaphoreType.DMA((3,)),
+            pltpu.SemaphoreType.DMA((4,)),
+        ],
+        compiler_params=pltpu.CompilerParams(vmem_limit_bytes=10 << 20),
+        name="own",
+    )(here, *[near(x) for x in (mix, *stack, *received)], far(basis))
+
+
+def join_kernel(here_ref, *refs):
+    parts, (_, out_hbm, sems) = refs[:4], refs[4:]
+    cols = out_hbm.shape[1] // 4
+    copies = []
+    for g, part in enumerate(parts):
+        at = pl.multiple_of(lax.rem(here_ref[0] + g, 4) * cols + SHARED, LANES)
+        target = out_hbm.at[:, pl.ds(at, cols - SHARED)]
+        copies.append(pltpu.make_async_copy(part, target, sems.at[g]))
+        copies[-1].start()
+    for copy in copies:
+        copy.wait()
+
+
+def join(here, parts, whole):
+    return pl.pallas_call(
+        join_kernel,
+        in_specs=[SMEM_SPEC] + [VMEM_SPEC] * 4 + [HBM_SPEC],
+        out_specs=HBM_SPEC,
+        out_shape=pltpu.HBM(whole.shape, jnp.float32),
+        scratch_shapes=[pltpu.SemaphoreType.DMA((4,))],
+        input_output_aliases={5: 0},
+        compiler_params=pltpu.CompilerParams(vmem_limit_bytes=2 << 20),
+        name="join",
+    )(here, *[near(x) for x in parts], far(whole))
 
 
 def program(velocity, basis, levels, profile_index, advect):
     n_space, n_mode = lax.axis_size("space"), lax.axis_size("mode")
     comps, cx, _, ny = velocity.shape
-    modes_here, cols_here = basis.shape
-    cols = cols_here // n_mode
+    here = lax.axis_index("mode").astype(jnp.int32).reshape(1)
 
     def shifted(x, axis, by):
         size = lax.axis_size(axis)
         return lax.ppermute(x, axis, [(i, (i + by) % size) for i in range(size)])
 
-    face_lo, face_hi = pack(velocity)
+    face_lo, face_hi, plane_lo, plane_hi, *blocks = pack(here, velocity, basis)
     zlo = shifted(face_hi, "mode", 1)
     zhi = shifted(face_lo, "mode", -1)
-    xlo = shifted(velocity[:, cx - 2 :], "space", 1)
-    xhi = shifted(velocity[:, :2], "space", -1)
+    lo = shifted(blocks[1], "mode", 1)
+    hi = shifted(blocks[3], "mode", -1)
+    over = shifted(blocks[2], "mode", 2)
+    xlo = shifted(plane_hi, "space", 1)
+    xhi = shifted(plane_lo, "space", -1)
     near_lo = zlo.reshape(comps, 2, cx, ny)[:, 1]
     near_hi = zhi.reshape(comps, 2, cx, ny)[:, 0]
     corner_lo = jnp.stack([near_lo[:, -1], near_hi[:, -1]], axis=1)
     corner_hi = jnp.stack([near_lo[:, 0], near_hi[:, 0]], axis=1)
     corner_lo = shifted(corner_lo, "space", 1)
     corner_hi = shifted(corner_hi, "space", -1)
-    shared = basis.reshape(modes_here, n_mode, cols).transpose(1, 0, 2)
-    shared = lax.all_to_all(shared, "mode", split_axis=0, concat_axis=0, tiled=True)
-
-    snap = snapshots(
+    snap, plus, minus, across = snapshots(
         velocity,
         levels,
         profile_index,
         advect,
+        here,
+        basis,
         (zlo, zhi, face_lo, face_hi, corner_lo, corner_hi, velocity, xlo, xhi),
     )
-    total = gram(snap, shared)
+    lo_early = shifted(plus, "mode", 1)
+    hi_early = shifted(minus, "mode", -1)
+    stack = (snap, blocks[0], hi, over, lo)
+    total = gram(here, stack)
     total = ring_sum(total, ring_parts(total, "space", n_space, 1, 2))
     total = ring_sum(total, ring_parts(total, "space", n_space, 2, 4))
     total = ring_sum(total, ring_parts(total, "space", n_space, 8, 4))
-    mix, sigma = factor([total] + ring_parts(total, "mode", n_mode, 1, n_mode))
-    updated = update(mix, snap, shared)
-    modes = lax.all_to_all(updated, "mode", split_axis=0, concat_axis=0, tiled=True)
-    modes = modes.transpose(1, 0, 2).reshape(modes_here, cols_here)
+    parts = [total] + ring_parts(total, "mode", n_mode, 1, n_mode)
+    over_early = shifted(across, "mode", 2)
+    mix, sigma = factor(parts)
+    out_own, out_next, out_over, out_prev = update(here, mix, stack)
+    back_lo = shifted(out_next, "mode", 1)
+    back_hi = shifted(out_prev, "mode", -1)
+    back_over = shifted(out_over, "mode", 2)
+    mine = own(here, mix, stack, (hi_early, over_early, lo_early), basis)
+    modes = join(here, (out_own, back_hi, back_over, back_lo), mine)
     return (modes, sigma[0, :MODES])
 
 

time: 158 us -> 147 us (0.930)
  waiting for transfers between devices: 74 us -> 58.1 us
  starting transfers between devices: 35.2 us -> 41 us
  local copies, waits for them, and re-layouts: 3.79 us -> 0.57 us
    all_to_all x2 -> x0, waiting for transfers between devices: 33.2 us -> none  [the longest x1 33.2 us: program(): lax.all_to_all(updated, 'mode', split_axis=0, concat_axis=0, tiled=True)]
    ppermute x10, waiting for transfers between devices: 11.6 us -> 29.8 us  [ring_parts(): lax.ppermute(x, axis, pairs)]
    ppermute x6 -> x15, starting transfers between devices: 13.7 us -> 25.7 us  [shifted(): return lax.ppermute(x, axis, [(i, (i + by) % size) for i in range(size)])]
    all_to_all x2 -> x0, starting transfers between devices: 8.12 us -> none  [the longest x1 4.42 us: program(): lax.all_to_all(shared, 'mode', split_axis=0, concat_axis=0, tiled=True)]
    ppermute x10, starting transfers between devices: 13.3 us -> 15.3 us  [ring_parts(): lax.ppermute(x, axis, pairs)]
    unnamed x15 -> x14, local copies, waits for them, and re-layouts: 1.71 us -> 0.04 us
    pallas_call x4 -> x6, Pallas kernels: 30.3 us -> 31.8 us  [the longest x1 22.4 us: snapshots(): pl.pallas_call(stencil_kernel, grid=(comps,), in_specs=[SMEM_SPEC, pl.Blo...]
    ppermute x6 -> x15, waiting for transfers between devices: 29.2 us -> 28.3 us  [shifted(): return lax.ppermute(x, axis, [(i, (i + by) % size) for i in range(size)])]
  transfers between devices with their start and end apart: 18 -> 25, of which waited for: 12 -> 14; matrix products, arithmetic and copies ran while one was open for 1% -> 0% of each run, Pallas kernels for 13% -> 28%
where the time goes in v1:
time: 147 us; the launch traced here: 146 us
  waiting for transfers between devices  58.1 us (40%)
  Pallas kernels  45 us (31%)
  starting transfers between devices  41 us (28%)
    ppermute x10, waiting for transfers between devices, ring_parts(): lax.ppermute(x, axis, pairs)  29.8 us
    ppermute x15, waiting for transfers between devices, shifted(): return lax.ppermute(x, axis, [(i, (i + by) % size) for i in range(size)])  28.3 us
    ppermute x15, starting transfers between devices, shifted(): return lax.ppermute(x, axis, [(i, (i + by) % size) for i in range(size)])  25.7 us
    pallas_call x1, Pallas kernels, snapshots(): pl.pallas_call(stencil_kernel, grid=(comps,), in_specs=[SMEM_SPEC, pl.Blo...  22.4 us
    ppermute x10, starting transfers between devices, ring_parts(): lax.ppermute(x, axis, pairs)  15.3 us
    pallas_call x1, Pallas kernels, factor(): pl.pallas_call(factor_kernel, in_specs=[VMEM_SPEC] * 7, out_specs=(VMEM_S...  13.2 us
    pallas_call x1, Pallas kernels, own(): pl.pallas_call(functools.partial(own_kernel, cols=cols, chunk=chunk), in_...  3.1 us
  transfers between devices with their start and end apart: 25, of which 14 were waited for; matrix products, arithmetic and copies ran while one was open for 0% of the time, Pallas kernels for 28%

profile of v1, /device:TPU:0, one launch (start us, length us, event | category | flops | bytes accessed | tf_op | source)
XLA Modules:
  0.0 145.6 jit_solution(11578656945493071900)
XLA Ops:
  0.6 0.0 copy-start
  0.6 0.0 copy-start.3
  0.7 2.8 %pack.1 = (f32[96,256]{1,0:T(8,128)S(1)}, f32[96,256]{1,0:T(8,128)S(1)}, f32[3,2,128,256]{3,2,1,0:T(8,128)S(1)}, f32[3,2,128,256]{3,2,1,0:T(8,128)S(1)}, f32[8,2...) custom-call(s32[1]{0:T(128)} %bitcast.here_ref, ...), custom_call_target="tpu_custom_call" | custom-call | tf_op jit(solution)/shard_map/pack/pallas_call | solution.py:103
  3.5 1.7 %collective-permute-start = (f32[96,256]{1,0:T(8,128)S(1)}, f32[96,256]{1,0:T(8,128)S(1)}, u32[]{:S(2)}, u32[]{:S(2)}) collective-permute-start(f32[96,256]{1,0:T(8,128)S(1)} %get-tuple-element.20.face_hi_ref), channel_id=1, source_target_pairs={{0,1},{1,2},{2,3},{3,0},{4,5},{5,6},{6,7},{7,4},{8,9},{9,10},{10,1... | collective-permute-start | bytes 294920 | tf_op jit(solution)/shard_map/ppermute | solution.py:662
  5.2 1.6 %collective-permute-start.1 = (f32[96,256]{1,0:T(8,128)S(1)}, f32[96,256]{1,0:T(8,128)S(1)}, u32[]{:S(2)}, u32[]{:S(2)}) collective-permute-start(f32[96,256]{1,0:T(8,128)S(1)} %get-tuple-element.21.face_lo_ref), channel_id=1, source_target_pairs={{0,3},{1,0},{2,1},{3,2},{4,7},{5,4},{6,5},{7,6},{8,11},{9,8},{10,9... | collective-permute-start | bytes 294920 | tf_op jit(solution)/shard_map/ppermute | solution.py:662
  6.8 0.0 collective-permute-start.4
  6.8 5.5 %collective-permute-start.5 = (f32[3,2,128,256]{3,2,1,0:T(8,128)S(1)}, f32[3,2,128,256]{3,2,1,0:T(8,128)S(1)}, u32[]{:S(2)}, u32[]{:S(2)}) collective-permute-start(f32[3,2,128,256]{3,2,1,0:T(8,128)S(1)} %get-tuple-element.23), channel_id=1, source_target_pairs={{0,124},{4,0},{8,4},{12,8},{16,12},{20,16},{24,20},{28,24},{32,28}... | collective-permute-start | bytes 2359304 | tf_op jit(solution)/shard_map/ppermute | solution.py:662
  12.3 0.0 collective-permute-done.zlo_ref
  12.3 0.0 collective-permute-done.1.zhi_ref
  12.3 0.1 collective-permute-start.2
  12.4 5.1 %collective-permute-start.3 = (f32[3,2,256]{2,1,0:T(2,128)S(1)}, f32[3,2,256]{2,1,0:T(2,128)S(1)}, u32[]{:S(2)}, u32[]{:S(2)}) collective-permute-start(f32[3,2,256]{2,1,0:T(2,128)S(1)} %pad_maximum_fusion.1), channel_id=1, source_target_pairs={{0,124},{4,0},{8,4},{12,8},{16,12},{20,16},{24,20},{28,24},{32,28}... | collective-permute-start | bytes 18440 | tf_op jit(solution)/shard_map/ppermute | solution.py:662
  17.6 1.5 %collective-permute-start.6 = (f32[8,24576]{1,0:T(8,128)S(1)}, f32[8,24576]{1,0:T(8,128)S(1)}, u32[]{:S(2)}, u32[]{:S(2)}) collective-permute-start(f32[8,24576]{1,0:T(8,128)S(1)} %get-tuple-element.26), channel_id=1, source_target_pairs={{0,3},{1,0},{2,1},{3,2},{4,7},{5,4},{6,5},{7,6},{8,11},{9,8},{10,9... | collective-permute-start | bytes 2359304 | tf_op jit(solution)/shard_map/ppermute | solution.py:662
  19.1 2.9 %collective-permute-done.2.corner_lo_ref = f32[3,2,256]{2,1,0:T(2,128)S(1)} collective-permute-done((f32[3,2,256]{2,1,0:T(2,128)S(1)}, f32[3,2,256]{2,1,0:T(2,128)S(1)}, u32[]{:S(2)}, u32[]{:S(2)}) %collective-permute-start.2) | collective-permute-done | bytes 6176 | tf_op jit(solution)/shard_map/ppermute | solution.py:662
  22.0 1.8 %collective-permute-start.7 = (f32[8,24576]{1,0:T(8,128)S(1)}, f32[8,24576]{1,0:T(8,128)S(1)}, u32[]{:S(2)}, u32[]{:S(2)}) collective-permute-start(f32[8,24576]{1,0:T(8,128)S(1)} %get-tuple-element.27), channel_id=1, source_target_pairs={{0,2},{1,3},{2,0},{3,1},{4,6},{5,7},{6,4},{7,5},{8,10},{9,11},{10,... | collective-permute-start | bytes 2359304 | tf_op jit(solution)/shard_map/ppermute | solution.py:662
  23.8 0.0 collective-permute-done.3.corner_hi_ref
  23.8 0.6 collective-permute-start.8
  24.4 0.0 collective-permute-done.4.xlo_hbm
  24.4 0.0 collective-permute-done.5.xhi_hbm
  24.5 22.4 %stencil.1 = (f32[8,24576]{1,0:T(8,128)S(1)}, f32[8,26624]{1,0:T(8,128)S(1)}, f32[8,26624]{1,0:T(8,128)S(1)}, f32[8,26624]{1,0:T(8,128)S(1)}) custom-call(f32[8]{0:T(128)S(1)} %copy-done.5, s32[1,256]{1,0:T(1,128)S(1)} %bitcast.17, f32[1,256]{1,0:T(1,128)S(1)} %bitcast.18, bf16[256,128]{1,0:T(8,128)(2,1)S(1)} %copy-done, ...), custom_call_target="tpu_custom_call" | custom-call | tf_op jit(solution)/shard_map/stencil/pallas_call | solution.py:347
  46.9 0.0 copy-start.1
  46.9 0.0 copy-start.2
  46.9 0.0 copy-start.6
  46.9 2.7 %collective-permute-start.22 = (f32[8,26624]{1,0:T(8,128)S(1)}, f32[8,26624]{1,0:T(8,128)S(1)}, u32[]{:S(2)}, u32[]{:S(2)}) collective-permute-start(f32[8,26624]{1,0:T(8,128)S(1)} %get-tuple-element.34), channel_id=1, source_target_pairs={{0,3},{1,0},{2,1},{3,2},{4,7},{5,4},{6,5},{7,6},{8,11},{9,8},{10,9... | collective-permute-start | bytes 2555912 | tf_op jit(solution)/shard_map/ppermute | solution.py:662
  49.6 0.0 collective-permute-done.6.refs_2_
  49.6 0.0 collective-permute-done.7.refs_3_
  49.6 5.7 %collective-permute-done.8.refs_4_ = f32[8,24576]{1,0:T(8,128)S(1)} collective-permute-done((f32[8,24576]{1,0:T(8,128)S(1)}, f32[8,24576]{1,0:T(8,128)S(1)}, u32[]{:S(2)}, u32[]{:S(2)}) %collective-permute-start.8) | collective-permute-done | bytes 786464 | tf_op jit(solution)/shard_map/ppermute | solution.py:662
  55.4 1.4 gram.1
  56.8 0.0 collective-permute-start.9
  56.8 1.2 collective-permute-done.9
  58.0 2.9 %collective-permute-start.12 = (f32[40,128]{1,0:T(8,128)S(1)}, f32[40,128]{1,0:T(8,128)S(1)}, u32[]{:S(2)}, u32[]{:S(2)}) collective-permute-start(f32[40,128]{1,0:T(8,128)S(1)} %add.21), channel_id=1, source_target_pairs={{0,24},{4,28},{8,0},{12,4},{16,8},{20,12},{24,16},{28,20},{32,56},... | collective-permute-start | bytes 61448 | tf_op jit(solution)/shard_map/ppermute | solution.py:439
  60.9 0.0 collective-permute-start.11
  60.9 2.0 %collective-permute-start.10 = (f32[40,128]{1,0:T(8,128)S(1)}, f32[40,128]{1,0:T(8,128)S(1)}, u32[]{:S(2)}, u32[]{:S(2)}) collective-permute-start(f32[40,128]{1,0:T(8,128)S(1)} %add.21), channel_id=1, source_target_pairs={{0,16},{4,20},{8,24},{12,28},{16,0},{20,4},{24,8},{28,12},{32,48},... | collective-permute-start | bytes 61448 | tf_op jit(solution)/shard_map/ppermute | solution.py:439
  62.9 1.8 %collective-permute-start.23 = (f32[8,26624]{1,0:T(8,128)S(1)}, f32[8,26624]{1,0:T(8,128)S(1)}, u32[]{:S(2)}, u32[]{:S(2)}) collective-permute-start(f32[8,26624]{1,0:T(8,128)S(1)} %get-tuple-element.35), channel_id=1, source_target_pairs={{0,2},{1,3},{2,0},{3,1},{4,6},{5,7},{6,4},{7,5},{8,10},{9,11},{10,... | collective-permute-start | bytes 2555912 | tf_op jit(solution)/shard_map/ppermute | solution.py:662
  64.7 0.0 collective-permute-done.12
  64.7 0.0 collective-permute-start.24
  64.7 1.2 collective-permute-done.11
  65.9 0.3 collective-permute-done.10
  66.2 3.2 %collective-permute-start.15 = (f32[40,128]{1,0:T(8,128)S(1)}, f32[40,128]{1,0:T(8,128)S(1)}, u32[]{:S(2)}, u32[]{:S(2)}) collective-permute-start(f32[40,128]{1,0:T(8,128)S(1)} %add_add_fusion.1), channel_id=1, source_target_pairs={{0,96},{4,100},{8,104},{12,108},{16,112},{20,116},{24,120},{28,124... | collective-permute-start | bytes 61448 | tf_op jit(solution)/shard_map/ppermute | solution.py:439
  69.4 0.0 collective-permute-start.14
  69.4 1.5 %collective-permute-done.15 = f32[40,128]{1,0:T(8,128)S(1)} collective-permute-done((f32[40,128]{1,0:T(8,128)S(1)}, f32[40,128]{1,0:T(8,128)S(1)}, u32[]{:S(2)}, u32[]{:S(2)}) %collective-permute-start.15) | collective-permute-done | bytes 20512 | tf_op jit(solution)/shard_map/ppermute | solution.py:439
  70.9 2.8 %collective-permute-start.13 = (f32[40,128]{1,0:T(8,128)S(1)}, f32[40,128]{1,0:T(8,128)S(1)}, u32[]{:S(2)}, u32[]{:S(2)}) collective-permute-start(f32[40,128]{1,0:T(8,128)S(1)} %add_add_fusion.1), channel_id=1, source_target_pairs={{0,64},{4,68},{8,72},{12,76},{16,80},{20,84},{24,88},{28,92},{32,9... | collective-permute-start | bytes 61448 | tf_op jit(solution)/shard_map/ppermute | solution.py:439
  73.7 0.7 collective-permute-done.14
  74.4 1.8 %collective-permute-done.13 = f32[40,128]{1,0:T(8,128)S(1)} collective-permute-done((f32[40,128]{1,0:T(8,128)S(1)}, f32[40,128]{1,0:T(8,128)S(1)}, u32[]{:S(2)}, u32[]{:S(2)}) %collective-permute-start.13) | collective-permute-done | bytes 20512 | tf_op jit(solution)/shard_map/ppermute | solution.py:439
  76.2 2.7 %collective-permute-start.18 = (f32[40,128]{1,0:T(8,128)S(1)}, f32[40,128]{1,0:T(8,128)S(1)}, u32[]{:S(2)}, u32[]{:S(2)}) collective-permute-start(f32[40,128]{1,0:T(8,128)S(1)} %add_add_fusion.g0_ref), channel_id=1, source_target_pairs={{0,3},{1,0},{2,1},{3,2},{4,7},{5,4},{6,5},{7,6},{8,11},{9,8},{10,9... | collective-permute-start | bytes 61448 | tf_op jit(solution)/shard_map/ppermute | solution.py:439
  78.9 0.5 collective-permute-start.17
  79.4 7.1 %collective-permute-done.18.g3_ref = f32[40,128]{1,0:T(8,128)S(1)} collective-permute-done((f32[40,128]{1,0:T(8,128)S(1)}, f32[40,128]{1,0:T(8,128)S(1)}, u32[]{:S(2)}, u32[]{:S(2)}) %collective-permute-start.18) | collective-permute-done | bytes 20512 | tf_op jit(solution)/shard_map/ppermute | solution.py:439
  86.6 1.1 collective-permute-start.16
  87.7 16.0 %collective-permute-done.17.g2_ref = f32[40,128]{1,0:T(8,128)S(1)} collective-permute-done((f32[40,128]{1,0:T(8,128)S(1)}, f32[40,128]{1,0:T(8,128)S(1)}, u32[]{:S(2)}, u32[]{:S(2)}) %collective-permute-start.17) | collective-permute-done | bytes 20512 | tf_op jit(solution)/shard_map/ppermute | solution.py:439
  103.7 0.1 collective-permute-done.16.g1_ref
  103.7 0.0 copy-done.2
  103.7 13.2 %factor.1 = (f32[32,128]{1,0:T(8,128)S(1)}, f32[8,128]{1,0:T(8,128)S(1)}) custom-call(f32[40,128]{1,0:T(8,128)S(1)} %add_add_fusion.g0_ref, f32[40,128]{1,0:T(8,128)S(1)} %collective-permute-done.16.g1_ref, f32[40,128]{1,0:T(8,128)S(1)} %collective-permute-done.17.g2_ref, f32[40,128]{1,0:T(8,128)S(1)} %collective-permute-done.18.g3_ref, ...), custom_call_target="tpu_custom_call" | custom-call | tf_op jit(solution)/shard_map/factor/pallas_call | solution.py:511
  117.0 0.8 update.1
  117.7 0.7 collective-permute-start.19
  118.4 1.8 %collective-permute-start.20 = (f32[8,16384]{1,0:T(8,128)S(1)}, f32[8,16384]{1,0:T(8,128)S(1)}, u32[]{:S(2)}, u32[]{:S(2)}) collective-permute-start(f32[8,16384]{1,0:T(8,128)S(1)} %get-tuple-element.32), channel_id=1, source_target_pairs={{0,2},{1,3},{2,0},{3,1},{4,6},{5,7},{6,4},{7,5},{8,10},{9,11},{10,... | collective-permute-start | bytes 1572872 | tf_op jit(solution)/shard_map/ppermute | solution.py:662
  120.2 0.0 collective-permute-done.22.refs_5_
  120.2 0.8 collective-permute-start.21
  121.0 0.5 slice_bitcast_fusion.2
  121.5 0.0 collective-permute-done.23.refs_6_
  121.5 0.0 collective-permute-done.24.refs_7_
  121.5 3.1 %own.1.refs_4_ = f32[8,98304]{1,0:T(8,128)} custom-call(s32[1]{0:T(128)} %bitcast.here_ref, f32[32,128]{1,0:T(8,128)S(1)} %get-tuple-element.29.mix_ref, f32[8,24576]{1,0:T(8,128)S(1)} %get-tuple-element.24.refs_0_, f32[8,24576]{1,0:T(8,128)S(1)} %get-tuple-element.25.refs_1_, f32[8,24576]{1,0:T(8,128)S(1)} %collective-permute-done.6.refs_2_, ...), custom_call_target="tpu_custom_call" | custom-call | tf_op jit(solution)/shard_map/own/pallas_call | solution.py:612
  124.6 8.0 %collective-permute-done.19.refs_1_ = f32[8,16384]{1,0:T(8,128)S(1)} collective-permute-done((f32[8,16384]{1,0:T(8,128)S(1)}, f32[8,16384]{1,0:T(8,128)S(1)}, u32[]{:S(2)}, u32[]{:S(2)}) %collective-permute-start.19) | collective-permute-done | bytes 524320 | tf_op jit(solution)/shard_map/ppermute | solution.py:662
  132.6 2.2 %collective-permute-done.20.refs_2_ = f32[8,16384]{1,0:T(8,128)S(1)} collective-permute-done((f32[8,16384]{1,0:T(8,128)S(1)}, f32[8,16384]{1,0:T(8,128)S(1)}, u32[]{:S(2)}, u32[]{:S(2)}) %collective-permute-start.20) | collective-permute-done | bytes 524320 | tf_op jit(solution)/shard_map/ppermute | solution.py:662
  134.8 9.5 %collective-permute-done.21.refs_3_ = f32[8,16384]{1,0:T(8,128)S(1)} collective-permute-done((f32[8,16384]{1,0:T(8,128)S(1)}, f32[8,16384]{1,0:T(8,128)S(1)}, u32[]{:S(2)}, u32[]{:S(2)}) %collective-permute-start.21) | collective-permute-done | bytes 524320 | tf_op jit(solution)/shard_map/ppermute | solution.py:662
  144.3 1.3 join.1
  (16 shorter events, 0.1 us)
Async XLA Ops:
  0.6 23.8 %copy-start = (bf16[256,128]{1,0:T(8,128)(2,1)S(1)}, bf16[256,128]{1,0:T(8,128)(2,1)}, u32[]{:S(2)}) copy-start(bf16[256,128]{1,0:T(8,128)(2,1)} %constant.12.clone.sum_ref) | copy-start | bytes 196612
  0.6 23.8 %copy-start.3 = (s32[256]{0:T(256)S(1)}, s32[256]{0:T(256)}, u32[]{:S(2)}) copy-start(s32[256]{0:T(256)} %param.12) | copy-start | bytes 3076
  0.7 23.8 %copy-start.4 = (f32[256]{0:T(256)S(1)}, f32[256]{0:T(256)}, u32[]{:S(2)}) copy-start(f32[256]{0:T(256)} %param.13) | copy-start | bytes 3076
  0.7 23.8 %copy-start.5 = (f32[8]{0:T(128)S(1)}, f32[8]{0:T(128)}, u32[]{:S(2)}) copy-start(f32[8]{0:T(128)} %levels_ref.1) | copy-start | bytes 100
  3.5 8.8 %collective-permute-start = (f32[96,256]{1,0:T(8,128)S(1)}, f32[96,256]{1,0:T(8,128)S(1)}, u32[]{:S(2)}, u32[]{:S(2)}) collective-permute-start(f32[96,256]{1,0:T(8,128)S(1)} %get-tuple-element.20.face_hi_ref), channel_id=1, source_target_pairs={{0,1},{1,2},{2,3},{3,0},{4,5},{5,6},{6,7},{7,4},{8,9},{9,10},{10,1... | collective-permute-start | bytes 294920 | tf_op jit(solution)/shard_map/ppermute | solution.py:662
  5.2 7.1 %collective-permute-start.1 = (f32[96,256]{1,0:T(8,128)S(1)}, f32[96,256]{1,0:T(8,128)S(1)}, u32[]{:S(2)}, u32[]{:S(2)}) collective-permute-start(f32[96,256]{1,0:T(8,128)S(1)} %get-tuple-element.21.face_lo_ref), channel_id=1, source_target_pairs={{0,3},{1,0},{2,1},{3,2},{4,7},{5,4},{6,5},{7,6},{8,11},{9,8},{10,9... | collective-permute-start | bytes 294920 | tf_op jit(solution)/shard_map/ppermute | solution.py:662
  6.8 17.6 %collective-permute-start.4 = (f32[3,2,128,256]{3,2,1,0:T(8,128)S(1)}, f32[3,2,128,256]{3,2,1,0:T(8,128)S(1)}, u32[]{:S(2)}, u32[]{:S(2)}) collective-permute-start(f32[3,2,128,256]{3,2,1,0:T(8,128)S(1)} %get-tuple-element.22), channel_id=1, source_target_pairs={{0,4},{4,8},{8,12},{12,16},{16,20},{20,24},{24,28},{28,32},{32,36}... | collective-permute-start | bytes 2359304 | tf_op jit(solution)/shard_map/ppermute | solution.py:662
  6.8 17.6 %collective-permute-start.5 = (f32[3,2,128,256]{3,2,1,0:T(8,128)S(1)}, f32[3,2,128,256]{3,2,1,0:T(8,128)S(1)}, u32[]{:S(2)}, u32[]{:S(2)}) collective-permute-start(f32[3,2,128,256]{3,2,1,0:T(8,128)S(1)} %get-tuple-element.23), channel_id=1, source_target_pairs={{0,124},{4,0},{8,4},{12,8},{16,12},{20,16},{24,20},{28,24},{32,28}... | collective-permute-start | bytes 2359304 | tf_op jit(solution)/shard_map/ppermute | solution.py:662
  12.3 9.7 %collective-permute-start.2 = (f32[3,2,256]{2,1,0:T(2,128)S(1)}, f32[3,2,256]{2,1,0:T(2,128)S(1)}, u32[]{:S(2)}, u32[]{:S(2)}) collective-permute-start(f32[3,2,256]{2,1,0:T(2,128)S(1)} %pad_maximum_fusion), channel_id=1, source_target_pairs={{0,4},{4,8},{8,12},{12,16},{16,20},{20,24},{24,28},{28,32},{32,36}... | collective-permute-start | bytes 18440 | tf_op jit(solution)/shard_map/ppermute | solution.py:662
  12.4 11.4 %collective-permute-start.3 = (f32[3,2,256]{2,1,0:T(2,128)S(1)}, f32[3,2,256]{2,1,0:T(2,128)S(1)}, u32[]{:S(2)}, u32[]{:S(2)}) collective-permute-start(f32[3,2,256]{2,1,0:T(2,128)S(1)} %pad_maximum_fusion.1), channel_id=1, source_target_pairs={{0,124},{4,0},{8,4},{12,8},{16,12},{20,16},{24,20},{28,24},{32,28}... | collective-permute-start | bytes 18440 | tf_op jit(solution)/shard_map/ppermute | solution.py:662
  17.6 32.1 %collective-permute-start.6 = (f32[8,24576]{1,0:T(8,128)S(1)}, f32[8,24576]{1,0:T(8,128)S(1)}, u32[]{:S(2)}, u32[]{:S(2)}) collective-permute-start(f32[8,24576]{1,0:T(8,128)S(1)} %get-tuple-element.26), channel_id=1, source_target_pairs={{0,3},{1,0},{2,1},{3,2},{4,7},{5,4},{6,5},{7,6},{8,11},{9,8},{10,9... | collective-permute-start | bytes 2359304 | tf_op jit(solution)/shard_map/ppermute | solution.py:662
  22.0 27.6 %collective-permute-start.7 = (f32[8,24576]{1,0:T(8,128)S(1)}, f32[8,24576]{1,0:T(8,128)S(1)}, u32[]{:S(2)}, u32[]{:S(2)}) collective-permute-start(f32[8,24576]{1,0:T(8,128)S(1)} %get-tuple-element.27), channel_id=1, source_target_pairs={{0,2},{1,3},{2,0},{3,1},{4,6},{5,7},{6,4},{7,5},{8,10},{9,11},{10,... | collective-permute-start | bytes 2359304 | tf_op jit(solution)/shard_map/ppermute | solution.py:662
  23.8 31.6 %collective-permute-start.8 = (f32[8,24576]{1,0:T(8,128)S(1)}, f32[8,24576]{1,0:T(8,128)S(1)}, u32[]{:S(2)}, u32[]{:S(2)}) collective-permute-start(f32[8,24576]{1,0:T(8,128)S(1)} %get-tuple-element.28), channel_id=1, source_target_pairs={{0,1},{1,2},{2,3},{3,0},{4,5},{5,6},{6,7},{7,4},{8,9},{9,10},{10,1... | collective-permute-start | bytes 2359304 | tf_op jit(solution)/shard_map/ppermute | solution.py:662
  46.9 56.9 %copy-start.1 = (f32[40,128]{1,0:T(8,128)S(1)}, f32[40,128]{1,0:T(8,128)}, u32[]{:S(2)}) copy-start(f32[40,128]{1,0:T(8,128)} %constant.14.clone.orient_ref) | copy-start | bytes 61444
  46.9 56.8 %copy-start.2 = (s32[40,128]{1,0:T(8,128)S(1)}, s32[40,128]{1,0:T(8,128)}, u32[]{:S(2)}) copy-start(s32[40,128]{1,0:T(8,128)} %constant.13.clone.partner_ref) | copy-start | bytes 61444
  46.9 56.8 %copy-start.6 = (s32[1,128]{1,0:T(1,128)S(1)}, s32[1,128]{1,0:T(1,128)}, u32[]{:S(2)}) copy-start(s32[1,128]{1,0:T(1,128)} %constant.15.clone.keep_ref) | copy-start | bytes 1540
  46.9 73.3 %collective-permute-start.22 = (f32[8,26624]{1,0:T(8,128)S(1)}, f32[8,26624]{1,0:T(8,128)S(1)}, u32[]{:S(2)}, u32[]{:S(2)}) collective-permute-start(f32[8,26624]{1,0:T(8,128)S(1)} %get-tuple-element.34), channel_id=1, source_target_pairs={{0,3},{1,0},{2,1},{3,2},{4,7},{5,4},{6,5},{7,6},{8,11},{9,8},{10,9... | collective-permute-start | bytes 2555912 | tf_op jit(solution)/shard_map/ppermute | solution.py:662
  56.8 1.2 collective-permute-start.9
  58.0 6.7 %collective-permute-start.12 = (f32[40,128]{1,0:T(8,128)S(1)}, f32[40,128]{1,0:T(8,128)S(1)}, u32[]{:S(2)}, u32[]{:S(2)}) collective-permute-start(f32[40,128]{1,0:T(8,128)S(1)} %add.21), channel_id=1, source_target_pairs={{0,24},{4,28},{8,0},{12,4},{16,8},{20,12},{24,16},{28,20},{32,56},... | collective-permute-start | bytes 61448 | tf_op jit(solution)/shard_map/ppermute | solution.py:439
  60.9 5.0 %collective-permute-start.11 = (f32[40,128]{1,0:T(8,128)S(1)}, f32[40,128]{1,0:T(8,128)S(1)}, u32[]{:S(2)}, u32[]{:S(2)}) collective-permute-start(f32[40,128]{1,0:T(8,128)S(1)} %add.21), channel_id=1, source_target_pairs={{0,8},{4,12},{8,16},{12,20},{16,24},{20,28},{24,0},{28,4},{32,40},... | collective-permute-start | bytes 61448 | tf_op jit(solution)/shard_map/ppermute | solution.py:439
  60.9 5.3 %collective-permute-start.10 = (f32[40,128]{1,0:T(8,128)S(1)}, f32[40,128]{1,0:T(8,128)S(1)}, u32[]{:S(2)}, u32[]{:S(2)}) collective-permute-start(f32[40,128]{1,0:T(8,128)S(1)} %add.21), channel_id=1, source_target_pairs={{0,16},{4,20},{8,24},{12,28},{16,0},{20,4},{24,8},{28,12},{32,48},... | collective-permute-start | bytes 61448 | tf_op jit(solution)/shard_map/ppermute | solution.py:439
  62.9 58.6 %collective-permute-start.23 = (f32[8,26624]{1,0:T(8,128)S(1)}, f32[8,26624]{1,0:T(8,128)S(1)}, u32[]{:S(2)}, u32[]{:S(2)}) collective-permute-start(f32[8,26624]{1,0:T(8,128)S(1)} %get-tuple-element.35), channel_id=1, source_target_pairs={{0,2},{1,3},{2,0},{3,1},{4,6},{5,7},{6,4},{7,5},{8,10},{9,11},{10,... | collective-permute-start | bytes 2555912 | tf_op jit(solution)/shard_map/ppermute | solution.py:662
  64.7 56.8 %collective-permute-start.24 = (f32[8,26624]{1,0:T(8,128)S(1)}, f32[8,26624]{1,0:T(8,128)S(1)}, u32[]{:S(2)}, u32[]{:S(2)}) collective-permute-start(f32[8,26624]{1,0:T(8,128)S(1)} %get-tuple-element.36), channel_id=1, source_target_pairs={{0,1},{1,2},{2,3},{3,0},{4,5},{5,6},{6,7},{7,4},{8,9},{9,10},{10,1... | collective-permute-start | bytes 2555912 | tf_op jit(solution)/shard_map/ppermute | solution.py:662
  66.2 4.7 %collective-permute-start.15 = (f32[40,128]{1,0:T(8,128)S(1)}, f32[40,128]{1,0:T(8,128)S(1)}, u32[]{:S(2)}, u32[]{:S(2)}) collective-permute-start(f32[40,128]{1,0:T(8,128)S(1)} %add_add_fusion.1), channel_id=1, source_target_pairs={{0,96},{4,100},{8,104},{12,108},{16,112},{20,116},{24,120},{28,124... | collective-permute-start | bytes 61448 | tf_op jit(solution)/shard_map/ppermute | solution.py:439
  69.4 5.0 %collective-permute-start.14 = (f32[40,128]{1,0:T(8,128)S(1)}, f32[40,128]{1,0:T(8,128)S(1)}, u32[]{:S(2)}, u32[]{:S(2)}) collective-permute-start(f32[40,128]{1,0:T(8,128)S(1)} %add_add_fusion.1), channel_id=1, source_target_pairs={{0,32},{4,36},{8,40},{12,44},{16,48},{20,52},{24,56},{28,60},{32,6... | collective-permute-start | bytes 61448 | tf_op jit(solution)/shard_map/ppermute | solution.py:439
  70.9 5.3 %collective-permute-start.13 = (f32[40,128]{1,0:T(8,128)S(1)}, f32[40,128]{1,0:T(8,128)S(1)}, u32[]{:S(2)}, u32[]{:S(2)}) collective-permute-start(f32[40,128]{1,0:T(8,128)S(1)} %add_add_fusion.1), channel_id=1, source_target_pairs={{0,64},{4,68},{8,72},{12,76},{16,80},{20,84},{24,88},{28,92},{32,9... | collective-permute-start | bytes 61448 | tf_op jit(solution)/shard_map/ppermute | solution.py:439
  76.2 10.4 %collective-permute-start.18 = (f32[40,128]{1,0:T(8,128)S(1)}, f32[40,128]{1,0:T(8,128)S(1)}, u32[]{:S(2)}, u32[]{:S(2)}) collective-permute-start(f32[40,128]{1,0:T(8,128)S(1)} %add_add_fusion.g0_ref), channel_id=1, source_target_pairs={{0,3},{1,0},{2,1},{3,2},{4,7},{5,4},{6,5},{7,6},{8,11},{9,8},{10,9... | collective-permute-start | bytes 61448 | tf_op jit(solution)/shard_map/ppermute | solution.py:439
  78.9 24.7 %collective-permute-start.17 = (f32[40,128]{1,0:T(8,128)S(1)}, f32[40,128]{1,0:T(8,128)S(1)}, u32[]{:S(2)}, u32[]{:S(2)}) collective-permute-start(f32[40,128]{1,0:T(8,128)S(1)} %add_add_fusion.g0_ref), channel_id=1, source_target_pairs={{0,2},{1,3},{2,0},{3,1},{4,6},{5,7},{6,4},{7,5},{8,10},{9,11},{10,... | collective-permute-start | bytes 61448 | tf_op jit(solution)/shard_map/ppermute | solution.py:439
  86.6 17.2 %collective-permute-start.16 = (f32[40,128]{1,0:T(8,128)S(1)}, f32[40,128]{1,0:T(8,128)S(1)}, u32[]{:S(2)}, u32[]{:S(2)}) collective-permute-start(f32[40,128]{1,0:T(8,128)S(1)} %add_add_fusion.g0_ref), channel_id=1, source_target_pairs={{0,1},{1,2},{2,3},{3,0},{4,5},{5,6},{6,7},{7,4},{8,9},{9,10},{10,1... | collective-permute-start | bytes 61448 | tf_op jit(solution)/shard_map/ppermute | solution.py:439
  117.7 14.9 %collective-permute-start.19 = (f32[8,16384]{1,0:T(8,128)S(1)}, f32[8,16384]{1,0:T(8,128)S(1)}, u32[]{:S(2)}, u32[]{:S(2)}) collective-permute-start(f32[8,16384]{1,0:T(8,128)S(1)} %get-tuple-element.31), channel_id=1, source_target_pairs={{0,3},{1,0},{2,1},{3,2},{4,7},{5,4},{6,5},{7,6},{8,11},{9,8},{10,9... | collective-permute-start | bytes 1572872 | tf_op jit(solution)/shard_map/ppermute | solution.py:662
  118.4 16.3 %collective-permute-start.20 = (f32[8,16384]{1,0:T(8,128)S(1)}, f32[8,16384]{1,0:T(8,128)S(1)}, u32[]{:S(2)}, u32[]{:S(2)}) collective-permute-start(f32[8,16384]{1,0:T(8,128)S(1)} %get-tuple-element.32), channel_id=1, source_target_pairs={{0,2},{1,3},{2,0},{3,1},{4,6},{5,7},{6,4},{7,5},{8,10},{9,11},{10,... | collective-permute-start | bytes 1572872 | tf_op jit(solution)/shard_map/ppermute | solution.py:662
  120.2 24.0 %collective-permute-start.21 = (f32[8,16384]{1,0:T(8,128)S(1)}, f32[8,16384]{1,0:T(8,128)S(1)}, u32[]{:S(2)}, u32[]{:S(2)}) collective-permute-start(f32[8,16384]{1,0:T(8,128)S(1)} %get-tuple-element.33), channel_id=1, source_target_pairs={{0,1},{1,2},{2,3},{3,0},{4,5},{5,6},{6,7},{7,4},{8,9},{9,10},{10,1... | collective-permute-start | bytes 1572872 | tf_op jit(solution)/shard_map/ppermute | solution.py:662

commit v2 on v1

--- a/solution.py
+++ b/solution.py
@@ -11,6 +11,7 @@
 STRIDE = 4
 MODES = 32
 SWEEPS = 2
+FACTOR_BLOCK = 8
 COUNT = 34
 ROWS = 40
 LANES = 128
@@ -20,7 +21,7 @@
 SMEM_SPEC = pl.BlockSpec(memory_space=pltpu.SMEM)
 
 
-SHARED = 8192
+SHARED = 6144
 FOLD = SHARED // 4
 
 PLACE = np.array([0, 1] + list(range(PAD, PAD + MODES)))
@@ -299,13 +300,6 @@
             at = pl.multiple_of(base + r * LANES, LANES)
             out_ref[which : which + 1, pl.ds(at, LANES)] = line
 
-            @pl.when(comp == 0)
-            def _(line=line, r=r):
-                group = which * (SHARED // LANES // 8) + box * (cz // 64) + r // 8
-                spot = pl.ds(pl.multiple_of(3 * SHARED + group * LANES, LANES), LANES)
-                for ref in offer_refs:
-                    ref[r % 8 : r % 8 + 1, spot] = line
-
     def box_step(box, carry):
         start = 1 + STRIDE * box
         for k in range(cz // chunk):
@@ -334,6 +328,16 @@
         return carry
 
     lax.fori_loop(0, cx // STRIDE, box_step, 0)
+
+    @pl.when(comp == 0)
+    def _():
+        tiles = SHARED // LANES
+        for k in range(2 * tiles):
+            which, tile = divmod(k, tiles)
+            line = out_ref[which : which + 1, tile * LANES : (tile + 1) * LANES]
+            at = 3 * SHARED + k // 8 * LANES
+            for ref in offer_refs:
+                ref[k % 8 : k % 8 + 1, at : at + LANES] = line
 
 
 def snapshots(velocity, levels, profile_index, advect, here, basis, halos):
@@ -466,14 +470,27 @@
     lane = lax.broadcasted_iota(jnp.int32, (ROWS, LANES), 1)
     row = lax.broadcasted_iota(jnp.int32, (ROWS, LANES), 0)
     upper = jnp.zeros((ROWS, LANES), jnp.float32)
-    for j in (int(k) for k in PLACE):
-        line = jnp.broadcast_to(a[j : j + 1, :], (ROWS, LANES))
-        column = jnp.broadcast_to(a[:, j : j + 1], (ROWS, LANES))
-        pivot = jnp.broadcast_to(line[:, j : j + 1], (ROWS, LANES))
-        scale = lax.rsqrt(pivot)
-        line = line * scale
-        a = a - (column * scale) * line
-        upper = jnp.where((row == j) & (lane >= j), line, upper)
+    places = [int(k) for k in PLACE]
+    while places:
+        block, places = places[:FACTOR_BLOCK], places[FACTOR_BLOCK:]
+        lines = [jnp.broadcast_to(a[j : j + 1, :], (8, LANES)) for j in block]
+        columns = [jnp.broadcast_to(a[:, j : j + 1], (ROWS, LANES)) for j in block]
+
+        def entry(column, j):
+            return jnp.broadcast_to(column[j : j + 1, :], (8, LANES))
+
+        for i, j in enumerate(block):
+            scale = lax.rsqrt(entry(columns[i], j))
+            lines[i] = lines[i] * scale
+            columns[i] = columns[i] * spread(scale)
+            for k in range(i + 1, len(block)):
+                cross = entry(columns[i], block[k])
+                lines[k] = lines[k] - cross * lines[i]
+                columns[k] = columns[k] - spread(cross) * columns[i]
+        for i, j in enumerate(block):
+            line = spread(lines[i])
+            a = a - columns[i] * line
+            upper = jnp.where((row == j) & (lane >= j), line, upper)
 
     def turn_step(i, state):
         x, v = state

time: 147 us -> 145 us (0.986)
  Pallas kernels: 45 us -> 37.5 us
  waiting for transfers between devices: 58.1 us -> 63.3 us
    ppermute x15, waiting for transfers between devices: 28.3 us -> 35.6 us  [shifted(): return lax.ppermute(x, axis, [(i, (i + by) % size) for i in range(size)])]
    pallas_call x1, Pallas kernels: 22.4 us -> 18.3 us  [snapshots(): pl.pallas_call(stencil_kernel, grid=(comps,), in_specs=[SMEM_SPEC, pl.Blo...]
    pallas_call x1, Pallas kernels: 13.2 us -> 9.94 us  [factor(): pl.pallas_call(factor_kernel, in_specs=[VMEM_SPEC] * 7, out_specs=(VMEM_S...]
    ppermute x10, waiting for transfers between devices: 29.8 us -> 27.7 us  [ring_parts(): lax.ppermute(x, axis, pairs)]
  transfers between devices with their start and end apart: 25 -> 25, of which waited for: 14 -> 13; matrix products, arithmetic and copies ran while one was open for 0% -> 0% of each run, Pallas kernels for 28% -> 23%
where the time goes in v2:
time: 145 us; the launch traced here: 144 us
  waiting for transfers between devices  63.3 us (44%)
  starting transfers between devices  41.6 us (29%)
  Pallas kernels  37.5 us (26%)
    ppermute x15, waiting for transfers between devices, shifted(): return lax.ppermute(x, axis, [(i, (i + by) % size) for i in range(size)])  35.6 us
    ppermute x10, waiting for transfers between devices, ring_parts(): lax.ppermute(x, axis, pairs)  27.7 us
    ppermute x15, starting transfers between devices, shifted(): return lax.ppermute(x, axis, [(i, (i + by) % size) for i in range(size)])  25.7 us
    pallas_call x1, Pallas kernels, snapshots(): pl.pallas_call(stencil_kernel, grid=(comps,), in_specs=[SMEM_SPEC, pl.Blo...  18.3 us
    ppermute x10, starting transfers between devices, ring_parts(): lax.ppermute(x, axis, pairs)  15.9 us
    pallas_call x1, Pallas kernels, factor(): pl.pallas_call(factor_kernel, in_specs=[VMEM_SPEC] * 7, out_specs=(VMEM_S...  9.94 us
  transfers between devices with their start and end apart: 25, of which 13 were waited for; matrix products, arithmetic and copies ran while one was open for 0% of the time, Pallas kernels for 23%

profile of v2, /device:TPU:0, one launch (start us, length us, event | category | flops | bytes accessed | tf_op | source)
XLA Modules:
  0.0 143.8 jit_solution(6479568358528662530)
XLA Ops:
  0.6 0.0 copy-start
  0.6 0.0 copy-start.3
  0.7 2.8 %pack.1 = (f32[96,256]{1,0:T(8,128)S(1)}, f32[96,256]{1,0:T(8,128)S(1)}, f32[3,2,128,256]{3,2,1,0:T(8,128)S(1)}, f32[3,2,128,256]{3,2,1,0:T(8,128)S(1)}, f32[8,2...) custom-call(s32[1]{0:T(128)} %bitcast.here_ref, ...), custom_call_target="tpu_custom_call" | custom-call | tf_op jit(solution)/shard_map/pack/pallas_call | solution.py:104
  3.5 1.7 %collective-permute-start = (f32[96,256]{1,0:T(8,128)S(1)}, f32[96,256]{1,0:T(8,128)S(1)}, u32[]{:S(2)}, u32[]{:S(2)}) collective-permute-start(f32[96,256]{1,0:T(8,128)S(1)} %get-tuple-element.20.face_hi_ref), channel_id=1, source_target_pairs={{0,1},{1,2},{2,3},{3,0},{4,5},{5,6},{6,7},{7,4},{8,9},{9,10},{10,1... | collective-permute-start | bytes 294920 | tf_op jit(solution)/shard_map/ppermute | solution.py:679
  5.2 1.6 %collective-permute-start.1 = (f32[96,256]{1,0:T(8,128)S(1)}, f32[96,256]{1,0:T(8,128)S(1)}, u32[]{:S(2)}, u32[]{:S(2)}) collective-permute-start(f32[96,256]{1,0:T(8,128)S(1)} %get-tuple-element.21.face_lo_ref), channel_id=1, source_target_pairs={{0,3},{1,0},{2,1},{3,2},{4,7},{5,4},{6,5},{7,6},{8,11},{9,8},{10,9... | collective-permute-start | bytes 294920 | tf_op jit(solution)/shard_map/ppermute | solution.py:679
  6.8 0.0 collective-permute-start.4
  6.8 5.5 %collective-permute-start.5 = (f32[3,2,128,256]{3,2,1,0:T(8,128)S(1)}, f32[3,2,128,256]{3,2,1,0:T(8,128)S(1)}, u32[]{:S(2)}, u32[]{:S(2)}) collective-permute-start(f32[3,2,128,256]{3,2,1,0:T(8,128)S(1)} %get-tuple-element.23), channel_id=1, source_target_pairs={{0,124},{4,0},{8,4},{12,8},{16,12},{20,16},{24,20},{28,24},{32,28}... | collective-permute-start | bytes 2359304 | tf_op jit(solution)/shard_map/ppermute | solution.py:679
  12.3 0.0 collective-permute-done.zlo_ref
  12.3 0.0 collective-permute-done.1.zhi_ref
  12.3 0.1 collective-permute-start.2
  12.4 5.1 %collective-permute-start.3 = (f32[3,2,256]{2,1,0:T(2,128)S(1)}, f32[3,2,256]{2,1,0:T(2,128)S(1)}, u32[]{:S(2)}, u32[]{:S(2)}) collective-permute-start(f32[3,2,256]{2,1,0:T(2,128)S(1)} %pad_maximum_fusion.1), channel_id=1, source_target_pairs={{0,124},{4,0},{8,4},{12,8},{16,12},{20,16},{24,20},{28,24},{32,28}... | collective-permute-start | bytes 18440 | tf_op jit(solution)/shard_map/ppermute | solution.py:679
  17.6 1.5 %collective-permute-start.6 = (f32[8,24576]{1,0:T(8,128)S(1)}, f32[8,24576]{1,0:T(8,128)S(1)}, u32[]{:S(2)}, u32[]{:S(2)}) collective-permute-start(f32[8,24576]{1,0:T(8,128)S(1)} %get-tuple-element.26), channel_id=1, source_target_pairs={{0,3},{1,0},{2,1},{3,2},{4,7},{5,4},{6,5},{7,6},{8,11},{9,8},{10,9... | collective-permute-start | bytes 2359304 | tf_op jit(solution)/shard_map/ppermute | solution.py:679
  19.1 2.9 %collective-permute-done.2.corner_lo_ref = f32[3,2,256]{2,1,0:T(2,128)S(1)} collective-permute-done((f32[3,2,256]{2,1,0:T(2,128)S(1)}, f32[3,2,256]{2,1,0:T(2,128)S(1)}, u32[]{:S(2)}, u32[]{:S(2)}) %collective-permute-start.2) | collective-permute-done | bytes 6176 | tf_op jit(solution)/shard_map/ppermute | solution.py:679
  22.0 1.8 %collective-permute-start.7 = (f32[8,24576]{1,0:T(8,128)S(1)}, f32[8,24576]{1,0:T(8,128)S(1)}, u32[]{:S(2)}, u32[]{:S(2)}) collective-permute-start(f32[8,24576]{1,0:T(8,128)S(1)} %get-tuple-element.27), channel_id=1, source_target_pairs={{0,2},{1,3},{2,0},{3,1},{4,6},{5,7},{6,4},{7,5},{8,10},{9,11},{10,... | collective-permute-start | bytes 2359304 | tf_op jit(solution)/shard_map/ppermute | solution.py:679
  23.8 0.0 collective-permute-done.3.corner_hi_ref
  23.8 0.6 collective-permute-start.8
  24.4 0.0 collective-permute-done.4.xlo_hbm
  24.4 0.0 collective-permute-done.5.xhi_hbm
  24.5 18.3 %stencil.1 = (f32[8,24576]{1,0:T(8,128)S(1)}, f32[8,19968]{1,0:T(8,128)S(1)}, f32[8,19968]{1,0:T(8,128)S(1)}, f32[8,19968]{1,0:T(8,128)S(1)}) custom-call(f32[8]{0:T(128)S(1)} %copy-done.5, s32[1,256]{1,0:T(1,128)S(1)} %bitcast.17, f32[1,256]{1,0:T(1,128)S(1)} %bitcast.18, bf16[256,128]{1,0:T(8,128)(2,1)S(1)} %copy-done, ...), custom_call_target="tpu_custom_call" | custom-call | tf_op jit(solution)/shard_map/stencil/pallas_call | solution.py:351
  42.7 0.0 copy-start.1
  42.8 0.0 copy-start.2
  42.8 0.0 copy-start.6
  42.8 2.7 %collective-permute-start.22 = (f32[8,19968]{1,0:T(8,128)S(1)}, f32[8,19968]{1,0:T(8,128)S(1)}, u32[]{:S(2)}, u32[]{:S(2)}) collective-permute-start(f32[8,19968]{1,0:T(8,128)S(1)} %get-tuple-element.34), channel_id=1, source_target_pairs={{0,3},{1,0},{2,1},{3,2},{4,7},{5,4},{6,5},{7,6},{8,11},{9,8},{10,9... | collective-permute-start | bytes 1916936 | tf_op jit(solution)/shard_map/ppermute | solution.py:679
  45.5 0.0 collective-permute-done.6.refs_2_
  45.5 0.0 collective-permute-done.7.refs_3_
  45.5 9.9 %collective-permute-done.8.refs_4_ = f32[8,24576]{1,0:T(8,128)S(1)} collective-permute-done((f32[8,24576]{1,0:T(8,128)S(1)}, f32[8,24576]{1,0:T(8,128)S(1)}, u32[]{:S(2)}, u32[]{:S(2)}) %collective-permute-start.8) | collective-permute-done | bytes 786464 | tf_op jit(solution)/shard_map/ppermute | solution.py:679
  55.4 1.4 gram.1
  56.8 0.0 collective-permute-start.9
  56.8 1.2 collective-permute-done.9
  58.0 2.9 %collective-permute-start.12 = (f32[40,128]{1,0:T(8,128)S(1)}, f32[40,128]{1,0:T(8,128)S(1)}, u32[]{:S(2)}, u32[]{:S(2)}) collective-permute-start(f32[40,128]{1,0:T(8,128)S(1)} %add.21), channel_id=1, source_target_pairs={{0,24},{4,28},{8,0},{12,4},{16,8},{20,12},{24,16},{28,20},{32,56},... | collective-permute-start | bytes 61448 | tf_op jit(solution)/shard_map/ppermute | solution.py:443
  60.9 0.0 collective-permute-start.11
  60.9 2.0 %collective-permute-start.10 = (f32[40,128]{1,0:T(8,128)S(1)}, f32[40,128]{1,0:T(8,128)S(1)}, u32[]{:S(2)}, u32[]{:S(2)}) collective-permute-start(f32[40,128]{1,0:T(8,128)S(1)} %add.21), channel_id=1, source_target_pairs={{0,16},{4,20},{8,24},{12,28},{16,0},{20,4},{24,8},{28,12},{32,48},... | collective-permute-start | bytes 61448 | tf_op jit(solution)/shard_map/ppermute | solution.py:443
  62.9 0.0 collective-permute-done.12
  62.9 3.0 %collective-permute-done.11 = f32[40,128]{1,0:T(8,128)S(1)} collective-permute-done((f32[40,128]{1,0:T(8,128)S(1)}, f32[40,128]{1,0:T(8,128)S(1)}, u32[]{:S(2)}, u32[]{:S(2)}) %collective-permute-start.11) | collective-permute-done | bytes 20512 | tf_op jit(solution)/shard_map/ppermute | solution.py:443
  65.9 0.3 collective-permute-done.10
  66.2 3.2 %collective-permute-start.15 = (f32[40,128]{1,0:T(8,128)S(1)}, f32[40,128]{1,0:T(8,128)S(1)}, u32[]{:S(2)}, u32[]{:S(2)}) collective-permute-start(f32[40,128]{1,0:T(8,128)S(1)} %add_add_fusion.1), channel_id=1, source_target_pairs={{0,96},{4,100},{8,104},{12,108},{16,112},{20,116},{24,120},{28,124... | collective-permute-start | bytes 61448 | tf_op jit(solution)/shard_map/ppermute | solution.py:443
  69.4 0.0 collective-permute-start.14
  69.4 2.5 %collective-permute-start.13 = (f32[40,128]{1,0:T(8,128)S(1)}, f32[40,128]{1,0:T(8,128)S(1)}, u32[]{:S(2)}, u32[]{:S(2)}) collective-permute-start(f32[40,128]{1,0:T(8,128)S(1)} %add_add_fusion.1), channel_id=1, source_target_pairs={{0,64},{4,68},{8,72},{12,76},{16,80},{20,84},{24,88},{28,92},{32,9... | collective-permute-start | bytes 61448 | tf_op jit(solution)/shard_map/ppermute | solution.py:443
  71.9 1.8 %collective-permute-start.23 = (f32[8,19968]{1,0:T(8,128)S(1)}, f32[8,19968]{1,0:T(8,128)S(1)}, u32[]{:S(2)}, u32[]{:S(2)}) collective-permute-start(f32[8,19968]{1,0:T(8,128)S(1)} %get-tuple-element.35), channel_id=1, source_target_pairs={{0,2},{1,3},{2,0},{3,1},{4,6},{5,7},{6,4},{7,5},{8,10},{9,11},{10,... | collective-permute-start | bytes 1916936 | tf_op jit(solution)/shard_map/ppermute | solution.py:679
  73.7 0.0 collective-permute-done.15
  73.7 0.0 collective-permute-start.24
  73.7 0.7 collective-permute-done.14
  74.4 0.3 collective-permute-done.13
  74.7 2.3 %collective-permute-start.18 = (f32[40,128]{1,0:T(8,128)S(1)}, f32[40,128]{1,0:T(8,128)S(1)}, u32[]{:S(2)}, u32[]{:S(2)}) collective-permute-start(f32[40,128]{1,0:T(8,128)S(1)} %add_add_fusion.g0_ref), channel_id=1, source_target_pairs={{0,3},{1,0},{2,1},{3,2},{4,7},{5,4},{6,5},{7,6},{8,11},{9,8},{10,9... | collective-permute-start | bytes 61448 | tf_op jit(solution)/shard_map/ppermute | solution.py:443
  77.0 0.5 collective-permute-start.17
  77.6 8.8 %collective-permute-done.18.g3_ref = f32[40,128]{1,0:T(8,128)S(1)} collective-permute-done((f32[40,128]{1,0:T(8,128)S(1)}, f32[40,128]{1,0:T(8,128)S(1)}, u32[]{:S(2)}, u32[]{:S(2)}) %collective-permute-start.18) | collective-permute-done | bytes 20512 | tf_op jit(solution)/shard_map/ppermute | solution.py:443
  86.3 2.4 %collective-permute-start.16 = (f32[40,128]{1,0:T(8,128)S(1)}, f32[40,128]{1,0:T(8,128)S(1)}, u32[]{:S(2)}, u32[]{:S(2)}) collective-permute-start(f32[40,128]{1,0:T(8,128)S(1)} %add_add_fusion.g0_ref), channel_id=1, source_target_pairs={{0,1},{1,2},{2,3},{3,0},{4,5},{5,6},{6,7},{7,4},{8,9},{9,10},{10,1... | collective-permute-start | bytes 61448 | tf_op jit(solution)/shard_map/ppermute | solution.py:443
  88.7 13.5 %collective-permute-done.17.g2_ref = f32[40,128]{1,0:T(8,128)S(1)} collective-permute-done((f32[40,128]{1,0:T(8,128)S(1)}, f32[40,128]{1,0:T(8,128)S(1)}, u32[]{:S(2)}, u32[]{:S(2)}) %collective-permute-start.17) | collective-permute-done | bytes 20512 | tf_op jit(solution)/shard_map/ppermute | solution.py:443
  102.1 0.1 collective-permute-done.16.g1_ref
  102.2 0.0 copy-done.6
  102.2 9.9 %factor.1 = (f32[32,128]{1,0:T(8,128)S(1)}, f32[8,128]{1,0:T(8,128)S(1)}) custom-call(f32[40,128]{1,0:T(8,128)S(1)} %add_add_fusion.g0_ref, f32[40,128]{1,0:T(8,128)S(1)} %collective-permute-done.16.g1_ref, f32[40,128]{1,0:T(8,128)S(1)} %collective-permute-done.17.g2_ref, f32[40,128]{1,0:T(8,128)S(1)} %collective-permute-done.18.g3_ref, ...), custom_call_target="tpu_custom_call" | custom-call | tf_op jit(solution)/shard_map/factor/pallas_call | solution.py:528
  112.2 0.8 update.1
  113.0 0.7 collective-permute-start.19
  113.7 1.8 %collective-permute-start.20 = (f32[8,18432]{1,0:T(8,128)S(1)}, f32[8,18432]{1,0:T(8,128)S(1)}, u32[]{:S(2)}, u32[]{:S(2)}) collective-permute-start(f32[8,18432]{1,0:T(8,128)S(1)} %get-tuple-element.32), channel_id=1, source_target_pairs={{0,2},{1,3},{2,0},{3,1},{4,6},{5,7},{6,4},{7,5},{8,10},{9,11},{10,... | collective-permute-start | bytes 1769480 | tf_op jit(solution)/shard_map/ppermute | solution.py:679
  115.5 0.0 collective-permute-done.22.refs_5_
  115.5 0.7 collective-permute-start.21
  116.2 0.5 slice_bitcast_fusion.2
  116.8 0.0 collective-permute-done.23.refs_6_
  116.8 0.0 collective-permute-done.24.refs_7_
  116.8 2.8 %own.1.refs_4_ = f32[8,98304]{1,0:T(8,128)} custom-call(s32[1]{0:T(128)} %bitcast.here_ref, f32[32,128]{1,0:T(8,128)S(1)} %get-tuple-element.29.mix_ref, f32[8,24576]{1,0:T(8,128)S(1)} %get-tuple-element.24.refs_0_, f32[8,24576]{1,0:T(8,128)S(1)} %get-tuple-element.25.refs_1_, f32[8,24576]{1,0:T(8,128)S(1)} %collective-permute-done.6.refs_2_, ...), custom_call_target="tpu_custom_call" | custom-call | tf_op jit(solution)/shard_map/own/pallas_call | solution.py:629
  119.6 9.7 %collective-permute-done.19.refs_1_ = f32[8,18432]{1,0:T(8,128)S(1)} collective-permute-done((f32[8,18432]{1,0:T(8,128)S(1)}, f32[8,18432]{1,0:T(8,128)S(1)}, u32[]{:S(2)}, u32[]{:S(2)}) %collective-permute-start.19) | collective-permute-done | bytes 589856 | tf_op jit(solution)/shard_map/ppermute | solution.py:679
  129.3 2.2 %collective-permute-done.20.refs_2_ = f32[8,18432]{1,0:T(8,128)S(1)} collective-permute-done((f32[8,18432]{1,0:T(8,128)S(1)}, f32[8,18432]{1,0:T(8,128)S(1)}, u32[]{:S(2)}, u32[]{:S(2)}) %collective-permute-start.20) | collective-permute-done | bytes 589856 | tf_op jit(solution)/shard_map/ppermute | solution.py:679
  131.4 10.9 %collective-permute-done.21.refs_3_ = f32[8,18432]{1,0:T(8,128)S(1)} collective-permute-done((f32[8,18432]{1,0:T(8,128)S(1)}, f32[8,18432]{1,0:T(8,128)S(1)}, u32[]{:S(2)}, u32[]{:S(2)}) %collective-permute-start.21) | collective-permute-done | bytes 589856 | tf_op jit(solution)/shard_map/ppermute | solution.py:679
  142.4 1.4 join.1
  (16 shorter events, 0.1 us)
Async XLA Ops:
  0.6 23.8 %copy-start = (bf16[256,128]{1,0:T(8,128)(2,1)S(1)}, bf16[256,128]{1,0:T(8,128)(2,1)}, u32[]{:S(2)}) copy-start(bf16[256,128]{1,0:T(8,128)(2,1)} %constant.12.clone.sum_ref) | copy-start | bytes 196612
  0.6 23.8 %copy-start.3 = (s32[256]{0:T(256)S(1)}, s32[256]{0:T(256)}, u32[]{:S(2)}) copy-start(s32[256]{0:T(256)} %param.12) | copy-start | bytes 3076
  0.7 23.8 %copy-start.4 = (f32[256]{0:T(256)S(1)}, f32[256]{0:T(256)}, u32[]{:S(2)}) copy-start(f32[256]{0:T(256)} %param.13) | copy-start | bytes 3076
  0.7 23.8 %copy-start.5 = (f32[8]{0:T(128)S(1)}, f32[8]{0:T(128)}, u32[]{:S(2)}) copy-start(f32[8]{0:T(128)} %levels_ref.1) | copy-start | bytes 100
  3.5 8.8 %collective-permute-start = (f32[96,256]{1,0:T(8,128)S(1)}, f32[96,256]{1,0:T(8,128)S(1)}, u32[]{:S(2)}, u32[]{:S(2)}) collective-permute-start(f32[96,256]{1,0:T(8,128)S(1)} %get-tuple-element.20.face_hi_ref), channel_id=1, source_target_pairs={{0,1},{1,2},{2,3},{3,0},{4,5},{5,6},{6,7},{7,4},{8,9},{9,10},{10,1... | collective-permute-start | bytes 294920 | tf_op jit(solution)/shard_map/ppermute | solution.py:679
  5.2 7.1 %collective-permute-start.1 = (f32[96,256]{1,0:T(8,128)S(1)}, f32[96,256]{1,0:T(8,128)S(1)}, u32[]{:S(2)}, u32[]{:S(2)}) collective-permute-start(f32[96,256]{1,0:T(8,128)S(1)} %get-tuple-element.21.face_lo_ref), channel_id=1, source_target_pairs={{0,3},{1,0},{2,1},{3,2},{4,7},{5,4},{6,5},{7,6},{8,11},{9,8},{10,9... | collective-permute-start | bytes 294920 | tf_op jit(solution)/shard_map/ppermute | solution.py:679
  6.8 17.6 %collective-permute-start.4 = (f32[3,2,128,256]{3,2,1,0:T(8,128)S(1)}, f32[3,2,128,256]{3,2,1,0:T(8,128)S(1)}, u32[]{:S(2)}, u32[]{:S(2)}) collective-permute-start(f32[3,2,128,256]{3,2,1,0:T(8,128)S(1)} %get-tuple-element.22), channel_id=1, source_target_pairs={{0,4},{4,8},{8,12},{12,16},{16,20},{20,24},{24,28},{28,32},{32,36}... | collective-permute-start | bytes 2359304 | tf_op jit(solution)/shard_map/ppermute | solution.py:679
  6.8 17.6 %collective-permute-start.5 = (f32[3,2,128,256]{3,2,1,0:T(8,128)S(1)}, f32[3,2,128,256]{3,2,1,0:T(8,128)S(1)}, u32[]{:S(2)}, u32[]{:S(2)}) collective-permute-start(f32[3,2,128,256]{3,2,1,0:T(8,128)S(1)} %get-tuple-element.23), channel_id=1, source_target_pairs={{0,124},{4,0},{8,4},{12,8},{16,12},{20,16},{24,20},{28,24},{32,28}... | collective-permute-start | bytes 2359304 | tf_op jit(solution)/shard_map/ppermute | solution.py:679
  12.3 9.7 %collective-permute-start.2 = (f32[3,2,256]{2,1,0:T(2,128)S(1)}, f32[3,2,256]{2,1,0:T(2,128)S(1)}, u32[]{:S(2)}, u32[]{:S(2)}) collective-permute-start(f32[3,2,256]{2,1,0:T(2,128)S(1)} %pad_maximum_fusion), channel_id=1, source_target_pairs={{0,4},{4,8},{8,12},{12,16},{16,20},{20,24},{24,28},{28,32},{32,36}... | collective-permute-start | bytes 18440 | tf_op jit(solution)/shard_map/ppermute | solution.py:679
  12.4 11.4 %collective-permute-start.3 = (f32[3,2,256]{2,1,0:T(2,128)S(1)}, f32[3,2,256]{2,1,0:T(2,128)S(1)}, u32[]{:S(2)}, u32[]{:S(2)}) collective-permute-start(f32[3,2,256]{2,1,0:T(2,128)S(1)} %pad_maximum_fusion.1), channel_id=1, source_target_pairs={{0,124},{4,0},{8,4},{12,8},{16,12},{20,16},{24,20},{28,24},{32,28}... | collective-permute-start | bytes 18440 | tf_op jit(solution)/shard_map/ppermute | solution.py:679
  17.6 27.9 %collective-permute-start.6 = (f32[8,24576]{1,0:T(8,128)S(1)}, f32[8,24576]{1,0:T(8,128)S(1)}, u32[]{:S(2)}, u32[]{:S(2)}) collective-permute-start(f32[8,24576]{1,0:T(8,128)S(1)} %get-tuple-element.26), channel_id=1, source_target_pairs={{0,3},{1,0},{2,1},{3,2},{4,7},{5,4},{6,5},{7,6},{8,11},{9,8},{10,9... | collective-permute-start | bytes 2359304 | tf_op jit(solution)/shard_map/ppermute | solution.py:679
  22.0 23.5 %collective-permute-start.7 = (f32[8,24576]{1,0:T(8,128)S(1)}, f32[8,24576]{1,0:T(8,128)S(1)}, u32[]{:S(2)}, u32[]{:S(2)}) collective-permute-start(f32[8,24576]{1,0:T(8,128)S(1)} %get-tuple-element.27), channel_id=1, source_target_pairs={{0,2},{1,3},{2,0},{3,1},{4,6},{5,7},{6,4},{7,5},{8,10},{9,11},{10,... | collective-permute-start | bytes 2359304 | tf_op jit(solution)/shard_map/ppermute | solution.py:679
  23.8 31.6 %collective-permute-start.8 = (f32[8,24576]{1,0:T(8,128)S(1)}, f32[8,24576]{1,0:T(8,128)S(1)}, u32[]{:S(2)}, u32[]{:S(2)}) collective-permute-start(f32[8,24576]{1,0:T(8,128)S(1)} %get-tuple-element.28), channel_id=1, source_target_pairs={{0,1},{1,2},{2,3},{3,0},{4,5},{5,6},{6,7},{7,4},{8,9},{9,10},{10,1... | collective-permute-start | bytes 2359304 | tf_op jit(solution)/shard_map/ppermute | solution.py:679
  42.7 59.5 %copy-start.1 = (f32[40,128]{1,0:T(8,128)S(1)}, f32[40,128]{1,0:T(8,128)}, u32[]{:S(2)}) copy-start(f32[40,128]{1,0:T(8,128)} %constant.14.clone.orient_ref) | copy-start | bytes 61444
  42.8 59.5 %copy-start.2 = (s32[40,128]{1,0:T(8,128)S(1)}, s32[40,128]{1,0:T(8,128)}, u32[]{:S(2)}) copy-start(s32[40,128]{1,0:T(8,128)} %constant.13.clone.partner_ref) | copy-start | bytes 61444
  42.8 59.5 %copy-start.6 = (s32[1,128]{1,0:T(1,128)S(1)}, s32[1,128]{1,0:T(1,128)}, u32[]{:S(2)}) copy-start(s32[1,128]{1,0:T(1,128)} %constant.15.clone.keep_ref) | copy-start | bytes 1540
  42.8 72.7 %collective-permute-start.22 = (f32[8,19968]{1,0:T(8,128)S(1)}, f32[8,19968]{1,0:T(8,128)S(1)}, u32[]{:S(2)}, u32[]{:S(2)}) collective-permute-start(f32[8,19968]{1,0:T(8,128)S(1)} %get-tuple-element.34), channel_id=1, source_target_pairs={{0,3},{1,0},{2,1},{3,2},{4,7},{5,4},{6,5},{7,6},{8,11},{9,8},{10,9... | collective-permute-start | bytes 1916936 | tf_op jit(solution)/shard_map/ppermute | solution.py:679
  56.8 1.2 collective-permute-start.9
  58.0 4.9 %collective-permute-start.12 = (f32[40,128]{1,0:T(8,128)S(1)}, f32[40,128]{1,0:T(8,128)S(1)}, u32[]{:S(2)}, u32[]{:S(2)}) collective-permute-start(f32[40,128]{1,0:T(8,128)S(1)} %add.21), channel_id=1, source_target_pairs={{0,24},{4,28},{8,0},{12,4},{16,8},{20,12},{24,16},{28,20},{32,56},... | collective-permute-start | bytes 61448 | tf_op jit(solution)/shard_map/ppermute | solution.py:443
  60.9 5.0 %collective-permute-start.11 = (f32[40,128]{1,0:T(8,128)S(1)}, f32[40,128]{1,0:T(8,128)S(1)}, u32[]{:S(2)}, u32[]{:S(2)}) collective-permute-start(f32[40,128]{1,0:T(8,128)S(1)} %add.21), channel_id=1, source_target_pairs={{0,8},{4,12},{8,16},{12,20},{16,24},{20,28},{24,0},{28,4},{32,40},... | collective-permute-start | bytes 61448 | tf_op jit(solution)/shard_map/ppermute | solution.py:443
  60.9 5.3 %collective-permute-start.10 = (f32[40,128]{1,0:T(8,128)S(1)}, f32[40,128]{1,0:T(8,128)S(1)}, u32[]{:S(2)}, u32[]{:S(2)}) collective-permute-start(f32[40,128]{1,0:T(8,128)S(1)} %add.21), channel_id=1, source_target_pairs={{0,16},{4,20},{8,24},{12,28},{16,0},{20,4},{24,8},{28,12},{32,48},... | collective-permute-start | bytes 61448 | tf_op jit(solution)/shard_map/ppermute | solution.py:443
  66.2 7.5 %collective-permute-start.15 = (f32[40,128]{1,0:T(8,128)S(1)}, f32[40,128]{1,0:T(8,128)S(1)}, u32[]{:S(2)}, u32[]{:S(2)}) collective-permute-start(f32[40,128]{1,0:T(8,128)S(1)} %add_add_fusion.1), channel_id=1, source_target_pairs={{0,96},{4,100},{8,104},{12,108},{16,112},{20,116},{24,120},{28,124... | collective-permute-start | bytes 61448 | tf_op jit(solution)/shard_map/ppermute | solution.py:443
  69.4 5.0 %collective-permute-start.14 = (f32[40,128]{1,0:T(8,128)S(1)}, f32[40,128]{1,0:T(8,128)S(1)}, u32[]{:S(2)}, u32[]{:S(2)}) collective-permute-start(f32[40,128]{1,0:T(8,128)S(1)} %add_add_fusion.1), channel_id=1, source_target_pairs={{0,32},{4,36},{8,40},{12,44},{16,48},{20,52},{24,56},{28,60},{32,6... | collective-permute-start | bytes 61448 | tf_op jit(solution)/shard_map/ppermute | solution.py:443
  69.4 5.3 %collective-permute-start.13 = (f32[40,128]{1,0:T(8,128)S(1)}, f32[40,128]{1,0:T(8,128)S(1)}, u32[]{:S(2)}, u32[]{:S(2)}) collective-permute-start(f32[40,128]{1,0:T(8,128)S(1)} %add_add_fusion.1), channel_id=1, source_target_pairs={{0,64},{4,68},{8,72},{12,76},{16,80},{20,84},{24,88},{28,92},{32,9... | collective-permute-start | bytes 61448 | tf_op jit(solution)/shard_map/ppermute | solution.py:443
  71.9 44.9 %collective-permute-start.23 = (f32[8,19968]{1,0:T(8,128)S(1)}, f32[8,19968]{1,0:T(8,128)S(1)}, u32[]{:S(2)}, u32[]{:S(2)}) collective-permute-start(f32[8,19968]{1,0:T(8,128)S(1)} %get-tuple-element.35), channel_id=1, source_target_pairs={{0,2},{1,3},{2,0},{3,1},{4,6},{5,7},{6,4},{7,5},{8,10},{9,11},{10,... | collective-permute-start | bytes 1916936 | tf_op jit(solution)/shard_map/ppermute | solution.py:679
  73.7 43.0 %collective-permute-start.24 = (f32[8,19968]{1,0:T(8,128)S(1)}, f32[8,19968]{1,0:T(8,128)S(1)}, u32[]{:S(2)}, u32[]{:S(2)}) collective-permute-start(f32[8,19968]{1,0:T(8,128)S(1)} %get-tuple-element.36), channel_id=1, source_target_pairs={{0,1},{1,2},{2,3},{3,0},{4,5},{5,6},{6,7},{7,4},{8,9},{9,10},{10,1... | collective-permute-start | bytes 1916936 | tf_op jit(solution)/shard_map/ppermute | solution.py:679
  74.7 11.6 %collective-permute-start.18 = (f32[40,128]{1,0:T(8,128)S(1)}, f32[40,128]{1,0:T(8,128)S(1)}, u32[]{:S(2)}, u32[]{:S(2)}) collective-permute-start(f32[40,128]{1,0:T(8,128)S(1)} %add_add_fusion.g0_ref), channel_id=1, source_target_pairs={{0,3},{1,0},{2,1},{3,2},{4,7},{5,4},{6,5},{7,6},{8,11},{9,8},{10,9... | collective-permute-start | bytes 61448 | tf_op jit(solution)/shard_map/ppermute | solution.py:443
  77.0 25.1 %collective-permute-start.17 = (f32[40,128]{1,0:T(8,128)S(1)}, f32[40,128]{1,0:T(8,128)S(1)}, u32[]{:S(2)}, u32[]{:S(2)}) collective-permute-start(f32[40,128]{1,0:T(8,128)S(1)} %add_add_fusion.g0_ref), channel_id=1, source_target_pairs={{0,2},{1,3},{2,0},{3,1},{4,6},{5,7},{6,4},{7,5},{8,10},{9,11},{10,... | collective-permute-start | bytes 61448 | tf_op jit(solution)/shard_map/ppermute | solution.py:443
  86.3 15.9 %collective-permute-start.16 = (f32[40,128]{1,0:T(8,128)S(1)}, f32[40,128]{1,0:T(8,128)S(1)}, u32[]{:S(2)}, u32[]{:S(2)}) collective-permute-start(f32[40,128]{1,0:T(8,128)S(1)} %add_add_fusion.g0_ref), channel_id=1, source_target_pairs={{0,1},{1,2},{2,3},{3,0},{4,5},{5,6},{6,7},{7,4},{8,9},{9,10},{10,1... | collective-permute-start | bytes 61448 | tf_op jit(solution)/shard_map/ppermute | solution.py:443
  113.0 16.3 %collective-permute-start.19 = (f32[8,18432]{1,0:T(8,128)S(1)}, f32[8,18432]{1,0:T(8,128)S(1)}, u32[]{:S(2)}, u32[]{:S(2)}) collective-permute-start(f32[8,18432]{1,0:T(8,128)S(1)} %get-tuple-element.31), channel_id=1, source_target_pairs={{0,3},{1,0},{2,1},{3,2},{4,7},{5,4},{6,5},{7,6},{8,11},{9,8},{10,9... | collective-permute-start | bytes 1769480 | tf_op jit(solution)/shard_map/ppermute | solution.py:679
  113.7 17.7 %collective-permute-start.20 = (f32[8,18432]{1,0:T(8,128)S(1)}, f32[8,18432]{1,0:T(8,128)S(1)}, u32[]{:S(2)}, u32[]{:S(2)}) collective-permute-start(f32[8,18432]{1,0:T(8,128)S(1)} %get-tuple-element.32), channel_id=1, source_target_pairs={{0,2},{1,3},{2,0},{3,1},{4,6},{5,7},{6,4},{7,5},{8,10},{9,11},{10,... | collective-permute-start | bytes 1769480 | tf_op jit(solution)/shard_map/ppermute | solution.py:679
  115.5 26.9 %collective-permute-start.21 = (f32[8,18432]{1,0:T(8,128)S(1)}, f32[8,18432]{1,0:T(8,128)S(1)}, u32[]{:S(2)}, u32[]{:S(2)}) collective-permute-start(f32[8,18432]{1,0:T(8,128)S(1)} %get-tuple-element.33), channel_id=1, source_target_pairs={{0,1},{1,2},{2,3},{3,0},{4,5},{5,6},{6,7},{7,4},{8,9},{9,10},{10,1... | collective-permute-start | bytes 1769480 | tf_op jit(solution)/shard_map/ppermute | solution.py:679

commit v3 on v2

--- a/solution.py
+++ b/solution.py
@@ -76,8 +76,10 @@
             source = vel_hbm.at[c, :, pl.ds(at, PAD), :]
             edges.append(pltpu.make_async_copy(source, buf.at[c, side], edge_sems.at[c, side]))
         for side, (at, ref) in enumerate(((0, xfirst_ref), (cx - 2, xlast_ref))):
-            source = vel_hbm.at[c, pl.ds(at, 2)]
-            rest.append(pltpu.make_async_copy(source, ref.at[c], face_sems.at[c, side]))
+            for k in range(2):
+                source = vel_hbm.at[c, at + k]
+                target = ref.at[pl.ds((2 * c + k) * cz, cz)]
+                rest.append(pltpu.make_async_copy(source, target, face_sems.at[c, side, k]))
     for k, ref in enumerate((mine_ref, next_ref, far_ref, prev_ref)):
         at = pl.multiple_of(lax.rem(here_ref[0] + k, 4) * cols, LANES)
         source = basis_hbm.at[:, pl.ds(at, cols)]
@@ -99,7 +101,7 @@
 def pack(here, velocity, basis):
     comps, cx, cz, ny = velocity.shape
     edge = pltpu.VMEM((comps * 2 * cx, ny), jnp.float32)
-    face = pltpu.VMEM((comps, 2, cz, ny), jnp.float32)
+    face = pltpu.VMEM((comps * 2 * cz + PAD, ny), jnp.float32)
     block = pltpu.VMEM((PAD, basis.shape[1] // 4), jnp.float32)
     return pl.pallas_call(
         pack_kernel,
@@ -109,12 +111,37 @@
         scratch_shapes=[
             pltpu.VMEM((comps, 2, cx, PAD, ny), jnp.float32),
             pltpu.SemaphoreType.DMA((comps, 2)),
-            pltpu.SemaphoreType.DMA((comps, 2)),
+            pltpu.SemaphoreType.DMA((comps, 2, 2)),
             pltpu.SemaphoreType.DMA((4,)),
         ],
         compiler_params=pltpu.CompilerParams(vmem_limit_bytes=4 << 20),
         name="pack",
     )(here, far(velocity), far(basis))
+
+
+def corner_kernel(zlo_ref, zhi_ref, _, __, xfirst_ref, xlast_ref, *, cx, comps):
+    base = xfirst_ref.shape[0] - PAD
+    zero = jnp.zeros((PAD, xfirst_ref.shape[1]), jnp.float32)
+    for ref, plane in ((xfirst_ref, 0), (xlast_ref, cx - 1)):
+        ref[base:, :] = zero
+        for c in range(comps):
+            low, high = (2 * c + 1) * cx + plane, 2 * c * cx + plane
+            at = base + 2 * c
+            ref[at : at + 1, :] = zlo_ref[low : low + 1, :]
+            ref[at + 1 : at + 2, :] = zhi_ref[high : high + 1, :]
+
+
+def add_corners(zlo, zhi, first, last, cx, comps):
+    face = pltpu.VMEM(first.shape, jnp.float32)
+    return pl.pallas_call(
+        functools.partial(corner_kernel, cx=cx, comps=comps),
+        in_specs=[VMEM_SPEC] * 4,
+        out_specs=[VMEM_SPEC] * 2,
+        out_shape=[face, face],
+        input_output_aliases={2: 0, 3: 1},
+        compiler_params=pltpu.CompilerParams(vmem_limit_bytes=1 << 20),
+        name="corners",
+    )(*[near(x) for x in (zlo, zhi, first, last)])
 
 
 def coefficients(levels_ref, index_ref, advect_ref):
@@ -182,13 +209,11 @@
     zhi_ref,
     face_lo_ref,
     face_hi_ref,
-    corner_lo_ref,
-    corner_hi_ref,
     here_ref,
     basis_hbm,
     vel_hbm,
-    xlo_hbm,
-    xhi_hbm,
+    xlo_ref,
+    xhi_ref,
     out_ref,
     plus_ref,
     minus_ref,
@@ -208,14 +233,17 @@
     def copies(c):
         return (
             pltpu.make_async_copy(
-                vel_hbm.at[c], field.at[c, pl.ds(2, cx), inner, :], sems.at[c, 0]
+                vel_hbm.at[c], field.at[c, pl.ds(2, cx), inner, :], sems.at[c, 0, 0]
             ),
-            pltpu.make_async_copy(
-                xlo_hbm.at[c], field.at[c, pl.ds(0, 2), inner, :], sems.at[c, 1]
-            ),
-            pltpu.make_async_copy(
-                xhi_hbm.at[c], field.at[c, pl.ds(cx + 2, 2), inner, :], sems.at[c, 2]
-            ),
+            *[
+                pltpu.make_async_copy(
+                    ref.at[pl.ds((2 * c + k) * cz, cz)],
+                    field.at[c, at + k, inner, :],
+                    sems.at[c, 1 + side, k],
+                )
+                for side, (at, ref) in enumerate(((0, xlo_ref), (cx + 2, xhi_ref)))
+                for k in range(2)
+            ],
         )
 
     @pl.when(comp == 0)
@@ -238,8 +266,9 @@
 
     zlo2, zlo1 = edge_row(zlo_ref, 0), edge_row(zlo_ref, 1)
     zhi1, zhi2 = edge_row(zhi_ref, 0), edge_row(zhi_ref, 1)
-    lo_before, lo_after = corner_lo_ref[comp, 0:1], corner_hi_ref[comp, 0:1]
-    hi_before, hi_after = corner_lo_ref[comp, 1:2], corner_hi_ref[comp, 1:2]
+    spot = 6 * cz + 2 * comp
+    lo_before, lo_after = xlo_ref[pl.ds(spot, 1), :], xhi_ref[pl.ds(spot, 1), :]
+    hi_before, hi_after = xlo_ref[pl.ds(spot + 1, 1), :], xhi_ref[pl.ds(spot + 1, 1), :]
     plane = lax.broadcasted_iota(jnp.int32, (cx, ny), 0)
 
     def edge(row, before, after, north, south):
@@ -356,7 +385,7 @@
             pl.BlockSpec((1, ny), lambda c: (0, 0)),
             pl.BlockSpec((1, ny), lambda c: (0, 0)),
             pl.BlockSpec((ny, LANES), lambda c: (0, 0)),
-            *[VMEM_SPEC] * 6,
+            *[VMEM_SPEC] * 4,
             SMEM_SPEC,
             HBM_SPEC,
             HBM_SPEC,
@@ -370,7 +399,7 @@
             pltpu.VMEM((comps, cx + 4, cz + 2 * PAD, ny), jnp.float32),
             pltpu.VMEM((cx + 2, cz + 2 * PAD, ny), jnp.float32),
             pltpu.VMEM((cz, ny), jnp.float32),
-            pltpu.SemaphoreType.DMA((comps, 3)),
+            pltpu.SemaphoreType.DMA((comps, 3, 2)),
             pltpu.SemaphoreType.DMA((3, 3)),
         ],
         compiler_params=pltpu.CompilerParams(vmem_limit_bytes=20 << 20),
@@ -380,11 +409,11 @@
         profile_index.reshape(1, ny),
         advect.reshape(1, ny),
         jnp.asarray(sums, jnp.bfloat16),
-        *[near(x) for x in halos[:6]],
+        *[near(x) for x in halos[:4]],
         here,
         far(basis),
-        far(halos[6]),
-        *[near(x) for x in halos[7:]],
+        far(halos[4]),
+        *[near(x) for x in halos[5:]],
     )
 
 
@@ -507,7 +536,7 @@
         tangent = jnp.where(
             positive, 2.0 * inner * toward / jnp.where(positive, d, 1.0), 0.0
         )
-        cosine = 1.0 / jnp.sqrt(1.0 + tangent * tangent)
+        cosine = lax.rsqrt(1.0 + tangent * tangent)
         sine = spread(cosine * tangent)
         cosine = spread(cosine)
         return cosine * x + sine * y, cosine * v + sine * vy
@@ -671,7 +700,7 @@
 
 def program(velocity, basis, levels, profile_index, advect):
     n_space, n_mode = lax.axis_size("space"), lax.axis_size("mode")
-    comps, cx, _, ny = velocity.shape
+    comps, cx, _, _ = velocity.shape
     here = lax.axis_index("mode").astype(jnp.int32).reshape(1)
 
     def shifted(x, axis, by):
@@ -684,14 +713,9 @@
     lo = shifted(blocks[1], "mode", 1)
     hi = shifted(blocks[3], "mode", -1)
     over = shifted(blocks[2], "mode", 2)
+    plane_lo, plane_hi = add_corners(zlo, zhi, plane_lo, plane_hi, cx, comps)
     xlo = shifted(plane_hi, "space", 1)
     xhi = shifted(plane_lo, "space", -1)
-    near_lo = zlo.reshape(comps, 2, cx, ny)[:, 1]
-    near_hi = zhi.reshape(comps, 2, cx, ny)[:, 0]
-    corner_lo = jnp.stack([near_lo[:, -1], near_hi[:, -1]], axis=1)
-    corner_hi = jnp.stack([near_lo[:, 0], near_hi[:, 0]], axis=1)
-    corner_lo = shifted(corner_lo, "space", 1)
-    corner_hi = shifted(corner_hi, "space", -1)
     snap, plus, minus, across = snapshots(
         velocity,
         levels,
@@ -699,17 +723,17 @@
         advect,
         here,
         basis,
-        (zlo, zhi, face_lo, face_hi, corner_lo, corner_hi, velocity, xlo, xhi),
+        (zlo, zhi, face_lo, face_hi, velocity, xlo, xhi),
     )
-    lo_early = shifted(plus, "mode", 1)
-    hi_early = shifted(minus, "mode", -1)
     stack = (snap, blocks[0], hi, over, lo)
     total = gram(here, stack)
     total = ring_sum(total, ring_parts(total, "space", n_space, 1, 2))
+    total = ring_sum(total, ring_parts(total, "mode", n_mode, 1, n_mode))
     total = ring_sum(total, ring_parts(total, "space", n_space, 2, 4))
-    total = ring_sum(total, ring_parts(total, "space", n_space, 8, 4))
-    parts = [total] + ring_parts(total, "mode", n_mode, 1, n_mode)
+    lo_early = shifted(plus, "mode", 1)
+    hi_early = shifted(minus, "mode", -1)
     over_early = shifted(across, "mode", 2)
+    parts = [total] + ring_parts(total, "space", n_space, 8, 4)
     mix, sigma = factor(parts)
     out_own, out_next, out_over, out_prev = update(here, mix, stack)
     back_lo = shifted(out_next, "mode", 1)

time: 145 us -> 125 us (0.86)
  waiting for transfers between devices: 63.3 us -> 50.3 us
  starting transfers between devices: 41.6 us -> 35.1 us
    ppermute x10, waiting for transfers between devices: 27.7 us -> 13.1 us  [ring_parts(): lax.ppermute(x, axis, pairs)]
    ppermute x10, starting transfers between devices: 15.9 us -> 12.3 us  [ring_parts(): lax.ppermute(x, axis, pairs)]
    ppermute x15 -> x13, starting transfers between devices: 25.7 us -> 22.8 us  [shifted(): return lax.ppermute(x, axis, [(i, (i + by) % size) for i in range(size)])]
    ppermute x15 -> x13, waiting for transfers between devices: 35.6 us -> 37.2 us  [shifted(): return lax.ppermute(x, axis, [(i, (i + by) % size) for i in range(size)])]
  transfers between devices with their start and end apart: 25 -> 23, of which waited for: 13 -> 14; matrix products, arithmetic and copies ran while one was open for 0% -> 0% of each run, Pallas kernels for 23% -> 27%
where the time goes in v3:
time: 125 us; the launch traced here: 124 us
  waiting for transfers between devices  50.3 us (40%)
  Pallas kernels  37.7 us (30%)
  starting transfers between devices  35.1 us (28%)
    ppermute x13, waiting for transfers between devices, shifted(): return lax.ppermute(x, axis, [(i, (i + by) % size) for i in range(size)])  37.2 us
    ppermute x13, starting transfers between devices, shifted(): return lax.ppermute(x, axis, [(i, (i + by) % size) for i in range(size)])  22.8 us
    pallas_call x1, Pallas kernels, snapshots(): pl.pallas_call(stencil_kernel, grid=(comps,), in_specs=[SMEM_SPEC, pl.Blo...  19 us
    ppermute x10, waiting for transfers between devices, ring_parts(): lax.ppermute(x, axis, pairs)  13.1 us
    ppermute x10, starting transfers between devices, ring_parts(): lax.ppermute(x, axis, pairs)  12.3 us
    pallas_call x1, Pallas kernels, factor(): pl.pallas_call(factor_kernel, in_specs=[VMEM_SPEC] * 7, out_specs=(VMEM_S...  9.42 us
    pallas_call x1, Pallas kernels, pack(): pl.pallas_call(pack_kernel, in_specs=[SMEM_SPEC, HBM_SPEC, HBM_SPEC], out...  2.9 us
    pallas_call x1, Pallas kernels, own(): pl.pallas_call(functools.partial(own_kernel, cols=cols, chunk=chunk), in_...  2.8 us
  transfers between devices with their start and end apart: 23, of which 14 were waited for; matrix products, arithmetic and copies ran while one was open for 0% of the time, Pallas kernels for 27%

profile of v3, /device:TPU:0, one launch (start us, length us, event | category | flops | bytes accessed | tf_op | source)
XLA Modules:
  0.0 124.4 jit_solution(7447078416155632236)
XLA Ops:
  0.6 0.0 copy-start
  0.6 0.0 copy-start.3
  0.7 0.0 copy-start.4
  0.7 0.0 copy-start.5
  0.7 2.9 %pack.1 = (f32[96,256]{1,0:T(8,128)S(1)}, f32[96,256]{1,0:T(8,128)S(1)}, f32[776,256]{1,0:T(8,128)S(1)}, f32[776,256]{1,0:T(8,128)S(1)}, f32[8,24576]{1,0:T(8,12...) custom-call(s32[1]{0:T(128)} %bitcast.here_ref, f32[3,16,128,256]{3,2,1,0:T(8,128)} %vel_hbm.3, ...), custom_call_target="tpu_custom_call" | custom-call | tf_op jit(solution)/shard_map/pack/pallas_call | solution.py:106
  3.6 1.7 %collective-permute-start = (f32[96,256]{1,0:T(8,128)S(1)}, f32[96,256]{1,0:T(8,128)S(1)}, u32[]{:S(2)}, u32[]{:S(2)}) collective-permute-start(f32[96,256]{1,0:T(8,128)S(1)} %get-tuple-element.22.face_hi_ref), channel_id=1, source_target_pairs={{0,1},{1,2},{2,3},{3,0},{4,5},{5,6},{6,7},{7,4},{8,9},{9,10},{10,1... | collective-permute-start | bytes 294920 | tf_op jit(solution)/shard_map/ppermute | solution.py:708
  5.3 1.6 %collective-permute-start.1 = (f32[96,256]{1,0:T(8,128)S(1)}, f32[96,256]{1,0:T(8,128)S(1)}, u32[]{:S(2)}, u32[]{:S(2)}) collective-permute-start(f32[96,256]{1,0:T(8,128)S(1)} %get-tuple-element.23.face_lo_ref), channel_id=1, source_target_pairs={{0,3},{1,0},{2,1},{3,2},{4,7},{5,4},{6,5},{7,6},{8,11},{9,8},{10,9... | collective-permute-start | bytes 294920 | tf_op jit(solution)/shard_map/ppermute | solution.py:708
  6.9 2.6 %collective-permute-done.zlo_ref = f32[96,256]{1,0:T(8,128)S(1)} collective-permute-done((f32[96,256]{1,0:T(8,128)S(1)}, f32[96,256]{1,0:T(8,128)S(1)}, u32[]{:S(2)}, u32[]{:S(2)}) %collective-permute-start) | collective-permute-done | bytes 98336 | tf_op jit(solution)/shard_map/ppermute | solution.py:708
  9.5 0.4 collective-permute-done.1.zhi_ref
  9.9 0.1 collective-permute-start.2
  10.0 5.1 %collective-permute-start.3 = (f32[776,256]{1,0:T(8,128)S(1)}, f32[776,256]{1,0:T(8,128)S(1)}, u32[]{:S(2)}, u32[]{:S(2)}) collective-permute-start(f32[776,256]{1,0:T(8,128)S(1)} %get-tuple-element.27), channel_id=1, source_target_pairs={{0,124},{4,0},{8,4},{12,8},{16,12},{20,16},{24,20},{28,24},{32,28}... | collective-permute-start | bytes 2383880 | tf_op jit(solution)/shard_map/ppermute | solution.py:708
  15.0 2.8 %collective-permute-start.4 = (f32[8,24576]{1,0:T(8,128)S(1)}, f32[8,24576]{1,0:T(8,128)S(1)}, u32[]{:S(2)}, u32[]{:S(2)}) collective-permute-start(f32[8,24576]{1,0:T(8,128)S(1)} %get-tuple-element.30), channel_id=1, source_target_pairs={{0,3},{1,0},{2,1},{3,2},{4,7},{5,4},{6,5},{7,6},{8,11},{9,8},{10,9... | collective-permute-start | bytes 2359304 | tf_op jit(solution)/shard_map/ppermute | solution.py:708
  17.9 0.7 collective-permute-start.5
  18.6 0.6 collective-permute-start.6
  19.2 5.6 %collective-permute-done.2.xlo_ref = f32[776,256]{1,0:T(8,128)S(1)} collective-permute-done((f32[776,256]{1,0:T(8,128)S(1)}, f32[776,256]{1,0:T(8,128)S(1)}, u32[]{:S(2)}, u32[]{:S(2)}) %collective-permute-start.2) | collective-permute-done | bytes 794656 | tf_op jit(solution)/shard_map/ppermute | solution.py:708
  24.8 0.0 collective-permute-done.3.xhi_ref
  24.8 0.0 copy-done
  24.8 0.0 copy-done.4
  24.8 0.0 copy-done.5
  24.8 19.0 %stencil.1 = (f32[8,24576]{1,0:T(8,128)S(1)}, f32[8,19968]{1,0:T(8,128)S(1)}, f32[8,19968]{1,0:T(8,128)S(1)}, f32[8,19968]{1,0:T(8,128)S(1)}) custom-call(f32[8]{0:T(128)S(1)} %copy-done.5, s32[1,256]{1,0:T(1,128)S(1)} %bitcast.5, f32[1,256]{1,0:T(1,128)S(1)} %bitcast.6, bf16[256,128]{1,0:T(8,128)(2,1)S(1)} %copy-done, ...), custom_call_target="tpu_custom_call" | custom-call | tf_op jit(solution)/shard_map/stencil/pallas_call | solution.py:380
  43.8 0.0 copy-start.1
  43.8 0.0 copy-start.2
  43.8 0.0 copy-start.6
  43.8 2.9 %collective-permute-start.20 = (f32[8,19968]{1,0:T(8,128)S(1)}, f32[8,19968]{1,0:T(8,128)S(1)}, u32[]{:S(2)}, u32[]{:S(2)}) collective-permute-start(f32[8,19968]{1,0:T(8,128)S(1)} %get-tuple-element.38), channel_id=1, source_target_pairs={{0,3},{1,0},{2,1},{3,2},{4,7},{5,4},{6,5},{7,6},{8,11},{9,8},{10,9... | collective-permute-start | bytes 1916936 | tf_op jit(solution)/shard_map/ppermute | solution.py:708
  46.7 1.2 collective-permute-done.4.refs_2_
  47.9 0.0 collective-permute-done.5.refs_3_
  47.9 4.2 %collective-permute-done.6.refs_4_ = f32[8,24576]{1,0:T(8,128)S(1)} collective-permute-done((f32[8,24576]{1,0:T(8,128)S(1)}, f32[8,24576]{1,0:T(8,128)S(1)}, u32[]{:S(2)}, u32[]{:S(2)}) %collective-permute-start.6) | collective-permute-done | bytes 786464 | tf_op jit(solution)/shard_map/ppermute | solution.py:708
  52.1 1.4 %gram.1 = f32[40,128]{1,0:T(8,128)S(1)} custom-call(s32[1]{0:T(128)} %bitcast.here_ref, f32[8,24576]{1,0:T(8,128)S(1)} %get-tuple-element.28.refs_0_, f32[8,24576]{1,0:T(8,128)S(1)} %get-tuple-element.29.refs_1_, f32[8,24576]{1,0:T(8,128)S(1)} %collective-permute-done.4.refs_2_, f32[8,24576]{1,0:T(8,128)S(1)} %collective-permute-done.5.refs_3_, ...), custom_call_target="tpu_custom_call" | custom-call | tf_op jit(solution)/shard_map/gram/pallas_call | solution.py:450
  53.5 0.0 collective-permute-start.7
  53.5 1.2 collective-permute-done.7
  54.7 1.4 %collective-permute-start.10 = (f32[40,128]{1,0:T(8,128)S(1)}, f32[40,128]{1,0:T(8,128)S(1)}, u32[]{:S(2)}, u32[]{:S(2)}) collective-permute-start(f32[40,128]{1,0:T(8,128)S(1)} %add.21), channel_id=1, source_target_pairs={{0,3},{1,0},{2,1},{3,2},{4,7},{5,4},{6,5},{7,6},{8,11},{9,8},{10,9... | collective-permute-start | bytes 61448 | tf_op jit(solution)/shard_map/ppermute | solution.py:472
  56.1 0.6 collective-permute-start.9
  56.7 0.9 collective-permute-start.8
  57.7 5.3 %collective-permute-done.10 = f32[40,128]{1,0:T(8,128)S(1)} collective-permute-done((f32[40,128]{1,0:T(8,128)S(1)}, f32[40,128]{1,0:T(8,128)S(1)}, u32[]{:S(2)}, u32[]{:S(2)}) %collective-permute-start.10) | collective-permute-done | bytes 20512 | tf_op jit(solution)/shard_map/ppermute | solution.py:472
  63.0 0.0 collective-permute-done.9
  63.0 0.0 collective-permute-done.8
  63.0 3.1 %collective-permute-start.13 = (f32[40,128]{1,0:T(8,128)S(1)}, f32[40,128]{1,0:T(8,128)S(1)}, u32[]{:S(2)}, u32[]{:S(2)}) collective-permute-start(f32[40,128]{1,0:T(8,128)S(1)} %add_add_fusion.1), channel_id=1, source_target_pairs={{0,24},{4,28},{8,0},{12,4},{16,8},{20,12},{24,16},{28,20},{32,56},... | collective-permute-start | bytes 61448 | tf_op jit(solution)/shard_map/ppermute | solution.py:472
  66.1 0.0 collective-permute-start.12
  66.1 1.9 %collective-permute-start.11 = (f32[40,128]{1,0:T(8,128)S(1)}, f32[40,128]{1,0:T(8,128)S(1)}, u32[]{:S(2)}, u32[]{:S(2)}) collective-permute-start(f32[40,128]{1,0:T(8,128)S(1)} %add_add_fusion.1), channel_id=1, source_target_pairs={{0,16},{4,20},{8,24},{12,28},{16,0},{20,4},{24,8},{28,12},{32,48},... | collective-permute-start | bytes 61448 | tf_op jit(solution)/shard_map/ppermute | solution.py:472
  68.0 2.1 %collective-permute-start.21 = (f32[8,19968]{1,0:T(8,128)S(1)}, f32[8,19968]{1,0:T(8,128)S(1)}, u32[]{:S(2)}, u32[]{:S(2)}) collective-permute-start(f32[8,19968]{1,0:T(8,128)S(1)} %get-tuple-element.39), channel_id=1, source_target_pairs={{0,2},{1,3},{2,0},{3,1},{4,6},{5,7},{6,4},{7,5},{8,10},{9,11},{10,... | collective-permute-start | bytes 1916936 | tf_op jit(solution)/shard_map/ppermute | solution.py:708
  70.1 0.0 collective-permute-done.13
  70.1 2.5 %collective-permute-start.22 = (f32[8,19968]{1,0:T(8,128)S(1)}, f32[8,19968]{1,0:T(8,128)S(1)}, u32[]{:S(2)}, u32[]{:S(2)}) collective-permute-start(f32[8,19968]{1,0:T(8,128)S(1)} %get-tuple-element.40), channel_id=1, source_target_pairs={{0,1},{1,2},{2,3},{3,0},{4,5},{5,6},{6,7},{7,4},{8,9},{9,10},{10,1... | collective-permute-start | bytes 1916936 | tf_op jit(solution)/shard_map/ppermute | solution.py:708
  72.6 0.0 collective-permute-done.12
  72.6 0.0 collective-permute-done.11
  72.6 4.1 %collective-permute-start.16 = (f32[40,128]{1,0:T(8,128)S(1)}, f32[40,128]{1,0:T(8,128)S(1)}, u32[]{:S(2)}, u32[]{:S(2)}) collective-permute-start(f32[40,128]{1,0:T(8,128)S(1)} %add_add_fusion.g0_ref), channel_id=1, source_target_pairs={{0,96},{4,100},{8,104},{12,108},{16,112},{20,116},{24,120},{28,124... | collective-permute-start | bytes 61448 | tf_op jit(solution)/shard_map/ppermute | solution.py:472
  76.7 0.0 collective-permute-start.15
  76.7 1.5 %collective-permute-done.16.g3_ref = f32[40,128]{1,0:T(8,128)S(1)} collective-permute-done((f32[40,128]{1,0:T(8,128)S(1)}, f32[40,128]{1,0:T(8,128)S(1)}, u32[]{:S(2)}, u32[]{:S(2)}) %collective-permute-start.16) | collective-permute-done | bytes 20512 | tf_op jit(solution)/shard_map/ppermute | solution.py:472
  78.2 0.2 collective-permute-start.14
  78.3 3.6 %collective-permute-done.15.g2_ref = f32[40,128]{1,0:T(8,128)S(1)} collective-permute-done((f32[40,128]{1,0:T(8,128)S(1)}, f32[40,128]{1,0:T(8,128)S(1)}, u32[]{:S(2)}, u32[]{:S(2)}) %collective-permute-start.15) | collective-permute-done | bytes 20512 | tf_op jit(solution)/shard_map/ppermute | solution.py:472
  82.0 1.5 %collective-permute-done.14.g1_ref = f32[40,128]{1,0:T(8,128)S(1)} collective-permute-done((f32[40,128]{1,0:T(8,128)S(1)}, f32[40,128]{1,0:T(8,128)S(1)}, u32[]{:S(2)}, u32[]{:S(2)}) %collective-permute-start.14) | collective-permute-done | bytes 20512 | tf_op jit(solution)/shard_map/ppermute | solution.py:472
  83.4 9.4 %factor.1 = (f32[32,128]{1,0:T(8,128)S(1)}, f32[8,128]{1,0:T(8,128)S(1)}) custom-call(f32[40,128]{1,0:T(8,128)S(1)} %add_add_fusion.g0_ref, f32[40,128]{1,0:T(8,128)S(1)} %collective-permute-done.14.g1_ref, f32[40,128]{1,0:T(8,128)S(1)} %collective-permute-done.15.g2_ref, f32[40,128]{1,0:T(8,128)S(1)} %collective-permute-done.16.g3_ref, ...), custom_call_target="tpu_custom_call" | custom-call | tf_op jit(solution)/shard_map/factor/pallas_call | solution.py:557
  92.9 0.8 update.1
  93.7 1.6 %collective-permute-start.17 = (f32[8,18432]{1,0:T(8,128)S(1)}, f32[8,18432]{1,0:T(8,128)S(1)}, u32[]{:S(2)}, u32[]{:S(2)}) collective-permute-start(f32[8,18432]{1,0:T(8,128)S(1)} %get-tuple-element.35), channel_id=1, source_target_pairs={{0,3},{1,0},{2,1},{3,2},{4,7},{5,4},{6,5},{7,6},{8,11},{9,8},{10,9... | collective-permute-start | bytes 1769480 | tf_op jit(solution)/shard_map/ppermute | solution.py:708
  95.3 0.6 collective-permute-start.18
  95.9 0.0 collective-permute-done.20.refs_5_
  95.9 0.6 collective-permute-start.19
  96.5 0.5 slice_bitcast_fusion
  97.0 0.0 collective-permute-done.21.refs_6_
  97.0 3.3 %collective-permute-done.22.refs_7_ = f32[8,19968]{1,0:T(8,128)S(1)} collective-permute-done((f32[8,19968]{1,0:T(8,128)S(1)}, f32[8,19968]{1,0:T(8,128)S(1)}, u32[]{:S(2)}, u32[]{:S(2)}) %collective-permute-start.22) | collective-permute-done | bytes 639008 | tf_op jit(solution)/shard_map/ppermute | solution.py:708
  100.3 2.8 %own.1.refs_4_ = f32[8,98304]{1,0:T(8,128)} custom-call(s32[1]{0:T(128)} %bitcast.here_ref, f32[32,128]{1,0:T(8,128)S(1)} %get-tuple-element.33.mix_ref, f32[8,24576]{1,0:T(8,128)S(1)} %get-tuple-element.28.refs_0_, f32[8,24576]{1,0:T(8,128)S(1)} %get-tuple-element.29.refs_1_, f32[8,24576]{1,0:T(8,128)S(1)} %collective-permute-done.4.refs_2_, ...), custom_call_target="tpu_custom_call" | custom-call | tf_op jit(solution)/shard_map/own/pallas_call | solution.py:658
  103.1 6.9 %collective-permute-done.17.refs_1_ = f32[8,18432]{1,0:T(8,128)S(1)} collective-permute-done((f32[8,18432]{1,0:T(8,128)S(1)}, f32[8,18432]{1,0:T(8,128)S(1)}, u32[]{:S(2)}, u32[]{:S(2)}) %collective-permute-start.17) | collective-permute-done | bytes 589856 | tf_op jit(solution)/shard_map/ppermute | solution.py:708
  110.0 3.1 %collective-permute-done.18.refs_2_ = f32[8,18432]{1,0:T(8,128)S(1)} collective-permute-done((f32[8,18432]{1,0:T(8,128)S(1)}, f32[8,18432]{1,0:T(8,128)S(1)}, u32[]{:S(2)}, u32[]{:S(2)}) %collective-permute-start.18) | collective-permute-done | bytes 589856 | tf_op jit(solution)/shard_map/ppermute | solution.py:708
  113.0 9.9 %collective-permute-done.19.refs_3_ = f32[8,18432]{1,0:T(8,128)S(1)} collective-permute-done((f32[8,18432]{1,0:T(8,128)S(1)}, f32[8,18432]{1,0:T(8,128)S(1)}, u32[]{:S(2)}, u32[]{:S(2)}) %collective-permute-start.19) | collective-permute-done | bytes 589856 | tf_op jit(solution)/shard_map/ppermute | solution.py:708
  123.0 1.4 %join.1 = f32[8,98304]{1,0:T(8,128)} custom-call(s32[1]{0:T(128)} %bitcast.here_ref, f32[8,18432]{1,0:T(8,128)S(1)} %get-tuple-element.34.refs_0_, f32[8,18432]{1,0:T(8,128)S(1)} %collective-permute-done.17.refs_1_, f32[8,18432]{1,0:T(8,128)S(1)} %collective-permute-done.18.refs_2_, ...), custom_call_target="tpu_custom_call", output_to_operand_aliasing={{}: (5, {})} | custom-call | tf_op jit(solution)/shard_map/join/pallas_call | solution.py:689
  (8 shorter events, 0.0 us)
Async XLA Ops:
  0.6 24.1 %copy-start = (bf16[256,128]{1,0:T(8,128)(2,1)S(1)}, bf16[256,128]{1,0:T(8,128)(2,1)}, u32[]{:S(2)}) copy-start(bf16[256,128]{1,0:T(8,128)(2,1)} %constant.12.clone.sum_ref) | copy-start | bytes 196612
  0.6 24.1 %copy-start.3 = (s32[256]{0:T(256)S(1)}, s32[256]{0:T(256)}, u32[]{:S(2)}) copy-start(s32[256]{0:T(256)} %param.12) | copy-start | bytes 3076
  0.7 24.1 %copy-start.4 = (f32[256]{0:T(256)S(1)}, f32[256]{0:T(256)}, u32[]{:S(2)}) copy-start(f32[256]{0:T(256)} %param.13) | copy-start | bytes 3076
  0.7 24.1 %copy-start.5 = (f32[8]{0:T(128)S(1)}, f32[8]{0:T(128)}, u32[]{:S(2)}) copy-start(f32[8]{0:T(128)} %levels_ref.1) | copy-start | bytes 100
  3.6 5.9 %collective-permute-start = (f32[96,256]{1,0:T(8,128)S(1)}, f32[96,256]{1,0:T(8,128)S(1)}, u32[]{:S(2)}, u32[]{:S(2)}) collective-permute-start(f32[96,256]{1,0:T(8,128)S(1)} %get-tuple-element.22.face_hi_ref), channel_id=1, source_target_pairs={{0,1},{1,2},{2,3},{3,0},{4,5},{5,6},{6,7},{7,4},{8,9},{9,10},{10,1... | collective-permute-start | bytes 294920 | tf_op jit(solution)/shard_map/ppermute | solution.py:708
  5.3 4.6 %collective-permute-start.1 = (f32[96,256]{1,0:T(8,128)S(1)}, f32[96,256]{1,0:T(8,128)S(1)}, u32[]{:S(2)}, u32[]{:S(2)}) collective-permute-start(f32[96,256]{1,0:T(8,128)S(1)} %get-tuple-element.23.face_lo_ref), channel_id=1, source_target_pairs={{0,3},{1,0},{2,1},{3,2},{4,7},{5,4},{6,5},{7,6},{8,11},{9,8},{10,9... | collective-permute-start | bytes 294920 | tf_op jit(solution)/shard_map/ppermute | solution.py:708
  9.9 14.9 %collective-permute-start.2 = (f32[776,256]{1,0:T(8,128)S(1)}, f32[776,256]{1,0:T(8,128)S(1)}, u32[]{:S(2)}, u32[]{:S(2)}) collective-permute-start(f32[776,256]{1,0:T(8,128)S(1)} %get-tuple-element.26), channel_id=1, source_target_pairs={{0,4},{4,8},{8,12},{12,16},{16,20},{20,24},{24,28},{28,32},{32,36}... | collective-permute-start | bytes 2383880 | tf_op jit(solution)/shard_map/ppermute | solution.py:708
  10.0 14.8 %collective-permute-start.3 = (f32[776,256]{1,0:T(8,128)S(1)}, f32[776,256]{1,0:T(8,128)S(1)}, u32[]{:S(2)}, u32[]{:S(2)}) collective-permute-start(f32[776,256]{1,0:T(8,128)S(1)} %get-tuple-element.27), channel_id=1, source_target_pairs={{0,124},{4,0},{8,4},{12,8},{16,12},{20,16},{24,20},{28,24},{32,28}... | collective-permute-start | bytes 2383880 | tf_op jit(solution)/shard_map/ppermute | solution.py:708
  15.0 32.9 %collective-permute-start.4 = (f32[8,24576]{1,0:T(8,128)S(1)}, f32[8,24576]{1,0:T(8,128)S(1)}, u32[]{:S(2)}, u32[]{:S(2)}) collective-permute-start(f32[8,24576]{1,0:T(8,128)S(1)} %get-tuple-element.30), channel_id=1, source_target_pairs={{0,3},{1,0},{2,1},{3,2},{4,7},{5,4},{6,5},{7,6},{8,11},{9,8},{10,9... | collective-permute-start | bytes 2359304 | tf_op jit(solution)/shard_map/ppermute | solution.py:708
  17.9 30.1 %collective-permute-start.5 = (f32[8,24576]{1,0:T(8,128)S(1)}, f32[8,24576]{1,0:T(8,128)S(1)}, u32[]{:S(2)}, u32[]{:S(2)}) collective-permute-start(f32[8,24576]{1,0:T(8,128)S(1)} %get-tuple-element.31), channel_id=1, source_target_pairs={{0,2},{1,3},{2,0},{3,1},{4,6},{5,7},{6,4},{7,5},{8,10},{9,11},{10,... | collective-permute-start | bytes 2359304 | tf_op jit(solution)/shard_map/ppermute | solution.py:708
  18.6 33.5 %collective-permute-start.6 = (f32[8,24576]{1,0:T(8,128)S(1)}, f32[8,24576]{1,0:T(8,128)S(1)}, u32[]{:S(2)}, u32[]{:S(2)}) collective-permute-start(f32[8,24576]{1,0:T(8,128)S(1)} %get-tuple-element.32), channel_id=1, source_target_pairs={{0,1},{1,2},{2,3},{3,0},{4,5},{5,6},{6,7},{7,4},{8,9},{9,10},{10,1... | collective-permute-start | bytes 2359304 | tf_op jit(solution)/shard_map/ppermute | solution.py:708
  43.8 39.7 %copy-start.1 = (f32[40,128]{1,0:T(8,128)S(1)}, f32[40,128]{1,0:T(8,128)}, u32[]{:S(2)}) copy-start(f32[40,128]{1,0:T(8,128)} %constant.14.clone.orient_ref) | copy-start | bytes 61444
  43.8 39.7 %copy-start.2 = (s32[40,128]{1,0:T(8,128)S(1)}, s32[40,128]{1,0:T(8,128)}, u32[]{:S(2)}) copy-start(s32[40,128]{1,0:T(8,128)} %constant.13.clone.partner_ref) | copy-start | bytes 61444
  43.8 39.6 %copy-start.6 = (s32[1,128]{1,0:T(1,128)S(1)}, s32[1,128]{1,0:T(1,128)}, u32[]{:S(2)}) copy-start(s32[1,128]{1,0:T(1,128)} %constant.15.clone.keep_ref) | copy-start | bytes 1540
  43.8 52.1 %collective-permute-start.20 = (f32[8,19968]{1,0:T(8,128)S(1)}, f32[8,19968]{1,0:T(8,128)S(1)}, u32[]{:S(2)}, u32[]{:S(2)}) collective-permute-start(f32[8,19968]{1,0:T(8,128)S(1)} %get-tuple-element.38), channel_id=1, source_target_pairs={{0,3},{1,0},{2,1},{3,2},{4,7},{5,4},{6,5},{7,6},{8,11},{9,8},{10,9... | collective-permute-start | bytes 1916936 | tf_op jit(solution)/shard_map/ppermute | solution.py:708
  53.5 1.2 collective-permute-start.7
  54.7 8.3 %collective-permute-start.10 = (f32[40,128]{1,0:T(8,128)S(1)}, f32[40,128]{1,0:T(8,128)S(1)}, u32[]{:S(2)}, u32[]{:S(2)}) collective-permute-start(f32[40,128]{1,0:T(8,128)S(1)} %add.21), channel_id=1, source_target_pairs={{0,3},{1,0},{2,1},{3,2},{4,7},{5,4},{6,5},{7,6},{8,11},{9,8},{10,9... | collective-permute-start | bytes 61448 | tf_op jit(solution)/shard_map/ppermute | solution.py:472
  56.1 6.9 %collective-permute-start.9 = (f32[40,128]{1,0:T(8,128)S(1)}, f32[40,128]{1,0:T(8,128)S(1)}, u32[]{:S(2)}, u32[]{:S(2)}) collective-permute-start(f32[40,128]{1,0:T(8,128)S(1)} %add.21), channel_id=1, source_target_pairs={{0,1},{1,2},{2,3},{3,0},{4,5},{5,6},{6,7},{7,4},{8,9},{9,10},{10,1... | collective-permute-start | bytes 61448 | tf_op jit(solution)/shard_map/ppermute | solution.py:472
  56.7 6.3 %collective-permute-start.8 = (f32[40,128]{1,0:T(8,128)S(1)}, f32[40,128]{1,0:T(8,128)S(1)}, u32[]{:S(2)}, u32[]{:S(2)}) collective-permute-start(f32[40,128]{1,0:T(8,128)S(1)} %add.21), channel_id=1, source_target_pairs={{0,2},{1,3},{2,0},{3,1},{4,6},{5,7},{6,4},{7,5},{8,10},{9,11},{10,... | collective-permute-start | bytes 61448 | tf_op jit(solution)/shard_map/ppermute | solution.py:472
  63.0 7.1 %collective-permute-start.13 = (f32[40,128]{1,0:T(8,128)S(1)}, f32[40,128]{1,0:T(8,128)S(1)}, u32[]{:S(2)}, u32[]{:S(2)}) collective-permute-start(f32[40,128]{1,0:T(8,128)S(1)} %add_add_fusion.1), channel_id=1, source_target_pairs={{0,24},{4,28},{8,0},{12,4},{16,8},{20,12},{24,16},{28,20},{32,56},... | collective-permute-start | bytes 61448 | tf_op jit(solution)/shard_map/ppermute | solution.py:472
  66.1 6.5 %collective-permute-start.12 = (f32[40,128]{1,0:T(8,128)S(1)}, f32[40,128]{1,0:T(8,128)S(1)}, u32[]{:S(2)}, u32[]{:S(2)}) collective-permute-start(f32[40,128]{1,0:T(8,128)S(1)} %add_add_fusion.1), channel_id=1, source_target_pairs={{0,8},{4,12},{8,16},{12,20},{16,24},{20,28},{24,0},{28,4},{32,40},... | collective-permute-start | bytes 61448 | tf_op jit(solution)/shard_map/ppermute | solution.py:472
  66.1 6.5 %collective-permute-start.11 = (f32[40,128]{1,0:T(8,128)S(1)}, f32[40,128]{1,0:T(8,128)S(1)}, u32[]{:S(2)}, u32[]{:S(2)}) collective-permute-start(f32[40,128]{1,0:T(8,128)S(1)} %add_add_fusion.1), channel_id=1, source_target_pairs={{0,16},{4,20},{8,24},{12,28},{16,0},{20,4},{24,8},{28,12},{32,48},... | collective-permute-start | bytes 61448 | tf_op jit(solution)/shard_map/ppermute | solution.py:472
  68.0 29.0 %collective-permute-start.21 = (f32[8,19968]{1,0:T(8,128)S(1)}, f32[8,19968]{1,0:T(8,128)S(1)}, u32[]{:S(2)}, u32[]{:S(2)}) collective-permute-start(f32[8,19968]{1,0:T(8,128)S(1)} %get-tuple-element.39), channel_id=1, source_target_pairs={{0,2},{1,3},{2,0},{3,1},{4,6},{5,7},{6,4},{7,5},{8,10},{9,11},{10,... | collective-permute-start | bytes 1916936 | tf_op jit(solution)/shard_map/ppermute | solution.py:708
  70.1 30.2 %collective-permute-start.22 = (f32[8,19968]{1,0:T(8,128)S(1)}, f32[8,19968]{1,0:T(8,128)S(1)}, u32[]{:S(2)}, u32[]{:S(2)}) collective-permute-start(f32[8,19968]{1,0:T(8,128)S(1)} %get-tuple-element.40), channel_id=1, source_target_pairs={{0,1},{1,2},{2,3},{3,0},{4,5},{5,6},{6,7},{7,4},{8,9},{9,10},{10,1... | collective-permute-start | bytes 1916936 | tf_op jit(solution)/shard_map/ppermute | solution.py:708
  72.6 5.6 %collective-permute-start.16 = (f32[40,128]{1,0:T(8,128)S(1)}, f32[40,128]{1,0:T(8,128)S(1)}, u32[]{:S(2)}, u32[]{:S(2)}) collective-permute-start(f32[40,128]{1,0:T(8,128)S(1)} %add_add_fusion.g0_ref), channel_id=1, source_target_pairs={{0,96},{4,100},{8,104},{12,108},{16,112},{20,116},{24,120},{28,124... | collective-permute-start | bytes 61448 | tf_op jit(solution)/shard_map/ppermute | solution.py:472
  76.7 5.3 %collective-permute-start.15 = (f32[40,128]{1,0:T(8,128)S(1)}, f32[40,128]{1,0:T(8,128)S(1)}, u32[]{:S(2)}, u32[]{:S(2)}) collective-permute-start(f32[40,128]{1,0:T(8,128)S(1)} %add_add_fusion.g0_ref), channel_id=1, source_target_pairs={{0,64},{4,68},{8,72},{12,76},{16,80},{20,84},{24,88},{28,92},{32,9... | collective-permute-start | bytes 61448 | tf_op jit(solution)/shard_map/ppermute | solution.py:472
  78.2 5.3 %collective-permute-start.14 = (f32[40,128]{1,0:T(8,128)S(1)}, f32[40,128]{1,0:T(8,128)S(1)}, u32[]{:S(2)}, u32[]{:S(2)}) collective-permute-start(f32[40,128]{1,0:T(8,128)S(1)} %add_add_fusion.g0_ref), channel_id=1, source_target_pairs={{0,32},{4,36},{8,40},{12,44},{16,48},{20,52},{24,56},{28,60},{32,6... | collective-permute-start | bytes 61448 | tf_op jit(solution)/shard_map/ppermute | solution.py:472
  93.7 16.3 %collective-permute-start.17 = (f32[8,18432]{1,0:T(8,128)S(1)}, f32[8,18432]{1,0:T(8,128)S(1)}, u32[]{:S(2)}, u32[]{:S(2)}) collective-permute-start(f32[8,18432]{1,0:T(8,128)S(1)} %get-tuple-element.35), channel_id=1, source_target_pairs={{0,3},{1,0},{2,1},{3,2},{4,7},{5,4},{6,5},{7,6},{8,11},{9,8},{10,9... | collective-permute-start | bytes 1769480 | tf_op jit(solution)/shard_map/ppermute | solution.py:708
  95.3 17.7 %collective-permute-start.18 = (f32[8,18432]{1,0:T(8,128)S(1)}, f32[8,18432]{1,0:T(8,128)S(1)}, u32[]{:S(2)}, u32[]{:S(2)}) collective-permute-start(f32[8,18432]{1,0:T(8,128)S(1)} %get-tuple-element.36), channel_id=1, source_target_pairs={{0,2},{1,3},{2,0},{3,1},{4,6},{5,7},{6,4},{7,5},{8,10},{9,11},{10,... | collective-permute-start | bytes 1769480 | tf_op jit(solution)/shard_map/ppermute | solution.py:708
  95.9 27.1 %collective-permute-start.19 = (f32[8,18432]{1,0:T(8,128)S(1)}, f32[8,18432]{1,0:T(8,128)S(1)}, u32[]{:S(2)}, u32[]{:S(2)}) collective-permute-start(f32[8,18432]{1,0:T(8,128)S(1)} %get-tuple-element.37), channel_id=1, source_target_pairs={{0,1},{1,2},{2,3},{3,0},{4,5},{5,6},{6,7},{7,4},{8,9},{9,10},{10,1... | collective-permute-start | bytes 1769480 | tf_op jit(solution)/shard_map/ppermute | solution.py:708

commit v4 on v3

--- a/solution.py
+++ b/solution.py
@@ -63,6 +63,8 @@
     next_ref,
     far_ref,
     prev_ref,
+    next_tail_ref,
+    prev_tail_ref,
     buf,
     edge_sems,
     face_sems,
@@ -80,10 +82,18 @@
                 source = vel_hbm.at[c, at + k]
                 target = ref.at[pl.ds((2 * c + k) * cz, cz)]
                 rest.append(pltpu.make_async_copy(source, target, face_sems.at[c, side, k]))
-    for k, ref in enumerate((mine_ref, next_ref, far_ref, prev_ref)):
-        at = pl.multiple_of(lax.rem(here_ref[0] + k, 4) * cols, LANES)
-        source = basis_hbm.at[:, pl.ds(at, cols)]
-        rest.append(pltpu.make_async_copy(source, ref, block_sems.at[k]))
+    targets = (
+        (0, 0, mine_ref),
+        (1, 0, next_ref),
+        (2, 0, far_ref),
+        (3, 0, prev_ref),
+        (1, SHARED, next_tail_ref),
+        (3, SHARED, prev_tail_ref),
+    )
+    for i, (k, skip, ref) in enumerate(targets):
+        at = pl.multiple_of(lax.rem(here_ref[0] + k, 4) * cols + skip, LANES)
+        source = basis_hbm.at[:, pl.ds(at, ref.shape[1])]
+        rest.append(pltpu.make_async_copy(source, ref, block_sems.at[i]))
     for copy in edges + rest:
         copy.start()
     for copy in edges:
@@ -102,17 +112,20 @@
     comps, cx, cz, ny = velocity.shape
     edge = pltpu.VMEM((comps * 2 * cx, ny), jnp.float32)
     face = pltpu.VMEM((comps * 2 * cz + PAD, ny), jnp.float32)
-    block = pltpu.VMEM((PAD, basis.shape[1] // 4), jnp.float32)
+    cols = basis.shape[1] // 4
+    block, head, tail = (
+        pltpu.VMEM((PAD, size), jnp.float32) for size in (cols, SHARED, cols - SHARED)
+    )
     return pl.pallas_call(
         pack_kernel,
         in_specs=[SMEM_SPEC, HBM_SPEC, HBM_SPEC],
-        out_specs=[VMEM_SPEC] * 8,
-        out_shape=[edge, edge, face, face] + [block] * 4,
+        out_specs=[VMEM_SPEC] * 10,
+        out_shape=[edge, edge, face, face, block, head, block, head, tail, tail],
         scratch_shapes=[
             pltpu.VMEM((comps, 2, cx, PAD, ny), jnp.float32),
             pltpu.SemaphoreType.DMA((comps, 2)),
             pltpu.SemaphoreType.DMA((comps, 2, 2)),
-            pltpu.SemaphoreType.DMA((4,)),
+            pltpu.SemaphoreType.DMA((6,)),
         ],
         compiler_params=pltpu.CompilerParams(vmem_limit_bytes=4 << 20),
         name="pack",
@@ -191,8 +204,8 @@
 def offer_copies(here, basis_hbm, refs, sems):
     cols = basis_hbm.shape[1] // 4
     copies = []
-    for side, (ref, skip) in enumerate(zip(refs, (2, 0, 3))):
-        for k in range(3):
+    for side, (ref, skip, count) in enumerate(zip(refs, (2, 0, 0), (3, 3, 1))):
+        for k in range(count):
             at = pl.multiple_of(lax.rem(here + skip + k, 4) * cols, LANES)
             source = basis_hbm.at[:, pl.ds(at, SHARED)]
             target = ref.at[:, pl.ds(k * SHARED, SHARED)]
@@ -364,8 +377,8 @@
         for k in range(2 * tiles):
             which, tile = divmod(k, tiles)
             line = out_ref[which : which + 1, tile * LANES : (tile + 1) * LANES]
-            at = 3 * SHARED + k // 8 * LANES
             for ref in offer_refs:
+                at = ref.shape[1] - FOLD + k // 8 * LANES
                 ref[k % 8 : k % 8 + 1, at : at + LANES] = line
 
 
@@ -394,7 +407,7 @@
         ],
         out_specs=[VMEM_SPEC] * 4,
         out_shape=[pltpu.VMEM((PAD, comps * cols), jnp.float32)]
-        + [pltpu.VMEM((PAD, 3 * SHARED + FOLD), jnp.float32)] * 3,
+        + [pltpu.VMEM((PAD, k * SHARED + FOLD), jnp.float32) for k in (3, 3, 1)],
         scratch_shapes=[
             pltpu.VMEM((comps, cx + 4, cz + 2 * PAD, ny), jnp.float32),
             pltpu.VMEM((cx + 2, cz + 2 * PAD, ny), jnp.float32),
@@ -417,16 +430,28 @@
     )
 
 
-def stacked(refs, at):
-    return jnp.concatenate([ref[:, at] for ref in refs], axis=0)
+def stacked(pieces, start, size):
+    rows = []
+    for piece in pieces:
+        if isinstance(piece, tuple):
+            ref, at = (piece[0], start) if start < SHARED else (piece[1], start - SHARED)
+        else:
+            ref, at = piece, start
+        rows.append(ref[:, at : at + size])
+    return jnp.concatenate(rows, axis=0)
+
+
+def pieces_of(refs):
+    snap, mine, hi, hi_tail, far_block, lo, lo_tail = refs
+    return [snap, mine, (hi, hi_tail), far_block, (lo, lo_tail)]
 
 
 def gram_kernel(here_ref, *refs, chunk):
-    stack_refs, out_ref = refs[:-1], refs[-1]
+    pieces, out_ref = pieces_of(refs[:-1]), refs[-1]
     here = here_ref[0]
     n, acc = ROWS, None
-    for start in range(0, stack_refs[0].shape[1], chunk):
-        stack = stacked(stack_refs, slice(start, start + chunk))
+    for start in range(0, pieces[0].shape[1], chunk):
+        stack = stacked(pieces, start, chunk)
         high = stack.astype(jnp.bfloat16).astype(jnp.float32)
         joined = jnp.concatenate([high, stack - high], axis=0).astype(jnp.bfloat16)
         part = lax.dot_general(
@@ -449,7 +474,7 @@
 def gram(here, stack, chunk=2048):
     return pl.pallas_call(
         functools.partial(gram_kernel, chunk=chunk),
-        in_specs=[SMEM_SPEC] + [VMEM_SPEC] * 5,
+        in_specs=[SMEM_SPEC] + [VMEM_SPEC] * 7,
         out_specs=VMEM_SPEC,
         out_shape=pltpu.VMEM((ROWS, LANES), jnp.float32),
         compiler_params=pltpu.CompilerParams(vmem_limit_bytes=8 << 20),
@@ -588,13 +613,12 @@
 
 
 def update_kernel(here_ref, mix_ref, *refs, chunk):
-    stack_refs, out_refs = refs[:5], refs[5:]
+    pieces, out_refs = pieces_of(refs[:7]), refs[7:]
     here = here_ref[0]
     mix = jnp.concatenate([mix_rows(mix_ref, here, g) for g in range(4)], axis=0)
     mix = turned_mix(mix, here)
     for start in range(0, out_refs[0].shape[1], chunk):
-        first = SHARED + start
-        out = mixed(mix, stacked(stack_refs, slice(first, first + chunk)))
+        out = mixed(mix, stacked(pieces, SHARED + start, chunk))
         for g, ref in enumerate(out_refs):
             ref[:, start : start + chunk] = out[PAD * g : PAD * g + PAD]
 
@@ -603,7 +627,7 @@
     cols = stack[0].shape[1] - SHARED
     return pl.pallas_call(
         functools.partial(update_kernel, chunk=chunk),
-        in_specs=[SMEM_SPEC] + [VMEM_SPEC] * 6,
+        in_specs=[SMEM_SPEC] + [VMEM_SPEC] * 8,
         out_specs=[VMEM_SPEC] * 4,
         out_shape=[pltpu.VMEM((PAD, cols), jnp.float32)] * 4,
         compiler_params=pltpu.CompilerParams(vmem_limit_bytes=8 << 20),
@@ -612,8 +636,8 @@
 
 
 def own_kernel(here_ref, mix_ref, *refs, cols, chunk):
-    stack_refs, (hi_ref, over_ref, lo_ref) = refs[:5], refs[5:8]
-    basis_hbm, out_hbm, mine, snap, buf, in_sems, out_sems = refs[8:]
+    pieces, (hi_ref, over_ref, lo_ref, hi_far_ref, lo_far_ref) = pieces_of(refs[:7]), refs[7:12]
+    basis_hbm, out_hbm, mine, snap, buf, in_sems, out_sems = refs[12:]
     here = here_ref[0]
     tiles = SHARED // LANES
     blocks = [lax.rem(here + 1 + b, 4) for b in range(4)]
@@ -629,7 +653,7 @@
         snap[b] = jnp.zeros((PAD, SHARED), jnp.float32)
         for k in range(2 * tiles):
             which, tile = divmod(k, tiles)
-            at = 3 * SHARED + k // 8 * LANES
+            at = ref.shape[1] - FOLD + k // 8 * LANES
             line = ref[k % 8 : k % 8 + 1, at : at + LANES]
             snap[b, which : which + 1, tile * LANES : (tile + 1) * LANES] = line
     for copy in reads:
@@ -639,11 +663,12 @@
         for start in range(0, SHARED, chunk):
             at = slice(start, start + chunk)
             if b == 3:
-                stack = stacked(stack_refs, at)
+                stack = stacked(pieces, start, chunk)
             else:
                 wide = slice(b * SHARED + start, b * SHARED + start + chunk)
+                opposite = (hi_far_ref, over_ref, lo_far_ref)[b]
                 rows = [snap[b, :, at], mine[b, :, at]]
-                rows += [ref[:, wide] for ref in (hi_ref, over_ref, lo_ref)]
+                rows += [hi_ref[:, wide], opposite[:, at], lo_ref[:, wide]]
                 stack = jnp.concatenate(rows, axis=0)
             buf[b, :, at] = mixed(mix, stack)
         target = pl.ds(pl.multiple_of(blocks[b] * cols, LANES), SHARED)
@@ -657,7 +682,7 @@
     cols = basis.shape[1] // 4
     return pl.pallas_call(
         functools.partial(own_kernel, cols=cols, chunk=chunk),
-        in_specs=[SMEM_SPEC] + [VMEM_SPEC] * 9 + [HBM_SPEC],
+        in_specs=[SMEM_SPEC] + [VMEM_SPEC] * 13 + [HBM_SPEC],
         out_specs=HBM_SPEC,
         out_shape=pltpu.HBM(basis.shape, jnp.float32),
         scratch_shapes=[
@@ -708,14 +733,19 @@
         return lax.ppermute(x, axis, [(i, (i + by) % size) for i in range(size)])
 
     face_lo, face_hi, plane_lo, plane_hi, *blocks = pack(here, velocity, basis)
+    block_own, block_next, block_far, block_prev, tail_next, tail_prev = blocks
     zlo = shifted(face_hi, "mode", 1)
     zhi = shifted(face_lo, "mode", -1)
-    lo = shifted(blocks[1], "mode", 1)
-    hi = shifted(blocks[3], "mode", -1)
-    over = shifted(blocks[2], "mode", 2)
+    lo = shifted(block_next, "mode", 1)
+    hi = shifted(block_prev, "mode", -1)
     plane_lo, plane_hi = add_corners(zlo, zhi, plane_lo, plane_hi, cx, comps)
     xlo = shifted(plane_hi, "space", 1)
     xhi = shifted(plane_lo, "space", -1)
+    lo_tail = shifted(tail_next, "mode", 1)
+    hi_tail = shifted(tail_prev, "mode", -1)
+    over = shifted(block_far, "mode", 2)
+    lo_far = shifted(lo, "mode", 1)
+    hi_far = shifted(hi, "mode", -1)
     snap, plus, minus, across = snapshots(
         velocity,
         levels,
@@ -725,21 +755,21 @@
         basis,
         (zlo, zhi, face_lo, face_hi, velocity, xlo, xhi),
     )
-    stack = (snap, blocks[0], hi, over, lo)
+    stack = (snap, block_own, hi, hi_tail, over, lo, lo_tail)
     total = gram(here, stack)
     total = ring_sum(total, ring_parts(total, "space", n_space, 1, 2))
     total = ring_sum(total, ring_parts(total, "mode", n_mode, 1, n_mode))
     total = ring_sum(total, ring_parts(total, "space", n_space, 2, 4))
     lo_early = shifted(plus, "mode", 1)
     hi_early = shifted(minus, "mode", -1)
+    parts = [total] + ring_parts(total, "space", n_space, 8, 4)
     over_early = shifted(across, "mode", 2)
-    parts = [total] + ring_parts(total, "space", n_space, 8, 4)
     mix, sigma = factor(parts)
     out_own, out_next, out_over, out_prev = update(here, mix, stack)
     back_lo = shifted(out_next, "mode", 1)
     back_hi = shifted(out_prev, "mode", -1)
     back_over = shifted(out_over, "mode", 2)
-    mine = own(here, mix, stack, (hi_early, over_early, lo_early), basis)
+    mine = own(here, mix, stack, (hi_early, over_early, lo_early, hi_far, lo_far), basis)
     modes = join(here, (out_own, back_hi, back_over, back_lo), mine)
     return (modes, sigma[0, :MODES])
 

time: 125 us -> 122 us (0.976)
  waiting for transfers between devices: 50.3 us -> 40.7 us
  starting transfers between devices: 35.1 us -> 41.3 us
    ppermute x13 -> x17, waiting for transfers between devices: 37.2 us -> 30.9 us  [shifted(): return lax.ppermute(x, axis, [(i, (i + by) % size) for i in range(size)])]
    ppermute x13 -> x17, starting transfers between devices: 22.8 us -> 27.5 us  [shifted(): return lax.ppermute(x, axis, [(i, (i + by) % size) for i in range(size)])]
    ppermute x10, waiting for transfers between devices: 13.1 us -> 9.79 us  [ring_parts(): lax.ppermute(x, axis, pairs)]
    ppermute x10, starting transfers between devices: 12.3 us -> 13.7 us  [ring_parts(): lax.ppermute(x, axis, pairs)]
  transfers between devices with their start and end apart: 23 -> 27, of which waited for: 14 -> 13; matrix products, arithmetic and copies ran while one was open for 0% -> 0% of each run, Pallas kernels for 27% -> 26%
where the time goes in v4:
time: 122 us; the launch traced here: 121 us
  starting transfers between devices  41.3 us (34%)
  waiting for transfers between devices  40.7 us (33%)
  Pallas kernels  37.7 us (31%)
    ppermute x17, waiting for transfers between devices, shifted(): return lax.ppermute(x, axis, [(i, (i + by) % size) for i in range(size)])  30.9 us
    ppermute x17, starting transfers between devices, shifted(): return lax.ppermute(x, axis, [(i, (i + by) % size) for i in range(size)])  27.5 us
    pallas_call x1, Pallas kernels, snapshots(): pl.pallas_call(stencil_kernel, grid=(comps,), in_specs=[SMEM_SPEC, pl.Blo...  18.9 us
    ppermute x10, starting transfers between devices, ring_parts(): lax.ppermute(x, axis, pairs)  13.7 us
    ppermute x10, waiting for transfers between devices, ring_parts(): lax.ppermute(x, axis, pairs)  9.79 us
    pallas_call x1, Pallas kernels, factor(): pl.pallas_call(factor_kernel, in_specs=[VMEM_SPEC] * 7, out_specs=(VMEM_S...  9.42 us
    pallas_call x1, Pallas kernels, pack(): pl.pallas_call(pack_kernel, in_specs=[SMEM_SPEC, HBM_SPEC, HBM_SPEC], out...  2.9 us
    pallas_call x1, Pallas kernels, own(): pl.pallas_call(functools.partial(own_kernel, cols=cols, chunk=chunk), in_...  2.82 us
  transfers between devices with their start and end apart: 27, of which 13 were waited for; matrix products, arithmetic and copies ran while one was open for 0% of the time, Pallas kernels for 26%

profile of v4, /device:TPU:0, one launch (start us, length us, event | category | flops | bytes accessed | tf_op | source)
XLA Modules:
  0.0 121.2 jit_solution(15771049942364536254)
XLA Ops:
  0.6 0.0 copy-start
  0.7 2.9 %pack.1 = (f32[96,256]{1,0:T(8,128)S(1)}, f32[96,256]{1,0:T(8,128)S(1)}, f32[776,256]{1,0:T(8,128)S(1)}, f32[776,256]{1,0:T(8,128)S(1)}, f32[8,24576]{1,0:T(8,12...) custom-call(s32[1]{0:T(128)} %bitcast.here_ref, ...), custom_call_target="tpu_custom_call" | custom-call | tf_op jit(solution)/shard_map/pack/pallas_call | solution.py:119
  3.6 1.7 %collective-permute-start = (f32[96,256]{1,0:T(8,128)S(1)}, f32[96,256]{1,0:T(8,128)S(1)}, u32[]{:S(2)}, u32[]{:S(2)}) collective-permute-start(f32[96,256]{1,0:T(8,128)S(1)} %get-tuple-element.24.face_hi_ref), channel_id=1, source_target_pairs={{0,1},{1,2},{2,3},{3,0},{4,5},{5,6},{6,7},{7,4},{8,9},{9,10},{10,1... | collective-permute-start | bytes 294920 | tf_op jit(solution)/shard_map/ppermute | solution.py:733
  5.3 1.6 %collective-permute-start.1 = (f32[96,256]{1,0:T(8,128)S(1)}, f32[96,256]{1,0:T(8,128)S(1)}, u32[]{:S(2)}, u32[]{:S(2)}) collective-permute-start(f32[96,256]{1,0:T(8,128)S(1)} %get-tuple-element.25.face_lo_ref), channel_id=1, source_target_pairs={{0,3},{1,0},{2,1},{3,2},{4,7},{5,4},{6,5},{7,6},{8,11},{9,8},{10,9... | collective-permute-start | bytes 294920 | tf_op jit(solution)/shard_map/ppermute | solution.py:733
  6.9 2.6 %collective-permute-done.zlo_ref = f32[96,256]{1,0:T(8,128)S(1)} collective-permute-done((f32[96,256]{1,0:T(8,128)S(1)}, f32[96,256]{1,0:T(8,128)S(1)}, u32[]{:S(2)}, u32[]{:S(2)}) %collective-permute-start) | collective-permute-done | bytes 98336 | tf_op jit(solution)/shard_map/ppermute | solution.py:733
  9.5 0.4 collective-permute-done.1.zhi_ref
  9.9 0.1 collective-permute-start.2
  10.0 5.1 %collective-permute-start.3 = (f32[776,256]{1,0:T(8,128)S(1)}, f32[776,256]{1,0:T(8,128)S(1)}, u32[]{:S(2)}, u32[]{:S(2)}) collective-permute-start(f32[776,256]{1,0:T(8,128)S(1)} %get-tuple-element.29), channel_id=1, source_target_pairs={{0,124},{4,0},{8,4},{12,8},{16,12},{20,16},{24,20},{28,24},{32,28}... | collective-permute-start | bytes 2383880 | tf_op jit(solution)/shard_map/ppermute | solution.py:733
  15.0 2.7 %collective-permute-start.6 = (f32[8,24576]{1,0:T(8,128)S(1)}, f32[8,24576]{1,0:T(8,128)S(1)}, u32[]{:S(2)}, u32[]{:S(2)}) collective-permute-start(f32[8,24576]{1,0:T(8,128)S(1)} %get-tuple-element.34), channel_id=1, source_target_pairs={{0,2},{1,3},{2,0},{3,1},{4,6},{5,7},{6,4},{7,5},{8,10},{9,11},{10,... | collective-permute-start | bytes 2359304 | tf_op jit(solution)/shard_map/ppermute | solution.py:733
  17.8 1.4 %collective-permute-start.5 = (f32[8,18432]{1,0:T(8,128)S(1)}, f32[8,18432]{1,0:T(8,128)S(1)}, u32[]{:S(2)}, u32[]{:S(2)}) collective-permute-start(f32[8,18432]{1,0:T(8,128)S(1)} %get-tuple-element.33), channel_id=1, source_target_pairs={{0,3},{1,0},{2,1},{3,2},{4,7},{5,4},{6,5},{7,6},{8,11},{9,8},{10,9... | collective-permute-start | bytes 1769480 | tf_op jit(solution)/shard_map/ppermute | solution.py:733
  19.2 0.6 collective-permute-start.8
  19.8 5.0 %collective-permute-done.2.xlo_ref = f32[776,256]{1,0:T(8,128)S(1)} collective-permute-done((f32[776,256]{1,0:T(8,128)S(1)}, f32[776,256]{1,0:T(8,128)S(1)}, u32[]{:S(2)}, u32[]{:S(2)}) %collective-permute-start.2) | collective-permute-done | bytes 794656 | tf_op jit(solution)/shard_map/ppermute | solution.py:733
  24.8 2.8 %collective-permute-start.4 = (f32[8,6144]{1,0:T(8,128)S(1)}, f32[8,6144]{1,0:T(8,128)S(1)}, u32[]{:S(2)}, u32[]{:S(2)}) collective-permute-start(f32[8,6144]{1,0:T(8,128)S(1)} %get-tuple-element.32), channel_id=1, source_target_pairs={{0,3},{1,0},{2,1},{3,2},{4,7},{5,4},{6,5},{7,6},{8,11},{9,8},{10,9... | collective-permute-start | bytes 589832 | tf_op jit(solution)/shard_map/ppermute | solution.py:733
  27.6 0.0 collective-permute-done.3.xhi_ref
  27.6 0.0 collective-permute-start.7
  27.7 18.9 %stencil.1 = (f32[8,24576]{1,0:T(8,128)S(1)}, f32[8,19968]{1,0:T(8,128)S(1)}, f32[8,19968]{1,0:T(8,128)S(1)}, f32[8,7680]{1,0:T(8,128)S(1)}) custom-call(f32[8]{0:T(128)S(1)} %copy-done.5, s32[1,256]{1,0:T(1,128)S(1)} %bitcast.5, f32[1,256]{1,0:T(1,128)S(1)} %bitcast.6, bf16[256,128]{1,0:T(8,128)(2,1)S(1)} %copy-done, ...), custom_call_target="tpu_custom_call" | custom-call | tf_op jit(solution)/shard_map/stencil/pallas_call | solution.py:393
  46.6 0.0 copy-start.1
  46.6 0.0 copy-start.2
  46.6 0.0 copy-start.6
  46.7 3.1 %collective-permute-done.4.refs_2_ = f32[8,6144]{1,0:T(8,128)S(1)} collective-permute-done((f32[8,6144]{1,0:T(8,128)S(1)}, f32[8,6144]{1,0:T(8,128)S(1)}, u32[]{:S(2)}, u32[]{:S(2)}) %collective-permute-start.4) | collective-permute-done | bytes 196640 | tf_op jit(solution)/shard_map/ppermute | solution.py:733
  49.8 0.0 collective-permute-done.7.refs_5_
  49.8 0.0 collective-permute-done.5.refs_3_
  49.8 0.0 collective-permute-done.8.refs_6_
  49.8 0.0 collective-permute-done.6.refs_4_
  49.8 1.4 %gram.1 = f32[40,128]{1,0:T(8,128)S(1)} custom-call(s32[1]{0:T(128)} %bitcast.here_ref, f32[8,24576]{1,0:T(8,128)S(1)} %get-tuple-element.30.refs_0_, f32[8,24576]{1,0:T(8,128)S(1)} %get-tuple-element.31.refs_1_, f32[8,6144]{1,0:T(8,128)S(1)} %collective-permute-done.4.refs_2_, f32[8,18432]{1,0:T(8,128)S(1)} %collective-permute-done.5.refs_3_, ...), custom_call_target="tpu_custom_call" | custom-call | tf_op jit(solution)/shard_map/gram/pallas_call | solution.py:475
  51.2 0.0 collective-permute-start.9
  51.2 1.2 collective-permute-done.9
  52.4 2.6 %collective-permute-start.12 = (f32[40,128]{1,0:T(8,128)S(1)}, f32[40,128]{1,0:T(8,128)S(1)}, u32[]{:S(2)}, u32[]{:S(2)}) collective-permute-start(f32[40,128]{1,0:T(8,128)S(1)} %add.21), channel_id=1, source_target_pairs={{0,3},{1,0},{2,1},{3,2},{4,7},{5,4},{6,5},{7,6},{8,11},{9,8},{10,9... | collective-permute-start | bytes 61448 | tf_op jit(solution)/shard_map/ppermute | solution.py:497
  55.0 0.0 collective-permute-start.11
  55.0 1.8 %collective-permute-start.10 = (f32[40,128]{1,0:T(8,128)S(1)}, f32[40,128]{1,0:T(8,128)S(1)}, u32[]{:S(2)}, u32[]{:S(2)}) collective-permute-start(f32[40,128]{1,0:T(8,128)S(1)} %add.21), channel_id=1, source_target_pairs={{0,2},{1,3},{2,0},{3,1},{4,6},{5,7},{6,4},{7,5},{8,10},{9,11},{10,... | collective-permute-start | bytes 61448 | tf_op jit(solution)/shard_map/ppermute | solution.py:497
  56.8 0.0 collective-permute-done.12
  56.8 3.2 %collective-permute-done.11 = f32[40,128]{1,0:T(8,128)S(1)} collective-permute-done((f32[40,128]{1,0:T(8,128)S(1)}, f32[40,128]{1,0:T(8,128)S(1)}, u32[]{:S(2)}, u32[]{:S(2)}) %collective-permute-start.11) | collective-permute-done | bytes 20512 | tf_op jit(solution)/shard_map/ppermute | solution.py:497
  60.0 0.3 collective-permute-done.10
  60.3 3.1 %collective-permute-start.15 = (f32[40,128]{1,0:T(8,128)S(1)}, f32[40,128]{1,0:T(8,128)S(1)}, u32[]{:S(2)}, u32[]{:S(2)}) collective-permute-start(f32[40,128]{1,0:T(8,128)S(1)} %add_add_fusion.1), channel_id=1, source_target_pairs={{0,24},{4,28},{8,0},{12,4},{16,8},{20,12},{24,16},{28,20},{32,56},... | collective-permute-start | bytes 61448 | tf_op jit(solution)/shard_map/ppermute | solution.py:497
  63.4 0.0 collective-permute-start.14
  63.4 1.9 %collective-permute-start.13 = (f32[40,128]{1,0:T(8,128)S(1)}, f32[40,128]{1,0:T(8,128)S(1)}, u32[]{:S(2)}, u32[]{:S(2)}) collective-permute-start(f32[40,128]{1,0:T(8,128)S(1)} %add_add_fusion.1), channel_id=1, source_target_pairs={{0,16},{4,20},{8,24},{12,28},{16,0},{20,4},{24,8},{28,12},{32,48},... | collective-permute-start | bytes 61448 | tf_op jit(solution)/shard_map/ppermute | solution.py:497
  65.3 3.2 %collective-permute-start.25 = (f32[8,6144]{1,0:T(8,128)S(1)}, f32[8,6144]{1,0:T(8,128)S(1)}, u32[]{:S(2)}, u32[]{:S(2)}) collective-permute-start(f32[8,6144]{1,0:T(8,128)S(1)} %collective-permute-done.4.refs_2_), channel_id=1, source_target_pairs={{0,3},{1,0},{2,1},{3,2},{4,7},{5,4},{6,5},{7,6},{8,11},{9,8},{10,9... | collective-permute-start | bytes 589832 | tf_op jit(solution)/shard_map/ppermute | solution.py:733
  68.6 0.0 collective-permute-start.26
  68.6 0.0 collective-permute-done.15
  68.6 1.5 %collective-permute-start.23 = (f32[8,7680]{1,0:T(8,128)S(1)}, f32[8,7680]{1,0:T(8,128)S(1)}, u32[]{:S(2)}, u32[]{:S(2)}) collective-permute-start(f32[8,7680]{1,0:T(8,128)S(1)} %get-tuple-element.43), channel_id=1, source_target_pairs={{0,2},{1,3},{2,0},{3,1},{4,6},{5,7},{6,4},{7,5},{8,10},{9,11},{10,... | collective-permute-start | bytes 737288 | tf_op jit(solution)/shard_map/ppermute | solution.py:733
  70.0 0.0 collective-permute-done.14
  70.0 0.0 collective-permute-done.13
  70.0 4.1 %collective-permute-start.18 = (f32[40,128]{1,0:T(8,128)S(1)}, f32[40,128]{1,0:T(8,128)S(1)}, u32[]{:S(2)}, u32[]{:S(2)}) collective-permute-start(f32[40,128]{1,0:T(8,128)S(1)} %add_add_fusion.g0_ref), channel_id=1, source_target_pairs={{0,96},{4,100},{8,104},{12,108},{16,112},{20,116},{24,120},{28,124... | collective-permute-start | bytes 61448 | tf_op jit(solution)/shard_map/ppermute | solution.py:497
  74.2 0.0 collective-permute-start.17
  74.2 1.5 %collective-permute-done.18.g3_ref = f32[40,128]{1,0:T(8,128)S(1)} collective-permute-done((f32[40,128]{1,0:T(8,128)S(1)}, f32[40,128]{1,0:T(8,128)S(1)}, u32[]{:S(2)}, u32[]{:S(2)}) %collective-permute-start.18) | collective-permute-done | bytes 20512 | tf_op jit(solution)/shard_map/ppermute | solution.py:497
  75.6 0.2 collective-permute-start.16
  75.8 3.6 %collective-permute-done.17.g2_ref = f32[40,128]{1,0:T(8,128)S(1)} collective-permute-done((f32[40,128]{1,0:T(8,128)S(1)}, f32[40,128]{1,0:T(8,128)S(1)}, u32[]{:S(2)}, u32[]{:S(2)}) %collective-permute-start.17) | collective-permute-done | bytes 20512 | tf_op jit(solution)/shard_map/ppermute | solution.py:497
  79.4 1.8 %collective-permute-start.22 = (f32[8,19968]{1,0:T(8,128)S(1)}, f32[8,19968]{1,0:T(8,128)S(1)}, u32[]{:S(2)}, u32[]{:S(2)}) collective-permute-start(f32[8,19968]{1,0:T(8,128)S(1)} %get-tuple-element.42), channel_id=1, source_target_pairs={{0,3},{1,0},{2,1},{3,2},{4,7},{5,4},{6,5},{7,6},{8,11},{9,8},{10,9... | collective-permute-start | bytes 1916936 | tf_op jit(solution)/shard_map/ppermute | solution.py:733
  81.2 0.0 collective-permute-done.16.g1_ref
  81.2 2.3 %collective-permute-start.24 = (f32[8,19968]{1,0:T(8,128)S(1)}, f32[8,19968]{1,0:T(8,128)S(1)}, u32[]{:S(2)}, u32[]{:S(2)}) collective-permute-start(f32[8,19968]{1,0:T(8,128)S(1)} %get-tuple-element.44), channel_id=1, source_target_pairs={{0,1},{1,2},{2,3},{3,0},{4,5},{5,6},{6,7},{7,4},{8,9},{9,10},{10,1... | collective-permute-start | bytes 1916936 | tf_op jit(solution)/shard_map/ppermute | solution.py:733
  83.5 9.4 %factor.1 = (f32[32,128]{1,0:T(8,128)S(1)}, f32[8,128]{1,0:T(8,128)S(1)}) custom-call(f32[40,128]{1,0:T(8,128)S(1)} %add_add_fusion.g0_ref, f32[40,128]{1,0:T(8,128)S(1)} %collective-permute-done.16.g1_ref, f32[40,128]{1,0:T(8,128)S(1)} %collective-permute-done.17.g2_ref, f32[40,128]{1,0:T(8,128)S(1)} %collective-permute-done.18.g3_ref, ...), custom_call_target="tpu_custom_call" | custom-call | tf_op jit(solution)/shard_map/factor/pallas_call | solution.py:582
  93.0 0.8 update.1
  93.8 0.0 collective-permute-done.25.refs_10_
  93.8 1.0 collective-permute-start.19
  94.8 0.0 collective-permute-done.26.refs_11_
  94.8 1.7 %collective-permute-start.20 = (f32[8,18432]{1,0:T(8,128)S(1)}, f32[8,18432]{1,0:T(8,128)S(1)}, u32[]{:S(2)}, u32[]{:S(2)}) collective-permute-start(f32[8,18432]{1,0:T(8,128)S(1)} %get-tuple-element.40), channel_id=1, source_target_pairs={{0,2},{1,3},{2,0},{3,1},{4,6},{5,7},{6,4},{7,5},{8,10},{9,11},{10,... | collective-permute-start | bytes 1769480 | tf_op jit(solution)/shard_map/ppermute | solution.py:733
  96.5 0.0 collective-permute-done.23.refs_8_
  96.5 0.5 slice_bitcast_fusion
  97.0 5.0 %collective-permute-done.24.refs_9_ = f32[8,19968]{1,0:T(8,128)S(1)} collective-permute-done((f32[8,19968]{1,0:T(8,128)S(1)}, f32[8,19968]{1,0:T(8,128)S(1)}, u32[]{:S(2)}, u32[]{:S(2)}) %collective-permute-start.24) | collective-permute-done | bytes 639008 | tf_op jit(solution)/shard_map/ppermute | solution.py:733
  102.0 2.8 %own.1.refs_4_ = f32[8,98304]{1,0:T(8,128)} custom-call(s32[1]{0:T(128)} %bitcast.here_ref, f32[32,128]{1,0:T(8,128)S(1)} %get-tuple-element.37.mix_ref, f32[8,24576]{1,0:T(8,128)S(1)} %get-tuple-element.30.refs_0_, f32[8,24576]{1,0:T(8,128)S(1)} %get-tuple-element.31.refs_1_, f32[8,6144]{1,0:T(8,128)S(1)} %collective-permute-done.4.refs_2_, ...), custom_call_target="tpu_custom_call" | custom-call | tf_op jit(solution)/shard_map/own/pallas_call | solution.py:683
  104.9 5.2 %collective-permute-done.19.refs_1_ = f32[8,18432]{1,0:T(8,128)S(1)} collective-permute-done((f32[8,18432]{1,0:T(8,128)S(1)}, f32[8,18432]{1,0:T(8,128)S(1)}, u32[]{:S(2)}, u32[]{:S(2)}) %collective-permute-start.19) | collective-permute-done | bytes 589856 | tf_op jit(solution)/shard_map/ppermute | solution.py:733
  110.1 2.4 %collective-permute-done.20.refs_2_ = f32[8,18432]{1,0:T(8,128)S(1)} collective-permute-done((f32[8,18432]{1,0:T(8,128)S(1)}, f32[8,18432]{1,0:T(8,128)S(1)}, u32[]{:S(2)}, u32[]{:S(2)}) %collective-permute-start.20) | collective-permute-done | bytes 589856 | tf_op jit(solution)/shard_map/ppermute | solution.py:733
  112.5 7.1 %collective-permute-done.21.refs_3_ = f32[8,18432]{1,0:T(8,128)S(1)} collective-permute-done((f32[8,18432]{1,0:T(8,128)S(1)}, f32[8,18432]{1,0:T(8,128)S(1)}, u32[]{:S(2)}, u32[]{:S(2)}) %collective-permute-start.21) | collective-permute-done | bytes 589856 | tf_op jit(solution)/shard_map/ppermute | solution.py:733
  119.6 1.4 %join.1 = f32[8,98304]{1,0:T(8,128)} custom-call(s32[1]{0:T(128)} %bitcast.here_ref, f32[8,18432]{1,0:T(8,128)S(1)} %get-tuple-element.38.refs_0_, f32[8,18432]{1,0:T(8,128)S(1)} %collective-permute-done.19.refs_1_, f32[8,18432]{1,0:T(8,128)S(1)} %collective-permute-done.20.refs_2_, ...), custom_call_target="tpu_custom_call", output_to_operand_aliasing={{}: (5, {})} | custom-call | tf_op jit(solution)/shard_map/join/pallas_call | solution.py:714
  (16 shorter events, 0.1 us)
Async XLA Ops:
  0.6 27.0 %copy-start = (bf16[256,128]{1,0:T(8,128)(2,1)S(1)}, bf16[256,128]{1,0:T(8,128)(2,1)}, u32[]{:S(2)}) copy-start(bf16[256,128]{1,0:T(8,128)(2,1)} %constant.12.clone.sum_ref) | copy-start | bytes 196612
  0.6 27.0 %copy-start.3 = (s32[256]{0:T(256)S(1)}, s32[256]{0:T(256)}, u32[]{:S(2)}) copy-start(s32[256]{0:T(256)} %param.12) | copy-start | bytes 3076
  0.7 27.0 %copy-start.4 = (f32[256]{0:T(256)S(1)}, f32[256]{0:T(256)}, u32[]{:S(2)}) copy-start(f32[256]{0:T(256)} %param.13) | copy-start | bytes 3076
  0.7 27.0 %copy-start.5 = (f32[8]{0:T(128)S(1)}, f32[8]{0:T(128)}, u32[]{:S(2)}) copy-start(f32[8]{0:T(128)} %levels_ref.1) | copy-start | bytes 100
  3.6 5.9 %collective-permute-start = (f32[96,256]{1,0:T(8,128)S(1)}, f32[96,256]{1,0:T(8,128)S(1)}, u32[]{:S(2)}, u32[]{:S(2)}) collective-permute-start(f32[96,256]{1,0:T(8,128)S(1)} %get-tuple-element.24.face_hi_ref), channel_id=1, source_target_pairs={{0,1},{1,2},{2,3},{3,0},{4,5},{5,6},{6,7},{7,4},{8,9},{9,10},{10,1... | collective-permute-start | bytes 294920 | tf_op jit(solution)/shard_map/ppermute | solution.py:733
  5.3 4.6 %collective-permute-start.1 = (f32[96,256]{1,0:T(8,128)S(1)}, f32[96,256]{1,0:T(8,128)S(1)}, u32[]{:S(2)}, u32[]{:S(2)}) collective-permute-start(f32[96,256]{1,0:T(8,128)S(1)} %get-tuple-element.25.face_lo_ref), channel_id=1, source_target_pairs={{0,3},{1,0},{2,1},{3,2},{4,7},{5,4},{6,5},{7,6},{8,11},{9,8},{10,9... | collective-permute-start | bytes 294920 | tf_op jit(solution)/shard_map/ppermute | solution.py:733
  9.9 14.9 %collective-permute-start.2 = (f32[776,256]{1,0:T(8,128)S(1)}, f32[776,256]{1,0:T(8,128)S(1)}, u32[]{:S(2)}, u32[]{:S(2)}) collective-permute-start(f32[776,256]{1,0:T(8,128)S(1)} %get-tuple-element.28), channel_id=1, source_target_pairs={{0,4},{4,8},{8,12},{12,16},{16,20},{20,24},{24,28},{28,32},{32,36}... | collective-permute-start | bytes 2383880 | tf_op jit(solution)/shard_map/ppermute | solution.py:733
  10.0 17.7 %collective-permute-start.3 = (f32[776,256]{1,0:T(8,128)S(1)}, f32[776,256]{1,0:T(8,128)S(1)}, u32[]{:S(2)}, u32[]{:S(2)}) collective-permute-start(f32[776,256]{1,0:T(8,128)S(1)} %get-tuple-element.29), channel_id=1, source_target_pairs={{0,124},{4,0},{8,4},{12,8},{16,12},{20,16},{24,20},{28,24},{32,28}... | collective-permute-start | bytes 2383880 | tf_op jit(solution)/shard_map/ppermute | solution.py:733
  15.0 34.8 %collective-permute-start.6 = (f32[8,24576]{1,0:T(8,128)S(1)}, f32[8,24576]{1,0:T(8,128)S(1)}, u32[]{:S(2)}, u32[]{:S(2)}) collective-permute-start(f32[8,24576]{1,0:T(8,128)S(1)} %get-tuple-element.34), channel_id=1, source_target_pairs={{0,2},{1,3},{2,0},{3,1},{4,6},{5,7},{6,4},{7,5},{8,10},{9,11},{10,... | collective-permute-start | bytes 2359304 | tf_op jit(solution)/shard_map/ppermute | solution.py:733
  17.8 32.0 %collective-permute-start.5 = (f32[8,18432]{1,0:T(8,128)S(1)}, f32[8,18432]{1,0:T(8,128)S(1)}, u32[]{:S(2)}, u32[]{:S(2)}) collective-permute-start(f32[8,18432]{1,0:T(8,128)S(1)} %get-tuple-element.33), channel_id=1, source_target_pairs={{0,3},{1,0},{2,1},{3,2},{4,7},{5,4},{6,5},{7,6},{8,11},{9,8},{10,9... | collective-permute-start | bytes 1769480 | tf_op jit(solution)/shard_map/ppermute | solution.py:733
  19.2 30.6 %collective-permute-start.8 = (f32[8,18432]{1,0:T(8,128)S(1)}, f32[8,18432]{1,0:T(8,128)S(1)}, u32[]{:S(2)}, u32[]{:S(2)}) collective-permute-start(f32[8,18432]{1,0:T(8,128)S(1)} %get-tuple-element.36), channel_id=1, source_target_pairs={{0,1},{1,2},{2,3},{3,0},{4,5},{5,6},{6,7},{7,4},{8,9},{9,10},{10,1... | collective-permute-start | bytes 1769480 | tf_op jit(solution)/shard_map/ppermute | solution.py:733
  24.8 25.0 %collective-permute-start.4 = (f32[8,6144]{1,0:T(8,128)S(1)}, f32[8,6144]{1,0:T(8,128)S(1)}, u32[]{:S(2)}, u32[]{:S(2)}) collective-permute-start(f32[8,6144]{1,0:T(8,128)S(1)} %get-tuple-element.32), channel_id=1, source_target_pairs={{0,3},{1,0},{2,1},{3,2},{4,7},{5,4},{6,5},{7,6},{8,11},{9,8},{10,9... | collective-permute-start | bytes 589832 | tf_op jit(solution)/shard_map/ppermute | solution.py:733
  27.6 22.2 %collective-permute-start.7 = (f32[8,6144]{1,0:T(8,128)S(1)}, f32[8,6144]{1,0:T(8,128)S(1)}, u32[]{:S(2)}, u32[]{:S(2)}) collective-permute-start(f32[8,6144]{1,0:T(8,128)S(1)} %get-tuple-element.35), channel_id=1, source_target_pairs={{0,1},{1,2},{2,3},{3,0},{4,5},{5,6},{6,7},{7,4},{8,9},{9,10},{10,1... | collective-permute-start | bytes 589832 | tf_op jit(solution)/shard_map/ppermute | solution.py:733
  46.6 36.9 %copy-start.1 = (f32[40,128]{1,0:T(8,128)S(1)}, f32[40,128]{1,0:T(8,128)}, u32[]{:S(2)}) copy-start(f32[40,128]{1,0:T(8,128)} %constant.14.clone.orient_ref) | copy-start | bytes 61444
  46.6 36.9 %copy-start.2 = (s32[40,128]{1,0:T(8,128)S(1)}, s32[40,128]{1,0:T(8,128)}, u32[]{:S(2)}) copy-start(s32[40,128]{1,0:T(8,128)} %constant.13.clone.partner_ref) | copy-start | bytes 61444
  46.6 36.9 %copy-start.6 = (s32[1,128]{1,0:T(1,128)S(1)}, s32[1,128]{1,0:T(1,128)}, u32[]{:S(2)}) copy-start(s32[1,128]{1,0:T(1,128)} %constant.15.clone.keep_ref) | copy-start | bytes 1540
  51.2 1.2 %collective-permute-start.9 = (f32[40,128]{1,0:T(8,128)S(1)}, f32[40,128]{1,0:T(8,128)S(1)}, u32[]{:S(2)}, u32[]{:S(2)}) collective-permute-start(f32[40,128]{1,0:T(8,128)S(1)} %gram.1), channel_id=1, source_target_pairs={{0,4},{4,0},{8,12},{12,8},{16,20},{20,16},{24,28},{28,24},{32,36},... | collective-permute-start | bytes 61448 | tf_op jit(solution)/shard_map/ppermute | solution.py:497
  52.4 4.4 %collective-permute-start.12 = (f32[40,128]{1,0:T(8,128)S(1)}, f32[40,128]{1,0:T(8,128)S(1)}, u32[]{:S(2)}, u32[]{:S(2)}) collective-permute-start(f32[40,128]{1,0:T(8,128)S(1)} %add.21), channel_id=1, source_target_pairs={{0,3},{1,0},{2,1},{3,2},{4,7},{5,4},{6,5},{7,6},{8,11},{9,8},{10,9... | collective-permute-start | bytes 61448 | tf_op jit(solution)/shard_map/ppermute | solution.py:497
  55.0 5.0 %collective-permute-start.11 = (f32[40,128]{1,0:T(8,128)S(1)}, f32[40,128]{1,0:T(8,128)S(1)}, u32[]{:S(2)}, u32[]{:S(2)}) collective-permute-start(f32[40,128]{1,0:T(8,128)S(1)} %add.21), channel_id=1, source_target_pairs={{0,1},{1,2},{2,3},{3,0},{4,5},{5,6},{6,7},{7,4},{8,9},{9,10},{10,1... | collective-permute-start | bytes 61448 | tf_op jit(solution)/shard_map/ppermute | solution.py:497
  55.0 5.3 %collective-permute-start.10 = (f32[40,128]{1,0:T(8,128)S(1)}, f32[40,128]{1,0:T(8,128)S(1)}, u32[]{:S(2)}, u32[]{:S(2)}) collective-permute-start(f32[40,128]{1,0:T(8,128)S(1)} %add.21), channel_id=1, source_target_pairs={{0,2},{1,3},{2,0},{3,1},{4,6},{5,7},{6,4},{7,5},{8,10},{9,11},{10,... | collective-permute-start | bytes 61448 | tf_op jit(solution)/shard_map/ppermute | solution.py:497
  60.3 8.2 %collective-permute-start.15 = (f32[40,128]{1,0:T(8,128)S(1)}, f32[40,128]{1,0:T(8,128)S(1)}, u32[]{:S(2)}, u32[]{:S(2)}) collective-permute-start(f32[40,128]{1,0:T(8,128)S(1)} %add_add_fusion.1), channel_id=1, source_target_pairs={{0,24},{4,28},{8,0},{12,4},{16,8},{20,12},{24,16},{28,20},{32,56},... | collective-permute-start | bytes 61448 | tf_op jit(solution)/shard_map/ppermute | solution.py:497
  63.4 6.6 %collective-permute-start.14 = (f32[40,128]{1,0:T(8,128)S(1)}, f32[40,128]{1,0:T(8,128)S(1)}, u32[]{:S(2)}, u32[]{:S(2)}) collective-permute-start(f32[40,128]{1,0:T(8,128)S(1)} %add_add_fusion.1), channel_id=1, source_target_pairs={{0,8},{4,12},{8,16},{12,20},{16,24},{20,28},{24,0},{28,4},{32,40},... | collective-permute-start | bytes 61448 | tf_op jit(solution)/shard_map/ppermute | solution.py:497
  63.4 6.6 %collective-permute-start.13 = (f32[40,128]{1,0:T(8,128)S(1)}, f32[40,128]{1,0:T(8,128)S(1)}, u32[]{:S(2)}, u32[]{:S(2)}) collective-permute-start(f32[40,128]{1,0:T(8,128)S(1)} %add_add_fusion.1), channel_id=1, source_target_pairs={{0,16},{4,20},{8,24},{12,28},{16,0},{20,4},{24,8},{28,12},{32,48},... | collective-permute-start | bytes 61448 | tf_op jit(solution)/shard_map/ppermute | solution.py:497
  65.3 28.5 %collective-permute-start.25 = (f32[8,6144]{1,0:T(8,128)S(1)}, f32[8,6144]{1,0:T(8,128)S(1)}, u32[]{:S(2)}, u32[]{:S(2)}) collective-permute-start(f32[8,6144]{1,0:T(8,128)S(1)} %collective-permute-done.4.refs_2_), channel_id=1, source_target_pairs={{0,3},{1,0},{2,1},{3,2},{4,7},{5,4},{6,5},{7,6},{8,11},{9,8},{10,9... | collective-permute-start | bytes 589832 | tf_op jit(solution)/shard_map/ppermute | solution.py:733
  68.6 26.3 %collective-permute-start.26 = (f32[8,6144]{1,0:T(8,128)S(1)}, f32[8,6144]{1,0:T(8,128)S(1)}, u32[]{:S(2)}, u32[]{:S(2)}) collective-permute-start(f32[8,6144]{1,0:T(8,128)S(1)} %collective-permute-done.7.refs_5_), channel_id=1, source_target_pairs={{0,1},{1,2},{2,3},{3,0},{4,5},{5,6},{6,7},{7,4},{8,9},{9,10},{10,1... | collective-permute-start | bytes 589832 | tf_op jit(solution)/shard_map/ppermute | solution.py:733
  68.6 28.0 %collective-permute-start.23 = (f32[8,7680]{1,0:T(8,128)S(1)}, f32[8,7680]{1,0:T(8,128)S(1)}, u32[]{:S(2)}, u32[]{:S(2)}) collective-permute-start(f32[8,7680]{1,0:T(8,128)S(1)} %get-tuple-element.43), channel_id=1, source_target_pairs={{0,2},{1,3},{2,0},{3,1},{4,6},{5,7},{6,4},{7,5},{8,10},{9,11},{10,... | collective-permute-start | bytes 737288 | tf_op jit(solution)/shard_map/ppermute | solution.py:733
  70.0 5.6 %collective-permute-start.18 = (f32[40,128]{1,0:T(8,128)S(1)}, f32[40,128]{1,0:T(8,128)S(1)}, u32[]{:S(2)}, u32[]{:S(2)}) collective-permute-start(f32[40,128]{1,0:T(8,128)S(1)} %add_add_fusion.g0_ref), channel_id=1, source_target_pairs={{0,96},{4,100},{8,104},{12,108},{16,112},{20,116},{24,120},{28,124... | collective-permute-start | bytes 61448 | tf_op jit(solution)/shard_map/ppermute | solution.py:497
  74.2 5.3 %collective-permute-start.17 = (f32[40,128]{1,0:T(8,128)S(1)}, f32[40,128]{1,0:T(8,128)S(1)}, u32[]{:S(2)}, u32[]{:S(2)}) collective-permute-start(f32[40,128]{1,0:T(8,128)S(1)} %add_add_fusion.g0_ref), channel_id=1, source_target_pairs={{0,64},{4,68},{8,72},{12,76},{16,80},{20,84},{24,88},{28,92},{32,9... | collective-permute-start | bytes 61448 | tf_op jit(solution)/shard_map/ppermute | solution.py:497
  75.6 5.6 %collective-permute-start.16 = (f32[40,128]{1,0:T(8,128)S(1)}, f32[40,128]{1,0:T(8,128)S(1)}, u32[]{:S(2)}, u32[]{:S(2)}) collective-permute-start(f32[40,128]{1,0:T(8,128)S(1)} %add_add_fusion.g0_ref), channel_id=1, source_target_pairs={{0,32},{4,36},{8,40},{12,44},{16,48},{20,52},{24,56},{28,60},{32,6... | collective-permute-start | bytes 61448 | tf_op jit(solution)/shard_map/ppermute | solution.py:497
  79.4 17.6 %collective-permute-start.22 = (f32[8,19968]{1,0:T(8,128)S(1)}, f32[8,19968]{1,0:T(8,128)S(1)}, u32[]{:S(2)}, u32[]{:S(2)}) collective-permute-start(f32[8,19968]{1,0:T(8,128)S(1)} %get-tuple-element.42), channel_id=1, source_target_pairs={{0,3},{1,0},{2,1},{3,2},{4,7},{5,4},{6,5},{7,6},{8,11},{9,8},{10,9... | collective-permute-start | bytes 1916936 | tf_op jit(solution)/shard_map/ppermute | solution.py:733
  81.2 20.8 %collective-permute-start.24 = (f32[8,19968]{1,0:T(8,128)S(1)}, f32[8,19968]{1,0:T(8,128)S(1)}, u32[]{:S(2)}, u32[]{:S(2)}) collective-permute-start(f32[8,19968]{1,0:T(8,128)S(1)} %get-tuple-element.44), channel_id=1, source_target_pairs={{0,1},{1,2},{2,3},{3,0},{4,5},{5,6},{6,7},{7,4},{8,9},{9,10},{10,1... | collective-permute-start | bytes 1916936 | tf_op jit(solution)/shard_map/ppermute | solution.py:733
  93.8 16.3 %collective-permute-start.19 = (f32[8,18432]{1,0:T(8,128)S(1)}, f32[8,18432]{1,0:T(8,128)S(1)}, u32[]{:S(2)}, u32[]{:S(2)}) collective-permute-start(f32[8,18432]{1,0:T(8,128)S(1)} %get-tuple-element.39), channel_id=1, source_target_pairs={{0,3},{1,0},{2,1},{3,2},{4,7},{5,4},{6,5},{7,6},{8,11},{9,8},{10,9... | collective-permute-start | bytes 1769480 | tf_op jit(solution)/shard_map/ppermute | solution.py:733
  94.8 17.7 %collective-permute-start.20 = (f32[8,18432]{1,0:T(8,128)S(1)}, f32[8,18432]{1,0:T(8,128)S(1)}, u32[]{:S(2)}, u32[]{:S(2)}) collective-permute-start(f32[8,18432]{1,0:T(8,128)S(1)} %get-tuple-element.40), channel_id=1, source_target_pairs={{0,2},{1,3},{2,0},{3,1},{4,6},{5,7},{6,4},{7,5},{8,10},{9,11},{10,... | collective-permute-start | bytes 1769480 | tf_op jit(solution)/shard_map/ppermute | solution.py:733
  96.5 23.1 %collective-permute-start.21 = (f32[8,18432]{1,0:T(8,128)S(1)}, f32[8,18432]{1,0:T(8,128)S(1)}, u32[]{:S(2)}, u32[]{:S(2)}) collective-permute-start(f32[8,18432]{1,0:T(8,128)S(1)} %get-tuple-element.41), channel_id=1, source_target_pairs={{0,1},{1,2},{2,3},{3,0},{4,5},{5,6},{6,7},{7,4},{8,9},{9,10},{10,1... | collective-permute-start | bytes 1769480 | tf_op jit(solution)/shard_map/ppermute | solution.py:733

commit v5 on v4

--- a/solution.py
+++ b/solution.py
@@ -21,7 +21,7 @@
 SMEM_SPEC = pl.BlockSpec(memory_space=pltpu.SMEM)
 
 
-SHARED = 6144
+SHARED = 5120
 FOLD = SHARED // 4
 
 PLACE = np.array([0, 1] + list(range(PAD, PAD + MODES)))
@@ -37,8 +37,8 @@
 
 def pair_tables():
     rounds = COUNT - 1
-    partner = np.tile(np.arange(LANES, dtype=np.int32), (ROWS, 1))
-    orient = np.ones((ROWS, LANES), np.float32)
+    partner = np.tile(np.arange(LANES), (rounds, 1))
+    orient = np.ones((rounds, LANES), np.float32)
     for turn in range(rounds):
         players = [0] + [1 + (i - 1 + turn) % rounds for i in range(1, COUNT)]
         for k in range(COUNT // 2):
@@ -46,9 +46,16 @@
             partner[turn, lead] = trail
             partner[turn, trail] = lead
             orient[turn, lead] = -1.0
+    moves = np.zeros((3, ROWS, LANES), np.int32)
+    signs = np.zeros((3, ROWS, LANES), np.float32)
+    for k in range(rounds):
+        one, two = 2 * k % rounds, (2 * k + 1) % rounds
+        after = partner[two]
+        moves[0, k], moves[1, k], moves[2, k] = partner[one], after, partner[one][after]
+        signs[0, k], signs[1, k], signs[2, k] = orient[one], orient[one][after], orient[two]
     keep = np.zeros((1, LANES), np.int32)
     keep[0, :MODES] = PLACE[:MODES]
-    return partner, orient, keep
+    return moves, signs, keep
 
 
 def pack_kernel(
@@ -471,7 +478,7 @@
         out_ref[pl.ds(at, PAD), :] = total[PAD + PAD * g : 2 * PAD + PAD * g]
 
 
-def gram(here, stack, chunk=2048):
+def gram(here, stack, chunk=1024):
     return pl.pallas_call(
         functools.partial(gram_kernel, chunk=chunk),
         in_specs=[SMEM_SPEC] + [VMEM_SPEC] * 7,
@@ -546,13 +553,7 @@
             a = a - columns[i] * line
             upper = jnp.where((row == j) & (lane >= j), line, upper)
 
-    def turn_step(i, state):
-        x, v = state
-        turn = lax.rem(i, COUNT - 1)
-        other = jnp.broadcast_to(partner_ref[pl.ds(turn, 1), :], (ROWS, LANES))
-        sign = jnp.broadcast_to(orient_ref[pl.ds(turn, 1), :], (8, LANES))
-        y = jnp.take_along_axis(x, other, axis=1)
-        vy = jnp.take_along_axis(v, other, axis=1)
+    def angle(x, y, sign):
         contrast = lane_sum(y * y) - lane_sum(x * x)
         inner = lane_sum(x * y)
         toward = jnp.where(contrast > 0.0, -1.0, jnp.where(contrast < 0.0, 1.0, sign))
@@ -562,12 +563,30 @@
             positive, 2.0 * inner * toward / jnp.where(positive, d, 1.0), 0.0
         )
         cosine = lax.rsqrt(1.0 + tangent * tangent)
-        sine = spread(cosine * tangent)
-        cosine = spread(cosine)
-        return cosine * x + sine * y, cosine * v + sine * vy
+        return spread(cosine), spread(cosine * tangent)
+
+    def two_rounds(k, state):
+        x, v = state
+        moves = [
+            jnp.broadcast_to(partner_ref[m, pl.ds(k, 1), :], (ROWS, LANES)) for m in range(3)
+        ]
+        signs = [
+            jnp.broadcast_to(orient_ref[m, pl.ds(k, 1), :], (8, LANES)) for m in range(3)
+        ]
+        pair, after, cross = (jnp.take_along_axis(x, move, axis=1) for move in moves)
+        c_self, s_self = angle(x, pair, signs[0])
+        c_next, s_next = angle(after, cross, signs[1])
+        x = c_self * x + s_self * pair
+        after = c_next * after + s_next * cross
+        c_last, s_last = angle(x, after, signs[2])
+        x = c_last * x + s_last * after
+        pair, after, cross = (jnp.take_along_axis(v, move, axis=1) for move in moves)
+        v = c_self * v + s_self * pair
+        after = c_next * after + s_next * cross
+        return x, c_last * v + s_last * after
 
     eye = jnp.where(row == lane, 1.0, 0.0)
-    x, v = lax.fori_loop(0, SWEEPS * (COUNT - 1), turn_step, (upper, eye))
+    x, v = lax.fori_loop(0, SWEEPS * (COUNT - 1) // 2, two_rounds, (upper, eye))
     keep = jnp.broadcast_to(keep_ref[...], (ROWS, LANES))
     sigma_ref[...] = jnp.take_along_axis(jnp.sqrt(lane_sum(x * x)), keep[0:8], axis=1)
     v = jnp.take_along_axis(v, keep, axis=1)
@@ -697,11 +716,11 @@
     )(here, *[near(x) for x in (mix, *stack, *received)], far(basis))
 
 
-def join_kernel(here_ref, *refs):
-    parts, (_, out_hbm, sems) = refs[:4], refs[4:]
+def join_kernel(here_ref, *refs, sources):
+    parts, (_, out_hbm, sems) = refs[: len(sources)], refs[len(sources) :]
     cols = out_hbm.shape[1] // 4
     copies = []
-    for g, part in enumerate(parts):
+    for g, part in zip(sources, parts):
         at = pl.multiple_of(lax.rem(here_ref[0] + g, 4) * cols + SHARED, LANES)
         target = out_hbm.at[:, pl.ds(at, cols - SHARED)]
         copies.append(pltpu.make_async_copy(part, target, sems.at[g]))
@@ -711,16 +730,17 @@
 
 
 def join(here, parts, whole):
+    count = len(parts)
     return pl.pallas_call(
-        join_kernel,
-        in_specs=[SMEM_SPEC] + [VMEM_SPEC] * 4 + [HBM_SPEC],
+        functools.partial(join_kernel, sources=tuple(parts)),
+        in_specs=[SMEM_SPEC] + [VMEM_SPEC] * count + [HBM_SPEC],
         out_specs=HBM_SPEC,
         out_shape=pltpu.HBM(whole.shape, jnp.float32),
         scratch_shapes=[pltpu.SemaphoreType.DMA((4,))],
-        input_output_aliases={5: 0},
+        input_output_aliases={1 + count: 0},
         compiler_params=pltpu.CompilerParams(vmem_limit_bytes=2 << 20),
         name="join",
-    )(here, *[near(x) for x in parts], far(whole))
+    )(here, *[near(x) for x in parts.values()], far(whole))
 
 
 def program(velocity, basis, levels, profile_index, advect):
@@ -738,12 +758,12 @@
     zhi = shifted(face_lo, "mode", -1)
     lo = shifted(block_next, "mode", 1)
     hi = shifted(block_prev, "mode", -1)
+    over = shifted(block_far, "mode", 2)
     plane_lo, plane_hi = add_corners(zlo, zhi, plane_lo, plane_hi, cx, comps)
     xlo = shifted(plane_hi, "space", 1)
     xhi = shifted(plane_lo, "space", -1)
     lo_tail = shifted(tail_next, "mode", 1)
     hi_tail = shifted(tail_prev, "mode", -1)
-    over = shifted(block_far, "mode", 2)
     lo_far = shifted(lo, "mode", 1)
     hi_far = shifted(hi, "mode", -1)
     snap, plus, minus, across = snapshots(
@@ -770,7 +790,8 @@
     back_hi = shifted(out_prev, "mode", -1)
     back_over = shifted(out_over, "mode", 2)
     mine = own(here, mix, stack, (hi_early, over_early, lo_early, hi_far, lo_far), basis)
-    modes = join(here, (out_own, back_hi, back_over, back_lo), mine)
+    modes = join(here, {0: out_own, 1: back_hi, 3: back_lo}, mine)
+    modes = join(here, {2: back_over}, modes)
     return (modes, sigma[0, :MODES])
 
 

time: 122 us -> 133 us (1.090)
  waiting for transfers between devices: 40.7 us -> 53.3 us
  Pallas kernels: 37.7 us -> 36.1 us
    ppermute x17, waiting for transfers between devices: 30.9 us -> 42 us  [shifted(): return lax.ppermute(x, axis, [(i, (i + by) % size) for i in range(size)])]
    pallas_call x1, Pallas kernels: 9.42 us -> 7.27 us  [factor(): pl.pallas_call(factor_kernel, in_specs=[VMEM_SPEC] * 7, out_specs=(VMEM_S...]
    ppermute x10, waiting for transfers between devices: 9.79 us -> 11.2 us  [ring_parts(): lax.ppermute(x, axis, pairs)]
  transfers between devices with their start and end apart: 27 -> 27, of which waited for: 13 -> 12; matrix products, arithmetic and copies ran while one was open for 0% -> 0% of each run, Pallas kernels for 26% -> 23%
where the time goes in v5:
time: 133 us
  waiting for transfers between devices  53.3 us (40%)
  starting transfers between devices  41.9 us (32%)
  Pallas kernels  36.1 us (27%)
    ppermute x17, waiting for transfers between devices, shifted(): return lax.ppermute(x, axis, [(i, (i + by) % size) for i in range(size)])  42 us
    ppermute x17, starting transfers between devices, shifted(): return lax.ppermute(x, axis, [(i, (i + by) % size) for i in range(size)])  28.1 us
    pallas_call x1, Pallas kernels, snapshots(): pl.pallas_call(stencil_kernel, grid=(comps,), in_specs=[SMEM_SPEC, pl.Blo...  18.9 us
    ppermute x10, starting transfers between devices, ring_parts(): lax.ppermute(x, axis, pairs)  13.7 us
    ppermute x10, waiting for transfers between devices, ring_parts(): lax.ppermute(x, axis, pairs)  11.2 us
    pallas_call x1, Pallas kernels, factor(): pl.pallas_call(factor_kernel, in_specs=[VMEM_SPEC] * 7, out_specs=(VMEM_S...  7.27 us
    pallas_call x1, Pallas kernels, pack(): pl.pallas_call(pack_kernel, in_specs=[SMEM_SPEC, HBM_SPEC, HBM_SPEC], out...  2.9 us
  transfers between devices with their start and end apart: 27, of which 12 were waited for; matrix products, arithmetic and copies ran while one was open for 0% of the time, Pallas kernels for 23%

profile of v5, /device:TPU:0, one launch (start us, length us, event | category | flops | bytes accessed | tf_op | source)
XLA Modules:
  0.0 132.7 jit_solution(2072413647607327188)
XLA Ops:
  0.6 0.0 copy-start
  0.7 2.9 %pack.1 = (f32[96,256]{1,0:T(8,128)S(1)}, f32[96,256]{1,0:T(8,128)S(1)}, f32[776,256]{1,0:T(8,128)S(1)}, f32[776,256]{1,0:T(8,128)S(1)}, f32[8,24576]{1,0:T(8,12...) custom-call(s32[1]{0:T(128)} %bitcast.here_ref, ...), custom_call_target="tpu_custom_call" | custom-call | tf_op jit(solution)/shard_map/pack/pallas_call | solution.py:126
  3.6 1.7 %collective-permute-start = (f32[96,256]{1,0:T(8,128)S(1)}, f32[96,256]{1,0:T(8,128)S(1)}, u32[]{:S(2)}, u32[]{:S(2)}) collective-permute-start(f32[96,256]{1,0:T(8,128)S(1)} %get-tuple-element.24.face_hi_ref), channel_id=1, source_target_pairs={{0,1},{1,2},{2,3},{3,0},{4,5},{5,6},{6,7},{7,4},{8,9},{9,10},{10,1... | collective-permute-start | bytes 294920 | tf_op jit(solution)/shard_map/ppermute | solution.py:753
  5.3 1.6 %collective-permute-start.1 = (f32[96,256]{1,0:T(8,128)S(1)}, f32[96,256]{1,0:T(8,128)S(1)}, u32[]{:S(2)}, u32[]{:S(2)}) collective-permute-start(f32[96,256]{1,0:T(8,128)S(1)} %get-tuple-element.25.face_lo_ref), channel_id=1, source_target_pairs={{0,3},{1,0},{2,1},{3,2},{4,7},{5,4},{6,5},{7,6},{8,11},{9,8},{10,9... | collective-permute-start | bytes 294920 | tf_op jit(solution)/shard_map/ppermute | solution.py:753
  6.9 2.6 %collective-permute-done.zlo_ref = f32[96,256]{1,0:T(8,128)S(1)} collective-permute-done((f32[96,256]{1,0:T(8,128)S(1)}, f32[96,256]{1,0:T(8,128)S(1)}, u32[]{:S(2)}, u32[]{:S(2)}) %collective-permute-start) | collective-permute-done | bytes 98336 | tf_op jit(solution)/shard_map/ppermute | solution.py:753
  9.5 0.4 collective-permute-done.1.zhi_ref
  9.9 0.1 collective-permute-start.2
  10.0 5.1 %collective-permute-start.3 = (f32[776,256]{1,0:T(8,128)S(1)}, f32[776,256]{1,0:T(8,128)S(1)}, u32[]{:S(2)}, u32[]{:S(2)}) collective-permute-start(f32[776,256]{1,0:T(8,128)S(1)} %get-tuple-element.29), channel_id=1, source_target_pairs={{0,124},{4,0},{8,4},{12,8},{16,12},{20,16},{24,20},{28,24},{32,28}... | collective-permute-start | bytes 2383880 | tf_op jit(solution)/shard_map/ppermute | solution.py:753
  15.0 2.7 %collective-permute-start.6 = (f32[8,24576]{1,0:T(8,128)S(1)}, f32[8,24576]{1,0:T(8,128)S(1)}, u32[]{:S(2)}, u32[]{:S(2)}) collective-permute-start(f32[8,24576]{1,0:T(8,128)S(1)} %get-tuple-element.34), channel_id=1, source_target_pairs={{0,2},{1,3},{2,0},{3,1},{4,6},{5,7},{6,4},{7,5},{8,10},{9,11},{10,... | collective-permute-start | bytes 2359304 | tf_op jit(solution)/shard_map/ppermute | solution.py:753
  17.8 1.4 %collective-permute-start.5 = (f32[8,19456]{1,0:T(8,128)S(1)}, f32[8,19456]{1,0:T(8,128)S(1)}, u32[]{:S(2)}, u32[]{:S(2)}) collective-permute-start(f32[8,19456]{1,0:T(8,128)S(1)} %get-tuple-element.33), channel_id=1, source_target_pairs={{0,3},{1,0},{2,1},{3,2},{4,7},{5,4},{6,5},{7,6},{8,11},{9,8},{10,9... | collective-permute-start | bytes 1867784 | tf_op jit(solution)/shard_map/ppermute | solution.py:753
  19.2 0.6 collective-permute-start.8
  19.8 5.0 %collective-permute-done.2.xlo_ref = f32[776,256]{1,0:T(8,128)S(1)} collective-permute-done((f32[776,256]{1,0:T(8,128)S(1)}, f32[776,256]{1,0:T(8,128)S(1)}, u32[]{:S(2)}, u32[]{:S(2)}) %collective-permute-start.2) | collective-permute-done | bytes 794656 | tf_op jit(solution)/shard_map/ppermute | solution.py:753
  24.8 2.8 %collective-permute-start.4 = (f32[8,5120]{1,0:T(8,128)S(1)}, f32[8,5120]{1,0:T(8,128)S(1)}, u32[]{:S(2)}, u32[]{:S(2)}) collective-permute-start(f32[8,5120]{1,0:T(8,128)S(1)} %get-tuple-element.32), channel_id=1, source_target_pairs={{0,3},{1,0},{2,1},{3,2},{4,7},{5,4},{6,5},{7,6},{8,11},{9,8},{10,9... | collective-permute-start | bytes 491528 | tf_op jit(solution)/shard_map/ppermute | solution.py:753
  27.6 0.0 collective-permute-done.3.xhi_ref
  27.6 0.0 collective-permute-start.7
  27.7 18.9 %stencil.1 = (f32[8,24576]{1,0:T(8,128)S(1)}, f32[8,16640]{1,0:T(8,128)S(1)}, f32[8,16640]{1,0:T(8,128)S(1)}, f32[8,6400]{1,0:T(8,128)S(1)}) custom-call(f32[8]{0:T(128)S(1)} %copy-done.5, s32[1,256]{1,0:T(1,128)S(1)} %bitcast.5, f32[1,256]{1,0:T(1,128)S(1)} %bitcast.6, bf16[256,128]{1,0:T(8,128)(2,1)S(1)} %copy-done, ...), custom_call_target="tpu_custom_call" | custom-call | tf_op jit(solution)/shard_map/stencil/pallas_call | solution.py:400
  46.6 0.0 copy-start.1
  46.6 0.0 copy-start.2
  46.6 0.0 copy-start.6
  46.6 3.1 %collective-permute-done.4.refs_2_ = f32[8,5120]{1,0:T(8,128)S(1)} collective-permute-done((f32[8,5120]{1,0:T(8,128)S(1)}, f32[8,5120]{1,0:T(8,128)S(1)}, u32[]{:S(2)}, u32[]{:S(2)}) %collective-permute-start.4) | collective-permute-done | bytes 163872 | tf_op jit(solution)/shard_map/ppermute | solution.py:753
  49.8 0.0 collective-permute-done.7.refs_5_
  49.8 0.0 collective-permute-done.5.refs_3_
  49.8 0.0 collective-permute-done.8.refs_6_
  49.8 0.0 collective-permute-done.6.refs_4_
  49.8 1.4 %gram.1 = f32[40,128]{1,0:T(8,128)S(1)} custom-call(s32[1]{0:T(128)} %bitcast.here_ref, f32[8,24576]{1,0:T(8,128)S(1)} %get-tuple-element.30.refs_0_, f32[8,24576]{1,0:T(8,128)S(1)} %get-tuple-element.31.refs_1_, f32[8,5120]{1,0:T(8,128)S(1)} %collective-permute-done.4.refs_2_, f32[8,19456]{1,0:T(8,128)S(1)} %collective-permute-done.5.refs_3_, ...), custom_call_target="tpu_custom_call" | custom-call | tf_op jit(solution)/shard_map/gram/pallas_call | solution.py:482
  51.2 0.0 collective-permute-start.9
  51.2 1.2 collective-permute-done.9
  52.4 2.6 %collective-permute-start.12 = (f32[40,128]{1,0:T(8,128)S(1)}, f32[40,128]{1,0:T(8,128)S(1)}, u32[]{:S(2)}, u32[]{:S(2)}) collective-permute-start(f32[40,128]{1,0:T(8,128)S(1)} %add.21), channel_id=1, source_target_pairs={{0,3},{1,0},{2,1},{3,2},{4,7},{5,4},{6,5},{7,6},{8,11},{9,8},{10,9... | collective-permute-start | bytes 61448 | tf_op jit(solution)/shard_map/ppermute | solution.py:504
  55.0 0.0 collective-permute-start.11
  55.0 1.8 %collective-permute-start.10 = (f32[40,128]{1,0:T(8,128)S(1)}, f32[40,128]{1,0:T(8,128)S(1)}, u32[]{:S(2)}, u32[]{:S(2)}) collective-permute-start(f32[40,128]{1,0:T(8,128)S(1)} %add.21), channel_id=1, source_target_pairs={{0,2},{1,3},{2,0},{3,1},{4,6},{5,7},{6,4},{7,5},{8,10},{9,11},{10,... | collective-permute-start | bytes 61448 | tf_op jit(solution)/shard_map/ppermute | solution.py:504
  56.8 0.0 collective-permute-done.12
  56.8 3.2 %collective-permute-done.11 = f32[40,128]{1,0:T(8,128)S(1)} collective-permute-done((f32[40,128]{1,0:T(8,128)S(1)}, f32[40,128]{1,0:T(8,128)S(1)}, u32[]{:S(2)}, u32[]{:S(2)}) %collective-permute-start.11) | collective-permute-done | bytes 20512 | tf_op jit(solution)/shard_map/ppermute | solution.py:504
  60.0 0.3 collective-permute-done.10
  60.3 3.1 %collective-permute-start.15 = (f32[40,128]{1,0:T(8,128)S(1)}, f32[40,128]{1,0:T(8,128)S(1)}, u32[]{:S(2)}, u32[]{:S(2)}) collective-permute-start(f32[40,128]{1,0:T(8,128)S(1)} %add_add_fusion.1), channel_id=1, source_target_pairs={{0,24},{4,28},{8,0},{12,4},{16,8},{20,12},{24,16},{28,20},{32,56},... | collective-permute-start | bytes 61448 | tf_op jit(solution)/shard_map/ppermute | solution.py:504
  63.4 0.0 collective-permute-start.14
  63.4 1.9 %collective-permute-start.13 = (f32[40,128]{1,0:T(8,128)S(1)}, f32[40,128]{1,0:T(8,128)S(1)}, u32[]{:S(2)}, u32[]{:S(2)}) collective-permute-start(f32[40,128]{1,0:T(8,128)S(1)} %add_add_fusion.1), channel_id=1, source_target_pairs={{0,16},{4,20},{8,24},{12,28},{16,0},{20,4},{24,8},{28,12},{32,48},... | collective-permute-start | bytes 61448 | tf_op jit(solution)/shard_map/ppermute | solution.py:504
  65.3 3.2 %collective-permute-start.25 = (f32[8,5120]{1,0:T(8,128)S(1)}, f32[8,5120]{1,0:T(8,128)S(1)}, u32[]{:S(2)}, u32[]{:S(2)}) collective-permute-start(f32[8,5120]{1,0:T(8,128)S(1)} %collective-permute-done.4.refs_2_), channel_id=1, source_target_pairs={{0,3},{1,0},{2,1},{3,2},{4,7},{5,4},{6,5},{7,6},{8,11},{9,8},{10,9... | collective-permute-start | bytes 491528 | tf_op jit(solution)/shard_map/ppermute | solution.py:753
  68.6 0.0 collective-permute-start.26
  68.6 0.0 collective-permute-done.15
  68.6 1.5 %collective-permute-start.23 = (f32[8,6400]{1,0:T(8,128)S(1)}, f32[8,6400]{1,0:T(8,128)S(1)}, u32[]{:S(2)}, u32[]{:S(2)}) collective-permute-start(f32[8,6400]{1,0:T(8,128)S(1)} %get-tuple-element.43), channel_id=1, source_target_pairs={{0,2},{1,3},{2,0},{3,1},{4,6},{5,7},{6,4},{7,5},{8,10},{9,11},{10,... | collective-permute-start | bytes 614408 | tf_op jit(solution)/shard_map/ppermute | solution.py:753
  70.0 0.0 collective-permute-done.14
  70.0 0.0 collective-permute-done.13
  70.0 4.1 %collective-permute-start.18 = (f32[40,128]{1,0:T(8,128)S(1)}, f32[40,128]{1,0:T(8,128)S(1)}, u32[]{:S(2)}, u32[]{:S(2)}) collective-permute-start(f32[40,128]{1,0:T(8,128)S(1)} %add_add_fusion.g0_ref), channel_id=1, source_target_pairs={{0,96},{4,100},{8,104},{12,108},{16,112},{20,116},{24,120},{28,124... | collective-permute-start | bytes 61448 | tf_op jit(solution)/shard_map/ppermute | solution.py:504
  74.1 0.0 collective-permute-start.17
  74.2 1.5 %collective-permute-done.18.g3_ref = f32[40,128]{1,0:T(8,128)S(1)} collective-permute-done((f32[40,128]{1,0:T(8,128)S(1)}, f32[40,128]{1,0:T(8,128)S(1)}, u32[]{:S(2)}, u32[]{:S(2)}) %collective-permute-start.18) | collective-permute-done | bytes 20512 | tf_op jit(solution)/shard_map/ppermute | solution.py:504
  75.6 0.2 collective-permute-start.16
  75.8 3.6 %collective-permute-done.17.g2_ref = f32[40,128]{1,0:T(8,128)S(1)} collective-permute-done((f32[40,128]{1,0:T(8,128)S(1)}, f32[40,128]{1,0:T(8,128)S(1)}, u32[]{:S(2)}, u32[]{:S(2)}) %collective-permute-start.17) | collective-permute-done | bytes 20512 | tf_op jit(solution)/shard_map/ppermute | solution.py:504
  79.4 1.5 %collective-permute-done.16.g1_ref = f32[40,128]{1,0:T(8,128)S(1)} collective-permute-done((f32[40,128]{1,0:T(8,128)S(1)}, f32[40,128]{1,0:T(8,128)S(1)}, u32[]{:S(2)}, u32[]{:S(2)}) %collective-permute-start.16) | collective-permute-done | bytes 20512 | tf_op jit(solution)/shard_map/ppermute | solution.py:504
  80.9 7.3 %factor.1 = (f32[32,128]{1,0:T(8,128)S(1)}, f32[8,128]{1,0:T(8,128)S(1)}) custom-call(f32[40,128]{1,0:T(8,128)S(1)} %add_add_fusion.g0_ref, f32[40,128]{1,0:T(8,128)S(1)} %collective-permute-done.16.g1_ref, f32[40,128]{1,0:T(8,128)S(1)} %collective-permute-done.17.g2_ref, f32[40,128]{1,0:T(8,128)S(1)} %collective-permute-done.18.g3_ref, ...), custom_call_target="tpu_custom_call" | custom-call | tf_op jit(solution)/shard_map/factor/pallas_call | solution.py:601
  88.2 0.9 update.1
  89.1 1.9 %collective-permute-start.20 = (f32[8,19456]{1,0:T(8,128)S(1)}, f32[8,19456]{1,0:T(8,128)S(1)}, u32[]{:S(2)}, u32[]{:S(2)}) collective-permute-start(f32[8,19456]{1,0:T(8,128)S(1)} %get-tuple-element.40), channel_id=1, source_target_pairs={{0,3},{1,0},{2,1},{3,2},{4,7},{5,4},{6,5},{7,6},{8,11},{9,8},{10,9... | collective-permute-start | bytes 1867784 | tf_op jit(solution)/shard_map/ppermute | solution.py:753
  90.9 0.9 collective-permute-start.21
  91.8 0.0 collective-permute-done.25.refs_10_
  91.8 2.0 %collective-permute-start.19 = (f32[8,19456]{1,0:T(8,128)S(1)}, f32[8,19456]{1,0:T(8,128)S(1)}, u32[]{:S(2)}, u32[]{:S(2)}) collective-permute-start(f32[8,19456]{1,0:T(8,128)S(1)} %get-tuple-element.38), channel_id=1, source_target_pairs={{0,2},{1,3},{2,0},{3,1},{4,6},{5,7},{6,4},{7,5},{8,10},{9,11},{10,... | collective-permute-start | bytes 1867784 | tf_op jit(solution)/shard_map/ppermute | solution.py:753
  93.8 2.6 %collective-permute-start.22 = (f32[8,16640]{1,0:T(8,128)S(1)}, f32[8,16640]{1,0:T(8,128)S(1)}, u32[]{:S(2)}, u32[]{:S(2)}) collective-permute-start(f32[8,16640]{1,0:T(8,128)S(1)} %get-tuple-element.42), channel_id=1, source_target_pairs={{0,3},{1,0},{2,1},{3,2},{4,7},{5,4},{6,5},{7,6},{8,11},{9,8},{10,9... | collective-permute-start | bytes 1597448 | tf_op jit(solution)/shard_map/ppermute | solution.py:753
  96.5 0.0 collective-permute-done.23.refs_8_
  96.5 0.5 slice_bitcast_fusion
  97.0 28.5 %collective-permute-done.22.refs_7_ = f32[8,16640]{1,0:T(8,128)S(1)} collective-permute-done((f32[8,16640]{1,0:T(8,128)S(1)}, f32[8,16640]{1,0:T(8,128)S(1)}, u32[]{:S(2)}, u32[]{:S(2)}) %collective-permute-start.22) | collective-permute-done | bytes 532512 | tf_op jit(solution)/shard_map/ppermute | solution.py:753
  125.5 2.4 %collective-permute-done.24.refs_9_ = f32[8,16640]{1,0:T(8,128)S(1)} collective-permute-done((f32[8,16640]{1,0:T(8,128)S(1)}, f32[8,16640]{1,0:T(8,128)S(1)}, u32[]{:S(2)}, u32[]{:S(2)}) %collective-permute-start.24) | collective-permute-done | bytes 532512 | tf_op jit(solution)/shard_map/ppermute | solution.py:753
  127.9 2.6 %own.1.refs_3_ = f32[8,98304]{1,0:T(8,128)} custom-call(s32[1]{0:T(128)} %bitcast.here_ref, f32[32,128]{1,0:T(8,128)S(1)} %get-tuple-element.37.mix_ref, f32[8,24576]{1,0:T(8,128)S(1)} %get-tuple-element.30.refs_0_, f32[8,24576]{1,0:T(8,128)S(1)} %get-tuple-element.31.refs_1_, f32[8,5120]{1,0:T(8,128)S(1)} %collective-permute-done.4.refs_2_, ...), custom_call_target="tpu_custom_call" | custom-call | tf_op jit(solution)/shard_map/own/pallas_call | solution.py:702
  130.5 0.0 collective-permute-done.20.refs_1_
  130.5 0.0 collective-permute-done.21.refs_2_
  130.5 1.3 join.2.refs_1_
  131.8 0.9 join.3
  (17 shorter events, 0.1 us)
Async XLA Ops:
  0.6 27.0 %copy-start = (bf16[256,128]{1,0:T(8,128)(2,1)S(1)}, bf16[256,128]{1,0:T(8,128)(2,1)}, u32[]{:S(2)}) copy-start(bf16[256,128]{1,0:T(8,128)(2,1)} %constant.12.clone.sum_ref) | copy-start | bytes 196612
  0.6 27.0 %copy-start.3 = (s32[256]{0:T(256)S(1)}, s32[256]{0:T(256)}, u32[]{:S(2)}) copy-start(s32[256]{0:T(256)} %param.12) | copy-start | bytes 3076
  0.7 27.0 %copy-start.4 = (f32[256]{0:T(256)S(1)}, f32[256]{0:T(256)}, u32[]{:S(2)}) copy-start(f32[256]{0:T(256)} %param.13) | copy-start | bytes 3076
  0.7 27.0 %copy-start.5 = (f32[8]{0:T(128)S(1)}, f32[8]{0:T(128)}, u32[]{:S(2)}) copy-start(f32[8]{0:T(128)} %levels_ref.1) | copy-start | bytes 100
  3.6 5.9 %collective-permute-start = (f32[96,256]{1,0:T(8,128)S(1)}, f32[96,256]{1,0:T(8,128)S(1)}, u32[]{:S(2)}, u32[]{:S(2)}) collective-permute-start(f32[96,256]{1,0:T(8,128)S(1)} %get-tuple-element.24.face_hi_ref), channel_id=1, source_target_pairs={{0,1},{1,2},{2,3},{3,0},{4,5},{5,6},{6,7},{7,4},{8,9},{9,10},{10,1... | collective-permute-start | bytes 294920 | tf_op jit(solution)/shard_map/ppermute | solution.py:753
  5.3 4.6 %collective-permute-start.1 = (f32[96,256]{1,0:T(8,128)S(1)}, f32[96,256]{1,0:T(8,128)S(1)}, u32[]{:S(2)}, u32[]{:S(2)}) collective-permute-start(f32[96,256]{1,0:T(8,128)S(1)} %get-tuple-element.25.face_lo_ref), channel_id=1, source_target_pairs={{0,3},{1,0},{2,1},{3,2},{4,7},{5,4},{6,5},{7,6},{8,11},{9,8},{10,9... | collective-permute-start | bytes 294920 | tf_op jit(solution)/shard_map/ppermute | solution.py:753
  9.9 14.9 %collective-permute-start.2 = (f32[776,256]{1,0:T(8,128)S(1)}, f32[776,256]{1,0:T(8,128)S(1)}, u32[]{:S(2)}, u32[]{:S(2)}) collective-permute-start(f32[776,256]{1,0:T(8,128)S(1)} %get-tuple-element.28), channel_id=1, source_target_pairs={{0,4},{4,8},{8,12},{12,16},{16,20},{20,24},{24,28},{28,32},{32,36}... | collective-permute-start | bytes 2383880 | tf_op jit(solution)/shard_map/ppermute | solution.py:753
  10.0 17.7 %collective-permute-start.3 = (f32[776,256]{1,0:T(8,128)S(1)}, f32[776,256]{1,0:T(8,128)S(1)}, u32[]{:S(2)}, u32[]{:S(2)}) collective-permute-start(f32[776,256]{1,0:T(8,128)S(1)} %get-tuple-element.29), channel_id=1, source_target_pairs={{0,124},{4,0},{8,4},{12,8},{16,12},{20,16},{24,20},{28,24},{32,28}... | collective-permute-start | bytes 2383880 | tf_op jit(solution)/shard_map/ppermute | solution.py:753
  15.0 34.8 %collective-permute-start.6 = (f32[8,24576]{1,0:T(8,128)S(1)}, f32[8,24576]{1,0:T(8,128)S(1)}, u32[]{:S(2)}, u32[]{:S(2)}) collective-permute-start(f32[8,24576]{1,0:T(8,128)S(1)} %get-tuple-element.34), channel_id=1, source_target_pairs={{0,2},{1,3},{2,0},{3,1},{4,6},{5,7},{6,4},{7,5},{8,10},{9,11},{10,... | collective-permute-start | bytes 2359304 | tf_op jit(solution)/shard_map/ppermute | solution.py:753
  17.8 32.0 %collective-permute-start.5 = (f32[8,19456]{1,0:T(8,128)S(1)}, f32[8,19456]{1,0:T(8,128)S(1)}, u32[]{:S(2)}, u32[]{:S(2)}) collective-permute-start(f32[8,19456]{1,0:T(8,128)S(1)} %get-tuple-element.33), channel_id=1, source_target_pairs={{0,3},{1,0},{2,1},{3,2},{4,7},{5,4},{6,5},{7,6},{8,11},{9,8},{10,9... | collective-permute-start | bytes 1867784 | tf_op jit(solution)/shard_map/ppermute | solution.py:753
  19.2 30.6 %collective-permute-start.8 = (f32[8,19456]{1,0:T(8,128)S(1)}, f32[8,19456]{1,0:T(8,128)S(1)}, u32[]{:S(2)}, u32[]{:S(2)}) collective-permute-start(f32[8,19456]{1,0:T(8,128)S(1)} %get-tuple-element.36), channel_id=1, source_target_pairs={{0,1},{1,2},{2,3},{3,0},{4,5},{5,6},{6,7},{7,4},{8,9},{9,10},{10,1... | collective-permute-start | bytes 1867784 | tf_op jit(solution)/shard_map/ppermute | solution.py:753
  24.8 25.0 %collective-permute-start.4 = (f32[8,5120]{1,0:T(8,128)S(1)}, f32[8,5120]{1,0:T(8,128)S(1)}, u32[]{:S(2)}, u32[]{:S(2)}) collective-permute-start(f32[8,5120]{1,0:T(8,128)S(1)} %get-tuple-element.32), channel_id=1, source_target_pairs={{0,3},{1,0},{2,1},{3,2},{4,7},{5,4},{6,5},{7,6},{8,11},{9,8},{10,9... | collective-permute-start | bytes 491528 | tf_op jit(solution)/shard_map/ppermute | solution.py:753
  27.6 22.2 %collective-permute-start.7 = (f32[8,5120]{1,0:T(8,128)S(1)}, f32[8,5120]{1,0:T(8,128)S(1)}, u32[]{:S(2)}, u32[]{:S(2)}) collective-permute-start(f32[8,5120]{1,0:T(8,128)S(1)} %get-tuple-element.35), channel_id=1, source_target_pairs={{0,1},{1,2},{2,3},{3,0},{4,5},{5,6},{6,7},{7,4},{8,9},{9,10},{10,1... | collective-permute-start | bytes 491528 | tf_op jit(solution)/shard_map/ppermute | solution.py:753
  46.6 34.3 %copy-start.1 = (f32[3,40,128]{2,1,0:T(8,128)S(1)}, f32[3,40,128]{2,1,0:T(8,128)}, u32[]{:S(2)}) copy-start(f32[3,40,128]{2,1,0:T(8,128)} %constant.14.clone.orient_ref) | copy-start | bytes 184324
  46.6 34.3 %copy-start.2 = (s32[3,40,128]{2,1,0:T(8,128)S(1)}, s32[3,40,128]{2,1,0:T(8,128)}, u32[]{:S(2)}) copy-start(s32[3,40,128]{2,1,0:T(8,128)} %constant.13.clone.partner_ref) | copy-start | bytes 184324
  46.6 34.3 %copy-start.6 = (s32[1,128]{1,0:T(1,128)S(1)}, s32[1,128]{1,0:T(1,128)}, u32[]{:S(2)}) copy-start(s32[1,128]{1,0:T(1,128)} %constant.15.clone.keep_ref) | copy-start | bytes 1540
  51.2 1.2 collective-permute-start.9
  52.4 4.4 %collective-permute-start.12 = (f32[40,128]{1,0:T(8,128)S(1)}, f32[40,128]{1,0:T(8,128)S(1)}, u32[]{:S(2)}, u32[]{:S(2)}) collective-permute-start(f32[40,128]{1,0:T(8,128)S(1)} %add.21), channel_id=1, source_target_pairs={{0,3},{1,0},{2,1},{3,2},{4,7},{5,4},{6,5},{7,6},{8,11},{9,8},{10,9... | collective-permute-start | bytes 61448 | tf_op jit(solution)/shard_map/ppermute | solution.py:504
  55.0 5.0 %collective-permute-start.11 = (f32[40,128]{1,0:T(8,128)S(1)}, f32[40,128]{1,0:T(8,128)S(1)}, u32[]{:S(2)}, u32[]{:S(2)}) collective-permute-start(f32[40,128]{1,0:T(8,128)S(1)} %add.21), channel_id=1, source_target_pairs={{0,1},{1,2},{2,3},{3,0},{4,5},{5,6},{6,7},{7,4},{8,9},{9,10},{10,1... | collective-permute-start | bytes 61448 | tf_op jit(solution)/shard_map/ppermute | solution.py:504
  55.0 5.3 %collective-permute-start.10 = (f32[40,128]{1,0:T(8,128)S(1)}, f32[40,128]{1,0:T(8,128)S(1)}, u32[]{:S(2)}, u32[]{:S(2)}) collective-permute-start(f32[40,128]{1,0:T(8,128)S(1)} %add.21), channel_id=1, source_target_pairs={{0,2},{1,3},{2,0},{3,1},{4,6},{5,7},{6,4},{7,5},{8,10},{9,11},{10,... | collective-permute-start | bytes 61448 | tf_op jit(solution)/shard_map/ppermute | solution.py:504
  60.3 8.2 %collective-permute-start.15 = (f32[40,128]{1,0:T(8,128)S(1)}, f32[40,128]{1,0:T(8,128)S(1)}, u32[]{:S(2)}, u32[]{:S(2)}) collective-permute-start(f32[40,128]{1,0:T(8,128)S(1)} %add_add_fusion.1), channel_id=1, source_target_pairs={{0,24},{4,28},{8,0},{12,4},{16,8},{20,12},{24,16},{28,20},{32,56},... | collective-permute-start | bytes 61448 | tf_op jit(solution)/shard_map/ppermute | solution.py:504
  63.4 6.6 %collective-permute-start.14 = (f32[40,128]{1,0:T(8,128)S(1)}, f32[40,128]{1,0:T(8,128)S(1)}, u32[]{:S(2)}, u32[]{:S(2)}) collective-permute-start(f32[40,128]{1,0:T(8,128)S(1)} %add_add_fusion.1), channel_id=1, source_target_pairs={{0,8},{4,12},{8,16},{12,20},{16,24},{20,28},{24,0},{28,4},{32,40},... | collective-permute-start | bytes 61448 | tf_op jit(solution)/shard_map/ppermute | solution.py:504
  63.4 6.6 %collective-permute-start.13 = (f32[40,128]{1,0:T(8,128)S(1)}, f32[40,128]{1,0:T(8,128)S(1)}, u32[]{:S(2)}, u32[]{:S(2)}) collective-permute-start(f32[40,128]{1,0:T(8,128)S(1)} %add_add_fusion.1), channel_id=1, source_target_pairs={{0,16},{4,20},{8,24},{12,28},{16,0},{20,4},{24,8},{28,12},{32,48},... | collective-permute-start | bytes 61448 | tf_op jit(solution)/shard_map/ppermute | solution.py:504
  65.3 26.5 %collective-permute-start.25 = (f32[8,5120]{1,0:T(8,128)S(1)}, f32[8,5120]{1,0:T(8,128)S(1)}, u32[]{:S(2)}, u32[]{:S(2)}) collective-permute-start(f32[8,5120]{1,0:T(8,128)S(1)} %collective-permute-done.4.refs_2_), channel_id=1, source_target_pairs={{0,3},{1,0},{2,1},{3,2},{4,7},{5,4},{6,5},{7,6},{8,11},{9,8},{10,9... | collective-permute-start | bytes 491528 | tf_op jit(solution)/shard_map/ppermute | solution.py:753
  68.6 25.3 %collective-permute-start.26 = (f32[8,5120]{1,0:T(8,128)S(1)}, f32[8,5120]{1,0:T(8,128)S(1)}, u32[]{:S(2)}, u32[]{:S(2)}) collective-permute-start(f32[8,5120]{1,0:T(8,128)S(1)} %collective-permute-done.7.refs_5_), channel_id=1, source_target_pairs={{0,1},{1,2},{2,3},{3,0},{4,5},{5,6},{6,7},{7,4},{8,9},{9,10},{10,1... | collective-permute-start | bytes 491528 | tf_op jit(solution)/shard_map/ppermute | solution.py:753
  68.6 27.9 %collective-permute-start.23 = (f32[8,6400]{1,0:T(8,128)S(1)}, f32[8,6400]{1,0:T(8,128)S(1)}, u32[]{:S(2)}, u32[]{:S(2)}) collective-permute-start(f32[8,6400]{1,0:T(8,128)S(1)} %get-tuple-element.43), channel_id=1, source_target_pairs={{0,2},{1,3},{2,0},{3,1},{4,6},{5,7},{6,4},{7,5},{8,10},{9,11},{10,... | collective-permute-start | bytes 614408 | tf_op jit(solution)/shard_map/ppermute | solution.py:753
  70.0 5.6 %collective-permute-start.18 = (f32[40,128]{1,0:T(8,128)S(1)}, f32[40,128]{1,0:T(8,128)S(1)}, u32[]{:S(2)}, u32[]{:S(2)}) collective-permute-start(f32[40,128]{1,0:T(8,128)S(1)} %add_add_fusion.g0_ref), channel_id=1, source_target_pairs={{0,96},{4,100},{8,104},{12,108},{16,112},{20,116},{24,120},{28,124... | collective-permute-start | bytes 61448 | tf_op jit(solution)/shard_map/ppermute | solution.py:504
  74.1 5.3 %collective-permute-start.17 = (f32[40,128]{1,0:T(8,128)S(1)}, f32[40,128]{1,0:T(8,128)S(1)}, u32[]{:S(2)}, u32[]{:S(2)}) collective-permute-start(f32[40,128]{1,0:T(8,128)S(1)} %add_add_fusion.g0_ref), channel_id=1, source_target_pairs={{0,64},{4,68},{8,72},{12,76},{16,80},{20,84},{24,88},{28,92},{32,9... | collective-permute-start | bytes 61448 | tf_op jit(solution)/shard_map/ppermute | solution.py:504
  75.6 5.3 %collective-permute-start.16 = (f32[40,128]{1,0:T(8,128)S(1)}, f32[40,128]{1,0:T(8,128)S(1)}, u32[]{:S(2)}, u32[]{:S(2)}) collective-permute-start(f32[40,128]{1,0:T(8,128)S(1)} %add_add_fusion.g0_ref), channel_id=1, source_target_pairs={{0,32},{4,36},{8,40},{12,44},{16,48},{20,52},{24,56},{28,60},{32,6... | collective-permute-start | bytes 61448 | tf_op jit(solution)/shard_map/ppermute | solution.py:504
  89.1 41.4 %collective-permute-start.20 = (f32[8,19456]{1,0:T(8,128)S(1)}, f32[8,19456]{1,0:T(8,128)S(1)}, u32[]{:S(2)}, u32[]{:S(2)}) collective-permute-start(f32[8,19456]{1,0:T(8,128)S(1)} %get-tuple-element.40), channel_id=1, source_target_pairs={{0,3},{1,0},{2,1},{3,2},{4,7},{5,4},{6,5},{7,6},{8,11},{9,8},{10,9... | collective-permute-start | bytes 1867784 | tf_op jit(solution)/shard_map/ppermute | solution.py:753
  90.9 39.6 %collective-permute-start.21 = (f32[8,19456]{1,0:T(8,128)S(1)}, f32[8,19456]{1,0:T(8,128)S(1)}, u32[]{:S(2)}, u32[]{:S(2)}) collective-permute-start(f32[8,19456]{1,0:T(8,128)S(1)} %get-tuple-element.41), channel_id=1, source_target_pairs={{0,1},{1,2},{2,3},{3,0},{4,5},{5,6},{6,7},{7,4},{8,9},{9,10},{10,1... | collective-permute-start | bytes 1867784 | tf_op jit(solution)/shard_map/ppermute | solution.py:753
  91.8 40.0 %collective-permute-start.19 = (f32[8,19456]{1,0:T(8,128)S(1)}, f32[8,19456]{1,0:T(8,128)S(1)}, u32[]{:S(2)}, u32[]{:S(2)}) collective-permute-start(f32[8,19456]{1,0:T(8,128)S(1)} %get-tuple-element.38), channel_id=1, source_target_pairs={{0,2},{1,3},{2,0},{3,1},{4,6},{5,7},{6,4},{7,5},{8,10},{9,11},{10,... | collective-permute-start | bytes 1867784 | tf_op jit(solution)/shard_map/ppermute | solution.py:753
  93.8 31.7 %collective-permute-start.22 = (f32[8,16640]{1,0:T(8,128)S(1)}, f32[8,16640]{1,0:T(8,128)S(1)}, u32[]{:S(2)}, u32[]{:S(2)}) collective-permute-start(f32[8,16640]{1,0:T(8,128)S(1)} %get-tuple-element.42), channel_id=1, source_target_pairs={{0,3},{1,0},{2,1},{3,2},{4,7},{5,4},{6,5},{7,6},{8,11},{9,8},{10,9... | collective-permute-start | bytes 1597448 | tf_op jit(solution)/shard_map/ppermute | solution.py:753
  96.5 31.4 %collective-permute-start.24 = (f32[8,16640]{1,0:T(8,128)S(1)}, f32[8,16640]{1,0:T(8,128)S(1)}, u32[]{:S(2)}, u32[]{:S(2)}) collective-permute-start(f32[8,16640]{1,0:T(8,128)S(1)} %get-tuple-element.44), channel_id=1, source_target_pairs={{0,1},{1,2},{2,3},{3,0},{4,5},{5,6},{6,7},{7,4},{8,9},{9,10},{10,1... | collective-permute-start | bytes 1597448 | tf_op jit(solution)/shard_map/ppermute | solution.py:753

commit v6 on v5

--- a/solution.py
+++ b/solution.py
@@ -58,14 +58,18 @@
     return moves, signs, keep
 
 
+def face_plane(here_ref, side, first, last):
+    return jnp.where(here_ref[1] == side, first, last)
+
+
 def pack_kernel(
     here_ref,
     vel_hbm,
     basis_hbm,
     zfirst_ref,
     zlast_ref,
-    xfirst_ref,
-    xlast_ref,
+    outer_ref,
+    inner_ref,
     mine_ref,
     next_ref,
     far_ref,
@@ -84,7 +88,8 @@
         for side, at in enumerate((0, cz - PAD)):
             source = vel_hbm.at[c, :, pl.ds(at, PAD), :]
             edges.append(pltpu.make_async_copy(source, buf.at[c, side], edge_sems.at[c, side]))
-        for side, (at, ref) in enumerate(((0, xfirst_ref), (cx - 2, xlast_ref))):
+        for side, ref in enumerate((outer_ref, inner_ref)):
+            at = face_plane(here_ref, side, 0, cx - 2)
             for k in range(2):
                 source = vel_hbm.at[c, at + k]
                 target = ref.at[pl.ds((2 * c + k) * cz, cz)]
@@ -139,29 +144,29 @@
     )(here, far(velocity), far(basis))
 
 
-def corner_kernel(zlo_ref, zhi_ref, _, __, xfirst_ref, xlast_ref, *, cx, comps):
-    base = xfirst_ref.shape[0] - PAD
-    zero = jnp.zeros((PAD, xfirst_ref.shape[1]), jnp.float32)
-    for ref, plane in ((xfirst_ref, 0), (xlast_ref, cx - 1)):
+def corner_kernel(here_ref, zlo_ref, zhi_ref, _, __, outer_ref, inner_ref, *, cx, comps):
+    base = outer_ref.shape[0] - PAD
+    zero = jnp.zeros((PAD, outer_ref.shape[1]), jnp.float32)
+    for side, ref in enumerate((outer_ref, inner_ref)):
+        plane = face_plane(here_ref, side, 0, cx - 1)
         ref[base:, :] = zero
         for c in range(comps):
-            low, high = (2 * c + 1) * cx + plane, 2 * c * cx + plane
             at = base + 2 * c
-            ref[at : at + 1, :] = zlo_ref[low : low + 1, :]
-            ref[at + 1 : at + 2, :] = zhi_ref[high : high + 1, :]
-
-
-def add_corners(zlo, zhi, first, last, cx, comps):
-    face = pltpu.VMEM(first.shape, jnp.float32)
+            ref[at : at + 1, :] = zlo_ref[pl.ds((2 * c + 1) * cx + plane, 1), :]
+            ref[at + 1 : at + 2, :] = zhi_ref[pl.ds(2 * c * cx + plane, 1), :]
+
+
+def add_corners(here, zlo, zhi, outer, inner, cx, comps):
+    face = pltpu.VMEM(outer.shape, jnp.float32)
     return pl.pallas_call(
         functools.partial(corner_kernel, cx=cx, comps=comps),
-        in_specs=[VMEM_SPEC] * 4,
+        in_specs=[SMEM_SPEC] + [VMEM_SPEC] * 4,
         out_specs=[VMEM_SPEC] * 2,
         out_shape=[face, face],
-        input_output_aliases={2: 0, 3: 1},
+        input_output_aliases={3: 0, 4: 1},
         compiler_params=pltpu.CompilerParams(vmem_limit_bytes=1 << 20),
         name="corners",
-    )(*[near(x) for x in (zlo, zhi, first, last)])
+    )(here, *[near(x) for x in (zlo, zhi, outer, inner)])
 
 
 def coefficients(levels_ref, index_ref, advect_ref):
@@ -232,8 +237,8 @@
     here_ref,
     basis_hbm,
     vel_hbm,
-    xlo_ref,
-    xhi_ref,
+    outer_ref,
+    inner_ref,
     out_ref,
     plus_ref,
     minus_ref,
@@ -258,10 +263,10 @@
             *[
                 pltpu.make_async_copy(
                     ref.at[pl.ds((2 * c + k) * cz, cz)],
-                    field.at[c, at + k, inner, :],
+                    field.at[c, face_plane(here_ref, side, 0, cx + 2) + k, inner, :],
                     sems.at[c, 1 + side, k],
                 )
-                for side, (at, ref) in enumerate(((0, xlo_ref), (cx + 2, xhi_ref)))
+                for side, ref in enumerate((outer_ref, inner_ref))
                 for k in range(2)
             ],
         )
@@ -287,8 +292,14 @@
     zlo2, zlo1 = edge_row(zlo_ref, 0), edge_row(zlo_ref, 1)
     zhi1, zhi2 = edge_row(zhi_ref, 0), edge_row(zhi_ref, 1)
     spot = 6 * cz + 2 * comp
-    lo_before, lo_after = xlo_ref[pl.ds(spot, 1), :], xhi_ref[pl.ds(spot, 1), :]
-    hi_before, hi_after = xlo_ref[pl.ds(spot + 1, 1), :], xhi_ref[pl.ds(spot + 1, 1), :]
+    first_core = here_ref[1] == 0
+
+    def before_after(at):
+        outer, other = outer_ref[pl.ds(at, 1), :], inner_ref[pl.ds(at, 1), :]
+        return jnp.where(first_core, outer, other), jnp.where(first_core, other, outer)
+
+    lo_before, lo_after = before_after(spot)
+    hi_before, hi_after = before_after(spot + 1)
     plane = lax.broadcasted_iota(jnp.int32, (cx, ny), 0)
 
     def edge(row, before, after, north, south):
@@ -746,22 +757,24 @@
 def program(velocity, basis, levels, profile_index, advect):
     n_space, n_mode = lax.axis_size("space"), lax.axis_size("mode")
     comps, cx, _, _ = velocity.shape
-    here = lax.axis_index("mode").astype(jnp.int32).reshape(1)
+    places = (lax.axis_index("mode"), lax.rem(lax.axis_index("space"), 2))
+    here = jnp.stack([place.astype(jnp.int32) for place in places])
 
     def shifted(x, axis, by):
         size = lax.axis_size(axis)
         return lax.ppermute(x, axis, [(i, (i + by) % size) for i in range(size)])
 
-    face_lo, face_hi, plane_lo, plane_hi, *blocks = pack(here, velocity, basis)
+    face_lo, face_hi, outer, inner, *blocks = pack(here, velocity, basis)
     block_own, block_next, block_far, block_prev, tail_next, tail_prev = blocks
     zlo = shifted(face_hi, "mode", 1)
     zhi = shifted(face_lo, "mode", -1)
     lo = shifted(block_next, "mode", 1)
     hi = shifted(block_prev, "mode", -1)
     over = shifted(block_far, "mode", 2)
-    plane_lo, plane_hi = add_corners(zlo, zhi, plane_lo, plane_hi, cx, comps)
-    xlo = shifted(plane_hi, "space", 1)
-    xhi = shifted(plane_lo, "space", -1)
+    outer, inner = add_corners(here, zlo, zhi, outer, inner, cx, comps)
+    pairs = [(i, (i + (1 if i % 2 else -1)) % n_space) for i in range(n_space)]
+    outer = lax.ppermute(outer, "space", pairs)
+    inner = lax.ppermute(inner, "space", [(i, i ^ 1) for i in range(n_space)])
     lo_tail = shifted(tail_next, "mode", 1)
     hi_tail = shifted(tail_prev, "mode", -1)
     lo_far = shifted(lo, "mode", 1)
@@ -773,7 +786,7 @@
         advect,
         here,
         basis,
-        (zlo, zhi, face_lo, face_hi, velocity, xlo, xhi),
+        (zlo, zhi, face_lo, face_hi, velocity, outer, inner),
     )
     stack = (snap, block_own, hi, hi_tail, over, lo, lo_tail)
     total = gram(here, stack)

time: 133 us -> 137 us (1.030)
  Pallas kernels: 36.1 us -> 40.1 us
  starting transfers between devices: 41.9 us -> 38 us
  waiting for transfers between devices: 53.3 us -> 57.1 us
    ppermute x0 -> x2, waiting for transfers between devices: none -> 5.27 us  [the longest x1 5.27 us: program(): outer = lax.ppermute(outer, 'space', pairs)]
    ppermute x17 -> x15, starting transfers between devices: 28.1 us -> 23.3 us  [shifted(): return lax.ppermute(x, axis, [(i, (i + by) % size) for i in range(size)])]
    ppermute x0 -> x2, starting transfers between devices: none -> 4.58 us  [the longest x1 4.58 us: program(): outer = lax.ppermute(outer, 'space', pairs)]
    ppermute x10, starting transfers between devices: 13.7 us -> 10.1 us  [ring_parts(): lax.ppermute(x, axis, pairs)]
    ppermute x17 -> x15, waiting for transfers between devices: 42 us -> 40.3 us  [shifted(): return lax.ppermute(x, axis, [(i, (i + by) % size) for i in range(size)])]
  transfers between devices with their start and end apart: 27 -> 27, of which waited for: 12 -> 13; matrix products, arithmetic and copies ran while one was open for 0% -> 0% of each run, Pallas kernels for 23% -> 24%
where the time goes in v6:
time: 137 us
  waiting for transfers between devices  57.1 us (42%)
  Pallas kernels  40.1 us (29%)
  starting transfers between devices  38 us (28%)
    ppermute x15, waiting for transfers between devices, shifted(): return lax.ppermute(x, axis, [(i, (i + by) % size) for i in range(size)])  40.3 us
    ppermute x15, starting transfers between devices, shifted(): return lax.ppermute(x, axis, [(i, (i + by) % size) for i in range(size)])  23.3 us
    pallas_call x1, Pallas kernels, snapshots(): pl.pallas_call(stencil_kernel, grid=(comps,), in_specs=[SMEM_SPEC, pl.Blo...  19.1 us
    ppermute x10, waiting for transfers between devices, ring_parts(): lax.ppermute(x, axis, pairs)  11.5 us
    ppermute x10, starting transfers between devices, ring_parts(): lax.ppermute(x, axis, pairs)  10.1 us
    pallas_call x1, Pallas kernels, factor(): pl.pallas_call(factor_kernel, in_specs=[VMEM_SPEC] * 7, out_specs=(VMEM_S...  7.27 us
    ppermute x1, waiting for transfers between devices, program(): outer = lax.ppermute(outer, 'space', pairs)  5.27 us
    ppermute x1, starting transfers between devices, program(): outer = lax.ppermute(outer, 'space', pairs)  4.58 us
  transfers between devices with their start and end apart: 27, of which 13 were waited for; matrix products, arithmetic and copies ran while one was open for 0% of the time, Pallas kernels for 24%

profile of v6, /device:TPU:0, one launch (start us, length us, event | category | flops | bytes accessed | tf_op | source)
XLA Modules:
  0.0 136.7 jit_solution(11118089034076096244)
XLA Ops:
  0.6 0.1 pad_add_fusion.here_ref
  0.7 3.4 %pack.1 = (f32[96,256]{1,0:T(8,128)S(1)}, f32[96,256]{1,0:T(8,128)S(1)}, f32[776,256]{1,0:T(8,128)S(1)}, f32[776,256]{1,0:T(8,128)S(1)}, f32[8,24576]{1,0:T(8,12...) custom-call(s32[2]{0:T(128)S(1)} %pad_add_fusion.here_ref, ...), custom_call_target="tpu_custom_call" | custom-call | tf_op jit(solution)/shard_map/pack/pallas_call | solution.py:131
  4.2 1.7 %collective-permute-start = (f32[96,256]{1,0:T(8,128)S(1)}, f32[96,256]{1,0:T(8,128)S(1)}, u32[]{:S(2)}, u32[]{:S(2)}) collective-permute-start(f32[96,256]{1,0:T(8,128)S(1)} %get-tuple-element.24.face_hi_ref), channel_id=1, source_target_pairs={{0,1},{1,2},{2,3},{3,0},{4,5},{5,6},{6,7},{7,4},{8,9},{9,10},{10,1... | collective-permute-start | bytes 294920 | tf_op jit(solution)/shard_map/ppermute | solution.py:765
  5.8 1.6 %collective-permute-start.1 = (f32[96,256]{1,0:T(8,128)S(1)}, f32[96,256]{1,0:T(8,128)S(1)}, u32[]{:S(2)}, u32[]{:S(2)}) collective-permute-start(f32[96,256]{1,0:T(8,128)S(1)} %get-tuple-element.25.face_lo_ref), channel_id=1, source_target_pairs={{0,3},{1,0},{2,1},{3,2},{4,7},{5,4},{6,5},{7,6},{8,11},{9,8},{10,9... | collective-permute-start | bytes 294920 | tf_op jit(solution)/shard_map/ppermute | solution.py:765
  7.5 2.6 %collective-permute-done.zlo_ref = f32[96,256]{1,0:T(8,128)S(1)} collective-permute-done((f32[96,256]{1,0:T(8,128)S(1)}, f32[96,256]{1,0:T(8,128)S(1)}, u32[]{:S(2)}, u32[]{:S(2)}) %collective-permute-start) | collective-permute-done | bytes 98336 | tf_op jit(solution)/shard_map/ppermute | solution.py:765
  10.1 0.4 collective-permute-done.1.zhi_ref
  10.4 0.6 corners.1
  11.0 4.6 %collective-permute-start.2 = (f32[776,256]{1,0:T(8,128)S(1)}, f32[776,256]{1,0:T(8,128)S(1)}, u32[]{:S(2)}, u32[]{:S(2)}) collective-permute-start(f32[776,256]{1,0:T(8,128)S(1)} %get-tuple-element.28), channel_id=1, source_target_pairs={{0,124},{4,8},{8,4},{12,16},{16,12},{20,24},{24,20},{28,32},{32,28... | collective-permute-start | bytes 2383880 | tf_op jit(solution)/shard_map/ppermute | solution.py:776
  15.6 0.0 collective-permute-start.3
  15.6 3.0 %collective-permute-start.6 = (f32[8,24576]{1,0:T(8,128)S(1)}, f32[8,24576]{1,0:T(8,128)S(1)}, u32[]{:S(2)}, u32[]{:S(2)}) collective-permute-start(f32[8,24576]{1,0:T(8,128)S(1)} %get-tuple-element.34), channel_id=1, source_target_pairs={{0,2},{1,3},{2,0},{3,1},{4,6},{5,7},{6,4},{7,5},{8,10},{9,11},{10,... | collective-permute-start | bytes 2359304 | tf_op jit(solution)/shard_map/ppermute | solution.py:765
  18.6 1.4 collective-permute-start.5
  20.0 0.7 collective-permute-start.8
  20.6 5.3 %collective-permute-done.2.outer_ref = f32[776,256]{1,0:T(8,128)S(1)} collective-permute-done((f32[776,256]{1,0:T(8,128)S(1)}, f32[776,256]{1,0:T(8,128)S(1)}, u32[]{:S(2)}, u32[]{:S(2)}) %collective-permute-start.2) | collective-permute-done | bytes 794656 | tf_op jit(solution)/shard_map/ppermute | solution.py:776
  25.9 2.8 %collective-permute-start.4 = (f32[8,5120]{1,0:T(8,128)S(1)}, f32[8,5120]{1,0:T(8,128)S(1)}, u32[]{:S(2)}, u32[]{:S(2)}) collective-permute-start(f32[8,5120]{1,0:T(8,128)S(1)} %get-tuple-element.32), channel_id=1, source_target_pairs={{0,3},{1,0},{2,1},{3,2},{4,7},{5,4},{6,5},{7,6},{8,11},{9,8},{10,9... | collective-permute-start | bytes 491528 | tf_op jit(solution)/shard_map/ppermute | solution.py:765
  28.8 0.0 collective-permute-done.3.inner_ref
  28.8 0.0 collective-permute-start.7
  28.8 19.1 %stencil.1 = (f32[8,24576]{1,0:T(8,128)S(1)}, f32[8,16640]{1,0:T(8,128)S(1)}, f32[8,16640]{1,0:T(8,128)S(1)}, f32[8,6400]{1,0:T(8,128)S(1)}) custom-call(f32[8]{0:T(128)S(1)} %copy-done.5, s32[1,256]{1,0:T(1,128)S(1)} %bitcast.6, f32[1,256]{1,0:T(1,128)S(1)} %bitcast.7, bf16[256,128]{1,0:T(8,128)(2,1)S(1)} %copy-done, ...), custom_call_target="tpu_custom_call" | custom-call | tf_op jit(solution)/shard_map/stencil/pallas_call | solution.py:411
  47.9 0.0 copy-start.1
  47.9 0.0 copy-start.2
  47.9 0.0 copy-start.6
  48.0 6.3 %collective-permute-done.4.refs_2_ = f32[8,5120]{1,0:T(8,128)S(1)} collective-permute-done((f32[8,5120]{1,0:T(8,128)S(1)}, f32[8,5120]{1,0:T(8,128)S(1)}, u32[]{:S(2)}, u32[]{:S(2)}) %collective-permute-start.4) | collective-permute-done | bytes 163872 | tf_op jit(solution)/shard_map/ppermute | solution.py:765
  54.2 0.0 collective-permute-done.7.refs_5_
  54.2 0.0 collective-permute-done.5.refs_3_
  54.2 0.0 collective-permute-done.8.refs_6_
  54.2 0.0 collective-permute-done.6.refs_4_
  54.3 1.9 %gram.1 = f32[40,128]{1,0:T(8,128)S(1)} custom-call(s32[2]{0:T(128)S(1)} %pad_add_fusion.here_ref, f32[8,24576]{1,0:T(8,128)S(1)} %get-tuple-element.30.refs_0_, f32[8,24576]{1,0:T(8,128)S(1)} %get-tuple-element.31.refs_1_, f32[8,5120]{1,0:T(8,128)S(1)} %collective-permute-done.4.refs_2_, f32[8,19456]{1,0:T(8,128)S(1)} %collective-permute-done.5.refs_3_, ...), custom_call_target="tpu_custom_call" | custom-call | tf_op jit(solution)/shard_map/gram/pallas_call | solution.py:493
  56.2 0.0 collective-permute-start.9
  56.2 1.2 collective-permute-done.9
  57.4 2.6 %collective-permute-start.12 = (f32[40,128]{1,0:T(8,128)S(1)}, f32[40,128]{1,0:T(8,128)S(1)}, u32[]{:S(2)}, u32[]{:S(2)}) collective-permute-start(f32[40,128]{1,0:T(8,128)S(1)} %add.21), channel_id=1, source_target_pairs={{0,3},{1,0},{2,1},{3,2},{4,7},{5,4},{6,5},{7,6},{8,11},{9,8},{10,9... | collective-permute-start | bytes 61448 | tf_op jit(solution)/shard_map/ppermute | solution.py:515
  60.0 0.0 collective-permute-start.11
  60.0 2.1 %collective-permute-start.10 = (f32[40,128]{1,0:T(8,128)S(1)}, f32[40,128]{1,0:T(8,128)S(1)}, u32[]{:S(2)}, u32[]{:S(2)}) collective-permute-start(f32[40,128]{1,0:T(8,128)S(1)} %add.21), channel_id=1, source_target_pairs={{0,2},{1,3},{2,0},{3,1},{4,6},{5,7},{6,4},{7,5},{8,10},{9,11},{10,... | collective-permute-start | bytes 61448 | tf_op jit(solution)/shard_map/ppermute | solution.py:515
  62.1 0.0 collective-permute-done.12
  62.1 2.9 %collective-permute-done.11 = f32[40,128]{1,0:T(8,128)S(1)} collective-permute-done((f32[40,128]{1,0:T(8,128)S(1)}, f32[40,128]{1,0:T(8,128)S(1)}, u32[]{:S(2)}, u32[]{:S(2)}) %collective-permute-start.11) | collective-permute-done | bytes 20512 | tf_op jit(solution)/shard_map/ppermute | solution.py:515
  65.0 0.3 collective-permute-done.10
  65.3 0.1 collective-permute-start.15
  65.4 2.0 %collective-permute-start.14 = (f32[40,128]{1,0:T(8,128)S(1)}, f32[40,128]{1,0:T(8,128)S(1)}, u32[]{:S(2)}, u32[]{:S(2)}) collective-permute-start(f32[40,128]{1,0:T(8,128)S(1)} %add_add_fusion.1), channel_id=1, source_target_pairs={{0,8},{4,12},{8,16},{12,20},{16,24},{20,28},{24,0},{28,4},{32,40},... | collective-permute-start | bytes 61448 | tf_op jit(solution)/shard_map/ppermute | solution.py:515
  67.4 0.0 collective-permute-start.13
  67.4 3.2 %collective-permute-start.25 = (f32[8,5120]{1,0:T(8,128)S(1)}, f32[8,5120]{1,0:T(8,128)S(1)}, u32[]{:S(2)}, u32[]{:S(2)}) collective-permute-start(f32[8,5120]{1,0:T(8,128)S(1)} %collective-permute-done.4.refs_2_), channel_id=1, source_target_pairs={{0,3},{1,0},{2,1},{3,2},{4,7},{5,4},{6,5},{7,6},{8,11},{9,8},{10,9... | collective-permute-start | bytes 491528 | tf_op jit(solution)/shard_map/ppermute | solution.py:765
  70.7 0.0 collective-permute-start.26
  70.7 0.0 collective-permute-done.15
  70.7 1.5 %collective-permute-start.23 = (f32[8,6400]{1,0:T(8,128)S(1)}, f32[8,6400]{1,0:T(8,128)S(1)}, u32[]{:S(2)}, u32[]{:S(2)}) collective-permute-start(f32[8,6400]{1,0:T(8,128)S(1)} %get-tuple-element.43), channel_id=1, source_target_pairs={{0,2},{1,3},{2,0},{3,1},{4,6},{5,7},{6,4},{7,5},{8,10},{9,11},{10,... | collective-permute-start | bytes 614408 | tf_op jit(solution)/shard_map/ppermute | solution.py:765
  72.1 0.6 collective-permute-done.13
  72.7 3.1 %collective-permute-start.18 = (f32[40,128]{1,0:T(8,128)S(1)}, f32[40,128]{1,0:T(8,128)S(1)}, u32[]{:S(2)}, u32[]{:S(2)}) collective-permute-start(f32[40,128]{1,0:T(8,128)S(1)} %add_add_fusion.g0_ref), channel_id=1, source_target_pairs={{0,96},{4,100},{8,104},{12,108},{16,112},{20,116},{24,120},{28,124... | collective-permute-start | bytes 61448 | tf_op jit(solution)/shard_map/ppermute | solution.py:515
  75.8 1.5 %collective-permute-done.18.g3_ref = f32[40,128]{1,0:T(8,128)S(1)} collective-permute-done((f32[40,128]{1,0:T(8,128)S(1)}, f32[40,128]{1,0:T(8,128)S(1)}, u32[]{:S(2)}, u32[]{:S(2)}) %collective-permute-start.18) | collective-permute-done | bytes 20512 | tf_op jit(solution)/shard_map/ppermute | solution.py:515
  77.3 0.2 collective-permute-start.16
  77.5 3.6 %collective-permute-done.17.g2_ref = f32[40,128]{1,0:T(8,128)S(1)} collective-permute-done((f32[40,128]{1,0:T(8,128)S(1)}, f32[40,128]{1,0:T(8,128)S(1)}, u32[]{:S(2)}, u32[]{:S(2)}) %collective-permute-start.17) | collective-permute-done | bytes 20512 | tf_op jit(solution)/shard_map/ppermute | solution.py:515
  81.1 1.5 %collective-permute-done.16.g1_ref = f32[40,128]{1,0:T(8,128)S(1)} collective-permute-done((f32[40,128]{1,0:T(8,128)S(1)}, f32[40,128]{1,0:T(8,128)S(1)}, u32[]{:S(2)}, u32[]{:S(2)}) %collective-permute-start.16) | collective-permute-done | bytes 20512 | tf_op jit(solution)/shard_map/ppermute | solution.py:515
  82.6 7.3 %factor.1 = (f32[32,128]{1,0:T(8,128)S(1)}, f32[8,128]{1,0:T(8,128)S(1)}) custom-call(f32[40,128]{1,0:T(8,128)S(1)} %add_add_fusion.g0_ref, f32[40,128]{1,0:T(8,128)S(1)} %collective-permute-done.16.g1_ref, f32[40,128]{1,0:T(8,128)S(1)} %collective-permute-done.17.g2_ref, f32[40,128]{1,0:T(8,128)S(1)} %collective-permute-done.18.g3_ref, ...), custom_call_target="tpu_custom_call" | custom-call | tf_op jit(solution)/shard_map/factor/pallas_call | solution.py:612
  89.9 1.4 %update.1 = (f32[8,19456]{1,0:T(8,128)S(1)}, f32[8,19456]{1,0:T(8,128)S(1)}, f32[8,19456]{1,0:T(8,128)S(1)}, f32[8,19456]{1,0:T(8,128)S(1)}) custom-call(s32[2]{0:T(128)S(1)} %pad_add_fusion.here_ref, f32[32,128]{1,0:T(8,128)S(1)} %get-tuple-element.37.mix_ref, f32[8,24576]{1,0:T(8,128)S(1)} %get-tuple-element.30.refs_0_, ...), custom_call_target="tpu_custom_call" | custom-call | tf_op jit(solution)/shard_map/update/pallas_call | solution.py:658
  91.3 2.3 %collective-permute-start.20 = (f32[8,19456]{1,0:T(8,128)S(1)}, f32[8,19456]{1,0:T(8,128)S(1)}, u32[]{:S(2)}, u32[]{:S(2)}) collective-permute-start(f32[8,19456]{1,0:T(8,128)S(1)} %get-tuple-element.40), channel_id=1, source_target_pairs={{0,3},{1,0},{2,1},{3,2},{4,7},{5,4},{6,5},{7,6},{8,11},{9,8},{10,9... | collective-permute-start | bytes 1867784 | tf_op jit(solution)/shard_map/ppermute | solution.py:765
  93.6 0.5 collective-permute-start.21
  94.1 0.0 collective-permute-done.25.refs_10_
  94.1 2.0 %collective-permute-start.19 = (f32[8,19456]{1,0:T(8,128)S(1)}, f32[8,19456]{1,0:T(8,128)S(1)}, u32[]{:S(2)}, u32[]{:S(2)}) collective-permute-start(f32[8,19456]{1,0:T(8,128)S(1)} %get-tuple-element.38), channel_id=1, source_target_pairs={{0,2},{1,3},{2,0},{3,1},{4,6},{5,7},{6,4},{7,5},{8,10},{9,11},{10,... | collective-permute-start | bytes 1867784 | tf_op jit(solution)/shard_map/ppermute | solution.py:765
  96.1 2.6 %collective-permute-start.22 = (f32[8,16640]{1,0:T(8,128)S(1)}, f32[8,16640]{1,0:T(8,128)S(1)}, u32[]{:S(2)}, u32[]{:S(2)}) collective-permute-start(f32[8,16640]{1,0:T(8,128)S(1)} %get-tuple-element.42), channel_id=1, source_target_pairs={{0,3},{1,0},{2,1},{3,2},{4,7},{5,4},{6,5},{7,6},{8,11},{9,8},{10,9... | collective-permute-start | bytes 1597448 | tf_op jit(solution)/shard_map/ppermute | solution.py:765
  98.7 0.0 collective-permute-done.23.refs_8_
  98.7 0.0 collective-permute-start.24
  98.7 0.5 slice_bitcast_fusion
  99.2 28.5 %collective-permute-done.22.refs_7_ = f32[8,16640]{1,0:T(8,128)S(1)} collective-permute-done((f32[8,16640]{1,0:T(8,128)S(1)}, f32[8,16640]{1,0:T(8,128)S(1)}, u32[]{:S(2)}, u32[]{:S(2)}) %collective-permute-start.22) | collective-permute-done | bytes 532512 | tf_op jit(solution)/shard_map/ppermute | solution.py:765
  127.7 2.5 %collective-permute-done.24.refs_9_ = f32[8,16640]{1,0:T(8,128)S(1)} collective-permute-done((f32[8,16640]{1,0:T(8,128)S(1)}, f32[8,16640]{1,0:T(8,128)S(1)}, u32[]{:S(2)}, u32[]{:S(2)}) %collective-permute-start.24) | collective-permute-done | bytes 532512 | tf_op jit(solution)/shard_map/ppermute | solution.py:765
  130.2 3.2 %own.1.refs_3_ = f32[8,98304]{1,0:T(8,128)} custom-call(s32[2]{0:T(128)S(1)} %pad_add_fusion.here_ref, f32[32,128]{1,0:T(8,128)S(1)} %get-tuple-element.37.mix_ref, f32[8,24576]{1,0:T(8,128)S(1)} %get-tuple-element.30.refs_0_, f32[8,24576]{1,0:T(8,128)S(1)} %get-tuple-element.31.refs_1_, f32[8,5120]{1,0:T(8,128)S(1)} %collective-permute-done.4.refs_2_, ...), custom_call_target="tpu_custom_call" | custom-call | tf_op jit(solution)/shard_map/own/pallas_call | solution.py:713
  133.4 0.0 collective-permute-done.20.refs_1_
  133.4 0.0 collective-permute-done.21.refs_2_
  133.4 1.8 %join.2.refs_1_ = f32[8,98304]{1,0:T(8,128)} custom-call(s32[2]{0:T(128)S(1)} %pad_add_fusion.here_ref, f32[8,19456]{1,0:T(8,128)S(1)} %get-tuple-element.39.refs_0_, f32[8,19456]{1,0:T(8,128)S(1)} %collective-permute-done.20.refs_1_, f32[8,19456]{1,0:T(8,128)S(1)} %collective-permute-done.21.refs_2_, ...), custom_call_target="tpu_custom_call", output_to_operand_aliasing={{}: (4, {})} | custom-call | tf_op jit(solution)/shard_map/join/pallas_call | solution.py:745
  135.2 1.4 %join.3 = f32[8,98304]{1,0:T(8,128)} custom-call(s32[2]{0:T(128)S(1)} %pad_add_fusion.here_ref, f32[8,19456]{1,0:T(8,128)S(1)} %collective-permute-done.19.refs_0_, f32[8,98304]{1,0:T(8,128)} %join.2.refs_1_), custom_call_target="tpu_custom_call", output_to_operand_aliasing={{}: (2, {})} | custom-call | tf_op jit(solution)/shard_map/join/pallas_call | solution.py:745
  (18 shorter events, 0.1 us)
Async XLA Ops:
  0.7 28.1 %copy-start = (bf16[256,128]{1,0:T(8,128)(2,1)S(1)}, bf16[256,128]{1,0:T(8,128)(2,1)}, u32[]{:S(2)}) copy-start(bf16[256,128]{1,0:T(8,128)(2,1)} %constant.22.clone.sum_ref) | copy-start | bytes 196612
  0.7 28.1 %copy-start.3 = (s32[256]{0:T(256)S(1)}, s32[256]{0:T(256)}, u32[]{:S(2)}) copy-start(s32[256]{0:T(256)} %param.12) | copy-start | bytes 3076
  0.7 28.1 %copy-start.4 = (f32[256]{0:T(256)S(1)}, f32[256]{0:T(256)}, u32[]{:S(2)}) copy-start(f32[256]{0:T(256)} %param.13) | copy-start | bytes 3076
  0.7 28.1 %copy-start.5 = (f32[8]{0:T(128)S(1)}, f32[8]{0:T(128)}, u32[]{:S(2)}) copy-start(f32[8]{0:T(128)} %levels_ref.1) | copy-start | bytes 100
  4.2 5.9 %collective-permute-start = (f32[96,256]{1,0:T(8,128)S(1)}, f32[96,256]{1,0:T(8,128)S(1)}, u32[]{:S(2)}, u32[]{:S(2)}) collective-permute-start(f32[96,256]{1,0:T(8,128)S(1)} %get-tuple-element.24.face_hi_ref), channel_id=1, source_target_pairs={{0,1},{1,2},{2,3},{3,0},{4,5},{5,6},{6,7},{7,4},{8,9},{9,10},{10,1... | collective-permute-start | bytes 294920 | tf_op jit(solution)/shard_map/ppermute | solution.py:765
  5.8 4.6 %collective-permute-start.1 = (f32[96,256]{1,0:T(8,128)S(1)}, f32[96,256]{1,0:T(8,128)S(1)}, u32[]{:S(2)}, u32[]{:S(2)}) collective-permute-start(f32[96,256]{1,0:T(8,128)S(1)} %get-tuple-element.25.face_lo_ref), channel_id=1, source_target_pairs={{0,3},{1,0},{2,1},{3,2},{4,7},{5,4},{6,5},{7,6},{8,11},{9,8},{10,9... | collective-permute-start | bytes 294920 | tf_op jit(solution)/shard_map/ppermute | solution.py:765
  11.0 14.9 %collective-permute-start.2 = (f32[776,256]{1,0:T(8,128)S(1)}, f32[776,256]{1,0:T(8,128)S(1)}, u32[]{:S(2)}, u32[]{:S(2)}) collective-permute-start(f32[776,256]{1,0:T(8,128)S(1)} %get-tuple-element.28), channel_id=1, source_target_pairs={{0,124},{4,8},{8,4},{12,16},{16,12},{20,24},{24,20},{28,32},{32,28... | collective-permute-start | bytes 2383880 | tf_op jit(solution)/shard_map/ppermute | solution.py:776
  15.6 13.2 %collective-permute-start.3 = (f32[776,256]{1,0:T(8,128)S(1)}, f32[776,256]{1,0:T(8,128)S(1)}, u32[]{:S(2)}, u32[]{:S(2)}) collective-permute-start(f32[776,256]{1,0:T(8,128)S(1)} %get-tuple-element.29), channel_id=1, source_target_pairs={{0,4},{4,0},{8,12},{12,8},{16,20},{20,16},{24,28},{28,24},{32,36},... | collective-permute-start | bytes 2383880 | tf_op jit(solution)/shard_map/ppermute | solution.py:777
  15.6 38.6 %collective-permute-start.6 = (f32[8,24576]{1,0:T(8,128)S(1)}, f32[8,24576]{1,0:T(8,128)S(1)}, u32[]{:S(2)}, u32[]{:S(2)}) collective-permute-start(f32[8,24576]{1,0:T(8,128)S(1)} %get-tuple-element.34), channel_id=1, source_target_pairs={{0,2},{1,3},{2,0},{3,1},{4,6},{5,7},{6,4},{7,5},{8,10},{9,11},{10,... | collective-permute-start | bytes 2359304 | tf_op jit(solution)/shard_map/ppermute | solution.py:765
  18.6 35.6 %collective-permute-start.5 = (f32[8,19456]{1,0:T(8,128)S(1)}, f32[8,19456]{1,0:T(8,128)S(1)}, u32[]{:S(2)}, u32[]{:S(2)}) collective-permute-start(f32[8,19456]{1,0:T(8,128)S(1)} %get-tuple-element.33), channel_id=1, source_target_pairs={{0,3},{1,0},{2,1},{3,2},{4,7},{5,4},{6,5},{7,6},{8,11},{9,8},{10,9... | collective-permute-start | bytes 1867784 | tf_op jit(solution)/shard_map/ppermute | solution.py:765
  20.0 34.3 %collective-permute-start.8 = (f32[8,19456]{1,0:T(8,128)S(1)}, f32[8,19456]{1,0:T(8,128)S(1)}, u32[]{:S(2)}, u32[]{:S(2)}) collective-permute-start(f32[8,19456]{1,0:T(8,128)S(1)} %get-tuple-element.36), channel_id=1, source_target_pairs={{0,1},{1,2},{2,3},{3,0},{4,5},{5,6},{6,7},{7,4},{8,9},{9,10},{10,1... | collective-permute-start | bytes 1867784 | tf_op jit(solution)/shard_map/ppermute | solution.py:765
  25.9 28.3 %collective-permute-start.4 = (f32[8,5120]{1,0:T(8,128)S(1)}, f32[8,5120]{1,0:T(8,128)S(1)}, u32[]{:S(2)}, u32[]{:S(2)}) collective-permute-start(f32[8,5120]{1,0:T(8,128)S(1)} %get-tuple-element.32), channel_id=1, source_target_pairs={{0,3},{1,0},{2,1},{3,2},{4,7},{5,4},{6,5},{7,6},{8,11},{9,8},{10,9... | collective-permute-start | bytes 491528 | tf_op jit(solution)/shard_map/ppermute | solution.py:765
  28.8 25.5 %collective-permute-start.7 = (f32[8,5120]{1,0:T(8,128)S(1)}, f32[8,5120]{1,0:T(8,128)S(1)}, u32[]{:S(2)}, u32[]{:S(2)}) collective-permute-start(f32[8,5120]{1,0:T(8,128)S(1)} %get-tuple-element.35), channel_id=1, source_target_pairs={{0,1},{1,2},{2,3},{3,0},{4,5},{5,6},{6,7},{7,4},{8,9},{9,10},{10,1... | collective-permute-start | bytes 491528 | tf_op jit(solution)/shard_map/ppermute | solution.py:765
  47.9 34.7 %copy-start.1 = (f32[3,40,128]{2,1,0:T(8,128)S(1)}, f32[3,40,128]{2,1,0:T(8,128)}, u32[]{:S(2)}) copy-start(f32[3,40,128]{2,1,0:T(8,128)} %constant.24.clone.orient_ref) | copy-start | bytes 184324
  47.9 34.7 %copy-start.2 = (s32[3,40,128]{2,1,0:T(8,128)S(1)}, s32[3,40,128]{2,1,0:T(8,128)}, u32[]{:S(2)}) copy-start(s32[3,40,128]{2,1,0:T(8,128)} %constant.23.clone.partner_ref) | copy-start | bytes 184324
  47.9 34.6 %copy-start.6 = (s32[1,128]{1,0:T(1,128)S(1)}, s32[1,128]{1,0:T(1,128)}, u32[]{:S(2)}) copy-start(s32[1,128]{1,0:T(1,128)} %constant.25.clone.keep_ref) | copy-start | bytes 1540
  56.2 1.2 collective-permute-start.9
  57.4 4.7 %collective-permute-start.12 = (f32[40,128]{1,0:T(8,128)S(1)}, f32[40,128]{1,0:T(8,128)S(1)}, u32[]{:S(2)}, u32[]{:S(2)}) collective-permute-start(f32[40,128]{1,0:T(8,128)S(1)} %add.21), channel_id=1, source_target_pairs={{0,3},{1,0},{2,1},{3,2},{4,7},{5,4},{6,5},{7,6},{8,11},{9,8},{10,9... | collective-permute-start | bytes 61448 | tf_op jit(solution)/shard_map/ppermute | solution.py:515
  60.0 5.0 %collective-permute-start.11 = (f32[40,128]{1,0:T(8,128)S(1)}, f32[40,128]{1,0:T(8,128)S(1)}, u32[]{:S(2)}, u32[]{:S(2)}) collective-permute-start(f32[40,128]{1,0:T(8,128)S(1)} %add.21), channel_id=1, source_target_pairs={{0,1},{1,2},{2,3},{3,0},{4,5},{5,6},{6,7},{7,4},{8,9},{9,10},{10,1... | collective-permute-start | bytes 61448 | tf_op jit(solution)/shard_map/ppermute | solution.py:515
  60.0 5.3 %collective-permute-start.10 = (f32[40,128]{1,0:T(8,128)S(1)}, f32[40,128]{1,0:T(8,128)S(1)}, u32[]{:S(2)}, u32[]{:S(2)}) collective-permute-start(f32[40,128]{1,0:T(8,128)S(1)} %add.21), channel_id=1, source_target_pairs={{0,2},{1,3},{2,0},{3,1},{4,6},{5,7},{6,4},{7,5},{8,10},{9,11},{10,... | collective-permute-start | bytes 61448 | tf_op jit(solution)/shard_map/ppermute | solution.py:515
  65.3 5.3 %collective-permute-start.15 = (f32[40,128]{1,0:T(8,128)S(1)}, f32[40,128]{1,0:T(8,128)S(1)}, u32[]{:S(2)}, u32[]{:S(2)}) collective-permute-start(f32[40,128]{1,0:T(8,128)S(1)} %add_add_fusion.1), channel_id=1, source_target_pairs={{0,24},{4,28},{8,0},{12,4},{16,8},{20,12},{24,16},{28,20},{32,56},... | collective-permute-start | bytes 61448 | tf_op jit(solution)/shard_map/ppermute | solution.py:515
  65.4 6.7 %collective-permute-start.14 = (f32[40,128]{1,0:T(8,128)S(1)}, f32[40,128]{1,0:T(8,128)S(1)}, u32[]{:S(2)}, u32[]{:S(2)}) collective-permute-start(f32[40,128]{1,0:T(8,128)S(1)} %add_add_fusion.1), channel_id=1, source_target_pairs={{0,8},{4,12},{8,16},{12,20},{16,24},{20,28},{24,0},{28,4},{32,40},... | collective-permute-start | bytes 61448 | tf_op jit(solution)/shard_map/ppermute | solution.py:515
  67.4 5.3 %collective-permute-start.13 = (f32[40,128]{1,0:T(8,128)S(1)}, f32[40,128]{1,0:T(8,128)S(1)}, u32[]{:S(2)}, u32[]{:S(2)}) collective-permute-start(f32[40,128]{1,0:T(8,128)S(1)} %add_add_fusion.1), channel_id=1, source_target_pairs={{0,16},{4,20},{8,24},{12,28},{16,0},{20,4},{24,8},{28,12},{32,48},... | collective-permute-start | bytes 61448 | tf_op jit(solution)/shard_map/ppermute | solution.py:515
  67.4 26.6 %collective-permute-start.25 = (f32[8,5120]{1,0:T(8,128)S(1)}, f32[8,5120]{1,0:T(8,128)S(1)}, u32[]{:S(2)}, u32[]{:S(2)}) collective-permute-start(f32[8,5120]{1,0:T(8,128)S(1)} %collective-permute-done.4.refs_2_), channel_id=1, source_target_pairs={{0,3},{1,0},{2,1},{3,2},{4,7},{5,4},{6,5},{7,6},{8,11},{9,8},{10,9... | collective-permute-start | bytes 491528 | tf_op jit(solution)/shard_map/ppermute | solution.py:765
  70.7 25.4 %collective-permute-start.26 = (f32[8,5120]{1,0:T(8,128)S(1)}, f32[8,5120]{1,0:T(8,128)S(1)}, u32[]{:S(2)}, u32[]{:S(2)}) collective-permute-start(f32[8,5120]{1,0:T(8,128)S(1)} %collective-permute-done.7.refs_5_), channel_id=1, source_target_pairs={{0,1},{1,2},{2,3},{3,0},{4,5},{5,6},{6,7},{7,4},{8,9},{9,10},{10,1... | collective-permute-start | bytes 491528 | tf_op jit(solution)/shard_map/ppermute | solution.py:765
  70.7 28.0 %collective-permute-start.23 = (f32[8,6400]{1,0:T(8,128)S(1)}, f32[8,6400]{1,0:T(8,128)S(1)}, u32[]{:S(2)}, u32[]{:S(2)}) collective-permute-start(f32[8,6400]{1,0:T(8,128)S(1)} %get-tuple-element.43), channel_id=1, source_target_pairs={{0,2},{1,3},{2,0},{3,1},{4,6},{5,7},{6,4},{7,5},{8,10},{9,11},{10,... | collective-permute-start | bytes 614408 | tf_op jit(solution)/shard_map/ppermute | solution.py:765
  72.7 4.6 %collective-permute-start.18 = (f32[40,128]{1,0:T(8,128)S(1)}, f32[40,128]{1,0:T(8,128)S(1)}, u32[]{:S(2)}, u32[]{:S(2)}) collective-permute-start(f32[40,128]{1,0:T(8,128)S(1)} %add_add_fusion.g0_ref), channel_id=1, source_target_pairs={{0,96},{4,100},{8,104},{12,108},{16,112},{20,116},{24,120},{28,124... | collective-permute-start | bytes 61448 | tf_op jit(solution)/shard_map/ppermute | solution.py:515
  75.8 5.3 %collective-permute-start.17 = (f32[40,128]{1,0:T(8,128)S(1)}, f32[40,128]{1,0:T(8,128)S(1)}, u32[]{:S(2)}, u32[]{:S(2)}) collective-permute-start(f32[40,128]{1,0:T(8,128)S(1)} %add_add_fusion.g0_ref), channel_id=1, source_target_pairs={{0,64},{4,68},{8,72},{12,76},{16,80},{20,84},{24,88},{28,92},{32,9... | collective-permute-start | bytes 61448 | tf_op jit(solution)/shard_map/ppermute | solution.py:515
  77.3 5.3 %collective-permute-start.16 = (f32[40,128]{1,0:T(8,128)S(1)}, f32[40,128]{1,0:T(8,128)S(1)}, u32[]{:S(2)}, u32[]{:S(2)}) collective-permute-start(f32[40,128]{1,0:T(8,128)S(1)} %add_add_fusion.g0_ref), channel_id=1, source_target_pairs={{0,32},{4,36},{8,40},{12,44},{16,48},{20,52},{24,56},{28,60},{32,6... | collective-permute-start | bytes 61448 | tf_op jit(solution)/shard_map/ppermute | solution.py:515
  91.3 42.1 %collective-permute-start.20 = (f32[8,19456]{1,0:T(8,128)S(1)}, f32[8,19456]{1,0:T(8,128)S(1)}, u32[]{:S(2)}, u32[]{:S(2)}) collective-permute-start(f32[8,19456]{1,0:T(8,128)S(1)} %get-tuple-element.40), channel_id=1, source_target_pairs={{0,3},{1,0},{2,1},{3,2},{4,7},{5,4},{6,5},{7,6},{8,11},{9,8},{10,9... | collective-permute-start | bytes 1867784 | tf_op jit(solution)/shard_map/ppermute | solution.py:765
  93.6 39.8 %collective-permute-start.21 = (f32[8,19456]{1,0:T(8,128)S(1)}, f32[8,19456]{1,0:T(8,128)S(1)}, u32[]{:S(2)}, u32[]{:S(2)}) collective-permute-start(f32[8,19456]{1,0:T(8,128)S(1)} %get-tuple-element.41), channel_id=1, source_target_pairs={{0,1},{1,2},{2,3},{3,0},{4,5},{5,6},{6,7},{7,4},{8,9},{9,10},{10,1... | collective-permute-start | bytes 1867784 | tf_op jit(solution)/shard_map/ppermute | solution.py:765
  94.1 41.2 %collective-permute-start.19 = (f32[8,19456]{1,0:T(8,128)S(1)}, f32[8,19456]{1,0:T(8,128)S(1)}, u32[]{:S(2)}, u32[]{:S(2)}) collective-permute-start(f32[8,19456]{1,0:T(8,128)S(1)} %get-tuple-element.38), channel_id=1, source_target_pairs={{0,2},{1,3},{2,0},{3,1},{4,6},{5,7},{6,4},{7,5},{8,10},{9,11},{10,... | collective-permute-start | bytes 1867784 | tf_op jit(solution)/shard_map/ppermute | solution.py:765
  96.1 31.7 %collective-permute-start.22 = (f32[8,16640]{1,0:T(8,128)S(1)}, f32[8,16640]{1,0:T(8,128)S(1)}, u32[]{:S(2)}, u32[]{:S(2)}) collective-permute-start(f32[8,16640]{1,0:T(8,128)S(1)} %get-tuple-element.42), channel_id=1, source_target_pairs={{0,3},{1,0},{2,1},{3,2},{4,7},{5,4},{6,5},{7,6},{8,11},{9,8},{10,9... | collective-permute-start | bytes 1597448 | tf_op jit(solution)/shard_map/ppermute | solution.py:765
  98.7 31.5 %collective-permute-start.24 = (f32[8,16640]{1,0:T(8,128)S(1)}, f32[8,16640]{1,0:T(8,128)S(1)}, u32[]{:S(2)}, u32[]{:S(2)}) collective-permute-start(f32[8,16640]{1,0:T(8,128)S(1)} %get-tuple-element.44), channel_id=1, source_target_pairs={{0,1},{1,2},{2,3},{3,0},{4,5},{5,6},{6,7},{7,4},{8,9},{9,10},{10,1... | collective-permute-start | bytes 1597448 | tf_op jit(solution)/shard_map/ppermute | solution.py:765

commit v7 on v6

--- a/solution.py
+++ b/solution.py
@@ -21,7 +21,8 @@
 SMEM_SPEC = pl.BlockSpec(memory_space=pltpu.SMEM)
 
 
-SHARED = 5120
+SHARED = 14336
+EARLY = 6144
 FOLD = SHARED // 4
 
 PLACE = np.array([0, 1] + list(range(PAD, PAD + MODES)))
@@ -58,12 +59,13 @@
     return moves, signs, keep
 
 
-def face_plane(here_ref, side, first, last):
-    return jnp.where(here_ref[1] == side, first, last)
+def face_plane(core_ref, side, first, last):
+    return jnp.where(core_ref[0] == side, first, last)
 
 
 def pack_kernel(
     here_ref,
+    core_ref,
     vel_hbm,
     basis_hbm,
     zfirst_ref,
@@ -74,8 +76,6 @@
     next_ref,
     far_ref,
     prev_ref,
-    next_tail_ref,
-    prev_tail_ref,
     buf,
     edge_sems,
     face_sems,
@@ -89,23 +89,15 @@
             source = vel_hbm.at[c, :, pl.ds(at, PAD), :]
             edges.append(pltpu.make_async_copy(source, buf.at[c, side], edge_sems.at[c, side]))
         for side, ref in enumerate((outer_ref, inner_ref)):
-            at = face_plane(here_ref, side, 0, cx - 2)
+            at = face_plane(core_ref, side, 0, cx - 2)
             for k in range(2):
                 source = vel_hbm.at[c, at + k]
                 target = ref.at[pl.ds((2 * c + k) * cz, cz)]
                 rest.append(pltpu.make_async_copy(source, target, face_sems.at[c, side, k]))
-    targets = (
-        (0, 0, mine_ref),
-        (1, 0, next_ref),
-        (2, 0, far_ref),
-        (3, 0, prev_ref),
-        (1, SHARED, next_tail_ref),
-        (3, SHARED, prev_tail_ref),
-    )
-    for i, (k, skip, ref) in enumerate(targets):
-        at = pl.multiple_of(lax.rem(here_ref[0] + k, 4) * cols + skip, LANES)
-        source = basis_hbm.at[:, pl.ds(at, ref.shape[1])]
-        rest.append(pltpu.make_async_copy(source, ref, block_sems.at[i]))
+    for k, ref in enumerate((mine_ref, next_ref, far_ref, prev_ref)):
+        at = pl.multiple_of(lax.rem(here_ref[0] + k, 4) * cols, LANES)
+        source = basis_hbm.at[:, pl.ds(at, cols)]
+        rest.append(pltpu.make_async_copy(source, ref, block_sems.at[k]))
     for copy in edges + rest:
         copy.start()
     for copy in edges:
@@ -120,35 +112,32 @@
         copy.wait()
 
 
-def pack(here, velocity, basis):
+def pack(here, core, velocity, basis):
     comps, cx, cz, ny = velocity.shape
     edge = pltpu.VMEM((comps * 2 * cx, ny), jnp.float32)
     face = pltpu.VMEM((comps * 2 * cz + PAD, ny), jnp.float32)
-    cols = basis.shape[1] // 4
-    block, head, tail = (
-        pltpu.VMEM((PAD, size), jnp.float32) for size in (cols, SHARED, cols - SHARED)
-    )
+    block = pltpu.VMEM((PAD, basis.shape[1] // 4), jnp.float32)
     return pl.pallas_call(
         pack_kernel,
-        in_specs=[SMEM_SPEC, HBM_SPEC, HBM_SPEC],
-        out_specs=[VMEM_SPEC] * 10,
-        out_shape=[edge, edge, face, face, block, head, block, head, tail, tail],
+        in_specs=[SMEM_SPEC, SMEM_SPEC, HBM_SPEC, HBM_SPEC],
+        out_specs=[VMEM_SPEC] * 8,
+        out_shape=[edge, edge, face, face] + [block] * 4,
         scratch_shapes=[
             pltpu.VMEM((comps, 2, cx, PAD, ny), jnp.float32),
             pltpu.SemaphoreType.DMA((comps, 2)),
             pltpu.SemaphoreType.DMA((comps, 2, 2)),
-            pltpu.SemaphoreType.DMA((6,)),
+            pltpu.SemaphoreType.DMA((4,)),
         ],
         compiler_params=pltpu.CompilerParams(vmem_limit_bytes=4 << 20),
         name="pack",
-    )(here, far(velocity), far(basis))
-
-
-def corner_kernel(here_ref, zlo_ref, zhi_ref, _, __, outer_ref, inner_ref, *, cx, comps):
+    )(here, core, far(velocity), far(basis))
+
+
+def corner_kernel(core_ref, zlo_ref, zhi_ref, _, __, outer_ref, inner_ref, *, cx, comps):
     base = outer_ref.shape[0] - PAD
     zero = jnp.zeros((PAD, outer_ref.shape[1]), jnp.float32)
     for side, ref in enumerate((outer_ref, inner_ref)):
-        plane = face_plane(here_ref, side, 0, cx - 1)
+        plane = face_plane(core_ref, side, 0, cx - 1)
         ref[base:, :] = zero
         for c in range(comps):
             at = base + 2 * c
@@ -156,7 +145,7 @@
             ref[at + 1 : at + 2, :] = zhi_ref[pl.ds(2 * c * cx + plane, 1), :]
 
 
-def add_corners(here, zlo, zhi, outer, inner, cx, comps):
+def add_corners(core, zlo, zhi, outer, inner, cx, comps):
     face = pltpu.VMEM(outer.shape, jnp.float32)
     return pl.pallas_call(
         functools.partial(corner_kernel, cx=cx, comps=comps),
@@ -166,7 +155,7 @@
         input_output_aliases={3: 0, 4: 1},
         compiler_params=pltpu.CompilerParams(vmem_limit_bytes=1 << 20),
         name="corners",
-    )(here, *[near(x) for x in (zlo, zhi, outer, inner)])
+    )(core, *[near(x) for x in (zlo, zhi, outer, inner)])
 
 
 def coefficients(levels_ref, index_ref, advect_ref):
@@ -216,12 +205,11 @@
 def offer_copies(here, basis_hbm, refs, sems):
     cols = basis_hbm.shape[1] // 4
     copies = []
-    for side, (ref, skip, count) in enumerate(zip(refs, (2, 0, 0), (3, 3, 1))):
-        for k in range(count):
-            at = pl.multiple_of(lax.rem(here + skip + k, 4) * cols, LANES)
-            source = basis_hbm.at[:, pl.ds(at, SHARED)]
-            target = ref.at[:, pl.ds(k * SHARED, SHARED)]
-            copies.append(pltpu.make_async_copy(source, target, sems.at[side, k]))
+    spans = ((3, 0, EARLY), (3, EARLY, SHARED), (1, 0, EARLY), (1, EARLY, SHARED), (0, 0, SHARED))
+    for i, (ref, (skip, first, last)) in enumerate(zip(refs, spans)):
+        at = pl.multiple_of(lax.rem(here + skip, 4) * cols + first, LANES)
+        source = basis_hbm.at[:, pl.ds(at, last - first)]
+        copies.append(pltpu.make_async_copy(source, ref.at[:, 0 : last - first], sems.at[i]))
     return copies
 
 
@@ -235,13 +223,16 @@
     face_lo_ref,
     face_hi_ref,
     here_ref,
+    core_ref,
     basis_hbm,
     vel_hbm,
     outer_ref,
     inner_ref,
     out_ref,
     plus_ref,
+    plus_rest_ref,
     minus_ref,
+    minus_rest_ref,
     over_ref,
     field,
     first,
@@ -250,7 +241,7 @@
     offer_sems,
 ):
     comp = pl.program_id(0)
-    offer_refs = (plus_ref, minus_ref, over_ref)
+    offer_refs = (plus_ref, plus_rest_ref, minus_ref, minus_rest_ref, over_ref)
     offers = offer_copies(here_ref[0], basis_hbm, offer_refs, offer_sems)
     cx, cz, ny = vel_hbm.shape[1:]
     inner = pl.ds(PAD, cz)
@@ -263,7 +254,7 @@
             *[
                 pltpu.make_async_copy(
                     ref.at[pl.ds((2 * c + k) * cz, cz)],
-                    field.at[c, face_plane(here_ref, side, 0, cx + 2) + k, inner, :],
+                    field.at[c, face_plane(core_ref, side, 0, cx + 2) + k, inner, :],
                     sems.at[c, 1 + side, k],
                 )
                 for side, ref in enumerate((outer_ref, inner_ref))
@@ -292,7 +283,7 @@
     zlo2, zlo1 = edge_row(zlo_ref, 0), edge_row(zlo_ref, 1)
     zhi1, zhi2 = edge_row(zhi_ref, 0), edge_row(zhi_ref, 1)
     spot = 6 * cz + 2 * comp
-    first_core = here_ref[1] == 0
+    first_core = core_ref[0] == 0
 
     def before_after(at):
         outer, other = outer_ref[pl.ds(at, 1), :], inner_ref[pl.ds(at, 1), :]
@@ -389,18 +380,17 @@
 
     lax.fori_loop(0, cx // STRIDE, box_step, 0)
 
-    @pl.when(comp == 0)
+    @pl.when(comp == pl.num_programs(0) - 1)
     def _():
         tiles = SHARED // LANES
         for k in range(2 * tiles):
             which, tile = divmod(k, tiles)
             line = out_ref[which : which + 1, tile * LANES : (tile + 1) * LANES]
-            for ref in offer_refs:
-                at = ref.shape[1] - FOLD + k // 8 * LANES
-                ref[k % 8 : k % 8 + 1, at : at + LANES] = line
-
-
-def snapshots(velocity, levels, profile_index, advect, here, basis, halos):
+            at = SHARED + k // 8 * LANES
+            over_ref[k % 8 : k % 8 + 1, at : at + LANES] = line
+
+
+def snapshots(velocity, levels, profile_index, advect, here, core, basis, halos):
     comps, cx, cz, ny = velocity.shape
     cols = (cx // STRIDE) * (cz // STRIDE) * (ny // STRIDE)
     half = LANES // 2
@@ -418,20 +408,22 @@
             pl.BlockSpec((ny, LANES), lambda c: (0, 0)),
             *[VMEM_SPEC] * 4,
             SMEM_SPEC,
+            SMEM_SPEC,
             HBM_SPEC,
             HBM_SPEC,
             VMEM_SPEC,
             VMEM_SPEC,
         ],
-        out_specs=[VMEM_SPEC] * 4,
+        out_specs=[VMEM_SPEC] * 6,
         out_shape=[pltpu.VMEM((PAD, comps * cols), jnp.float32)]
-        + [pltpu.VMEM((PAD, k * SHARED + FOLD), jnp.float32) for k in (3, 3, 1)],
+        + [pltpu.VMEM((PAD, size), jnp.float32) for size in (EARLY, SHARED - EARLY) * 2]
+        + [pltpu.VMEM((PAD, SHARED + FOLD), jnp.float32)],
         scratch_shapes=[
             pltpu.VMEM((comps, cx + 4, cz + 2 * PAD, ny), jnp.float32),
             pltpu.VMEM((cx + 2, cz + 2 * PAD, ny), jnp.float32),
             pltpu.VMEM((cz, ny), jnp.float32),
             pltpu.SemaphoreType.DMA((comps, 3, 2)),
-            pltpu.SemaphoreType.DMA((3, 3)),
+            pltpu.SemaphoreType.DMA((5,)),
         ],
         compiler_params=pltpu.CompilerParams(vmem_limit_bytes=20 << 20),
         name="stencil",
@@ -442,30 +434,19 @@
         jnp.asarray(sums, jnp.bfloat16),
         *[near(x) for x in halos[:4]],
         here,
+        core,
         far(basis),
         far(halos[4]),
         *[near(x) for x in halos[5:]],
     )
 
 
-def stacked(pieces, start, size):
-    rows = []
-    for piece in pieces:
-        if isinstance(piece, tuple):
-            ref, at = (piece[0], start) if start < SHARED else (piece[1], start - SHARED)
-        else:
-            ref, at = piece, start
-        rows.append(ref[:, at : at + size])
-    return jnp.concatenate(rows, axis=0)
-
-
-def pieces_of(refs):
-    snap, mine, hi, hi_tail, far_block, lo, lo_tail = refs
-    return [snap, mine, (hi, hi_tail), far_block, (lo, lo_tail)]
+def stacked(refs, start, size):
+    return jnp.concatenate([ref[:, start : start + size] for ref in refs], axis=0)
 
 
 def gram_kernel(here_ref, *refs, chunk):
-    pieces, out_ref = pieces_of(refs[:-1]), refs[-1]
+    pieces, out_ref = refs[:-1], refs[-1]
     here = here_ref[0]
     n, acc = ROWS, None
     for start in range(0, pieces[0].shape[1], chunk):
@@ -489,10 +470,10 @@
         out_ref[pl.ds(at, PAD), :] = total[PAD + PAD * g : 2 * PAD + PAD * g]
 
 
-def gram(here, stack, chunk=1024):
+def gram(here, stack, chunk=2048):
     return pl.pallas_call(
         functools.partial(gram_kernel, chunk=chunk),
-        in_specs=[SMEM_SPEC] + [VMEM_SPEC] * 7,
+        in_specs=[SMEM_SPEC] + [VMEM_SPEC] * 5,
         out_specs=VMEM_SPEC,
         out_shape=pltpu.VMEM((ROWS, LANES), jnp.float32),
         compiler_params=pltpu.CompilerParams(vmem_limit_bytes=8 << 20),
@@ -643,88 +624,73 @@
 
 
 def update_kernel(here_ref, mix_ref, *refs, chunk):
-    pieces, out_refs = pieces_of(refs[:7]), refs[7:]
+    pieces, out_refs = refs[:5], refs[5:]
     here = here_ref[0]
     mix = jnp.concatenate([mix_rows(mix_ref, here, g) for g in range(4)], axis=0)
     mix = turned_mix(mix, here)
     for start in range(0, out_refs[0].shape[1], chunk):
-        out = mixed(mix, stacked(pieces, SHARED + start, chunk))
+        out = mixed(mix, stacked(pieces, start, chunk))
         for g, ref in enumerate(out_refs):
-            ref[:, start : start + chunk] = out[PAD * g : PAD * g + PAD]
+            at = start - (pieces[0].shape[1] - ref.shape[1])
+            if at >= 0:
+                ref[:, at : at + chunk] = out[PAD * g : PAD * g + PAD]
 
 
 def update(here, mix, stack, chunk=1024):
-    cols = stack[0].shape[1] - SHARED
+    cols = stack[0].shape[1]
+    sizes = (cols, cols, cols - SHARED, cols)
     return pl.pallas_call(
         functools.partial(update_kernel, chunk=chunk),
-        in_specs=[SMEM_SPEC] + [VMEM_SPEC] * 8,
+        in_specs=[SMEM_SPEC] + [VMEM_SPEC] * 6,
         out_specs=[VMEM_SPEC] * 4,
-        out_shape=[pltpu.VMEM((PAD, cols), jnp.float32)] * 4,
+        out_shape=[pltpu.VMEM((PAD, size), jnp.float32) for size in sizes],
         compiler_params=pltpu.CompilerParams(vmem_limit_bytes=8 << 20),
         name="update",
     )(here, near(mix), *[near(x) for x in stack])
 
 
 def own_kernel(here_ref, mix_ref, *refs, cols, chunk):
-    pieces, (hi_ref, over_ref, lo_ref, hi_far_ref, lo_far_ref) = pieces_of(refs[:7]), refs[7:12]
-    basis_hbm, out_hbm, mine, snap, buf, in_sems, out_sems = refs[12:]
+    hi_ref, hi_rest_ref, over_ref, lo_ref, lo_rest_ref = refs[:5]
+    basis_hbm, out_hbm, mine, snap, buf, in_sem, out_sem = refs[5:]
     here = here_ref[0]
     tiles = SHARED // LANES
-    blocks = [lax.rem(here + 1 + b, 4) for b in range(4)]
-    reads = []
-    for b in range(3):
-        at = pl.multiple_of(blocks[b] * cols, LANES)
-        source = basis_hbm.at[:, pl.ds(at, SHARED)]
-        reads.append(pltpu.make_async_copy(source, mine.at[b], in_sems.at[b]))
-    for copy in reads:
-        copy.start()
+    spot = pl.ds(pl.multiple_of(lax.rem(here + 2, 4) * cols, LANES), SHARED)
+    read = pltpu.make_async_copy(basis_hbm.at[:, spot], mine, in_sem)
+    read.start()
     mix = turned_mix(mix_rows(mix_ref, here, 0), here)
-    for b, ref in enumerate((hi_ref, over_ref, lo_ref)):
-        snap[b] = jnp.zeros((PAD, SHARED), jnp.float32)
-        for k in range(2 * tiles):
-            which, tile = divmod(k, tiles)
-            at = ref.shape[1] - FOLD + k // 8 * LANES
-            line = ref[k % 8 : k % 8 + 1, at : at + LANES]
-            snap[b, which : which + 1, tile * LANES : (tile + 1) * LANES] = line
-    for copy in reads:
-        copy.wait()
-    writes = []
-    for b in range(4):
-        for start in range(0, SHARED, chunk):
-            at = slice(start, start + chunk)
-            if b == 3:
-                stack = stacked(pieces, start, chunk)
-            else:
-                wide = slice(b * SHARED + start, b * SHARED + start + chunk)
-                opposite = (hi_far_ref, over_ref, lo_far_ref)[b]
-                rows = [snap[b, :, at], mine[b, :, at]]
-                rows += [hi_ref[:, wide], opposite[:, at], lo_ref[:, wide]]
-                stack = jnp.concatenate(rows, axis=0)
-            buf[b, :, at] = mixed(mix, stack)
-        target = pl.ds(pl.multiple_of(blocks[b] * cols, LANES), SHARED)
-        writes.append(pltpu.make_async_copy(buf.at[b], out_hbm.at[:, target], out_sems.at[b]))
-        writes[-1].start()
-    for copy in writes:
-        copy.wait()
-
-
-def own(here, mix, stack, received, basis, chunk=1024):
+    snap[...] = jnp.zeros((PAD, SHARED), jnp.float32)
+    for k in range(2 * tiles):
+        which, tile = divmod(k, tiles)
+        at = SHARED + k // 8 * LANES
+        line = over_ref[k % 8 : k % 8 + 1, at : at + LANES]
+        snap[which : which + 1, tile * LANES : (tile + 1) * LANES] = line
+    read.wait()
+    for start in range(0, SHARED, chunk):
+        at = slice(start, start + chunk)
+        if start < EARLY:
+            hi, lo = hi_ref[:, at], lo_ref[:, at]
+        else:
+            rest = slice(start - EARLY, start - EARLY + chunk)
+            hi, lo = hi_rest_ref[:, rest], lo_rest_ref[:, rest]
+        stack = jnp.concatenate([snap[:, at], mine[:, at], hi, over_ref[:, at], lo], axis=0)
+        buf[:, at] = mixed(mix, stack)
+    write = pltpu.make_async_copy(buf, out_hbm.at[:, spot], out_sem)
+    write.start()
+    write.wait()
+
+
+def own(here, mix, received, basis, chunk=1024):
     cols = basis.shape[1] // 4
     return pl.pallas_call(
         functools.partial(own_kernel, cols=cols, chunk=chunk),
-        in_specs=[SMEM_SPEC] + [VMEM_SPEC] * 13 + [HBM_SPEC],
+        in_specs=[SMEM_SPEC] + [VMEM_SPEC] * 6 + [HBM_SPEC],
         out_specs=HBM_SPEC,
         out_shape=pltpu.HBM(basis.shape, jnp.float32),
-        scratch_shapes=[
-            pltpu.VMEM((3, PAD, SHARED), jnp.float32),
-            pltpu.VMEM((3, PAD, SHARED), jnp.float32),
-            pltpu.VMEM((4, PAD, SHARED), jnp.float32),
-            pltpu.SemaphoreType.DMA((3,)),
-            pltpu.SemaphoreType.DMA((4,)),
-        ],
+        scratch_shapes=[pltpu.VMEM((PAD, SHARED), jnp.float32)] * 3
+        + [pltpu.SemaphoreType.DMA(())] * 2,
         compiler_params=pltpu.CompilerParams(vmem_limit_bytes=10 << 20),
         name="own",
-    )(here, *[near(x) for x in (mix, *stack, *received)], far(basis))
+    )(here, *[near(x) for x in (mix, *received)], far(basis))
 
 
 def join_kernel(here_ref, *refs, sources):
@@ -732,8 +698,9 @@
     cols = out_hbm.shape[1] // 4
     copies = []
     for g, part in zip(sources, parts):
-        at = pl.multiple_of(lax.rem(here_ref[0] + g, 4) * cols + SHARED, LANES)
-        target = out_hbm.at[:, pl.ds(at, cols - SHARED)]
+        size = part.shape[1]
+        at = pl.multiple_of(lax.rem(here_ref[0] + g, 4) * cols + cols - size, LANES)
+        target = out_hbm.at[:, pl.ds(at, size)]
         copies.append(pltpu.make_async_copy(part, target, sems.at[g]))
         copies[-1].start()
     for copy in copies:
@@ -757,44 +724,43 @@
 def program(velocity, basis, levels, profile_index, advect):
     n_space, n_mode = lax.axis_size("space"), lax.axis_size("mode")
     comps, cx, _, _ = velocity.shape
-    places = (lax.axis_index("mode"), lax.rem(lax.axis_index("space"), 2))
-    here = jnp.stack([place.astype(jnp.int32) for place in places])
+    here = lax.axis_index("mode").astype(jnp.int32).reshape(1)
+    core = lax.rem(lax.axis_index("space").astype(jnp.int32), 2).reshape(1)
 
     def shifted(x, axis, by):
         size = lax.axis_size(axis)
         return lax.ppermute(x, axis, [(i, (i + by) % size) for i in range(size)])
 
-    face_lo, face_hi, outer, inner, *blocks = pack(here, velocity, basis)
-    block_own, block_next, block_far, block_prev, tail_next, tail_prev = blocks
+    face_lo, face_hi, outer, inner, *blocks = pack(here, core, velocity, basis)
+    block_own, block_next, block_far, block_prev = blocks
     zlo = shifted(face_hi, "mode", 1)
     zhi = shifted(face_lo, "mode", -1)
     lo = shifted(block_next, "mode", 1)
     hi = shifted(block_prev, "mode", -1)
     over = shifted(block_far, "mode", 2)
-    outer, inner = add_corners(here, zlo, zhi, outer, inner, cx, comps)
+    outer, inner = add_corners(core, zlo, zhi, outer, inner, cx, comps)
     pairs = [(i, (i + (1 if i % 2 else -1)) % n_space) for i in range(n_space)]
     outer = lax.ppermute(outer, "space", pairs)
     inner = lax.ppermute(inner, "space", [(i, i ^ 1) for i in range(n_space)])
-    lo_tail = shifted(tail_next, "mode", 1)
-    hi_tail = shifted(tail_prev, "mode", -1)
-    lo_far = shifted(lo, "mode", 1)
-    hi_far = shifted(hi, "mode", -1)
-    snap, plus, minus, across = snapshots(
+    snap, plus, plus_rest, minus, minus_rest, across = snapshots(
         velocity,
         levels,
         profile_index,
         advect,
         here,
+        core,
         basis,
         (zlo, zhi, face_lo, face_hi, velocity, outer, inner),
     )
-    stack = (snap, block_own, hi, hi_tail, over, lo, lo_tail)
+    lo_early = shifted(plus, "mode", 1)
+    hi_early = shifted(minus, "mode", -1)
+    stack = (snap, block_own, hi, over, lo)
     total = gram(here, stack)
     total = ring_sum(total, ring_parts(total, "space", n_space, 1, 2))
     total = ring_sum(total, ring_parts(total, "mode", n_mode, 1, n_mode))
     total = ring_sum(total, ring_parts(total, "space", n_space, 2, 4))
-    lo_early = shifted(plus, "mode", 1)
-    hi_early = shifted(minus, "mode", -1)
+    lo_rest = shifted(plus_rest, "mode", 1)
+    hi_rest = shifted(minus_rest, "mode", -1)
     parts = [total] + ring_parts(total, "space", n_space, 8, 4)
     over_early = shifted(across, "mode", 2)
     mix, sigma = factor(parts)
@@ -802,7 +768,8 @@
     back_lo = shifted(out_next, "mode", 1)
     back_hi = shifted(out_prev, "mode", -1)
     back_over = shifted(out_over, "mode", 2)
-    mine = own(here, mix, stack, (hi_early, over_early, lo_early, hi_far, lo_far), basis)
+    received = (hi_early, hi_rest, over_early, lo_early, lo_rest)
+    mine = own(here, mix, received, basis)
     modes = join(here, {0: out_own, 1: back_hi, 3: back_lo}, mine)
     modes = join(here, {2: back_over}, modes)
     return (modes, sigma[0, :MODES])

time: 137 us -> 148 us (1.080)
  waiting for transfers between devices: 57.1 us -> 80.2 us
  starting transfers between devices: 38 us -> 29.7 us
  Pallas kernels: 40.1 us -> 36.5 us
    ppermute x15 -> x13, waiting for transfers between devices: 40.3 us -> 59.5 us  [shifted(): return lax.ppermute(x, axis, [(i, (i + by) % size) for i in range(size)])]
    ppermute x15 -> x13, starting transfers between devices: 23.3 us -> 17.4 us  [shifted(): return lax.ppermute(x, axis, [(i, (i + by) % size) for i in range(size)])]
    ppermute x10, waiting for transfers between devices: 11.5 us -> 14.9 us  [ring_parts(): lax.ppermute(x, axis, pairs)]
    ppermute x10, starting transfers between devices: 10.1 us -> 7.72 us  [ring_parts(): lax.ppermute(x, axis, pairs)]
  transfers between devices with their start and end apart: 27 -> 25, of which waited for: 13 -> 18; matrix products, arithmetic and copies ran while one was open for 0% -> 0% of each run, Pallas kernels for 24% -> 16%
where the time goes in v7:
time: 148 us
  waiting for transfers between devices  80.2 us (54%)
  Pallas kernels  36.5 us (25%)
  starting transfers between devices  29.7 us (20%)
    ppermute x13, waiting for transfers between devices, shifted(): return lax.ppermute(x, axis, [(i, (i + by) % size) for i in range(size)])  59.5 us
    pallas_call x1, Pallas kernels, snapshots(): pl.pallas_call(stencil_kernel, grid=(comps,), in_specs=[SMEM_SPEC, pl.Blo...  19.3 us
    ppermute x13, starting transfers between devices, shifted(): return lax.ppermute(x, axis, [(i, (i + by) % size) for i in range(size)])  17.4 us
    ppermute x10, waiting for transfers between devices, ring_parts(): lax.ppermute(x, axis, pairs)  14.9 us
    ppermute x10, starting transfers between devices, ring_parts(): lax.ppermute(x, axis, pairs)  7.72 us
    pallas_call x1, Pallas kernels, factor(): pl.pallas_call(factor_kernel, in_specs=[VMEM_SPEC] * 7, out_specs=(VMEM_S...  7.27 us
    ppermute x1, waiting for transfers between devices, program(): outer = lax.ppermute(outer, 'space', pairs)  5.88 us
    ppermute x1, starting transfers between devices, program(): outer = lax.ppermute(outer, 'space', pairs)  4.58 us
  transfers between devices with their start and end apart: 25, of which 18 were waited for; matrix products, arithmetic and copies ran while one was open for 0% of the time, Pallas kernels for 16%

profile of v7, /device:TPU:0, one launch (start us, length us, event | category | flops | bytes accessed | tf_op | source)
XLA Modules:
  0.0 147.8 jit_solution(1076395159146864153)
XLA Ops:
  0.6 0.0 copy-start
  0.7 2.9 %pack.1 = (f32[96,256]{1,0:T(8,128)S(1)}, f32[96,256]{1,0:T(8,128)S(1)}, f32[776,256]{1,0:T(8,128)S(1)}, f32[776,256]{1,0:T(8,128)S(1)}, f32[8,24576]{1,0:T(8,12...) custom-call(s32[1]{0:T(128)} %bitcast.here_ref, s32[1]{0:T(128)} %bitcast.3.core_ref, ...), custom_call_target="tpu_custom_call" | custom-call | tf_op jit(solution)/shard_map/pack/pallas_call | solution.py:120
  3.6 1.7 %collective-permute-start = (f32[96,256]{1,0:T(8,128)S(1)}, f32[96,256]{1,0:T(8,128)S(1)}, u32[]{:S(2)}, u32[]{:S(2)}) collective-permute-start(f32[96,256]{1,0:T(8,128)S(1)} %get-tuple-element.24.face_hi_ref), channel_id=1, source_target_pairs={{0,1},{1,2},{2,3},{3,0},{4,5},{5,6},{6,7},{7,4},{8,9},{9,10},{10,1... | collective-permute-start | bytes 294920 | tf_op jit(solution)/shard_map/ppermute | solution.py:732
  5.3 1.6 %collective-permute-start.1 = (f32[96,256]{1,0:T(8,128)S(1)}, f32[96,256]{1,0:T(8,128)S(1)}, u32[]{:S(2)}, u32[]{:S(2)}) collective-permute-start(f32[96,256]{1,0:T(8,128)S(1)} %get-tuple-element.25.face_lo_ref), channel_id=1, source_target_pairs={{0,3},{1,0},{2,1},{3,2},{4,7},{5,4},{6,5},{7,6},{8,11},{9,8},{10,9... | collective-permute-start | bytes 294920 | tf_op jit(solution)/shard_map/ppermute | solution.py:732
  6.9 2.6 %collective-permute-done.zlo_ref = f32[96,256]{1,0:T(8,128)S(1)} collective-permute-done((f32[96,256]{1,0:T(8,128)S(1)}, f32[96,256]{1,0:T(8,128)S(1)}, u32[]{:S(2)}, u32[]{:S(2)}) %collective-permute-start) | collective-permute-done | bytes 98336 | tf_op jit(solution)/shard_map/ppermute | solution.py:732
  9.5 0.4 collective-permute-done.1.zhi_ref
  9.9 4.6 %collective-permute-start.2 = (f32[776,256]{1,0:T(8,128)S(1)}, f32[776,256]{1,0:T(8,128)S(1)}, u32[]{:S(2)}, u32[]{:S(2)}) collective-permute-start(f32[776,256]{1,0:T(8,128)S(1)} %get-tuple-element.28), channel_id=1, source_target_pairs={{0,124},{4,8},{8,4},{12,16},{16,12},{20,24},{24,20},{28,32},{32,28... | collective-permute-start | bytes 2383880 | tf_op jit(solution)/shard_map/ppermute | solution.py:743
  14.5 0.0 collective-permute-start.3
  14.5 3.0 %collective-permute-start.4 = (f32[8,24576]{1,0:T(8,128)S(1)}, f32[8,24576]{1,0:T(8,128)S(1)}, u32[]{:S(2)}, u32[]{:S(2)}) collective-permute-start(f32[8,24576]{1,0:T(8,128)S(1)} %get-tuple-element.32), channel_id=1, source_target_pairs={{0,3},{1,0},{2,1},{3,2},{4,7},{5,4},{6,5},{7,6},{8,11},{9,8},{10,9... | collective-permute-start | bytes 2359304 | tf_op jit(solution)/shard_map/ppermute | solution.py:732
  17.4 0.8 collective-permute-start.5
  18.3 0.7 collective-permute-start.6
  18.9 5.9 %collective-permute-done.2.outer_ref = f32[776,256]{1,0:T(8,128)S(1)} collective-permute-done((f32[776,256]{1,0:T(8,128)S(1)}, f32[776,256]{1,0:T(8,128)S(1)}, u32[]{:S(2)}, u32[]{:S(2)}) %collective-permute-start.2) | collective-permute-done | bytes 794656 | tf_op jit(solution)/shard_map/ppermute | solution.py:743
  24.8 0.0 collective-permute-done.3.inner_ref
  24.8 0.0 copy-done.3
  24.8 19.3 %stencil.1 = (f32[8,24576]{1,0:T(8,128)S(1)}, f32[8,6144]{1,0:T(8,128)S(1)}, f32[8,8192]{1,0:T(8,128)S(1)}, f32[8,6144]{1,0:T(8,128)S(1)}, f32[8,8192]{1,0:T(8,128)S(1)}, /*index=5*/f32[8,17920]{1,0:T(8,128)S(1)}) custom-call(f32[8]{0:T(128)S(1)} %copy-done.5, s32[1,256]{1,0:T(1,128)S(1)} %bitcast.6, f32[1,256]{1,0:T(1,128)S(1)} %bitcast.7, ...), custom_call_target="tpu_custom_call" | custom-call | tf_op jit(solution)/shard_map/stencil/pallas_call | solution.py:401
  44.1 0.0 copy-start.1
  44.1 0.0 copy-start.2
  44.1 0.0 copy-start.6
  44.2 7.6 %collective-permute-done.4.refs_2_ = f32[8,24576]{1,0:T(8,128)S(1)} collective-permute-done((f32[8,24576]{1,0:T(8,128)S(1)}, f32[8,24576]{1,0:T(8,128)S(1)}, u32[]{:S(2)}, u32[]{:S(2)}) %collective-permute-start.4) | collective-permute-done | bytes 786464 | tf_op jit(solution)/shard_map/ppermute | solution.py:732
  51.8 0.0 collective-permute-done.5.refs_3_
  51.8 3.7 %collective-permute-done.6.refs_4_ = f32[8,24576]{1,0:T(8,128)S(1)} collective-permute-done((f32[8,24576]{1,0:T(8,128)S(1)}, f32[8,24576]{1,0:T(8,128)S(1)}, u32[]{:S(2)}, u32[]{:S(2)}) %collective-permute-start.6) | collective-permute-done | bytes 786464 | tf_op jit(solution)/shard_map/ppermute | solution.py:732
  55.5 1.4 gram.1
  56.8 0.0 collective-permute-start.7
  56.9 1.2 collective-permute-done.7
  58.1 0.6 collective-permute-start.10
  58.7 1.4 collective-permute-start.9
  60.1 0.8 collective-permute-start.8
  60.9 0.9 collective-permute-done.10
  61.8 1.8 %collective-permute-done.9 = f32[40,128]{1,0:T(8,128)S(1)} collective-permute-done((f32[40,128]{1,0:T(8,128)S(1)}, f32[40,128]{1,0:T(8,128)S(1)}, u32[]{:S(2)}, u32[]{:S(2)}) %collective-permute-start.9) | collective-permute-done | bytes 20512 | tf_op jit(solution)/shard_map/ppermute | solution.py:496
  63.7 1.7 %collective-permute-done.8 = f32[40,128]{1,0:T(8,128)S(1)} collective-permute-done((f32[40,128]{1,0:T(8,128)S(1)}, f32[40,128]{1,0:T(8,128)S(1)}, u32[]{:S(2)}, u32[]{:S(2)}) %collective-permute-start.8) | collective-permute-done | bytes 20512 | tf_op jit(solution)/shard_map/ppermute | solution.py:496
  65.4 0.1 collective-permute-start.13
  65.5 2.0 %collective-permute-start.12 = (f32[40,128]{1,0:T(8,128)S(1)}, f32[40,128]{1,0:T(8,128)S(1)}, u32[]{:S(2)}, u32[]{:S(2)}) collective-permute-start(f32[40,128]{1,0:T(8,128)S(1)} %add_add_fusion.1), channel_id=1, source_target_pairs={{0,8},{4,12},{8,16},{12,20},{16,24},{20,28},{24,0},{28,4},{32,40},... | collective-permute-start | bytes 61448 | tf_op jit(solution)/shard_map/ppermute | solution.py:496
  67.5 0.0 collective-permute-start.11
  67.5 1.8 %collective-permute-done.13 = f32[40,128]{1,0:T(8,128)S(1)} collective-permute-done((f32[40,128]{1,0:T(8,128)S(1)}, f32[40,128]{1,0:T(8,128)S(1)}, u32[]{:S(2)}, u32[]{:S(2)}) %collective-permute-start.13) | collective-permute-done | bytes 20512 | tf_op jit(solution)/shard_map/ppermute | solution.py:496
  69.2 1.3 collective-permute-done.12
  70.5 2.2 %collective-permute-done.11 = f32[40,128]{1,0:T(8,128)S(1)} collective-permute-done((f32[40,128]{1,0:T(8,128)S(1)}, f32[40,128]{1,0:T(8,128)S(1)}, u32[]{:S(2)}, u32[]{:S(2)}) %collective-permute-start.11) | collective-permute-done | bytes 20512 | tf_op jit(solution)/shard_map/ppermute | solution.py:496
  72.8 0.8 collective-permute-start.16
  73.6 0.9 collective-permute-start.15
  74.5 1.0 collective-permute-start.14
  75.5 1.1 collective-permute-done.16.g3_ref
  76.6 2.2 %collective-permute-done.15.g2_ref = f32[40,128]{1,0:T(8,128)S(1)} collective-permute-done((f32[40,128]{1,0:T(8,128)S(1)}, f32[40,128]{1,0:T(8,128)S(1)}, u32[]{:S(2)}, u32[]{:S(2)}) %collective-permute-start.15) | collective-permute-done | bytes 20512 | tf_op jit(solution)/shard_map/ppermute | solution.py:496
  78.8 0.6 collective-permute-done.14.g1_ref
  79.5 7.3 %factor.1 = (f32[32,128]{1,0:T(8,128)S(1)}, f32[8,128]{1,0:T(8,128)S(1)}) custom-call(f32[40,128]{1,0:T(8,128)S(1)} %add_add_fusion.g0_ref, f32[40,128]{1,0:T(8,128)S(1)} %collective-permute-done.14.g1_ref, f32[40,128]{1,0:T(8,128)S(1)} %collective-permute-done.15.g2_ref, f32[40,128]{1,0:T(8,128)S(1)} %collective-permute-done.16.g3_ref, ...), custom_call_target="tpu_custom_call" | custom-call | tf_op jit(solution)/shard_map/factor/pallas_call | solution.py:593
  86.8 1.0 update.1
  87.8 1.9 %collective-permute-start.18 = (f32[8,24576]{1,0:T(8,128)S(1)}, f32[8,24576]{1,0:T(8,128)S(1)}, u32[]{:S(2)}, u32[]{:S(2)}) collective-permute-start(f32[8,24576]{1,0:T(8,128)S(1)} %get-tuple-element.38), channel_id=1, source_target_pairs={{0,3},{1,0},{2,1},{3,2},{4,7},{5,4},{6,5},{7,6},{8,11},{9,8},{10,9... | collective-permute-start | bytes 2359304 | tf_op jit(solution)/shard_map/ppermute | solution.py:732
  89.7 0.2 collective-permute-start.19
  89.9 3.0 %collective-permute-start.20 = (f32[8,6144]{1,0:T(8,128)S(1)}, f32[8,6144]{1,0:T(8,128)S(1)}, u32[]{:S(2)}, u32[]{:S(2)}) collective-permute-start(f32[8,6144]{1,0:T(8,128)S(1)} %get-tuple-element.40), channel_id=1, source_target_pairs={{0,3},{1,0},{2,1},{3,2},{4,7},{5,4},{6,5},{7,6},{8,11},{9,8},{10,9... | collective-permute-start | bytes 589832 | tf_op jit(solution)/shard_map/ppermute | solution.py:732
  92.9 0.0 collective-permute-start.22
  92.9 1.7 %collective-permute-start.21 = (f32[8,8192]{1,0:T(8,128)S(1)}, f32[8,8192]{1,0:T(8,128)S(1)}, u32[]{:S(2)}, u32[]{:S(2)}) collective-permute-start(f32[8,8192]{1,0:T(8,128)S(1)} %get-tuple-element.41), channel_id=1, source_target_pairs={{0,3},{1,0},{2,1},{3,2},{4,7},{5,4},{6,5},{7,6},{8,11},{9,8},{10,9... | collective-permute-start | bytes 786440 | tf_op jit(solution)/shard_map/ppermute | solution.py:732
  94.6 29.7 %collective-permute-done.20.refs_0_ = f32[8,6144]{1,0:T(8,128)S(1)} collective-permute-done((f32[8,6144]{1,0:T(8,128)S(1)}, f32[8,6144]{1,0:T(8,128)S(1)}, u32[]{:S(2)}, u32[]{:S(2)}) %collective-permute-start.20) | collective-permute-done | bytes 196640 | tf_op jit(solution)/shard_map/ppermute | solution.py:732
  124.3 0.0 collective-permute-start.23
  124.3 7.5 %collective-permute-done.23.refs_3_ = f32[8,6144]{1,0:T(8,128)S(1)} collective-permute-done((f32[8,6144]{1,0:T(8,128)S(1)}, f32[8,6144]{1,0:T(8,128)S(1)}, u32[]{:S(2)}, u32[]{:S(2)}) %collective-permute-start.23) | collective-permute-done | bytes 196640 | tf_op jit(solution)/shard_map/ppermute | solution.py:732
  131.8 1.0 collective-permute-start.17
  132.8 0.0 collective-permute-done.21.refs_1_
  132.8 1.9 %collective-permute-start.24 = (f32[8,8192]{1,0:T(8,128)S(1)}, f32[8,8192]{1,0:T(8,128)S(1)}, u32[]{:S(2)}, u32[]{:S(2)}) collective-permute-start(f32[8,8192]{1,0:T(8,128)S(1)} %get-tuple-element.44), channel_id=1, source_target_pairs={{0,1},{1,2},{2,3},{3,0},{4,5},{5,6},{6,7},{7,4},{8,9},{9,10},{10,1... | collective-permute-start | bytes 786440 | tf_op jit(solution)/shard_map/ppermute | solution.py:732
  134.7 0.5 slice_bitcast_fusion
  135.2 8.0 %collective-permute-done.24.refs_4_ = f32[8,8192]{1,0:T(8,128)S(1)} collective-permute-done((f32[8,8192]{1,0:T(8,128)S(1)}, f32[8,8192]{1,0:T(8,128)S(1)}, u32[]{:S(2)}, u32[]{:S(2)}) %collective-permute-start.24) | collective-permute-done | bytes 262176 | tf_op jit(solution)/shard_map/ppermute | solution.py:732
  143.2 0.0 collective-permute-done.22.refs_2_
  143.2 2.4 %own.1.refs_3_ = f32[8,98304]{1,0:T(8,128)} custom-call(s32[1]{0:T(128)} %bitcast.here_ref, f32[32,128]{1,0:T(8,128)S(1)} %get-tuple-element.35.mix_ref, f32[8,6144]{1,0:T(8,128)S(1)} %collective-permute-done.20.refs_0_, f32[8,8192]{1,0:T(8,128)S(1)} %collective-permute-done.21.refs_1_, f32[8,17920]{1,0:T(8,128)S(1)} %collective-permute-done.22.refs_2_, ...), custom_call_target="tpu_custom_call" | custom-call | tf_op jit(solution)/shard_map/own/pallas_call | solution.py:684
  145.6 0.0 collective-permute-done.18.refs_1_
  145.6 0.0 collective-permute-done.19.refs_2_
  145.6 1.4 join.2.refs_1_
  147.1 0.0 collective-permute-done.17.refs_0_
  147.1 0.8 join.3
  (13 shorter events, 0.1 us)
Async XLA Ops:
  0.6 24.2 %copy-start = (bf16[256,128]{1,0:T(8,128)(2,1)S(1)}, bf16[256,128]{1,0:T(8,128)(2,1)}, u32[]{:S(2)}) copy-start(bf16[256,128]{1,0:T(8,128)(2,1)} %constant.22.clone.sum_ref) | copy-start | bytes 196612
  0.6 24.2 %copy-start.3 = (s32[256]{0:T(256)S(1)}, s32[256]{0:T(256)}, u32[]{:S(2)}) copy-start(s32[256]{0:T(256)} %param.12) | copy-start | bytes 3076
  0.7 24.2 %copy-start.4 = (f32[256]{0:T(256)S(1)}, f32[256]{0:T(256)}, u32[]{:S(2)}) copy-start(f32[256]{0:T(256)} %param.13) | copy-start | bytes 3076
  0.7 24.2 %copy-start.5 = (f32[8]{0:T(128)S(1)}, f32[8]{0:T(128)}, u32[]{:S(2)}) copy-start(f32[8]{0:T(128)} %levels_ref.1) | copy-start | bytes 100
  3.6 5.9 %collective-permute-start = (f32[96,256]{1,0:T(8,128)S(1)}, f32[96,256]{1,0:T(8,128)S(1)}, u32[]{:S(2)}, u32[]{:S(2)}) collective-permute-start(f32[96,256]{1,0:T(8,128)S(1)} %get-tuple-element.24.face_hi_ref), channel_id=1, source_target_pairs={{0,1},{1,2},{2,3},{3,0},{4,5},{5,6},{6,7},{7,4},{8,9},{9,10},{10,1... | collective-permute-start | bytes 294920 | tf_op jit(solution)/shard_map/ppermute | solution.py:732
  5.3 4.6 %collective-permute-start.1 = (f32[96,256]{1,0:T(8,128)S(1)}, f32[96,256]{1,0:T(8,128)S(1)}, u32[]{:S(2)}, u32[]{:S(2)}) collective-permute-start(f32[96,256]{1,0:T(8,128)S(1)} %get-tuple-element.25.face_lo_ref), channel_id=1, source_target_pairs={{0,3},{1,0},{2,1},{3,2},{4,7},{5,4},{6,5},{7,6},{8,11},{9,8},{10,9... | collective-permute-start | bytes 294920 | tf_op jit(solution)/shard_map/ppermute | solution.py:732
  9.9 14.9 %collective-permute-start.2 = (f32[776,256]{1,0:T(8,128)S(1)}, f32[776,256]{1,0:T(8,128)S(1)}, u32[]{:S(2)}, u32[]{:S(2)}) collective-permute-start(f32[776,256]{1,0:T(8,128)S(1)} %get-tuple-element.28), channel_id=1, source_target_pairs={{0,124},{4,8},{8,4},{12,16},{16,12},{20,24},{24,20},{28,32},{32,28... | collective-permute-start | bytes 2383880 | tf_op jit(solution)/shard_map/ppermute | solution.py:743
  14.5 10.3 %collective-permute-start.3 = (f32[776,256]{1,0:T(8,128)S(1)}, f32[776,256]{1,0:T(8,128)S(1)}, u32[]{:S(2)}, u32[]{:S(2)}) collective-permute-start(f32[776,256]{1,0:T(8,128)S(1)} %get-tuple-element.29), channel_id=1, source_target_pairs={{0,4},{4,0},{8,12},{12,8},{16,20},{20,16},{24,28},{28,24},{32,36},... | collective-permute-start | bytes 2383880 | tf_op jit(solution)/shard_map/ppermute | solution.py:744
  14.5 37.3 %collective-permute-start.4 = (f32[8,24576]{1,0:T(8,128)S(1)}, f32[8,24576]{1,0:T(8,128)S(1)}, u32[]{:S(2)}, u32[]{:S(2)}) collective-permute-start(f32[8,24576]{1,0:T(8,128)S(1)} %get-tuple-element.32), channel_id=1, source_target_pairs={{0,3},{1,0},{2,1},{3,2},{4,7},{5,4},{6,5},{7,6},{8,11},{9,8},{10,9... | collective-permute-start | bytes 2359304 | tf_op jit(solution)/shard_map/ppermute | solution.py:732
  17.4 34.3 %collective-permute-start.5 = (f32[8,24576]{1,0:T(8,128)S(1)}, f32[8,24576]{1,0:T(8,128)S(1)}, u32[]{:S(2)}, u32[]{:S(2)}) collective-permute-start(f32[8,24576]{1,0:T(8,128)S(1)} %get-tuple-element.33), channel_id=1, source_target_pairs={{0,2},{1,3},{2,0},{3,1},{4,6},{5,7},{6,4},{7,5},{8,10},{9,11},{10,... | collective-permute-start | bytes 2359304 | tf_op jit(solution)/shard_map/ppermute | solution.py:732
  18.3 37.2 %collective-permute-start.6 = (f32[8,24576]{1,0:T(8,128)S(1)}, f32[8,24576]{1,0:T(8,128)S(1)}, u32[]{:S(2)}, u32[]{:S(2)}) collective-permute-start(f32[8,24576]{1,0:T(8,128)S(1)} %get-tuple-element.34), channel_id=1, source_target_pairs={{0,1},{1,2},{2,3},{3,0},{4,5},{5,6},{6,7},{7,4},{8,9},{9,10},{10,1... | collective-permute-start | bytes 2359304 | tf_op jit(solution)/shard_map/ppermute | solution.py:732
  44.1 35.4 %copy-start.1 = (f32[3,40,128]{2,1,0:T(8,128)S(1)}, f32[3,40,128]{2,1,0:T(8,128)}, u32[]{:S(2)}) copy-start(f32[3,40,128]{2,1,0:T(8,128)} %constant.24.clone.orient_ref) | copy-start | bytes 184324
  44.1 35.4 %copy-start.2 = (s32[3,40,128]{2,1,0:T(8,128)S(1)}, s32[3,40,128]{2,1,0:T(8,128)}, u32[]{:S(2)}) copy-start(s32[3,40,128]{2,1,0:T(8,128)} %constant.23.clone.partner_ref) | copy-start | bytes 184324
  44.1 35.4 %copy-start.6 = (s32[1,128]{1,0:T(1,128)S(1)}, s32[1,128]{1,0:T(1,128)}, u32[]{:S(2)}) copy-start(s32[1,128]{1,0:T(1,128)} %constant.25.clone.keep_ref) | copy-start | bytes 1540
  56.8 1.2 collective-permute-start.7
  58.1 3.8 %collective-permute-start.10 = (f32[40,128]{1,0:T(8,128)S(1)}, f32[40,128]{1,0:T(8,128)S(1)}, u32[]{:S(2)}, u32[]{:S(2)}) collective-permute-start(f32[40,128]{1,0:T(8,128)S(1)} %add.21), channel_id=1, source_target_pairs={{0,3},{1,0},{2,1},{3,2},{4,7},{5,4},{6,5},{7,6},{8,11},{9,8},{10,9... | collective-permute-start | bytes 61448 | tf_op jit(solution)/shard_map/ppermute | solution.py:496
  58.7 5.0 %collective-permute-start.9 = (f32[40,128]{1,0:T(8,128)S(1)}, f32[40,128]{1,0:T(8,128)S(1)}, u32[]{:S(2)}, u32[]{:S(2)}) collective-permute-start(f32[40,128]{1,0:T(8,128)S(1)} %add.21), channel_id=1, source_target_pairs={{0,1},{1,2},{2,3},{3,0},{4,5},{5,6},{6,7},{7,4},{8,9},{9,10},{10,1... | collective-permute-start | bytes 61448 | tf_op jit(solution)/shard_map/ppermute | solution.py:496
  60.1 5.3 %collective-permute-start.8 = (f32[40,128]{1,0:T(8,128)S(1)}, f32[40,128]{1,0:T(8,128)S(1)}, u32[]{:S(2)}, u32[]{:S(2)}) collective-permute-start(f32[40,128]{1,0:T(8,128)S(1)} %add.21), channel_id=1, source_target_pairs={{0,2},{1,3},{2,0},{3,1},{4,6},{5,7},{6,4},{7,5},{8,10},{9,11},{10,... | collective-permute-start | bytes 61448 | tf_op jit(solution)/shard_map/ppermute | solution.py:496
  65.4 3.8 %collective-permute-start.13 = (f32[40,128]{1,0:T(8,128)S(1)}, f32[40,128]{1,0:T(8,128)S(1)}, u32[]{:S(2)}, u32[]{:S(2)}) collective-permute-start(f32[40,128]{1,0:T(8,128)S(1)} %add_add_fusion.1), channel_id=1, source_target_pairs={{0,24},{4,28},{8,0},{12,4},{16,8},{20,12},{24,16},{28,20},{32,56},... | collective-permute-start | bytes 61448 | tf_op jit(solution)/shard_map/ppermute | solution.py:496
  65.5 5.1 %collective-permute-start.12 = (f32[40,128]{1,0:T(8,128)S(1)}, f32[40,128]{1,0:T(8,128)S(1)}, u32[]{:S(2)}, u32[]{:S(2)}) collective-permute-start(f32[40,128]{1,0:T(8,128)S(1)} %add_add_fusion.1), channel_id=1, source_target_pairs={{0,8},{4,12},{8,16},{12,20},{16,24},{20,28},{24,0},{28,4},{32,40},... | collective-permute-start | bytes 61448 | tf_op jit(solution)/shard_map/ppermute | solution.py:496
  67.5 5.3 %collective-permute-start.11 = (f32[40,128]{1,0:T(8,128)S(1)}, f32[40,128]{1,0:T(8,128)S(1)}, u32[]{:S(2)}, u32[]{:S(2)}) collective-permute-start(f32[40,128]{1,0:T(8,128)S(1)} %add_add_fusion.1), channel_id=1, source_target_pairs={{0,16},{4,20},{8,24},{12,28},{16,0},{20,4},{24,8},{28,12},{32,48},... | collective-permute-start | bytes 61448 | tf_op jit(solution)/shard_map/ppermute | solution.py:496
  72.8 3.8 %collective-permute-start.16 = (f32[40,128]{1,0:T(8,128)S(1)}, f32[40,128]{1,0:T(8,128)S(1)}, u32[]{:S(2)}, u32[]{:S(2)}) collective-permute-start(f32[40,128]{1,0:T(8,128)S(1)} %add_add_fusion.g0_ref), channel_id=1, source_target_pairs={{0,96},{4,100},{8,104},{12,108},{16,112},{20,116},{24,120},{28,124... | collective-permute-start | bytes 61448 | tf_op jit(solution)/shard_map/ppermute | solution.py:496
  73.6 5.3 %collective-permute-start.15 = (f32[40,128]{1,0:T(8,128)S(1)}, f32[40,128]{1,0:T(8,128)S(1)}, u32[]{:S(2)}, u32[]{:S(2)}) collective-permute-start(f32[40,128]{1,0:T(8,128)S(1)} %add_add_fusion.g0_ref), channel_id=1, source_target_pairs={{0,64},{4,68},{8,72},{12,76},{16,80},{20,84},{24,88},{28,92},{32,9... | collective-permute-start | bytes 61448 | tf_op jit(solution)/shard_map/ppermute | solution.py:496
  74.5 5.0 %collective-permute-start.14 = (f32[40,128]{1,0:T(8,128)S(1)}, f32[40,128]{1,0:T(8,128)S(1)}, u32[]{:S(2)}, u32[]{:S(2)}) collective-permute-start(f32[40,128]{1,0:T(8,128)S(1)} %add_add_fusion.g0_ref), channel_id=1, source_target_pairs={{0,32},{4,36},{8,40},{12,44},{16,48},{20,52},{24,56},{28,60},{32,6... | collective-permute-start | bytes 61448 | tf_op jit(solution)/shard_map/ppermute | solution.py:496
  87.8 57.8 %collective-permute-start.18 = (f32[8,24576]{1,0:T(8,128)S(1)}, f32[8,24576]{1,0:T(8,128)S(1)}, u32[]{:S(2)}, u32[]{:S(2)}) collective-permute-start(f32[8,24576]{1,0:T(8,128)S(1)} %get-tuple-element.38), channel_id=1, source_target_pairs={{0,3},{1,0},{2,1},{3,2},{4,7},{5,4},{6,5},{7,6},{8,11},{9,8},{10,9... | collective-permute-start | bytes 2359304 | tf_op jit(solution)/shard_map/ppermute | solution.py:732
  89.7 55.9 %collective-permute-start.19 = (f32[8,24576]{1,0:T(8,128)S(1)}, f32[8,24576]{1,0:T(8,128)S(1)}, u32[]{:S(2)}, u32[]{:S(2)}) collective-permute-start(f32[8,24576]{1,0:T(8,128)S(1)} %get-tuple-element.39), channel_id=1, source_target_pairs={{0,1},{1,2},{2,3},{3,0},{4,5},{5,6},{6,7},{7,4},{8,9},{9,10},{10,1... | collective-permute-start | bytes 2359304 | tf_op jit(solution)/shard_map/ppermute | solution.py:732
  89.9 34.4 %collective-permute-start.20 = (f32[8,6144]{1,0:T(8,128)S(1)}, f32[8,6144]{1,0:T(8,128)S(1)}, u32[]{:S(2)}, u32[]{:S(2)}) collective-permute-start(f32[8,6144]{1,0:T(8,128)S(1)} %get-tuple-element.40), channel_id=1, source_target_pairs={{0,3},{1,0},{2,1},{3,2},{4,7},{5,4},{6,5},{7,6},{8,11},{9,8},{10,9... | collective-permute-start | bytes 589832 | tf_op jit(solution)/shard_map/ppermute | solution.py:732
  92.9 50.2 %collective-permute-start.22 = (f32[8,17920]{1,0:T(8,128)S(1)}, f32[8,17920]{1,0:T(8,128)S(1)}, u32[]{:S(2)}, u32[]{:S(2)}) collective-permute-start(f32[8,17920]{1,0:T(8,128)S(1)} %get-tuple-element.42), channel_id=1, source_target_pairs={{0,2},{1,3},{2,0},{3,1},{4,6},{5,7},{6,4},{7,5},{8,10},{9,11},{10,... | collective-permute-start | bytes 1720328 | tf_op jit(solution)/shard_map/ppermute | solution.py:732
  92.9 39.8 %collective-permute-start.21 = (f32[8,8192]{1,0:T(8,128)S(1)}, f32[8,8192]{1,0:T(8,128)S(1)}, u32[]{:S(2)}, u32[]{:S(2)}) collective-permute-start(f32[8,8192]{1,0:T(8,128)S(1)} %get-tuple-element.41), channel_id=1, source_target_pairs={{0,3},{1,0},{2,1},{3,2},{4,7},{5,4},{6,5},{7,6},{8,11},{9,8},{10,9... | collective-permute-start | bytes 786440 | tf_op jit(solution)/shard_map/ppermute | solution.py:732
  124.3 7.5 %collective-permute-start.23 = (f32[8,6144]{1,0:T(8,128)S(1)}, f32[8,6144]{1,0:T(8,128)S(1)}, u32[]{:S(2)}, u32[]{:S(2)}) collective-permute-start(f32[8,6144]{1,0:T(8,128)S(1)} %get-tuple-element.43), channel_id=1, source_target_pairs={{0,1},{1,2},{2,3},{3,0},{4,5},{5,6},{6,7},{7,4},{8,9},{9,10},{10,1... | collective-permute-start | bytes 589832 | tf_op jit(solution)/shard_map/ppermute | solution.py:732
  131.8 15.3 %collective-permute-start.17 = (f32[8,10240]{1,0:T(8,128)S(1)}, f32[8,10240]{1,0:T(8,128)S(1)}, u32[]{:S(2)}, u32[]{:S(2)}) collective-permute-start(f32[8,10240]{1,0:T(8,128)S(1)} %get-tuple-element.36), channel_id=1, source_target_pairs={{0,2},{1,3},{2,0},{3,1},{4,6},{5,7},{6,4},{7,5},{8,10},{9,11},{10,... | collective-permute-start | bytes 983048 | tf_op jit(solution)/shard_map/ppermute | solution.py:732
  132.8 10.4 %collective-permute-start.24 = (f32[8,8192]{1,0:T(8,128)S(1)}, f32[8,8192]{1,0:T(8,128)S(1)}, u32[]{:S(2)}, u32[]{:S(2)}) collective-permute-start(f32[8,8192]{1,0:T(8,128)S(1)} %get-tuple-element.44), channel_id=1, source_target_pairs={{0,1},{1,2},{2,3},{3,0},{4,5},{5,6},{6,7},{7,4},{8,9},{9,10},{10,1... | collective-permute-start | bytes 786440 | tf_op jit(solution)/shard_map/ppermute | solution.py:732

commit v8 on v7

--- a/solution.py
+++ b/solution.py
@@ -21,8 +21,7 @@
 SMEM_SPEC = pl.BlockSpec(memory_space=pltpu.SMEM)
 
 
-SHARED = 14336
-EARLY = 6144
+SHARED = 12288
 FOLD = SHARED // 4
 
 PLACE = np.array([0, 1] + list(range(PAD, PAD + MODES)))
@@ -205,11 +204,10 @@
 def offer_copies(here, basis_hbm, refs, sems):
     cols = basis_hbm.shape[1] // 4
     copies = []
-    spans = ((3, 0, EARLY), (3, EARLY, SHARED), (1, 0, EARLY), (1, EARLY, SHARED), (0, 0, SHARED))
-    for i, (ref, (skip, first, last)) in enumerate(zip(refs, spans)):
-        at = pl.multiple_of(lax.rem(here + skip, 4) * cols + first, LANES)
-        source = basis_hbm.at[:, pl.ds(at, last - first)]
-        copies.append(pltpu.make_async_copy(source, ref.at[:, 0 : last - first], sems.at[i]))
+    for i, (ref, skip) in enumerate(zip(refs, (3, 1, 0))):
+        at = pl.multiple_of(lax.rem(here + skip, 4) * cols, LANES)
+        source = basis_hbm.at[:, pl.ds(at, SHARED)]
+        copies.append(pltpu.make_async_copy(source, ref.at[:, 0:SHARED], sems.at[i]))
     return copies
 
 
@@ -230,9 +228,7 @@
     inner_ref,
     out_ref,
     plus_ref,
-    plus_rest_ref,
     minus_ref,
-    minus_rest_ref,
     over_ref,
     field,
     first,
@@ -241,7 +237,7 @@
     offer_sems,
 ):
     comp = pl.program_id(0)
-    offer_refs = (plus_ref, plus_rest_ref, minus_ref, minus_rest_ref, over_ref)
+    offer_refs = (plus_ref, minus_ref, over_ref)
     offers = offer_copies(here_ref[0], basis_hbm, offer_refs, offer_sems)
     cx, cz, ny = vel_hbm.shape[1:]
     inner = pl.ds(PAD, cz)
@@ -414,16 +410,16 @@
             VMEM_SPEC,
             VMEM_SPEC,
         ],
-        out_specs=[VMEM_SPEC] * 6,
+        out_specs=[VMEM_SPEC] * 4,
         out_shape=[pltpu.VMEM((PAD, comps * cols), jnp.float32)]
-        + [pltpu.VMEM((PAD, size), jnp.float32) for size in (EARLY, SHARED - EARLY) * 2]
+        + [pltpu.VMEM((PAD, SHARED), jnp.float32)] * 2
         + [pltpu.VMEM((PAD, SHARED + FOLD), jnp.float32)],
         scratch_shapes=[
             pltpu.VMEM((comps, cx + 4, cz + 2 * PAD, ny), jnp.float32),
             pltpu.VMEM((cx + 2, cz + 2 * PAD, ny), jnp.float32),
             pltpu.VMEM((cz, ny), jnp.float32),
             pltpu.SemaphoreType.DMA((comps, 3, 2)),
-            pltpu.SemaphoreType.DMA((5,)),
+            pltpu.SemaphoreType.DMA((3,)),
         ],
         compiler_params=pltpu.CompilerParams(vmem_limit_bytes=20 << 20),
         name="stencil",
@@ -650,8 +646,8 @@
 
 
 def own_kernel(here_ref, mix_ref, *refs, cols, chunk):
-    hi_ref, hi_rest_ref, over_ref, lo_ref, lo_rest_ref = refs[:5]
-    basis_hbm, out_hbm, mine, snap, buf, in_sem, out_sem = refs[5:]
+    hi_ref, over_ref, lo_ref = refs[:3]
+    basis_hbm, out_hbm, mine, snap, buf, in_sem, out_sem = refs[3:]
     here = here_ref[0]
     tiles = SHARED // LANES
     spot = pl.ds(pl.multiple_of(lax.rem(here + 2, 4) * cols, LANES), SHARED)
@@ -667,12 +663,8 @@
     read.wait()
     for start in range(0, SHARED, chunk):
         at = slice(start, start + chunk)
-        if start < EARLY:
-            hi, lo = hi_ref[:, at], lo_ref[:, at]
-        else:
-            rest = slice(start - EARLY, start - EARLY + chunk)
-            hi, lo = hi_rest_ref[:, rest], lo_rest_ref[:, rest]
-        stack = jnp.concatenate([snap[:, at], mine[:, at], hi, over_ref[:, at], lo], axis=0)
+        rows = [snap, mine, hi_ref, over_ref, lo_ref]
+        stack = jnp.concatenate([ref[:, at] for ref in rows], axis=0)
         buf[:, at] = mixed(mix, stack)
     write = pltpu.make_async_copy(buf, out_hbm.at[:, spot], out_sem)
     write.start()
@@ -683,7 +675,7 @@
     cols = basis.shape[1] // 4
     return pl.pallas_call(
         functools.partial(own_kernel, cols=cols, chunk=chunk),
-        in_specs=[SMEM_SPEC] + [VMEM_SPEC] * 6 + [HBM_SPEC],
+        in_specs=[SMEM_SPEC] + [VMEM_SPEC] * 4 + [HBM_SPEC],
         out_specs=HBM_SPEC,
         out_shape=pltpu.HBM(basis.shape, jnp.float32),
         scratch_shapes=[pltpu.VMEM((PAD, SHARED), jnp.float32)] * 3
@@ -742,7 +734,7 @@
     pairs = [(i, (i + (1 if i % 2 else -1)) % n_space) for i in range(n_space)]
     outer = lax.ppermute(outer, "space", pairs)
     inner = lax.ppermute(inner, "space", [(i, i ^ 1) for i in range(n_space)])
-    snap, plus, plus_rest, minus, minus_rest, across = snapshots(
+    snap, plus, minus, across = snapshots(
         velocity,
         levels,
         profile_index,
@@ -757,10 +749,8 @@
     stack = (snap, block_own, hi, over, lo)
     total = gram(here, stack)
     total = ring_sum(total, ring_parts(total, "space", n_space, 1, 2))
+    total = ring_sum(total, ring_parts(total, "space", n_space, 2, 4))
     total = ring_sum(total, ring_parts(total, "mode", n_mode, 1, n_mode))
-    total = ring_sum(total, ring_parts(total, "space", n_space, 2, 4))
-    lo_rest = shifted(plus_rest, "mode", 1)
-    hi_rest = shifted(minus_rest, "mode", -1)
     parts = [total] + ring_parts(total, "space", n_space, 8, 4)
     over_early = shifted(across, "mode", 2)
     mix, sigma = factor(parts)
@@ -768,8 +758,7 @@
     back_lo = shifted(out_next, "mode", 1)
     back_hi = shifted(out_prev, "mode", -1)
     back_over = shifted(out_over, "mode", 2)
-    received = (hi_early, hi_rest, over_early, lo_early, lo_rest)
-    mine = own(here, mix, received, basis)
+    mine = own(here, mix, (hi_early, over_early, lo_early), basis)
     modes = join(here, {0: out_own, 1: back_hi, 3: back_lo}, mine)
     modes = join(here, {2: back_over}, modes)
     return (modes, sigma[0, :MODES])

time: 148 us -> 136 us (0.919)
  waiting for transfers between devices: 80.2 us -> 72 us
  starting transfers between devices: 29.7 us -> 26 us
    ppermute x13 -> x11, waiting for transfers between devices: 59.5 us -> 51.3 us  [shifted(): return lax.ppermute(x, axis, [(i, (i + by) % size) for i in range(size)])]
    ppermute x13 -> x11, starting transfers between devices: 17.4 us -> 13.7 us  [shifted(): return lax.ppermute(x, axis, [(i, (i + by) % size) for i in range(size)])]
  transfers between devices with their start and end apart: 25 -> 23, of which waited for: 18 -> 18; matrix products, arithmetic and copies ran while one was open for 0% -> 0% of each run, Pallas kernels for 16% -> 17%
where the time goes in v8:
time: 136 us; the launch traced here: 135 us
  waiting for transfers between devices  72 us (53%)
  Pallas kernels  35.9 us (26%)
  starting transfers between devices  26 us (19%)
    ppermute x11, waiting for transfers between devices, shifted(): return lax.ppermute(x, axis, [(i, (i + by) % size) for i in range(size)])  51.3 us
    pallas_call x1, Pallas kernels, snapshots(): pl.pallas_call(stencil_kernel, grid=(comps,), in_specs=[SMEM_SPEC, pl.Blo...  18.8 us
    ppermute x10, waiting for transfers between devices, ring_parts(): lax.ppermute(x, axis, pairs)  14.9 us
    ppermute x11, starting transfers between devices, shifted(): return lax.ppermute(x, axis, [(i, (i + by) % size) for i in range(size)])  13.7 us
    ppermute x10, starting transfers between devices, ring_parts(): lax.ppermute(x, axis, pairs)  7.73 us
    pallas_call x1, Pallas kernels, factor(): pl.pallas_call(factor_kernel, in_specs=[VMEM_SPEC] * 7, out_specs=(VMEM_S...  7.27 us
    ppermute x1, waiting for transfers between devices, program(): outer = lax.ppermute(outer, 'space', pairs)  5.88 us
    ppermute x1, starting transfers between devices, program(): outer = lax.ppermute(outer, 'space', pairs)  4.58 us
  transfers between devices with their start and end apart: 23, of which 18 were waited for; matrix products, arithmetic and copies ran while one was open for 0% of the time, Pallas kernels for 17%

profile of v8, /device:TPU:0, one launch (start us, length us, event | category | flops | bytes accessed | tf_op | source)
XLA Modules:
  0.0 135.3 jit_solution(3370456911212934774)
XLA Ops:
  0.6 0.0 copy-start
  0.6 0.0 copy-start.3
  0.7 0.0 copy-start.4
  0.7 0.0 copy-start.5
  0.7 2.9 %pack.1 = (f32[96,256]{1,0:T(8,128)S(1)}, f32[96,256]{1,0:T(8,128)S(1)}, f32[776,256]{1,0:T(8,128)S(1)}, f32[776,256]{1,0:T(8,128)S(1)}, f32[8,24576]{1,0:T(8,12...) custom-call(s32[1]{0:T(128)} %bitcast.here_ref, s32[1]{0:T(128)} %bitcast.3.core_ref, ...), custom_call_target="tpu_custom_call" | custom-call | tf_op jit(solution)/shard_map/pack/pallas_call | solution.py:119
  3.6 1.7 %collective-permute-start = (f32[96,256]{1,0:T(8,128)S(1)}, f32[96,256]{1,0:T(8,128)S(1)}, u32[]{:S(2)}, u32[]{:S(2)}) collective-permute-start(f32[96,256]{1,0:T(8,128)S(1)} %get-tuple-element.22.face_hi_ref), channel_id=1, source_target_pairs={{0,1},{1,2},{2,3},{3,0},{4,5},{5,6},{6,7},{7,4},{8,9},{9,10},{10,1... | collective-permute-start | bytes 294920 | tf_op jit(solution)/shard_map/ppermute | solution.py:724
  5.3 1.6 %collective-permute-start.1 = (f32[96,256]{1,0:T(8,128)S(1)}, f32[96,256]{1,0:T(8,128)S(1)}, u32[]{:S(2)}, u32[]{:S(2)}) collective-permute-start(f32[96,256]{1,0:T(8,128)S(1)} %get-tuple-element.23.face_lo_ref), channel_id=1, source_target_pairs={{0,3},{1,0},{2,1},{3,2},{4,7},{5,4},{6,5},{7,6},{8,11},{9,8},{10,9... | collective-permute-start | bytes 294920 | tf_op jit(solution)/shard_map/ppermute | solution.py:724
  6.9 2.6 %collective-permute-done.zlo_ref = f32[96,256]{1,0:T(8,128)S(1)} collective-permute-done((f32[96,256]{1,0:T(8,128)S(1)}, f32[96,256]{1,0:T(8,128)S(1)}, u32[]{:S(2)}, u32[]{:S(2)}) %collective-permute-start) | collective-permute-done | bytes 98336 | tf_op jit(solution)/shard_map/ppermute | solution.py:724
  9.5 0.4 collective-permute-done.1.zhi_ref
  9.9 4.6 %collective-permute-start.2 = (f32[776,256]{1,0:T(8,128)S(1)}, f32[776,256]{1,0:T(8,128)S(1)}, u32[]{:S(2)}, u32[]{:S(2)}) collective-permute-start(f32[776,256]{1,0:T(8,128)S(1)} %get-tuple-element.26), channel_id=1, source_target_pairs={{0,124},{4,8},{8,4},{12,16},{16,12},{20,24},{24,20},{28,32},{32,28... | collective-permute-start | bytes 2383880 | tf_op jit(solution)/shard_map/ppermute | solution.py:735
  14.5 0.0 collective-permute-start.3
  14.5 3.0 %collective-permute-start.4 = (f32[8,24576]{1,0:T(8,128)S(1)}, f32[8,24576]{1,0:T(8,128)S(1)}, u32[]{:S(2)}, u32[]{:S(2)}) collective-permute-start(f32[8,24576]{1,0:T(8,128)S(1)} %get-tuple-element.30), channel_id=1, source_target_pairs={{0,3},{1,0},{2,1},{3,2},{4,7},{5,4},{6,5},{7,6},{8,11},{9,8},{10,9... | collective-permute-start | bytes 2359304 | tf_op jit(solution)/shard_map/ppermute | solution.py:724
  17.4 0.8 collective-permute-start.5
  18.3 0.7 collective-permute-start.6
  18.9 5.9 %collective-permute-done.2.outer_ref = f32[776,256]{1,0:T(8,128)S(1)} collective-permute-done((f32[776,256]{1,0:T(8,128)S(1)}, f32[776,256]{1,0:T(8,128)S(1)}, u32[]{:S(2)}, u32[]{:S(2)}) %collective-permute-start.2) | collective-permute-done | bytes 794656 | tf_op jit(solution)/shard_map/ppermute | solution.py:735
  24.8 0.0 collective-permute-done.3.inner_ref
  24.8 0.0 copy-done
  24.8 0.0 copy-done.3
  24.8 18.8 %stencil.1 = (f32[8,24576]{1,0:T(8,128)S(1)}, f32[8,12288]{1,0:T(8,128)S(1)}, f32[8,12288]{1,0:T(8,128)S(1)}, f32[8,15360]{1,0:T(8,128)S(1)}) custom-call(f32[8]{0:T(128)S(1)} %copy-done.5, s32[1,256]{1,0:T(1,128)S(1)} %bitcast.6, f32[1,256]{1,0:T(1,128)S(1)} %bitcast.7, bf16[256,128]{1,0:T(8,128)(2,1)S(1)} %copy-done, ...), custom_call_target="tpu_custom_call" | custom-call | tf_op jit(solution)/shard_map/stencil/pallas_call | solution.py:397
  43.6 0.0 copy-start.1
  43.6 0.0 copy-start.2
  43.7 0.0 copy-start.6
  43.7 8.1 %collective-permute-done.4.refs_2_ = f32[8,24576]{1,0:T(8,128)S(1)} collective-permute-done((f32[8,24576]{1,0:T(8,128)S(1)}, f32[8,24576]{1,0:T(8,128)S(1)}, u32[]{:S(2)}, u32[]{:S(2)}) %collective-permute-start.4) | collective-permute-done | bytes 786464 | tf_op jit(solution)/shard_map/ppermute | solution.py:724
  51.8 0.0 collective-permute-done.5.refs_3_
  51.8 3.7 %collective-permute-done.6.refs_4_ = f32[8,24576]{1,0:T(8,128)S(1)} collective-permute-done((f32[8,24576]{1,0:T(8,128)S(1)}, f32[8,24576]{1,0:T(8,128)S(1)}, u32[]{:S(2)}, u32[]{:S(2)}) %collective-permute-start.6) | collective-permute-done | bytes 786464 | tf_op jit(solution)/shard_map/ppermute | solution.py:724
  55.5 1.4 %gram.1 = f32[40,128]{1,0:T(8,128)S(1)} custom-call(s32[1]{0:T(128)} %bitcast.here_ref, f32[8,24576]{1,0:T(8,128)S(1)} %get-tuple-element.28.refs_0_, f32[8,24576]{1,0:T(8,128)S(1)} %get-tuple-element.29.refs_1_, f32[8,24576]{1,0:T(8,128)S(1)} %collective-permute-done.4.refs_2_, f32[8,24576]{1,0:T(8,128)S(1)} %collective-permute-done.5.refs_3_, ...), custom_call_target="tpu_custom_call" | custom-call | tf_op jit(solution)/shard_map/gram/pallas_call | solution.py:470
  56.8 0.0 collective-permute-start.7
  56.9 1.2 collective-permute-done.7
  58.1 0.0 collective-permute-start.10
  58.1 2.0 %collective-permute-start.9 = (f32[40,128]{1,0:T(8,128)S(1)}, f32[40,128]{1,0:T(8,128)S(1)}, u32[]{:S(2)}, u32[]{:S(2)}) collective-permute-start(f32[40,128]{1,0:T(8,128)S(1)} %add.21), channel_id=1, source_target_pairs={{0,8},{4,12},{8,16},{12,20},{16,24},{20,28},{24,0},{28,4},{32,40},... | collective-permute-start | bytes 61448 | tf_op jit(solution)/shard_map/ppermute | solution.py:492
  60.1 0.0 collective-permute-start.8
  60.1 1.8 %collective-permute-done.10 = f32[40,128]{1,0:T(8,128)S(1)} collective-permute-done((f32[40,128]{1,0:T(8,128)S(1)}, f32[40,128]{1,0:T(8,128)S(1)}, u32[]{:S(2)}, u32[]{:S(2)}) %collective-permute-start.10) | collective-permute-done | bytes 20512 | tf_op jit(solution)/shard_map/ppermute | solution.py:492
  61.8 1.3 collective-permute-done.9
  63.1 2.2 %collective-permute-done.8 = f32[40,128]{1,0:T(8,128)S(1)} collective-permute-done((f32[40,128]{1,0:T(8,128)S(1)}, f32[40,128]{1,0:T(8,128)S(1)}, u32[]{:S(2)}, u32[]{:S(2)}) %collective-permute-start.8) | collective-permute-done | bytes 20512 | tf_op jit(solution)/shard_map/ppermute | solution.py:492
  65.4 0.7 collective-permute-start.13
  66.1 1.4 %collective-permute-start.12 = (f32[40,128]{1,0:T(8,128)S(1)}, f32[40,128]{1,0:T(8,128)S(1)}, u32[]{:S(2)}, u32[]{:S(2)}) collective-permute-start(f32[40,128]{1,0:T(8,128)S(1)} %add_add_fusion.1), channel_id=1, source_target_pairs={{0,1},{1,2},{2,3},{3,0},{4,5},{5,6},{6,7},{7,4},{8,9},{9,10},{10,1... | collective-permute-start | bytes 61448 | tf_op jit(solution)/shard_map/ppermute | solution.py:492
  67.5 0.8 collective-permute-start.11
  68.3 0.9 collective-permute-done.13
  69.2 1.8 %collective-permute-done.12 = f32[40,128]{1,0:T(8,128)S(1)} collective-permute-done((f32[40,128]{1,0:T(8,128)S(1)}, f32[40,128]{1,0:T(8,128)S(1)}, u32[]{:S(2)}, u32[]{:S(2)}) %collective-permute-start.12) | collective-permute-done | bytes 20512 | tf_op jit(solution)/shard_map/ppermute | solution.py:492
  71.0 1.7 %collective-permute-done.11 = f32[40,128]{1,0:T(8,128)S(1)} collective-permute-done((f32[40,128]{1,0:T(8,128)S(1)}, f32[40,128]{1,0:T(8,128)S(1)}, u32[]{:S(2)}, u32[]{:S(2)}) %collective-permute-start.11) | collective-permute-done | bytes 20512 | tf_op jit(solution)/shard_map/ppermute | solution.py:492
  72.8 0.8 collective-permute-start.16
  73.6 0.9 collective-permute-start.15
  74.5 1.0 collective-permute-start.14
  75.5 1.1 collective-permute-done.16.g3_ref
  76.6 2.2 %collective-permute-done.15.g2_ref = f32[40,128]{1,0:T(8,128)S(1)} collective-permute-done((f32[40,128]{1,0:T(8,128)S(1)}, f32[40,128]{1,0:T(8,128)S(1)}, u32[]{:S(2)}, u32[]{:S(2)}) %collective-permute-start.15) | collective-permute-done | bytes 20512 | tf_op jit(solution)/shard_map/ppermute | solution.py:492
  78.8 0.6 collective-permute-done.14.g1_ref
  79.5 7.3 %factor.1 = (f32[32,128]{1,0:T(8,128)S(1)}, f32[8,128]{1,0:T(8,128)S(1)}) custom-call(f32[40,128]{1,0:T(8,128)S(1)} %add_add_fusion.g0_ref, f32[40,128]{1,0:T(8,128)S(1)} %collective-permute-done.14.g1_ref, f32[40,128]{1,0:T(8,128)S(1)} %collective-permute-done.15.g2_ref, f32[40,128]{1,0:T(8,128)S(1)} %collective-permute-done.16.g3_ref, ...), custom_call_target="tpu_custom_call" | custom-call | tf_op jit(solution)/shard_map/factor/pallas_call | solution.py:589
  86.8 1.0 update.1
  87.8 1.9 %collective-permute-start.18 = (f32[8,24576]{1,0:T(8,128)S(1)}, f32[8,24576]{1,0:T(8,128)S(1)}, u32[]{:S(2)}, u32[]{:S(2)}) collective-permute-start(f32[8,24576]{1,0:T(8,128)S(1)} %get-tuple-element.36), channel_id=1, source_target_pairs={{0,3},{1,0},{2,1},{3,2},{4,7},{5,4},{6,5},{7,6},{8,11},{9,8},{10,9... | collective-permute-start | bytes 2359304 | tf_op jit(solution)/shard_map/ppermute | solution.py:724
  89.7 0.2 collective-permute-start.19
  89.9 3.0 %collective-permute-start.20 = (f32[8,12288]{1,0:T(8,128)S(1)}, f32[8,12288]{1,0:T(8,128)S(1)}, u32[]{:S(2)}, u32[]{:S(2)}) collective-permute-start(f32[8,12288]{1,0:T(8,128)S(1)} %get-tuple-element.38), channel_id=1, source_target_pairs={{0,3},{1,0},{2,1},{3,2},{4,7},{5,4},{6,5},{7,6},{8,11},{9,8},{10,9... | collective-permute-start | bytes 1179656 | tf_op jit(solution)/shard_map/ppermute | solution.py:724
  92.9 0.0 collective-permute-start.21
  92.9 0.9 collective-permute-start.22
  93.8 31.5 %collective-permute-done.20.refs_0_ = f32[8,12288]{1,0:T(8,128)S(1)} collective-permute-done((f32[8,12288]{1,0:T(8,128)S(1)}, f32[8,12288]{1,0:T(8,128)S(1)}, u32[]{:S(2)}, u32[]{:S(2)}) %collective-permute-start.20) | collective-permute-done | bytes 393248 | tf_op jit(solution)/shard_map/ppermute | solution.py:724
  125.3 0.0 collective-permute-start.17
  125.3 0.5 slice_bitcast_fusion
  125.8 2.9 %collective-permute-done.22.refs_2_ = f32[8,12288]{1,0:T(8,128)S(1)} collective-permute-done((f32[8,12288]{1,0:T(8,128)S(1)}, f32[8,12288]{1,0:T(8,128)S(1)}, u32[]{:S(2)}, u32[]{:S(2)}) %collective-permute-start.22) | collective-permute-done | bytes 393248 | tf_op jit(solution)/shard_map/ppermute | solution.py:724
  128.7 0.0 collective-permute-done.21.refs_1_
  128.7 2.3 %own.1.refs_3_ = f32[8,98304]{1,0:T(8,128)} custom-call(s32[1]{0:T(128)} %bitcast.here_ref, f32[32,128]{1,0:T(8,128)S(1)} %get-tuple-element.33.mix_ref, f32[8,12288]{1,0:T(8,128)S(1)} %collective-permute-done.20.refs_0_, f32[8,15360]{1,0:T(8,128)S(1)} %collective-permute-done.21.refs_1_, f32[8,12288]{1,0:T(8,128)S(1)} %collective-permute-done.22.refs_2_, ...), custom_call_target="tpu_custom_call" | custom-call | tf_op jit(solution)/shard_map/own/pallas_call | solution.py:676
  131.0 0.0 collective-permute-done.18.refs_1_
  131.0 0.0 collective-permute-done.19.refs_2_
  131.0 1.4 %join.2.refs_1_ = f32[8,98304]{1,0:T(8,128)} custom-call(s32[1]{0:T(128)} %bitcast.here_ref, f32[8,24576]{1,0:T(8,128)S(1)} %get-tuple-element.35.refs_0_, f32[8,24576]{1,0:T(8,128)S(1)} %collective-permute-done.18.refs_1_, f32[8,24576]{1,0:T(8,128)S(1)} %collective-permute-done.19.refs_2_, f32[8,98304]{1,0:T(8,128)} %own.1.refs_3_), custom_call_target="tpu_custom_call", output_to_operand_aliasing={{}: (4, {})} | custom-call | tf_op jit(solution)/shard_map/join/pallas_call | solution.py:704
  132.4 2.1 %collective-permute-done.17.refs_0_ = f32[8,12288]{1,0:T(8,128)S(1)} collective-permute-done((f32[8,12288]{1,0:T(8,128)S(1)}, f32[8,12288]{1,0:T(8,128)S(1)}, u32[]{:S(2)}, u32[]{:S(2)}) %collective-permute-start.17) | collective-permute-done | bytes 393248 | tf_op jit(solution)/shard_map/ppermute | solution.py:724
  134.6 0.8 join.3
  (9 shorter events, 0.0 us)
Async XLA Ops:
  0.6 24.2 %copy-start = (bf16[256,128]{1,0:T(8,128)(2,1)S(1)}, bf16[256,128]{1,0:T(8,128)(2,1)}, u32[]{:S(2)}) copy-start(bf16[256,128]{1,0:T(8,128)(2,1)} %constant.22.clone.sum_ref) | copy-start | bytes 196612
  0.6 24.2 %copy-start.3 = (s32[256]{0:T(256)S(1)}, s32[256]{0:T(256)}, u32[]{:S(2)}) copy-start(s32[256]{0:T(256)} %param.12) | copy-start | bytes 3076
  0.7 24.2 %copy-start.4 = (f32[256]{0:T(256)S(1)}, f32[256]{0:T(256)}, u32[]{:S(2)}) copy-start(f32[256]{0:T(256)} %param.13) | copy-start | bytes 3076
  0.7 24.2 %copy-start.5 = (f32[8]{0:T(128)S(1)}, f32[8]{0:T(128)}, u32[]{:S(2)}) copy-start(f32[8]{0:T(128)} %levels_ref.1) | copy-start | bytes 100
  3.6 5.9 %collective-permute-start = (f32[96,256]{1,0:T(8,128)S(1)}, f32[96,256]{1,0:T(8,128)S(1)}, u32[]{:S(2)}, u32[]{:S(2)}) collective-permute-start(f32[96,256]{1,0:T(8,128)S(1)} %get-tuple-element.22.face_hi_ref), channel_id=1, source_target_pairs={{0,1},{1,2},{2,3},{3,0},{4,5},{5,6},{6,7},{7,4},{8,9},{9,10},{10,1... | collective-permute-start | bytes 294920 | tf_op jit(solution)/shard_map/ppermute | solution.py:724
  5.3 4.6 %collective-permute-start.1 = (f32[96,256]{1,0:T(8,128)S(1)}, f32[96,256]{1,0:T(8,128)S(1)}, u32[]{:S(2)}, u32[]{:S(2)}) collective-permute-start(f32[96,256]{1,0:T(8,128)S(1)} %get-tuple-element.23.face_lo_ref), channel_id=1, source_target_pairs={{0,3},{1,0},{2,1},{3,2},{4,7},{5,4},{6,5},{7,6},{8,11},{9,8},{10,9... | collective-permute-start | bytes 294920 | tf_op jit(solution)/shard_map/ppermute | solution.py:724
  9.9 14.9 %collective-permute-start.2 = (f32[776,256]{1,0:T(8,128)S(1)}, f32[776,256]{1,0:T(8,128)S(1)}, u32[]{:S(2)}, u32[]{:S(2)}) collective-permute-start(f32[776,256]{1,0:T(8,128)S(1)} %get-tuple-element.26), channel_id=1, source_target_pairs={{0,124},{4,8},{8,4},{12,16},{16,12},{20,24},{24,20},{28,32},{32,28... | collective-permute-start | bytes 2383880 | tf_op jit(solution)/shard_map/ppermute | solution.py:735
  14.5 10.3 %collective-permute-start.3 = (f32[776,256]{1,0:T(8,128)S(1)}, f32[776,256]{1,0:T(8,128)S(1)}, u32[]{:S(2)}, u32[]{:S(2)}) collective-permute-start(f32[776,256]{1,0:T(8,128)S(1)} %get-tuple-element.27), channel_id=1, source_target_pairs={{0,4},{4,0},{8,12},{12,8},{16,20},{20,16},{24,28},{28,24},{32,36},... | collective-permute-start | bytes 2383880 | tf_op jit(solution)/shard_map/ppermute | solution.py:736
  14.5 37.3 %collective-permute-start.4 = (f32[8,24576]{1,0:T(8,128)S(1)}, f32[8,24576]{1,0:T(8,128)S(1)}, u32[]{:S(2)}, u32[]{:S(2)}) collective-permute-start(f32[8,24576]{1,0:T(8,128)S(1)} %get-tuple-element.30), channel_id=1, source_target_pairs={{0,3},{1,0},{2,1},{3,2},{4,7},{5,4},{6,5},{7,6},{8,11},{9,8},{10,9... | collective-permute-start | bytes 2359304 | tf_op jit(solution)/shard_map/ppermute | solution.py:724
  17.4 34.3 %collective-permute-start.5 = (f32[8,24576]{1,0:T(8,128)S(1)}, f32[8,24576]{1,0:T(8,128)S(1)}, u32[]{:S(2)}, u32[]{:S(2)}) collective-permute-start(f32[8,24576]{1,0:T(8,128)S(1)} %get-tuple-element.31), channel_id=1, source_target_pairs={{0,2},{1,3},{2,0},{3,1},{4,6},{5,7},{6,4},{7,5},{8,10},{9,11},{10,... | collective-permute-start | bytes 2359304 | tf_op jit(solution)/shard_map/ppermute | solution.py:724
  18.3 37.2 %collective-permute-start.6 = (f32[8,24576]{1,0:T(8,128)S(1)}, f32[8,24576]{1,0:T(8,128)S(1)}, u32[]{:S(2)}, u32[]{:S(2)}) collective-permute-start(f32[8,24576]{1,0:T(8,128)S(1)} %get-tuple-element.32), channel_id=1, source_target_pairs={{0,1},{1,2},{2,3},{3,0},{4,5},{5,6},{6,7},{7,4},{8,9},{9,10},{10,1... | collective-permute-start | bytes 2359304 | tf_op jit(solution)/shard_map/ppermute | solution.py:724
  43.6 35.9 %copy-start.1 = (f32[3,40,128]{2,1,0:T(8,128)S(1)}, f32[3,40,128]{2,1,0:T(8,128)}, u32[]{:S(2)}) copy-start(f32[3,40,128]{2,1,0:T(8,128)} %constant.24.clone.orient_ref) | copy-start | bytes 184324
  43.6 35.8 %copy-start.2 = (s32[3,40,128]{2,1,0:T(8,128)S(1)}, s32[3,40,128]{2,1,0:T(8,128)}, u32[]{:S(2)}) copy-start(s32[3,40,128]{2,1,0:T(8,128)} %constant.23.clone.partner_ref) | copy-start | bytes 184324
  43.7 35.8 %copy-start.6 = (s32[1,128]{1,0:T(1,128)S(1)}, s32[1,128]{1,0:T(1,128)}, u32[]{:S(2)}) copy-start(s32[1,128]{1,0:T(1,128)} %constant.25.clone.keep_ref) | copy-start | bytes 1540
  56.8 1.2 collective-permute-start.7
  58.1 3.8 %collective-permute-start.10 = (f32[40,128]{1,0:T(8,128)S(1)}, f32[40,128]{1,0:T(8,128)S(1)}, u32[]{:S(2)}, u32[]{:S(2)}) collective-permute-start(f32[40,128]{1,0:T(8,128)S(1)} %add.21), channel_id=1, source_target_pairs={{0,24},{4,28},{8,0},{12,4},{16,8},{20,12},{24,16},{28,20},{32,56},... | collective-permute-start | bytes 61448 | tf_op jit(solution)/shard_map/ppermute | solution.py:492
  58.1 5.1 %collective-permute-start.9 = (f32[40,128]{1,0:T(8,128)S(1)}, f32[40,128]{1,0:T(8,128)S(1)}, u32[]{:S(2)}, u32[]{:S(2)}) collective-permute-start(f32[40,128]{1,0:T(8,128)S(1)} %add.21), channel_id=1, source_target_pairs={{0,8},{4,12},{8,16},{12,20},{16,24},{20,28},{24,0},{28,4},{32,40},... | collective-permute-start | bytes 61448 | tf_op jit(solution)/shard_map/ppermute | solution.py:492
  60.1 5.3 %collective-permute-start.8 = (f32[40,128]{1,0:T(8,128)S(1)}, f32[40,128]{1,0:T(8,128)S(1)}, u32[]{:S(2)}, u32[]{:S(2)}) collective-permute-start(f32[40,128]{1,0:T(8,128)S(1)} %add.21), channel_id=1, source_target_pairs={{0,16},{4,20},{8,24},{12,28},{16,0},{20,4},{24,8},{28,12},{32,48},... | collective-permute-start | bytes 61448 | tf_op jit(solution)/shard_map/ppermute | solution.py:492
  65.4 3.8 %collective-permute-start.13 = (f32[40,128]{1,0:T(8,128)S(1)}, f32[40,128]{1,0:T(8,128)S(1)}, u32[]{:S(2)}, u32[]{:S(2)}) collective-permute-start(f32[40,128]{1,0:T(8,128)S(1)} %add_add_fusion.1), channel_id=1, source_target_pairs={{0,3},{1,0},{2,1},{3,2},{4,7},{5,4},{6,5},{7,6},{8,11},{9,8},{10,9... | collective-permute-start | bytes 61448 | tf_op jit(solution)/shard_map/ppermute | solution.py:492
  66.1 5.0 %collective-permute-start.12 = (f32[40,128]{1,0:T(8,128)S(1)}, f32[40,128]{1,0:T(8,128)S(1)}, u32[]{:S(2)}, u32[]{:S(2)}) collective-permute-start(f32[40,128]{1,0:T(8,128)S(1)} %add_add_fusion.1), channel_id=1, source_target_pairs={{0,1},{1,2},{2,3},{3,0},{4,5},{5,6},{6,7},{7,4},{8,9},{9,10},{10,1... | collective-permute-start | bytes 61448 | tf_op jit(solution)/shard_map/ppermute | solution.py:492
  67.5 5.3 %collective-permute-start.11 = (f32[40,128]{1,0:T(8,128)S(1)}, f32[40,128]{1,0:T(8,128)S(1)}, u32[]{:S(2)}, u32[]{:S(2)}) collective-permute-start(f32[40,128]{1,0:T(8,128)S(1)} %add_add_fusion.1), channel_id=1, source_target_pairs={{0,2},{1,3},{2,0},{3,1},{4,6},{5,7},{6,4},{7,5},{8,10},{9,11},{10,... | collective-permute-start | bytes 61448 | tf_op jit(solution)/shard_map/ppermute | solution.py:492
  72.8 3.8 %collective-permute-start.16 = (f32[40,128]{1,0:T(8,128)S(1)}, f32[40,128]{1,0:T(8,128)S(1)}, u32[]{:S(2)}, u32[]{:S(2)}) collective-permute-start(f32[40,128]{1,0:T(8,128)S(1)} %add_add_fusion.g0_ref), channel_id=1, source_target_pairs={{0,96},{4,100},{8,104},{12,108},{16,112},{20,116},{24,120},{28,124... | collective-permute-start | bytes 61448 | tf_op jit(solution)/shard_map/ppermute | solution.py:492
  73.6 5.3 %collective-permute-start.15 = (f32[40,128]{1,0:T(8,128)S(1)}, f32[40,128]{1,0:T(8,128)S(1)}, u32[]{:S(2)}, u32[]{:S(2)}) collective-permute-start(f32[40,128]{1,0:T(8,128)S(1)} %add_add_fusion.g0_ref), channel_id=1, source_target_pairs={{0,64},{4,68},{8,72},{12,76},{16,80},{20,84},{24,88},{28,92},{32,9... | collective-permute-start | bytes 61448 | tf_op jit(solution)/shard_map/ppermute | solution.py:492
  74.5 5.0 %collective-permute-start.14 = (f32[40,128]{1,0:T(8,128)S(1)}, f32[40,128]{1,0:T(8,128)S(1)}, u32[]{:S(2)}, u32[]{:S(2)}) collective-permute-start(f32[40,128]{1,0:T(8,128)S(1)} %add_add_fusion.g0_ref), channel_id=1, source_target_pairs={{0,32},{4,36},{8,40},{12,44},{16,48},{20,52},{24,56},{28,60},{32,6... | collective-permute-start | bytes 61448 | tf_op jit(solution)/shard_map/ppermute | solution.py:492
  87.8 43.2 %collective-permute-start.18 = (f32[8,24576]{1,0:T(8,128)S(1)}, f32[8,24576]{1,0:T(8,128)S(1)}, u32[]{:S(2)}, u32[]{:S(2)}) collective-permute-start(f32[8,24576]{1,0:T(8,128)S(1)} %get-tuple-element.36), channel_id=1, source_target_pairs={{0,3},{1,0},{2,1},{3,2},{4,7},{5,4},{6,5},{7,6},{8,11},{9,8},{10,9... | collective-permute-start | bytes 2359304 | tf_op jit(solution)/shard_map/ppermute | solution.py:724
  89.7 41.3 %collective-permute-start.19 = (f32[8,24576]{1,0:T(8,128)S(1)}, f32[8,24576]{1,0:T(8,128)S(1)}, u32[]{:S(2)}, u32[]{:S(2)}) collective-permute-start(f32[8,24576]{1,0:T(8,128)S(1)} %get-tuple-element.37), channel_id=1, source_target_pairs={{0,1},{1,2},{2,3},{3,0},{4,5},{5,6},{6,7},{7,4},{8,9},{9,10},{10,1... | collective-permute-start | bytes 2359304 | tf_op jit(solution)/shard_map/ppermute | solution.py:724
  89.9 35.4 %collective-permute-start.20 = (f32[8,12288]{1,0:T(8,128)S(1)}, f32[8,12288]{1,0:T(8,128)S(1)}, u32[]{:S(2)}, u32[]{:S(2)}) collective-permute-start(f32[8,12288]{1,0:T(8,128)S(1)} %get-tuple-element.38), channel_id=1, source_target_pairs={{0,3},{1,0},{2,1},{3,2},{4,7},{5,4},{6,5},{7,6},{8,11},{9,8},{10,9... | collective-permute-start | bytes 1179656 | tf_op jit(solution)/shard_map/ppermute | solution.py:724
  92.9 35.7 %collective-permute-start.21 = (f32[8,15360]{1,0:T(8,128)S(1)}, f32[8,15360]{1,0:T(8,128)S(1)}, u32[]{:S(2)}, u32[]{:S(2)}) collective-permute-start(f32[8,15360]{1,0:T(8,128)S(1)} %get-tuple-element.39), channel_id=1, source_target_pairs={{0,2},{1,3},{2,0},{3,1},{4,6},{5,7},{6,4},{7,5},{8,10},{9,11},{10,... | collective-permute-start | bytes 1474568 | tf_op jit(solution)/shard_map/ppermute | solution.py:724
  92.9 35.7 %collective-permute-start.22 = (f32[8,12288]{1,0:T(8,128)S(1)}, f32[8,12288]{1,0:T(8,128)S(1)}, u32[]{:S(2)}, u32[]{:S(2)}) collective-permute-start(f32[8,12288]{1,0:T(8,128)S(1)} %get-tuple-element.40), channel_id=1, source_target_pairs={{0,1},{1,2},{2,3},{3,0},{4,5},{5,6},{6,7},{7,4},{8,9},{9,10},{10,1... | collective-permute-start | bytes 1179656 | tf_op jit(solution)/shard_map/ppermute | solution.py:724
  125.3 9.3 %collective-permute-start.17 = (f32[8,12288]{1,0:T(8,128)S(1)}, f32[8,12288]{1,0:T(8,128)S(1)}, u32[]{:S(2)}, u32[]{:S(2)}) collective-permute-start(f32[8,12288]{1,0:T(8,128)S(1)} %get-tuple-element.34), channel_id=1, source_target_pairs={{0,2},{1,3},{2,0},{3,1},{4,6},{5,7},{6,4},{7,5},{8,10},{9,11},{10,... | collective-permute-start | bytes 1179656 | tf_op jit(solution)/shard_map/ppermute | solution.py:724
